TPU v7x, 32 devices: a whole 2x2x4 slice. The times are simulated.
32 devices in a mesh: row: 8 (over z, x), col: 4 (over y, core).
Axes of the slice: x: 2, y: 2, z: 4, core: 2. Of those that a mesh axis runs over, the one named last changes fastest.
Arguments:
- tokens: bfloat16 [2, 8192, 768], P(None, ('row', 'col')), may hold values from -6 to 6
- segments: int32 [2, 8192], P(None, ('row', 'col')), may hold values from 0 to 17, as said below
- positions: int32 [2, 8192], P(None, ('row', 'col')), may hold values from 0 to 799, as said below
- w_qkv: bfloat16 [768, 3, 768], P('row', None, 'col'), may hold values from -0.21875 to 0.21875
- w_out: bfloat16 [768, 768], P('col', 'row'), may hold values from -0.875 to 0.875
- w_gate_up: bfloat16 [768, 2, 3072], P('row', None, 'col'), may hold values from -0.21875 to 0.21875
- w_down: bfloat16 [3072, 768], P('col', 'row'), may hold values from -0.109375 to 0.109375
- norm_gain: bfloat16 [768, 2], P('row'), may hold values from 0.5 to 1.5
- norm_bias: bfloat16 [768, 2], P('row'), may hold values from -1.1953125 to 1.1953125
- cotangent: float32 [2, 8192, 768], P(None, ('row', 'col')), may hold values from -6 to 6
Outputs:
- layer_out: bfloat16 [2, 8192, 768], P(None, ('row', 'col'))
- input_grad: float32 [2, 8192, 768], P(None, ('row', 'col'))
- grad_qkv: float32 [768, 3, 768], P('row', None, 'col')
- grad_out: float32 [768, 768], P('col', 'row')
- grad_gate_up: float32 [768, 2, 3072], P('row', None, 'col')
- grad_down: float32 [3072, 768], P('col', 'row')
- grad_gain: float32 [768, 2], P('row')
- grad_bias: float32 [768, 2], P('row')
Inputs may be any that keep to these rules, and one draw needn't show every extreme that they name: `segments`: within each sequence documents are numbered from 0 upward and never fall; a document has at most 800 tokens and at least 60 unless it is the last of its sequence; some document has exactly 800 tokens, and in some sequence every document but the last has exactly 60 tokens. `positions`: the place of each token within its document, counted from 0.
All inputs are finite; a program needn't handle non-finite values.
Results may differ from a plain program's by a relative error of at most 0.017.
Values may be sent and summed in bfloat16 or wider, within the bound.
No kernel may reach another device: no remote copies, remote signals or barrier semaphores. Data moves between devices by JAX's collectives and lax.ppermute only.
A program may use at most 192 MiB of HBM per device.

v0:
```python
import math

import jax
import jax.numpy as jnp
from jax import lax
from jax.sharding import PartitionSpec as P

HD = 64
LEN = 1024


epsilon = 1e-12
rope_base = 1000.0
masked_score = -1e30


def in_blocks(array, dim, peers):
    dims = array.shape
    blocks = array.reshape(*dims[:dim], peers, dims[dim] // peers, *dims[dim + 1 :])
    return jnp.moveaxis(blocks, dim, 0)


def summed_on_arrival(array, axis, dim):
    blocks = in_blocks(array, dim, lax.axis_size(axis))
    arrived = lax.all_to_all(blocks, axis, split_axis=0, concat_axis=0, tiled=True)
    return arrived.astype(jnp.float32).sum(axis=0)


def sent_together(arrays, axis, dim, along):
    widths = [math.prod(a.shape[along:]) for a in arrays]
    both = jnp.concatenate(
        [a.reshape(*a.shape[:along], w) for a, w in zip(arrays, widths)], axis=along
    )
    out = summed_on_arrival(both, axis, dim)
    blocks = jnp.split(out, [sum(widths[:k]) for k in range(1, len(widths))], axis=along)
    return tuple((b.reshape(*out.shape[:along], *a.shape[along:]) for a, b in zip(arrays, blocks)))


def sent_together_2(arrays, axis, dim, along):
    widths = [a.shape[along] for a in arrays]
    both = jnp.concatenate(arrays, axis=along)
    out = summed_on_arrival(both, axis, dim)
    return tuple(jnp.split(out, [sum(widths[:k]) for k in range(1, len(widths))], axis=along))


def rope_tables(positions):
    half_dim = HD // 2
    freq = rope_base ** (-jnp.arange(half_dim, dtype=jnp.float32) / half_dim)
    angles = positions.astype(jnp.float32)[:, None] * freq[None, :]
    return (jnp.cos(angles), jnp.sin(angles))


def rotate(values, cosine, sine):
    half_dim = HD // 2
    first = values[..., :half_dim]
    second = values[..., half_dim:]
    cosine = cosine[:, None, :]
    sine = sine[:, None, :]
    return jnp.concatenate(
        [first * cosine - second * sine, second * cosine + first * sine], axis=-1
    )


def unrotate(grad_vals, cosine, sine):
    half_dim = HD // 2
    first = grad_vals[..., :half_dim]
    second = grad_vals[..., half_dim:]
    cosine = cosine[:, None, :]
    sine = sine[:, None, :]
    return jnp.concatenate(
        [first * cosine + second * sine, second * cosine - first * sine], axis=-1
    )


def normalize(hidden):
    centred = hidden - jnp.mean(hidden, axis=-1, keepdims=True)
    variance = jnp.mean(centred * centred, axis=-1, keepdims=True)
    inv_std = lax.rsqrt(variance + epsilon)
    return (centred * inv_std, inv_std)


def norm_back(grad_norm, normed, inv_std):
    return inv_std * (
        grad_norm
        - jnp.mean(grad_norm, axis=-1, keepdims=True)
        - normed * jnp.mean(grad_norm * normed, axis=-1, keepdims=True)
    )


def gather_tokens(values):
    return lax.all_gather(values, "col", axis=0, tiled=True)


def token_sums(left, right, contract):
    row_count = left.shape[0] // lax.axis_size("col")
    piece = lax.slice_in_dim(left, 0, lax.axis_size("col") * row_count, axis=0)
    return lax.psum_scatter(
        lax.dot_general(
            piece, right, (((1,), (contract,)), ((), ())), preferred_element_type=jnp.float32
        ).astype(jnp.bfloat16),
        "col",
        scatter_dimension=0,
        tiled=True,
    ).astype(jnp.float32)


def fetch_weights(w_qkv, w_out, w_gate_up, w_down, norm_gain, norm_bias):
    qkv_full, gate_up_full, gain_full, bias_full = (
        lax.all_gather(w_qkv, "row", axis=0, tiled=True),
        lax.all_gather(w_gate_up, "row", axis=0, tiled=True),
        lax.all_gather(norm_gain, "row", axis=0, tiled=True),
        lax.all_gather(norm_bias, "row", axis=0, tiled=True),
    )
    out_full, down_full = (
        lax.all_gather(w_out, "row", axis=1, tiled=True),
        lax.all_gather(w_down, "row", axis=1, tiled=True),
    )
    width = qkv_full.shape[0]
    return (
        qkv_full.reshape(width, -1),
        out_full,
        gate_up_full.reshape(width, -1),
        down_full,
        gain_full.astype(jnp.float32),
        bias_full.astype(jnp.float32),
    )


def key_window(seq_len, low_row):
    span = min(LEN, seq_len)
    return (low_row // span * span, span)


def attend(queries, keys, values, segment):
    seq_len = queries.shape[0]
    block_rows = min(512, LEN, seq_len)
    scale = 1.0 / math.sqrt(HD)
    outs_list = []
    totals_list = []
    for block_number in range(seq_len // block_rows):
        low_row = block_number * block_rows
        key_start, span = key_window(seq_len, low_row)
        rows_q = queries[low_row : low_row + block_rows]
        scores = (
            jnp.einsum("qhd,khd->hqk", rows_q, keys, preferred_element_type=jnp.float32) * scale
        )
        same_doc = (
            segment[low_row : low_row + block_rows, None]
            == segment[None, key_start : key_start + span]
        )
        scores = jnp.where(same_doc[None], scores, masked_score)
        row_max = jnp.max(scores, axis=-1, keepdims=True)
        expo = jnp.exp(scores - row_max)
        row_sum = jnp.sum(expo, axis=-1, keepdims=True)
        probs = (expo / row_sum).astype(jnp.bfloat16)
        outs_list.append(
            jnp.einsum("hqk,khd->qhd", probs, values, preferred_element_type=jnp.float32).astype(
                jnp.bfloat16
            )
        )
        totals_list.append(row_max + jnp.log(row_sum))
    return (jnp.concatenate(outs_list, axis=0), jnp.concatenate(totals_list, axis=1))


def attend_back(queries, keys, values, log_total, grad_att, segment):
    seq_len = queries.shape[0]
    block_rows = min(512, LEN, seq_len)
    scale = 1.0 / math.sqrt(HD)
    grad_q_list = []
    grad_k = jnp.zeros(keys.shape, jnp.float32)
    grad_v = jnp.zeros(values.shape, jnp.float32)
    for block_number in range(seq_len // block_rows):
        low_row = block_number * block_rows
        key_start, span = key_window(seq_len, low_row)
        rows_q = queries[low_row : low_row + block_rows]
        rows_grad = grad_att[low_row : low_row + block_rows]
        keys_seq = keys[key_start : key_start + span]
        values_seq = values[key_start : key_start + span]
        scores = (
            jnp.einsum("qhd,khd->hqk", rows_q, keys_seq, preferred_element_type=jnp.float32) * scale
        )
        same_doc = (
            segment[low_row : low_row + block_rows, None]
            == segment[None, key_start : key_start + span]
        )
        scores = jnp.where(same_doc[None], scores, masked_score)
        probs = jnp.exp(scores - log_total[:, low_row : low_row + block_rows])
        probs_low = probs.astype(jnp.bfloat16)
        grad_probs = jnp.einsum(
            "qhd,khd->hqk", rows_grad, values_seq, preferred_element_type=jnp.float32
        )
        delta_sum = jnp.sum(probs * grad_probs, axis=-1, keepdims=True)
        grad_scores = (probs * (grad_probs - delta_sum)).astype(jnp.bfloat16)
        grad_q_list.append(
            jnp.einsum("hqk,khd->qhd", grad_scores, keys_seq, preferred_element_type=jnp.float32)
            * scale
        )
        grad_k = grad_k.at[key_start : key_start + span].add(
            jnp.einsum("hqk,qhd->khd", grad_scores, rows_q, preferred_element_type=jnp.float32)
            * scale
        )
        grad_v = grad_v.at[key_start : key_start + span].add(
            jnp.einsum("hqk,qhd->khd", probs_low, rows_grad, preferred_element_type=jnp.float32)
        )
    return (jnp.concatenate(grad_q_list, axis=0), grad_k, grad_v)


def on_device(
    tokens, segments, positions, w_qkv, w_out, w_gate_up, w_down, norm_gain, norm_bias, cotangent
):
    doc_ids, doc_places = (
        lax.all_gather(segments, "col", axis=1, tiled=True),
        lax.all_gather(positions, "col", axis=1, tiled=True),
    )

    def current_weights():
        return fetch_weights(w_qkv, w_out, w_gate_up, w_down, norm_gain, norm_bias)

    def forward_step(carry, items):
        inputs, segment, place = items
        qkv_w, out_w, gate_up_w, down_w, gains, biases = current_weights()
        seq_inputs = gather_tokens(inputs)
        seq_len = seq_inputs.shape[0]
        proj = jnp.dot(seq_inputs, qkv_w, preferred_element_type=jnp.float32).reshape(
            seq_len, 3, -1, HD
        )
        cosine, sine = rope_tables(place)
        queries = rotate(proj[:, 0], cosine, sine).astype(jnp.bfloat16)
        keys = rotate(proj[:, 1], cosine, sine).astype(jnp.bfloat16)
        values = proj[:, 2].astype(jnp.bfloat16)
        attended, log_total = attend(queries, keys, values, segment)
        flat_attended = attended.reshape(seq_len, -1)
        branch = token_sums(flat_attended, out_w, 0)
        first_normed, first_inv = normalize(inputs.astype(jnp.float32) + branch)
        first_out = first_normed * gains[:, 0] + biases[:, 0]
        seq_normed = gather_tokens(first_out.astype(jnp.bfloat16))
        gate_up = jnp.dot(seq_normed, gate_up_w, preferred_element_type=jnp.float32)
        half_cols = gate_up.shape[1] // 2
        hidden = (jax.nn.silu(gate_up[:, :half_cols]) * gate_up[:, half_cols:]).astype(jnp.bfloat16)
        feed = token_sums(hidden, down_w, 0)
        second_normed, second_inv = normalize(first_out + feed)
        outputs = (second_normed * gains[:, 1] + biases[:, 1]).astype(jnp.bfloat16)
        kept = (
            seq_inputs,
            queries,
            keys,
            values,
            flat_attended,
            log_total,
            seq_normed,
            gate_up,
            first_normed,
            first_inv,
            second_normed,
            second_inv,
        )
        return (carry, (outputs, kept))

    unused, (layer_out, kept_all) = lax.scan(
        forward_step, jnp.zeros((), jnp.float32), (tokens, doc_ids, doc_places)
    )

    def backward_step(totals, items):
        grad_y, segment, place, kept = items
        (
            seq_inputs,
            queries,
            keys,
            values,
            flat_attended,
            log_total,
            seq_normed,
            gate_up,
            first_normed,
            first_inv,
            second_normed,
            second_inv,
        ) = kept
        total_qkv, total_out, total_gate_up, total_down, total_gain, total_bias = totals
        qkv_w, out_w, gate_up_w, down_w, gains, biases = current_weights()
        seq_len = seq_inputs.shape[0]
        gain_two = jnp.sum(grad_y * second_normed, axis=0)
        bias_two = jnp.sum(grad_y, axis=0)
        grad_h2 = norm_back(grad_y * gains[:, 1], second_normed, second_inv)
        seq_grad_feed = gather_tokens(grad_h2.astype(jnp.bfloat16))
        grad_hidden = lax.dot_general(
            seq_grad_feed, down_w, (((1,), (1,)), ((), ())), preferred_element_type=jnp.float32
        )
        half_cols = gate_up.shape[1] // 2
        gate = gate_up[:, :half_cols]
        up_part = gate_up[:, half_cols:]
        sigma = jax.nn.sigmoid(gate)
        silu_gate = gate * sigma
        grad_gate = grad_hidden * up_part * sigma * (1.0 + gate * (1.0 - sigma))
        grad_up = grad_hidden * silu_gate
        grad_gate_up = jnp.concatenate([grad_gate, grad_up], axis=1).astype(jnp.bfloat16)
        hidden = (silu_gate * up_part).astype(jnp.bfloat16)
        total_down = total_down + lax.dot_general(
            hidden, seq_grad_feed, (((0,), (0,)), ((), ())), preferred_element_type=jnp.float32
        )
        total_gate_up = total_gate_up + lax.dot_general(
            seq_normed, grad_gate_up, (((0,), (0,)), ((), ())), preferred_element_type=jnp.float32
        )
        grad_first = grad_h2 + token_sums(grad_gate_up, gate_up_w, 1)
        gain_one = jnp.sum(grad_first * first_normed, axis=0)
        bias_one = jnp.sum(grad_first, axis=0)
        grad_h1 = norm_back(grad_first * gains[:, 0], first_normed, first_inv)
        seq_grad_branch = gather_tokens(grad_h1.astype(jnp.bfloat16))
        total_out = total_out + lax.dot_general(
            flat_attended,
            seq_grad_branch,
            (((0,), (0,)), ((), ())),
            preferred_element_type=jnp.float32,
        )
        grad_att = lax.dot_general(
            seq_grad_branch, out_w, (((1,), (1,)), ((), ())), preferred_element_type=jnp.float32
        )
        grad_att = grad_att.astype(jnp.bfloat16).reshape(seq_len, -1, HD)
        grad_q, grad_k, grad_v = attend_back(queries, keys, values, log_total, grad_att, segment)
        cosine, sine = rope_tables(place)
        grad_proj = jnp.stack(
            [unrotate(grad_q, cosine, sine), unrotate(grad_k, cosine, sine), grad_v], axis=1
        )
        grad_proj = grad_proj.reshape(seq_len, -1).astype(jnp.bfloat16)
        total_qkv = total_qkv + lax.dot_general(
            seq_inputs, grad_proj, (((0,), (0,)), ((), ())), preferred_element_type=jnp.float32
        )
        grad_inputs = grad_h1 + token_sums(grad_proj, qkv_w, 1)
        total_gain = total_gain + jnp.stack([gain_one, gain_two], axis=1)
        total_bias = total_bias + jnp.stack([bias_one, bias_two], axis=1)
        return (
            (total_qkv, total_out, total_gate_up, total_down, total_gain, total_bias),
            grad_inputs,
        )

    width = tokens.shape[2]
    head_cols = w_qkv.shape[2]
    hidden_cols = w_gate_up.shape[2]
    zero_sums = (
        jnp.zeros((width, 3 * head_cols), jnp.float32),
        jnp.zeros((head_cols, width), jnp.float32),
        jnp.zeros((width, 2 * hidden_cols), jnp.float32),
        jnp.zeros((hidden_cols, width), jnp.float32),
        jnp.zeros((width, 2), jnp.float32),
        jnp.zeros((width, 2), jnp.float32),
    )
    totals, input_grad = lax.scan(
        backward_step, zero_sums, (cotangent, doc_ids, doc_places, kept_all)
    )
    total_qkv = totals[0].reshape(width, 3, head_cols)
    total_gate_up = totals[2].reshape(width, 2, hidden_cols)
    grad_qkv, grad_gate_up, grad_gain, grad_bias = sent_together(
        (
            total_qkv.astype(jnp.bfloat16),
            total_gate_up.astype(jnp.bfloat16),
            totals[4].astype(jnp.bfloat16),
            totals[5].astype(jnp.bfloat16),
        ),
        "row",
        0,
        1,
    )
    grad_out, grad_down = sent_together_2(
        (totals[1].astype(jnp.bfloat16), totals[3].astype(jnp.bfloat16)), "row", 1, 0
    )
    grad_gain, grad_bias = lax.psum((grad_gain, grad_bias), "col")
    return (
        layer_out,
        input_grad,
        grad_qkv,
        grad_out,
        grad_gate_up,
        grad_down,
        grad_gain,
        grad_bias,
    )


def solution(mesh):
    in_specs = (
        P(None, ("row", "col"), None),
        P(None, ("row", "col")),
        P(None, ("row", "col")),
        P("row", None, "col"),
        P("col", "row"),
        P("row", None, "col"),
        P("col", "row"),
        P("row", None),
        P("row", None),
        P(None, ("row", "col"), None),
    )
    out_specs = (
        P(None, ("row", "col"), None),
        P(None, ("row", "col"), None),
        P("row", None, "col"),
        P("col", "row"),
        P("row", None, "col"),
        P("col", "row"),
        P("row", None),
        P("row", None),
    )
    return jax.shard_map(
        on_device, mesh=mesh, in_specs=in_specs, out_specs=out_specs, check_vma=False
    )
```

profile of v0, /device:TPU:0, one launch (start us, length us, event | category | flops | bytes accessed | tf_op | source)
XLA Modules:
  0.0 1322.1 jit_solution(584793681520028164)
XLA Ops:
  7.3 6.4 all_gather.79
  13.8 6.9 all_gather.80
  25.1 542.4 %while.68 = (s32[]{:T(128)}, bf16[2,256,768]{2,1,0:T(8,128)(2,1)}, bf16[2,1024,768]{2,1,0:T(8,128)(2,1)}, bf16[2,1024,3,64]{1,3,2,0:T(8,128)(2,1)}, bf16[2,1024,...) while((s32[]{:T(128)}, bf16[2,256,768]{2,1,0:T(8,128)(2,1)}, ...), condition=%wide.region_11.12_spmd, body=%wide.region_0.11_spmd.sunk | while | flops 5697212928 | bytes 190405408 | solution.py:259
  26.1 37.9 %all_gather.99 = bf16[768,3,192]{2,1,0:T(4,128)(2,1)S(1)} all-gather(bf16[96,3,192]{2,1,0:T(4,128)(2,1)S(1)} %get-tuple-element.1742), channel_id=1, replica_groups=mesh['row'=8,'col'=4] {'row'}, dimensions={0}, use_global_device_ids=true | all-gather | bytes 995328 | tf_op jit(solution)/shard_map/while/body/eval_jaxpr/all_gather | solution.py:109
  66.8 31.1 %all_gather.100 = bf16[192,768]{0,1:T(8,128)(2,1)S(1)} all-gather(bf16[192,96]{0,1:T(8,128)(2,1)S(1)} %get-tuple-element.1745), channel_id=1, replica_groups=mesh['row'=8,'col'=4] {'row'}, dimensions={1}, use_global_device_ids=true | all-gather | bytes 331776 | tf_op jit(solution)/shard_map/while/body/eval_jaxpr/all_gather | solution.py:115
  115.7 18.5 %all-gather.11 = bf16[8,96,2]{1,2,0:T(2,128)(2,1)S(1)} all-gather(bf16[1,96,2]{1,2,0:T(2,128)(2,1)} %bitcast.350), channel_id=1, replica_groups=mesh['row'=8,'col'=4] {'row'}, dimensions={0}, use_global_device_ids=true | all-gather | bytes 3456 | tf_op jit(solution)/shard_map/while/body/eval_jaxpr/all_gather | solution.py:111
  134.3 16.4 %all-gather.10 = bf16[8,96,2]{1,2,0:T(2,128)(2,1)S(1)} all-gather(bf16[1,96,2]{1,2,0:T(2,128)(2,1)} %bitcast.349), channel_id=1, replica_groups=mesh['row'=8,'col'=4] {'row'}, dimensions={0}, use_global_device_ids=true | all-gather | bytes 3456 | tf_op jit(solution)/shard_map/while/body/eval_jaxpr/all_gather | solution.py:112
  157.1 38.9 %all-gather.28.cloned.1.call-done = bf16[768,2,768]{2,1,0:T(2,128)(2,1)} async-done(((bf16[96,2,768]{2,1,0:T(2,128)(2,1)}), bf16[768,2,768]{2,1,0:T(2,128)(2,1)}) %all-gather.28.cloned.1.call-update) | async-done | bytes 2359312 | tf_op jit(solution)/shard_map/while/body/eval_jaxpr/all_gather | solution.py:110
  198.1 18.2 %all-gather.26.cloned.1.call-done = bf16[1024,768]{1,0:T(8,128)(2,1)} async-done(((bf16[256,768]{1,0:T(8,128)(2,1)}), bf16[1024,768]{1,0:T(8,128)(2,1)}) %all-gather.26.cloned.1.call-update) | async-done | bytes 1572880 | tf_op jit(solution)/shard_map/while/body/eval_jaxpr/all_gather | solution.py:91
  216.3 7.5 bitcast_dynamic-update-slice_fusion.12
  223.8 35.6 %all-gather.22.cloned.1.call-done = bf16[768,768]{0,1:T(8,128)(2,1)} async-done(((bf16[768,96]{0,1:T(8,128)(2,1)}), bf16[768,768]{0,1:T(8,128)(2,1)}) %all-gather.22.cloned.1.call-update) | async-done | bytes 1179664 | tf_op jit(solution)/shard_map/while/body/eval_jaxpr/all_gather | solution.py:116
  259.5 6.2 convolution_convert_fusion.9
  276.4 16.5 %reduce-scatter.7.cloned.1.call-done = bf16[256,768]{1,0:T(8,128)(2,1)} async-done(((bf16[1024,768]{1,0:T(8,128)(2,1)}), bf16[256,768]{1,0:T(8,128)(2,1)}) %reduce-scatter.7.cloned.1.call-update) | async-done | bytes 393232 | tf_op jit(solution)/shard_map/while/body/eval_jaxpr/reduce_scatter | solution.py:97
  297.7 37.2 %all_gather.99 = bf16[768,3,192]{2,1,0:T(4,128)(2,1)S(1)} all-gather(bf16[96,3,192]{2,1,0:T(4,128)(2,1)S(1)} %get-tuple-element.1742), channel_id=1, replica_groups=mesh['row'=8,'col'=4] {'row'}, dimensions={0}, use_global_device_ids=true | all-gather | bytes 995328 | tf_op jit(solution)/shard_map/while/body/eval_jaxpr/all_gather | solution.py:109
  337.7 31.2 %all_gather.100 = bf16[192,768]{0,1:T(8,128)(2,1)S(1)} all-gather(bf16[192,96]{0,1:T(8,128)(2,1)S(1)} %get-tuple-element.1745), channel_id=1, replica_groups=mesh['row'=8,'col'=4] {'row'}, dimensions={1}, use_global_device_ids=true | all-gather | bytes 331776 | tf_op jit(solution)/shard_map/while/body/eval_jaxpr/all_gather | solution.py:115
  386.7 18.3 %all-gather.11 = bf16[8,96,2]{1,2,0:T(2,128)(2,1)S(1)} all-gather(bf16[1,96,2]{1,2,0:T(2,128)(2,1)} %bitcast.350), channel_id=1, replica_groups=mesh['row'=8,'col'=4] {'row'}, dimensions={0}, use_global_device_ids=true | all-gather | bytes 3456 | tf_op jit(solution)/shard_map/while/body/eval_jaxpr/all_gather | solution.py:111
  405.1 16.4 %all-gather.10 = bf16[8,96,2]{1,2,0:T(2,128)(2,1)S(1)} all-gather(bf16[1,96,2]{1,2,0:T(2,128)(2,1)} %bitcast.349), channel_id=1, replica_groups=mesh['row'=8,'col'=4] {'row'}, dimensions={0}, use_global_device_ids=true | all-gather | bytes 3456 | tf_op jit(solution)/shard_map/while/body/eval_jaxpr/all_gather | solution.py:112
  428.0 38.5 %all-gather.28.cloned.1.call-done = bf16[768,2,768]{2,1,0:T(2,128)(2,1)} async-done(((bf16[96,2,768]{2,1,0:T(2,128)(2,1)}), bf16[768,2,768]{2,1,0:T(2,128)(2,1)}) %all-gather.28.cloned.1.call-update) | async-done | bytes 2359312 | tf_op jit(solution)/shard_map/while/body/eval_jaxpr/all_gather | solution.py:110
  468.7 18.2 %all-gather.26.cloned.1.call-done = bf16[1024,768]{1,0:T(8,128)(2,1)} async-done(((bf16[256,768]{1,0:T(8,128)(2,1)}), bf16[1024,768]{1,0:T(8,128)(2,1)}) %all-gather.26.cloned.1.call-update) | async-done | bytes 1572880 | tf_op jit(solution)/shard_map/while/body/eval_jaxpr/all_gather | solution.py:91
  486.9 7.5 bitcast_dynamic-update-slice_fusion.12
  494.4 35.7 %all-gather.22.cloned.1.call-done = bf16[768,768]{0,1:T(8,128)(2,1)} async-done(((bf16[768,96]{0,1:T(8,128)(2,1)}), bf16[768,768]{0,1:T(8,128)(2,1)}) %all-gather.22.cloned.1.call-update) | async-done | bytes 1179664 | tf_op jit(solution)/shard_map/while/body/eval_jaxpr/all_gather | solution.py:116
  530.2 6.2 convolution_convert_fusion.9
  547.1 16.5 %reduce-scatter.7.cloned.1.call-done = bf16[256,768]{1,0:T(8,128)(2,1)} async-done(((bf16[1024,768]{1,0:T(8,128)(2,1)}), bf16[256,768]{1,0:T(8,128)(2,1)}) %reduce-scatter.7.cloned.1.call-update) | async-done | bytes 393232 | tf_op jit(solution)/shard_map/while/body/eval_jaxpr/reduce_scatter | solution.py:97
  568.7 603.9 %while.69 = (s32[]{:T(128)}, f32[768,576]{0,1:T(8,128)}, f32[192,768]{1,0:T(8,128)}, f32[768,1536]{1,0:T(8,128)}, f32[768,768]{1,0:T(8,128)}, /*index=5*/f32[768...) while((s32[]{:T(128)}, f32[768,576]{0,1:T(8,128)}, ...), condition=%wide.region_25.26_spmd.clone, body=%wide.region_12.25_spmd.clone.sunk | while | flops 11771122688 | bytes 393030208 | solution.py:347
  589.5 20.5 %all-gather.12 = bf16[8,96,2]{1,2,0:T(2,128)(2,1)S(1)} all-gather(bf16[1,96,2]{1,2,0:T(2,128)(2,1)} %bitcast.403), channel_id=1, replica_groups=mesh['row'=8,'col'=4] {'row'}, dimensions={0}, use_global_device_ids=true | all-gather | bytes 3456 | tf_op jit(solution)/shard_map/while/body/eval_jaxpr/all_gather | solution.py:111
  615.5 6.0 constant_dynamic-slice_fusion.22
  621.5 6.6 copy.127
  632.8 19.9 %all-gather.32.cloned.1.call-done = bf16[1024,768]{1,0:T(8,128)(2,1)} async-done(((bf16[256,768]{1,0:T(8,128)(2,1)}), bf16[1024,768]{1,0:T(8,128)(2,1)}) %all-gather.32.cloned.1.call-update) | async-done | bytes 1572880 | tf_op jit(solution)/shard_map/while/body/eval_jaxpr/all_gather | solution.py:91
  652.7 7.8 multiply_convert_fusion.13
  660.5 46.3 %all-gather.30.cloned.1.call-done = bf16[768,2,768]{2,1,0:T(2,128)(2,1)} async-done(((bf16[96,2,768]{2,1,0:T(2,128)(2,1)}), bf16[768,2,768]{2,1,0:T(2,128)(2,1)}) %all-gather.30.cloned.1.call-update) | async-done | bytes 2359312 | tf_op jit(solution)/shard_map/while/body/eval_jaxpr/all_gather | solution.py:110
  713.3 26.8 %reduce-scatter.9.cloned.1.call-done = bf16[256,768]{1,0:T(8,128)(2,1)} async-done(((bf16[1024,768]{1,0:T(8,128)(2,1)}), bf16[256,768]{1,0:T(8,128)(2,1)}) %reduce-scatter.9.cloned.1.call-update) | async-done | bytes 393232 | tf_op jit(solution)/shard_map/while/body/eval_jaxpr/reduce_scatter | solution.py:97
  744.3 37.3 %all_gather.108 = bf16[768,3,192]{2,1,0:T(4,128)(2,1)S(1)} all-gather(bf16[96,3,192]{2,1,0:T(4,128)(2,1)S(1)} %get-tuple-element.1842), channel_id=1, replica_groups=mesh['row'=8,'col'=4] {'row'}, dimensions={0}, use_global_device_ids=true | all-gather | bytes 995328 | tf_op jit(solution)/shard_map/while/body/eval_jaxpr/all_gather | solution.py:109
  784.5 31.0 %all_gather.107 = bf16[192,768]{0,1:T(8,128)(2,1)S(1)} all-gather(bf16[192,96]{0,1:T(8,128)(2,1)S(1)} %get-tuple-element.1837), channel_id=1, replica_groups=mesh['row'=8,'col'=4] {'row'}, dimensions={1}, use_global_device_ids=true | all-gather | bytes 331776 | tf_op jit(solution)/shard_map/while/body/eval_jaxpr/all_gather | solution.py:115
  852.9 7.5 select_add_fusion.7
  868.2 9.8 reduce-scatter.11.cloned.1.call-done
  880.8 20.6 %all-gather.12 = bf16[8,96,2]{1,2,0:T(2,128)(2,1)S(1)} all-gather(bf16[1,96,2]{1,2,0:T(2,128)(2,1)} %bitcast.403), channel_id=1, replica_groups=mesh['row'=8,'col'=4] {'row'}, dimensions={0}, use_global_device_ids=true | all-gather | bytes 3456 | tf_op jit(solution)/shard_map/while/body/eval_jaxpr/all_gather | solution.py:111
  913.0 6.6 copy.127
  924.1 19.9 %all-gather.32.cloned.1.call-done = bf16[1024,768]{1,0:T(8,128)(2,1)} async-done(((bf16[256,768]{1,0:T(8,128)(2,1)}), bf16[1024,768]{1,0:T(8,128)(2,1)}) %all-gather.32.cloned.1.call-update) | async-done | bytes 1572880 | tf_op jit(solution)/shard_map/while/body/eval_jaxpr/all_gather | solution.py:91
  944.0 7.8 multiply_convert_fusion.13
  951.8 46.5 %all-gather.30.cloned.1.call-done = bf16[768,2,768]{2,1,0:T(2,128)(2,1)} async-done(((bf16[96,2,768]{2,1,0:T(2,128)(2,1)}), bf16[768,2,768]{2,1,0:T(2,128)(2,1)}) %all-gather.30.cloned.1.call-update) | async-done | bytes 2359312 | tf_op jit(solution)/shard_map/while/body/eval_jaxpr/all_gather | solution.py:110
  1004.8 26.8 %reduce-scatter.9.cloned.1.call-done = bf16[256,768]{1,0:T(8,128)(2,1)} async-done(((bf16[1024,768]{1,0:T(8,128)(2,1)}), bf16[256,768]{1,0:T(8,128)(2,1)}) %reduce-scatter.9.cloned.1.call-update) | async-done | bytes 393232 | tf_op jit(solution)/shard_map/while/body/eval_jaxpr/reduce_scatter | solution.py:97
  1035.7 37.0 %all_gather.108 = bf16[768,3,192]{2,1,0:T(4,128)(2,1)S(1)} all-gather(bf16[96,3,192]{2,1,0:T(4,128)(2,1)S(1)} %get-tuple-element.1842), channel_id=1, replica_groups=mesh['row'=8,'col'=4] {'row'}, dimensions={0}, use_global_device_ids=true | all-gather | bytes 995328 | tf_op jit(solution)/shard_map/while/body/eval_jaxpr/all_gather | solution.py:109
  1075.6 31.2 %all_gather.107 = bf16[192,768]{0,1:T(8,128)(2,1)S(1)} all-gather(bf16[192,96]{0,1:T(8,128)(2,1)S(1)} %get-tuple-element.1837), channel_id=1, replica_groups=mesh['row'=8,'col'=4] {'row'}, dimensions={1}, use_global_device_ids=true | all-gather | bytes 331776 | tf_op jit(solution)/shard_map/while/body/eval_jaxpr/all_gather | solution.py:115
  1144.2 8.9 select_add_fusion.7
  1162.6 8.0 reduce-scatter.11.cloned.1.call-done
  1194.5 25.8 %all-to-all-done.1 = bf16[8,960,96]{1,2,0:T(8,128)(2,1)} async-done(((bf16[8,960,96]{1,2,0:T(8,128)(2,1)}), bf16[8,960,96]{1,2,0:T(8,128)(2,1)}, u32[]{:S(2)}, u32[]{:S(2)}) %all-to-all-start.1) | async-done | bytes 1474592 | tf_op jit(solution)/shard_map/all_to_all | solution.py:25
  1227.4 71.7 %all-to-all-done = bf16[8,96,2116]{2,1,0:T(8,128)(2,1)S(1)} async-done(((bf16[8,96,2116]{2,1,0:T(8,128)(2,1)}), bf16[8,96,2116]{2,1,0:T(8,128)(2,1)S(1)}, u32[]{:S(2)}, u32[]{:S(2)}) %all-to-all-start) | async-done | bytes 3250208 | tf_op jit(solution)/shard_map/all_to_all | solution.py:25
  1299.9 11.5 all-reduce
  (595 shorter events, 276.9 us)
Async XLA Ops:
  25.1 73.9 %copy-start.9 = (bf16[96,3,192]{2,1,0:T(4,128)(2,1)}, bf16[96,3,192]{2,1,0:T(4,128)(2,1)S(1)}, u32[]{:S(2)}) copy-start(bf16[96,3,192]{2,1,0:T(4,128)(2,1)S(1)} %get-tuple-element.1742) | copy-start | bytes 331780 | tf_op jit(solution)/shard_map/while
  25.1 73.9 %copy-start.25 = (bf16[192,96]{0,1:T(8,128)(2,1)}, bf16[192,96]{0,1:T(8,128)(2,1)S(1)}, u32[]{:S(2)}) copy-start(bf16[192,96]{0,1:T(8,128)(2,1)S(1)} %get-tuple-element.1745) | copy-start | bytes 110596 | tf_op jit(solution)/shard_map/while
  25.1 74.0 %all-gather.24.cloned.1.call-start = ((), (), s32[]{:S(2)}) async-start(), calls=%async_computation.7 | async-start | bytes 1966080 | tf_op jit(solution)/shard_map/while/body/eval_jaxpr/all_gather | solution.py:91
  26.0 125.4 %reduce-scatter.5.cloned.1.call-start = ((), (), s32[]{:S(2)}) async-start(), calls=%async_computation.8 | async-start | bytes 1966080 | tf_op jit(solution)/shard_map/while/body/eval_jaxpr/reduce_scatter | solution.py:97
  114.9 81.1 %all-gather.28.cloned.1.call-start = ((), (), s32[]{:S(2)}) async-start(), calls=%async_computation.10 | async-start | bytes 2654208 | tf_op jit(solution)/shard_map/while/body/eval_jaxpr/all_gather | solution.py:110
  115.6 100.7 %all-gather.26.cloned.1.call-start = ((), (), s32[]{:S(2)}) async-start(), calls=%async_computation.9 | async-start | bytes 1966080 | tf_op jit(solution)/shard_map/while/body/eval_jaxpr/all_gather | solution.py:91
  156.4 103.0 %all-gather.22.cloned.1.call-start = ((), (), s32[]{:S(2)}) async-start(), calls=%async_computation.6 | async-start | bytes 1327104 | tf_op jit(solution)/shard_map/while/body/eval_jaxpr/all_gather | solution.py:116
  157.0 135.8 %reduce-scatter.7.cloned.1.call-start = ((), (), s32[]{:S(2)}) async-start(), calls=%async_computation.11 | async-start | bytes 1966080 | tf_op jit(solution)/shard_map/while/body/eval_jaxpr/reduce_scatter | solution.py:97
  271.9 21.0 %copy-start.42 = (f32[256]{0:T(256)S(1)}, f32[256]{0:T(256)}, u32[]{:S(2)}) copy-start(f32[256]{0:T(256)} %copy-done.40) | copy-start | bytes 3076 | tf_op jit(solution)/shard_map/while
  271.9 21.0 %copy-start.45 = (f32[256]{0:T(256)S(1)}, f32[256]{0:T(256)}, u32[]{:S(2)}) copy-start(f32[256]{0:T(256)} %copy-done.43) | copy-start | bytes 3076 | tf_op jit(solution)/shard_map/while
  275.1 20.6 %copy-start.57 = (f32[2,256,1]{1,2,0:T(1,128)S(1)}, f32[2,256,1]{1,2,0:T(1,128)}, u32[]{:S(2)}) copy-start(f32[2,256,1]{1,2,0:T(1,128)} %get-tuple-element.1714) | copy-start | bytes 6148 | tf_op jit(solution)/shard_map/while
  275.1 20.6 %copy-start.46 = (f32[768]{0:T(1024)S(1)}, f32[768]{0:T(1024)}, u32[]{:S(2)}) copy-start(f32[768]{0:T(1024)} %get-tuple-element.1602) | copy-start | bytes 9220 | tf_op jit(solution)/shard_map/while
  275.1 20.6 %copy-start.47 = (f32[768]{0:T(1024)S(1)}, f32[768]{0:T(1024)}, u32[]{:S(2)}) copy-start(f32[768]{0:T(1024)} %get-tuple-element.1603) | copy-start | bytes 9220 | tf_op jit(solution)/shard_map/while
  296.8 73.3 %copy-start.9 = (bf16[96,3,192]{2,1,0:T(4,128)(2,1)}, bf16[96,3,192]{2,1,0:T(4,128)(2,1)S(1)}, u32[]{:S(2)}) copy-start(bf16[96,3,192]{2,1,0:T(4,128)(2,1)S(1)} %get-tuple-element.1742) | copy-start | bytes 331780 | tf_op jit(solution)/shard_map/while
  296.8 73.3 %copy-start.25 = (bf16[192,96]{0,1:T(8,128)(2,1)}, bf16[192,96]{0,1:T(8,128)(2,1)S(1)}, u32[]{:S(2)}) copy-start(bf16[192,96]{0,1:T(8,128)(2,1)S(1)} %get-tuple-element.1745) | copy-start | bytes 110596 | tf_op jit(solution)/shard_map/while
  296.8 73.4 %all-gather.24.cloned.1.call-start = ((), (), s32[]{:S(2)}) async-start(), calls=%async_computation.7 | async-start | bytes 1966080 | tf_op jit(solution)/shard_map/while/body/eval_jaxpr/all_gather | solution.py:91
  297.7 124.6 %reduce-scatter.5.cloned.1.call-start = ((), (), s32[]{:S(2)}) async-start(), calls=%async_computation.8 | async-start | bytes 1966080 | tf_op jit(solution)/shard_map/while/body/eval_jaxpr/reduce_scatter | solution.py:97
  386.0 80.6 %all-gather.28.cloned.1.call-start = ((), (), s32[]{:S(2)}) async-start(), calls=%async_computation.10 | async-start | bytes 2654208 | tf_op jit(solution)/shard_map/while/body/eval_jaxpr/all_gather | solution.py:110
  386.7 100.2 %all-gather.26.cloned.1.call-start = ((), (), s32[]{:S(2)}) async-start(), calls=%async_computation.9 | async-start | bytes 1966080 | tf_op jit(solution)/shard_map/while/body/eval_jaxpr/all_gather | solution.py:91
  427.3 102.9 %all-gather.22.cloned.1.call-start = ((), (), s32[]{:S(2)}) async-start(), calls=%async_computation.6 | async-start | bytes 1327104 | tf_op jit(solution)/shard_map/while/body/eval_jaxpr/all_gather | solution.py:116
  428.0 135.6 %reduce-scatter.7.cloned.1.call-start = ((), (), s32[]{:S(2)}) async-start(), calls=%async_computation.11 | async-start | bytes 1966080 | tf_op jit(solution)/shard_map/while/body/eval_jaxpr/reduce_scatter | solution.py:97
  542.6 21.0 %copy-start.42 = (f32[256]{0:T(256)S(1)}, f32[256]{0:T(256)}, u32[]{:S(2)}) copy-start(f32[256]{0:T(256)} %copy-done.40) | copy-start | bytes 3076 | tf_op jit(solution)/shard_map/while
  542.6 21.0 %copy-start.45 = (f32[256]{0:T(256)S(1)}, f32[256]{0:T(256)}, u32[]{:S(2)}) copy-start(f32[256]{0:T(256)} %copy-done.43) | copy-start | bytes 3076 | tf_op jit(solution)/shard_map/while
  545.8 20.6 %copy-start.57 = (f32[2,256,1]{1,2,0:T(1,128)S(1)}, f32[2,256,1]{1,2,0:T(1,128)}, u32[]{:S(2)}) copy-start(f32[2,256,1]{1,2,0:T(1,128)} %get-tuple-element.1714) | copy-start | bytes 6148 | tf_op jit(solution)/shard_map/while
  545.8 20.6 %copy-start.46 = (f32[768]{0:T(1024)S(1)}, f32[768]{0:T(1024)}, u32[]{:S(2)}) copy-start(f32[768]{0:T(1024)} %get-tuple-element.1602) | copy-start | bytes 9220 | tf_op jit(solution)/shard_map/while
  545.8 20.6 %copy-start.47 = (f32[768]{0:T(1024)S(1)}, f32[768]{0:T(1024)}, u32[]{:S(2)}) copy-start(f32[768]{0:T(1024)} %get-tuple-element.1603) | copy-start | bytes 9220 | tf_op jit(solution)/shard_map/while
  588.7 155.6 %copy-start.11 = (bf16[96,3,192]{2,1,0:T(4,128)(2,1)}, bf16[96,3,192]{2,1,0:T(4,128)(2,1)S(1)}, u32[]{:S(2)}) copy-start(bf16[96,3,192]{2,1,0:T(4,128)(2,1)S(1)} %get-tuple-element.1842) | copy-start | bytes 331780 | tf_op jit(solution)/shard_map/while
  588.7 195.8 %copy-start.27 = (bf16[192,96]{0,1:T(8,128)(2,1)}, bf16[192,96]{0,1:T(8,128)(2,1)S(1)}, u32[]{:S(2)}) copy-start(bf16[192,96]{0,1:T(8,128)(2,1)S(1)} %get-tuple-element.1837) | copy-start | bytes 110596 | tf_op jit(solution)/shard_map/while
  588.7 44.1 %all-gather.34.cloned.1.call-start = ((), (), s32[]{:S(2)}) async-start(), calls=%async_computation.14 | async-start | bytes 1327104 | tf_op jit(solution)/shard_map/while/body/eval_jaxpr/all_gather | solution.py:116
  589.4 63.2 %all-gather.32.cloned.1.call-start = ((), (), s32[]{:S(2)}) async-start(), calls=%async_computation.13 | async-start | bytes 1966080 | tf_op jit(solution)/shard_map/while/body/eval_jaxpr/all_gather | solution.py:91
  614.8 92.0 %all-gather.30.cloned.1.call-start = ((), (), s32[]{:S(2)}) async-start(), calls=%async_computation.12 | async-start | bytes 2654208 | tf_op jit(solution)/shard_map/while/body/eval_jaxpr/all_gather | solution.py:110
  615.4 124.7 %reduce-scatter.9.cloned.1.call-start = ((), (), s32[]{:S(2)}) async-start(), calls=%async_computation.15 | async-start | bytes 1966080 | tf_op jit(solution)/shard_map/while/body/eval_jaxpr/reduce_scatter | solution.py:97
  713.2 112.7 %all-gather.36.cloned.1.call-start = ((), (), s32[]{:S(2)}) async-start(), calls=%async_computation.16 | async-start | bytes 1966080 | tf_op jit(solution)/shard_map/while/body/eval_jaxpr/all_gather | solution.py:91
  741.7 42.8 %copy-start.56 = (f32[2,3,1024,1]{2,1,3,0:T(4,128)S(1)}, f32[2,3,1024,1]{2,1,3,0:T(4,128)}, u32[]{:S(2)}) copy-start(f32[2,3,1024,1]{2,1,3,0:T(4,128)} %get-tuple-element.1827) | copy-start | bytes 73732 | tf_op jit(solution)/shard_map/while
  744.2 71.9 %copy-start.6 = (bf16[2,1024,3,64]{1,3,2,0:T(8,128)(2,1)S(1)}, bf16[2,1024,3,64]{1,3,2,0:T(8,128)(2,1)}, u32[]{:S(2)}) copy-start(bf16[2,1024,3,64]{1,3,2,0:T(8,128)(2,1)} %get-tuple-element.1824) | copy-start | bytes 2359300 | tf_op jit(solution)/shard_map/while
  744.2 133.8 %reduce-scatter.11.cloned.1.call-start = ((), (), s32[]{:S(2)}) async-start(), calls=%async_computation.17 | async-start | bytes 1966080 | tf_op jit(solution)/shard_map/while/body/eval_jaxpr/reduce_scatter | solution.py:97
  880.0 155.7 %copy-start.11 = (bf16[96,3,192]{2,1,0:T(4,128)(2,1)}, bf16[96,3,192]{2,1,0:T(4,128)(2,1)S(1)}, u32[]{:S(2)}) copy-start(bf16[96,3,192]{2,1,0:T(4,128)(2,1)S(1)} %get-tuple-element.1842) | copy-start | bytes 331780 | tf_op jit(solution)/shard_map/while
  880.0 195.6 %copy-start.27 = (bf16[192,96]{0,1:T(8,128)(2,1)}, bf16[192,96]{0,1:T(8,128)(2,1)S(1)}, u32[]{:S(2)}) copy-start(bf16[192,96]{0,1:T(8,128)(2,1)S(1)} %get-tuple-element.1837) | copy-start | bytes 110596 | tf_op jit(solution)/shard_map/while
  880.0 44.1 %all-gather.34.cloned.1.call-start = ((), (), s32[]{:S(2)}) async-start(), calls=%async_computation.14 | async-start | bytes 1327104 | tf_op jit(solution)/shard_map/while/body/eval_jaxpr/all_gather | solution.py:116
  880.7 63.3 %all-gather.32.cloned.1.call-start = ((), (), s32[]{:S(2)}) async-start(), calls=%async_computation.13 | async-start | bytes 1966080 | tf_op jit(solution)/shard_map/while/body/eval_jaxpr/all_gather | solution.py:91
  906.1 92.1 %all-gather.30.cloned.1.call-start = ((), (), s32[]{:S(2)}) async-start(), calls=%async_computation.12 | async-start | bytes 2654208 | tf_op jit(solution)/shard_map/while/body/eval_jaxpr/all_gather | solution.py:110
  906.9 124.7 %reduce-scatter.9.cloned.1.call-start = ((), (), s32[]{:S(2)}) async-start(), calls=%async_computation.15 | async-start | bytes 1966080 | tf_op jit(solution)/shard_map/while/body/eval_jaxpr/reduce_scatter | solution.py:97
  1004.7 112.6 %all-gather.36.cloned.1.call-start = ((), (), s32[]{:S(2)}) async-start(), calls=%async_computation.16 | async-start | bytes 1966080 | tf_op jit(solution)/shard_map/while/body/eval_jaxpr/all_gather | solution.py:91
  1033.1 42.4 %copy-start.56 = (f32[2,3,1024,1]{2,1,3,0:T(4,128)S(1)}, f32[2,3,1024,1]{2,1,3,0:T(4,128)}, u32[]{:S(2)}) copy-start(f32[2,3,1024,1]{2,1,3,0:T(4,128)} %get-tuple-element.1827) | copy-start | bytes 73732 | tf_op jit(solution)/shard_map/while
  1035.6 71.8 %copy-start.6 = (bf16[2,1024,3,64]{1,3,2,0:T(8,128)(2,1)S(1)}, bf16[2,1024,3,64]{1,3,2,0:T(8,128)(2,1)}, u32[]{:S(2)}) copy-start(bf16[2,1024,3,64]{1,3,2,0:T(8,128)(2,1)} %get-tuple-element.1824) | copy-start | bytes 2359300 | tf_op jit(solution)/shard_map/while
  1035.6 134.9 %reduce-scatter.11.cloned.1.call-start = ((), (), s32[]{:S(2)}) async-start(), calls=%async_computation.17 | async-start | bytes 1966080 | tf_op jit(solution)/shard_map/while/body/eval_jaxpr/reduce_scatter | solution.py:97
  1177.7 42.6 %all-to-all-start.1 = ((bf16[8,960,96]{1,2,0:T(8,128)(2,1)}), bf16[8,960,96]{1,2,0:T(8,128)(2,1)}, u32[]{:S(2)}, u32[]{:S(2)}) async-start(bf16[8,960,96]{1,2,0:T(8,128)(2,1)} %bitcast.41), calls=%async_computation.5 | async-start | bytes 3145728 | tf_op jit(solution)/shard_map/all_to_all | solution.py:25
  1220.3 78.7 %all-to-all-start = ((bf16[8,96,2116]{2,1,0:T(8,128)(2,1)}), bf16[8,96,2116]{2,1,0:T(8,128)(2,1)S(1)}, u32[]{:S(2)}, u32[]{:S(2)}) async-start(bf16[8,96,2116]{2,1,0:T(8,128)(2,1)} %concatenate.100), calls=%async_computation.4 | async-start | bytes 6684672 | tf_op jit(solution)/shard_map/all_to_all | solution.py:25
  (123 other events, 633.4 us)
Sparse Core Ops, SparseCore 0:
  27.5 20.1 all-gather.23
  115.0 26.4 reduce-scatter.4
  143.9 52.0 all-gather.27
  198.1 18.1 all-gather.25
  218.3 41.0 all-gather.21
  265.9 26.9 reduce-scatter.6
  299.2 19.6 all-gather.23
  386.1 25.9 reduce-scatter.4
  414.5 52.0 all-gather.27
  468.6 18.1 all-gather.25
  489.1 41.0 all-gather.21
  536.6 26.9 reduce-scatter.6
  591.7 41.0 all-gather.33
  634.2 18.4 all-gather.31
  654.7 52.0 all-gather.29
  713.4 26.7 reduce-scatter.8
  744.3 19.6 all-gather.35
  851.6 26.3 reduce-scatter.10
  883.0 41.0 all-gather.33
  925.5 18.4 all-gather.31
  946.2 52.0 all-gather.29
  1004.8 26.6 reduce-scatter.8
  1035.7 19.6 all-gather.35
  1142.9 27.5 reduce-scatter.10
where the time goes:
time: 1340 us; the launch traced here: 1320 us
  waiting for transfers between devices  535 us (40%)
  blocking collectives  409 us (31%)
  matrix products  162 us (12%)
  local copies, waits for them, and re-layouts  95.7 us (7%)
  other arithmetic  73 us (5%)
  loops' own time  22.6 us (2%)
  between operations  14.7 us (1%)
    all_gather x4, waiting for transfers between devices, fetch_weights(): lax.all_gather(w_gate_up, 'row', axis=0, tiled=True)  170 us
    all_gather x4, blocking collectives, fetch_weights(): lax.all_gather(w_qkv, 'row', axis=0, tiled=True)  149 us
    all_gather x4, blocking collectives, fetch_weights(): lax.all_gather(w_out, 'row', axis=1, tiled=True)  124 us
    reduce_scatter x8, waiting for transfers between devices, token_sums(): lax.psum_scatter(lax.dot_general(piece, right, (((1,), (contract,)), ((),...  104 us
    all_to_all x2, waiting for transfers between devices, summed_on_arrival(): lax.all_to_all(blocks, axis, split_axis=0, concat_axis=0, tiled=True)  97.5 us
    all_gather x4, waiting for transfers between devices, fetch_weights(): lax.all_gather(w_down, 'row', axis=1, tiled=True)  80.7 us
    all_gather x4, blocking collectives, fetch_weights(): lax.all_gather(norm_gain, 'row', axis=0, tiled=True)  77.9 us
    all_gather x8, waiting for transfers between devices, gather_tokens(): return lax.all_gather(values, 'col', axis=0, tiled=True)  76.2 us
  transfers between devices with their start and end apart: 26, of which 20 were waited for; matrix products, arithmetic and copies ran while one was open for 14% of the time, Pallas kernels for 0%

commit v1 on v0

v1 whole, which is shorter than its diff:
```python
import functools
import math

import jax
import jax.numpy as jnp
from jax import lax
from jax.experimental import pallas as pl
from jax.experimental.pallas import tpu as pltpu
from jax.sharding import PartitionSpec as P

HD = 64
PAIR = 2 * HD
QROWS = 256
epsilon = 1e-12
rope_base = 1000.0
masked_score = -1e30
f32 = jnp.float32
bf16 = jnp.bfloat16

NN = (((1,), (0,)), ((), ()))
NT = (((1,), (1,)), ((), ()))
TN = (((0,), (0,)), ((), ()))


def dot(a, b, dims=NN):
    return lax.dot_general(a, b, dims, preferred_element_type=f32)


def rope_tables(positions, heads):
    half_dim = HD // 2
    freq = rope_base ** (-jnp.arange(half_dim, dtype=f32) / half_dim)
    angles = positions.astype(f32)[:, None] * freq[None, :]
    cosine, sine = jnp.cos(angles), jnp.sin(angles)
    return (
        jnp.concatenate([cosine, cosine], axis=1)[:, None, :],
        jnp.concatenate([-sine, sine], axis=1)[:, None, :],
    )


def rotate(values, cosine, sine):
    rows, width = values.shape
    heads = values.reshape(rows, width // HD, HD)
    swapped = jnp.concatenate([heads[..., HD // 2 :], heads[..., : HD // 2]], axis=-1)
    return (heads * cosine + swapped * sine).reshape(rows, width)


def normalize(hidden):
    centred = hidden - jnp.mean(hidden, axis=-1, keepdims=True)
    variance = jnp.mean(centred * centred, axis=-1, keepdims=True)
    inv_std = lax.rsqrt(variance + epsilon)
    return (centred * inv_std, inv_std)


def norm_back(grad_norm, normed, inv_std):
    return inv_std * (
        grad_norm
        - jnp.mean(grad_norm, axis=-1, keepdims=True)
        - normed * jnp.mean(grad_norm * normed, axis=-1, keepdims=True)
    )


def attend_kernel(q_ref, k_ref, v_ref, segq_ref, segk_ref, out_ref, log_ref):
    rows = q_ref.shape[0]
    low_half = lax.broadcasted_iota(jnp.int32, (QROWS, PAIR), 1) < HD
    keys = k_ref[...]
    values = v_ref[...]
    for block in range(rows // QROWS):
        span = slice(block * QROWS, (block + 1) * QROWS)
        q = q_ref[span, :]
        same = segq_ref[span, :] == segk_ref[...]
        bias = jnp.where(same, 0.0, masked_score)
        parts = []
        logs = []
        for head in range(2):
            mine = low_half if head == 0 else jnp.logical_not(low_half)
            scores = dot(jnp.where(mine, q, jnp.zeros_like(q)), keys, NT) + bias
            top = jnp.max(scores, axis=1, keepdims=True)
            expo = jnp.exp(scores - top)
            total = jnp.sum(expo, axis=1, keepdims=True)
            parts.append(dot(expo.astype(bf16), values) / total)
            logs.append(top + jnp.log(total))
        out_ref[span, :] = jnp.where(low_half, parts[0], parts[1]).astype(bf16)
        log_ref[0, span, :] = jnp.concatenate(logs, axis=1)


def attend(q, k, v, seg_q, seg_k):
    rows, width = q.shape
    keys = k.shape[0]
    pairs = width // PAIR
    return pl.pallas_call(
        attend_kernel,
        grid=(pairs,),
        in_specs=[
            pl.BlockSpec((rows, PAIR), lambda j: (0, j)),
            pl.BlockSpec((keys, PAIR), lambda j: (0, j)),
            pl.BlockSpec((keys, PAIR), lambda j: (0, j)),
            pl.BlockSpec((rows, 1), lambda j: (0, 0)),
            pl.BlockSpec((1, keys), lambda j: (0, 0)),
        ],
        out_specs=[
            pl.BlockSpec((rows, PAIR), lambda j: (0, j)),
            pl.BlockSpec((1, rows, 2), lambda j: (j, 0, 0)),
        ],
        out_shape=[
            jax.ShapeDtypeStruct((rows, width), bf16),
            jax.ShapeDtypeStruct((pairs, rows, 2), f32),
        ],
        cost_estimate=pl.CostEstimate(
            flops=16 * rows * keys * width, bytes_accessed=8 * keys * width, transcendentals=rows * keys * width // HD
        ),
        name="attend",
    )(q, k, v, seg_q[:, None], seg_k[None, :])


def attend_back_kernel(
    q_ref, k_ref, v_ref, do_ref, log_ref, delta_ref, segq_ref, segk_ref, dq_ref, dk_ref, dv_ref
):
    rows = q_ref.shape[0]
    low_half = lax.broadcasted_iota(jnp.int32, (QROWS, PAIR), 1) < HD
    low_out = lax.broadcasted_iota(jnp.int32, (k_ref.shape[0], PAIR), 1) < HD
    low_rows = lax.broadcasted_iota(jnp.int32, (PAIR, QROWS), 0) < HD
    keys = k_ref[...]
    values = v_ref[...]
    keys_t = keys.T
    for block in range(rows // QROWS):
        span = slice(block * QROWS, (block + 1) * QROWS)
        q = q_ref[span, :]
        do = do_ref[span, :]
        same = segk_ref[...] == segq_ref[:, span]
        bias = jnp.where(same, 0.0, masked_score)
        dq = []
        dk = []
        dv = []
        for head in range(2):
            mine = low_half if head == 0 else jnp.logical_not(low_half)
            scores = dot(keys, jnp.where(mine, q, jnp.zeros_like(q)), NT) + bias
            probs = jnp.exp(scores - log_ref[0, head : head + 1, span])
            dprobs = dot(values, jnp.where(mine, do, jnp.zeros_like(do)), NT)
            dscores = (probs * (dprobs - delta_ref[0, head : head + 1, span])).astype(bf16)
            dv.append(dot(probs.astype(bf16), do))
            dk.append(dot(dscores, q))
            dq.append(dot(keys_t, dscores))
        dq_ref[span, :] = (jnp.where(low_rows, dq[0], dq[1]) * (1.0 / math.sqrt(HD))).T
        dk_part = jnp.where(low_out, dk[0], dk[1])
        dv_part = jnp.where(low_out, dv[0], dv[1])
        if block == 0:
            dk_ref[...] = dk_part
            dv_ref[...] = dv_part
        else:
            dk_ref[...] += dk_part
            dv_ref[...] += dv_part


def attend_back(q, k, v, do, logs, delta, seg_q, seg_k):
    rows, width = q.shape
    keys = k.shape[0]
    pairs = width // PAIR
    by_pair = lambda j: (0, j)
    return pl.pallas_call(
        attend_back_kernel,
        grid=(pairs,),
        in_specs=[
            pl.BlockSpec((rows, PAIR), by_pair),
            pl.BlockSpec((keys, PAIR), by_pair),
            pl.BlockSpec((keys, PAIR), by_pair),
            pl.BlockSpec((rows, PAIR), by_pair),
            pl.BlockSpec((1, 2, rows), lambda j: (j, 0, 0)),
            pl.BlockSpec((1, 2, rows), lambda j: (j, 0, 0)),
            pl.BlockSpec((1, rows), lambda j: (0, 0)),
            pl.BlockSpec((keys, 1), lambda j: (0, 0)),
        ],
        out_specs=[
            pl.BlockSpec((rows, PAIR), by_pair),
            pl.BlockSpec((keys, PAIR), by_pair),
            pl.BlockSpec((keys, PAIR), by_pair),
        ],
        out_shape=[
            jax.ShapeDtypeStruct((rows, width), f32),
            jax.ShapeDtypeStruct((keys, width), f32),
            jax.ShapeDtypeStruct((keys, width), f32),
        ],
        cost_estimate=pl.CostEstimate(
            flops=40 * rows * keys * width, bytes_accessed=20 * keys * width, transcendentals=rows * keys * width // HD
        ),
        name="attend_back",
    )(q, k, v, do, logs, delta, seg_q[None, :], seg_k[:, None])


def on_device(
    tokens, segments, positions, w_qkv, w_out, w_gate_up, w_down, norm_gain, norm_bias, cotangent
):
    peers = lax.axis_size("col")
    rings = lax.axis_size("row")
    half = tokens.shape[0]
    side = lax.axis_index("col") // (peers // half)
    scale = 1.0 / math.sqrt(HD)

    def across(v):
        return lax.ppermute(v, "col", [(i, (i + peers // 2) % peers) for i in range(peers)])

    def beside(v):
        return lax.ppermute(v, "col", [(i, i ^ 1) for i in range(peers)])

    def to_sequence(v):
        own = lax.dynamic_index_in_dim(v, side, 0, keepdims=False)
        other = lax.dynamic_index_in_dim(v, 1 - side, 0, keepdims=False)
        return jnp.concatenate([own, across(other)], axis=0)

    def from_sequence(v):
        rows = v.shape[0] // 2
        came = across(v[rows:])
        own = v[:rows]
        first = side == 0
        return jnp.stack([jnp.where(first, own, came), jnp.where(first, came, own)], axis=0)

    depth = w_qkv.shape[0]
    width = tokens.shape[2]
    head_cols = w_qkv.shape[2]
    hid = w_gate_up.shape[2]

    norms = jnp.concatenate([norm_gain, norm_bias], axis=1)
    norms = jnp.pad(norms, ((0, 0), (0, 128 - norms.shape[1])))
    pack_a = jnp.concatenate([w_qkv.reshape(depth, -1), w_out.T, norms], axis=1)
    pack_b = jnp.concatenate([w_gate_up.reshape(depth, -1), w_down.T], axis=1)

    def gathered(v):
        return lax.all_gather(v, ("col", "row"), axis=0, tiled=True).reshape(peers, width, -1)

    full_a = gathered(pack_a)
    full_b = gathered(pack_b)

    x = to_sequence(tokens)
    seg_pos = to_sequence(jnp.stack([segments, positions], axis=2))
    seg = seg_pos[:, 0]
    seg_all = jnp.concatenate([seg, beside(seg)], axis=0)
    cosine, sine = rope_tables(seg_pos[:, 1], width // HD)
    dy = to_sequence(cotangent)

    def columns(lo):
        return jnp.concatenate(
            [full_a[c, :, lo : lo + head_cols] for c in range(peers)], axis=1
        )

    wq, wk, wv = columns(0), columns(head_cols), columns(2 * head_cols)
    wo_t = columns(3 * head_cols)
    gains = full_a[0, :, 4 * head_cols : 4 * head_cols + 2].astype(f32)
    biases = full_a[0, :, 4 * head_cols + 2 : 4 * head_cols + 4].astype(f32)

    q = (rotate(dot(x, wq), cosine, sine)).astype(bf16)
    k = rotate(dot(x, wk), cosine, sine).astype(bf16)
    v = dot(x, wv).astype(bf16)
    kv = jnp.concatenate([k, v], axis=1)
    kv_all = jnp.concatenate([kv, beside(kv)], axis=0)
    k_all = kv_all[:, :width]
    v_all = kv_all[:, width:]
    q_small = q * jnp.asarray(scale, bf16)
    attended, logs = attend(q_small, k_all, v_all, seg, seg_all)
    branch = dot(attended, wo_t, NT)
    n1, s1 = normalize(x.astype(f32) + branch)
    first = n1 * gains[:, 0] + biases[:, 0]
    first_low = first.astype(bf16)
    gates = []
    ups = []
    feed = jnp.zeros(first.shape, f32)
    for c in range(peers):
        gates.append(dot(first_low, full_b[c, :, :hid]))
        ups.append(dot(first_low, full_b[c, :, hid : 2 * hid]))
        hidden = (jax.nn.silu(gates[c]) * ups[c]).astype(bf16)
        feed = feed + dot(hidden, full_b[c, :, 2 * hid :], NT)
    n2, s2 = normalize(first + feed)
    layer_out = (n2 * gains[:, 1] + biases[:, 1]).astype(bf16)

    gain_two = jnp.sum(dy * n2, axis=0)
    bias_two = jnp.sum(dy, axis=0)
    dh2 = norm_back(dy * gains[:, 1], n2, s2)
    dfeed = dh2.astype(bf16)
    dfirst = dh2
    grads_b = []
    for c in range(peers):
        dhidden = dot(dfeed, full_b[c, :, 2 * hid :])
        sg = jax.nn.sigmoid(gates[c])
        silu = gates[c] * sg
        dgate = (dhidden * ups[c] * sg * (1.0 + gates[c] * (1.0 - sg))).astype(bf16)
        dup = (dhidden * silu).astype(bf16)
        hidden = (silu * ups[c]).astype(bf16)
        grads_b.append(
            jnp.concatenate(
                [
                    dot(first_low, dgate, TN).astype(bf16),
                    dot(first_low, dup, TN).astype(bf16),
                    dot(dfeed, hidden, TN).astype(bf16),
                ],
                axis=1,
            )
        )
        dfirst = (
            dfirst
            + dot(dgate, full_b[c, :, :hid], NT)
            + dot(dup, full_b[c, :, hid : 2 * hid], NT)
        )

    def scattered(grads):
        both = jnp.stack(grads, axis=0).reshape(peers * width, -1)
        return lax.psum_scatter(both, ("col", "row"), scatter_dimension=0, tiled=True).astype(f32)

    own_b = scattered(grads_b)

    gain_one = jnp.sum(dfirst * n1, axis=0)
    bias_one = jnp.sum(dfirst, axis=0)
    dh1 = norm_back(dfirst * gains[:, 0], n1, s1)
    dbranch = dh1.astype(bf16)
    do = dot(dbranch, wo_t).astype(bf16)
    delta = jnp.sum(
        (do.astype(f32) * attended.astype(f32)).reshape(do.shape[0], -1, 2, HD), axis=3
    )
    dq, dk, dv = attend_back(
        q_small,
        k_all,
        v_all,
        do,
        logs.transpose(0, 2, 1),
        delta.transpose(1, 2, 0),
        seg,
        seg_all,
    )
    rows = x.shape[0]
    dkv = jnp.concatenate([dk, dv], axis=1)
    dkv_sum = dkv[:rows] + beside(dkv[rows:].astype(bf16)).astype(f32)
    dproj = jnp.concatenate(
        [rotate(dq, cosine, -sine), rotate(dkv_sum[:, :width], cosine, -sine), dkv_sum[:, width:]],
        axis=1,
    ).astype(bf16)
    d_qkv = dot(x, dproj, TN).astype(bf16)
    d_out = dot(dbranch, attended, TN).astype(bf16)
    grads_a = []
    for c in range(peers):
        lo = c * head_cols
        grads_a.append(
            jnp.concatenate(
                [d_qkv[:, p * width + lo : p * width + lo + head_cols] for p in range(3)]
                + [d_out[:, lo : lo + head_cols]],
                axis=1,
            )
        )
    own_a = scattered(grads_a)
    w_all = jnp.concatenate([wq, wk, wv], axis=1)
    input_grad = from_sequence(dh1 + dot(dproj, w_all, NT))
    layer_out = from_sequence(layer_out)

    small = lax.psum(
        jnp.stack([gain_one, gain_two, bias_one, bias_two], axis=1), ("row", "col")
    )
    small = lax.dynamic_slice_in_dim(small, lax.axis_index("row") * depth, depth, axis=0)
    return (
        layer_out,
        input_grad,
        own_a[:, : 3 * head_cols].reshape(depth, 3, head_cols),
        own_a[:, 3 * head_cols :].T,
        own_b[:, : 2 * hid].reshape(depth, 2, hid),
        own_b[:, 2 * hid :].T,
        small[:, :2],
        small[:, 2:],
    )


def solution(mesh):
    in_specs = (
        P(None, ("row", "col"), None),
        P(None, ("row", "col")),
        P(None, ("row", "col")),
        P("row", None, "col"),
        P("col", "row"),
        P("row", None, "col"),
        P("col", "row"),
        P("row", None),
        P("row", None),
        P(None, ("row", "col"), None),
    )
    out_specs = (
        P(None, ("row", "col"), None),
        P(None, ("row", "col"), None),
        P("row", None, "col"),
        P("col", "row"),
        P("row", None, "col"),
        P("col", "row"),
        P("row", None),
        P("row", None),
    )
    return jax.shard_map(
        on_device, mesh=mesh, in_specs=in_specs, out_specs=out_specs, check_vma=False
    )
```

time: 1340 us -> 617 us (0.46)
  blocking collectives: 409 us -> 61.1 us
  waiting for transfers between devices: 535 us -> 260 us
  matrix products: 162 us -> 75.2 us
  Pallas kernels: 0 us -> 36.2 us
  other arithmetic: 73 us -> 47.9 us
  loops' own time: 22.6 us -> 0 us
    all_gather x16 -> x0, blocking collectives: 398 us -> none  [the longest x4 149 us: fetch_weights(): lax.all_gather(w_qkv, 'row', axis=0, tiled=True)]
    all_gather x16 -> x2, waiting for transfers between devices: 327 us -> 92.8 us  [gathered(): lax.all_gather(v, ('col', 'row'), axis=0, tiled=True)]
    all_to_all x2 -> x0, waiting for transfers between devices: 97.5 us -> none  [summed_on_arrival(): lax.all_to_all(blocks, axis, split_axis=0, concat_axis=0, tiled=True)]
    dot_general x52 -> x44, matrix products: 162 us -> 75.2 us  [dot(): return lax.dot_general(a, b, dims, preferred_element_type=f32)]
    reduce_scatter x8 -> x1, waiting for transfers between devices: 104 us -> 157 us  [scattered(): lax.psum_scatter(both, ('col', 'row'), scatter_dimension=0, tiled=True)]
    psum x1, blocking collectives: 11.5 us -> 61.1 us  [on_device(): lax.psum(jnp.stack([gain_one, gain_two, bias_one, bias_two], axis=1), ('r...]
    pallas_call x0 -> x2, Pallas kernels: none -> 36.2 us  [the longest x1 20.1 us: attend_back(): pl.pallas_call(attend_back_kernel, grid=(pairs,), in_specs=[pl.BlockSpec(...]
    dynamic_slice x12 -> x1, local copies, waits for them, and re-layouts: 28.2 us -> 0.07 us  [on_device(): lax.dynamic_slice_in_dim(small, lax.axis_index('row') * depth, depth, axi...]
  transfers between devices with their start and end apart: 26 -> 12, of which waited for: 20 -> 5; matrix products, arithmetic and copies ran while one was open for 14% -> 23% of each run, Pallas kernels for 0% -> 3%
where the time goes in v1:
time: 617 us; the launch traced here: 609 us
  waiting for transfers between devices  260 us (42%)
  local copies, waits for them, and re-layouts  106 us (17%)
  matrix products  75.2 us (12%)
  blocking collectives  61.1 us (10%)
  other arithmetic  47.9 us (8%)
  Pallas kernels  36.2 us (6%)
  between operations  15.1 us (2%)
  starting transfers between devices  7.36 us (1%)
    reduce_scatter x1, waiting for transfers between devices, scattered(): lax.psum_scatter(both, ('col', 'row'), scatter_dimension=0, tiled=True)  157 us
    all_gather x2, waiting for transfers between devices, gathered(): lax.all_gather(v, ('col', 'row'), axis=0, tiled=True)  92.8 us
    dot_general x44, matrix products, dot(): return lax.dot_general(a, b, dims, preferred_element_type=f32)  75.2 us
    psum x1, blocking collectives, on_device(): lax.psum(jnp.stack([gain_one, gain_two, bias_one, bias_two], axis=1), ('r...  61.1 us
    unnamed x187, local copies, waits for them, and re-layouts  24.8 us
    pallas_call x1, Pallas kernels, attend_back(): pl.pallas_call(attend_back_kernel, grid=(pairs,), in_specs=[pl.BlockSpec(...  20.1 us
    another operation x1, local copies, waits for them, and re-layouts, scattered(): both = jnp.stack(grads, axis=0).reshape(peers * width, -1)  19.2 us
    pallas_call x1, Pallas kernels, attend(): pl.pallas_call(attend_kernel, grid=(pairs,), in_specs=[pl.BlockSpec((rows...  16.1 us
  transfers between devices with their start and end apart: 12, of which 5 were waited for; matrix products, arithmetic and copies ran while one was open for 23% of the time, Pallas kernels for 3%

profile of v1, /device:TPU:0, one launch (start us, length us, event | category | flops | bytes accessed | tf_op | source)
XLA Modules:
  0.0 609.3 jit_solution(16417995493019929634)
XLA Ops:
  12.8 3.0 collective-permute-start
  15.9 9.8 %collective-permute-done.1 = s32[256,2]{0,1:T(2,128)S(1)} collective-permute-done((s32[256,2]{0,1:T(2,128)S(1)}, s32[256,2]{0,1:T(2,128)S(1)}, u32[]{:S(2)}, u32[]{:S(2)}) %collective-permute-start.1) | collective-permute-done | bytes 2080 | tf_op jit(solution)/shard_map/ppermute | solution.py:199
  27.4 53.1 %all-gather.3.cloned.1.call-done = bf16[3072,896]{1,0:T(8,128)(2,1)} async-done(((bf16[96,896]{1,0:T(8,128)(2,1)}), bf16[3072,896]{1,0:T(8,128)(2,1)}) %all-gather.3.cloned.1.call-update) | async-done | bytes 5505040 | tf_op jit(solution)/shard_map/all_gather | solution.py:227
  80.5 7.0 %slice_bitcast_fusion.39 = (bf16[768,192]{1,0:T(8,128)(2,1)}, bf16[768,192]{1,0:T(8,128)(2,1)}, bf16[768,192]{1,0:T(8,128)(2,1)}, bf16[768,192]{1,0:T(8,128)(2,1...) fusion(bf16[4,768,896]{2,1,0:T(8,128)(2,1)} %bitcast.240), kind=kLoop, calls=%fused_computation.156 | loop fusion | bytes 9437184 | tf_op jit(solution)/shard_map/squeeze | solution.py:241
  88.6 1.9 fusion.13
  92.2 2.5 fusion.5
  96.4 2.3 fusion.77
  102.1 2.5 convolution_convert_fusion.15
  112.6 3.1 copy.129
  118.0 2.7 fusion.50.q_ref
  122.4 1.9 fusion.74
  124.3 16.1 %attend.1 = (bf16[512,768]{1,0:T(8,128)(2,1)}, f32[6,512,2]{2,1,0:T(8,128)}) custom-call(bf16[512,768]{1,0:T(8,128)(2,1)} %fusion.50.q_ref, bf16[1024,768]{1,0:T(8,128)(2,1)} %get-tuple-element.102.k_ref, bf16[1024,768]{1,0:T(8,128)(2,1)} %get-tuple-element.101.v_ref, s32[512,1]{1,0:T(8,128)} %copy.160.segq_ref, s32[1,1024]{1,0:T(1,128)} %bitcast.290), custom_call_target="tpu_custom_call" | custom-call | flops 6442450944 | bytes 6291456 | tf_op jit(solution)/shard_map/attend/pallas_call | solution.py:90
  140.4 2.9 copy.138
  143.3 2.7 fusion.81
  147.8 39.7 %all-gather.5.cloned.1.call-done = bf16[3072,2304]{1,0:T(8,128)(2,1)} async-done(((bf16[96,2304]{1,0:T(8,128)(2,1)}), bf16[3072,2304]{1,0:T(8,128)(2,1)}) %all-gather.5.cloned.1.call-update) | async-done | bytes 14155792 | tf_op jit(solution)/shard_map/all_gather | solution.py:227
  187.5 2.4 fusion.47
  189.9 2.1 fusion.41
  192.0 2.0 fusion.29
  194.0 2.2 fusion.35
  196.3 2.7 multiply_convert_fusion.8
  208.4 2.4 multiply_reduce_fusion
  210.9 2.6 fusion.72
  213.5 10.8 %multiply_convert_fusion = (bf16[512,768]{1,0:T(8,128)(2,1)S(1)}, bf16[512,768]{1,0:T(8,128)(2,1)S(1)}) fusion(f32[512,768]{1,0:T(8,128)S(1)} %fusion.47, f32[512,768]{1,0:T(8,128)S(1)} %get-tuple-element.151, bf16[512,768]{1,0:T(8,128)(2,1)S(1)} %get-tuple-element.61, bf16[4,768,2304]{2,1,0:T(8,128)(2,1)S(1)} %bitcast.267), kind=kOutput, calls=%fused_computation.26 | convolution fusion | flops 609091584 | bytes 6684672 | tf_op jit(solution)/shard_map/dot_general | solution.py:26
  234.7 2.4 multiply_reduce_fusion.1
  238.6 2.3 convert_multiply_fusion
  240.9 1.9 copy.139
  243.6 20.1 %attend_back.1 = (f32[512,768]{1,0:T(8,128)}, f32[1024,768]{1,0:T(8,128)}, f32[1024,768]{1,0:T(8,128)}) custom-call(bf16[512,768]{1,0:T(8,128)(2,1)} %fusion.50.q_ref, bf16[1024,768]{1,0:T(8,128)(2,1)} %get-tuple-element.102.k_ref, bf16[1024,768]{1,0:T(8,128)(2,1)} %get-tuple-element.101.v_ref, bf16[512,768]{1,0:T(8,128)(2,1)} %get-tuple-element.156.do_ref, ...), custom_call_target="tpu_custom_call" | custom-call | flops 16106127360 | bytes 15728640 | tf_op jit(solution)/shard_map/attend_back/pallas_call | solution.py:159
  263.7 2.5 constant_dynamic-update-slice_fusion.2
  267.0 2.6 copy-done.1
  271.2 3.2 copy.142
  274.4 2.1 convolution_convert_fusion.13
  279.7 1.8 convolution_convert_fusion.1
  281.5 1.9 convolution_convert_fusion.2
  283.5 1.9 slice_add_fusion
  288.5 3.1 copy.145
  293.4 2.3 maximum_multiply_fusion.2
  295.7 3.1 copy.143
  298.8 3.0 copy.146
  301.8 3.4 add_convert_fusion.1
  306.4 3.0 convolution_convert_fusion
  313.5 2.5 pad_maximum_fusion.1
  317.1 2.0 convolution_convert_fusion.3
  331.7 6.6 %pad_maximum_fusion = bf16[4,768,2304]{1,2,0:T(8,128)(2,1)} fusion(bf16[1,768,2304]{1,2,0:T(8,128)(2,1)S(1)} %maximum_bitcast_fusion.3, bf16[1,768,2304]{1,2,0:T(8,128)(2,1)S(1)} %maximum_bitcast_fusion.2, bf16[1,768,2304]{1,2,0:T(8,128)(2,1)S(1)} %maximum_bitcast_fusion.1, bf16[1,768,2304]{1,2,0:T(8,128)(2,1)S(1)} %maximum_bitcast_fusion), kind=kLoop, calls=%fused_computation | loop fusion | flops 21233664 | bytes 28311552 | tf_op jit(solution)/shard_map/stack | solution.py:303
  338.3 19.2 %copy.150 = bf16[4,768,2304]{2,1,0:T(8,128)(2,1)} copy(bf16[4,768,2304]{1,2,0:T(8,128)(2,1)} %pad_maximum_fusion) | data formatting | bytes 28311552 | tf_op jit(solution)/shard_map/stack | solution.py:303
  358.9 7.0 %concatenate.117 = bf16[768,2304]{1,0:T(8,128)(2,1)} concatenate(bf16[768,192]{1,0:T(8,128)(2,1)} %get-tuple-element.80, bf16[768,192]{1,0:T(8,128)(2,1)} %get-tuple-element.79, bf16[768,192]{1,0:T(8,128)(2,1)} %get-tuple-element.78, bf16[768,192]{1,0:T(8,128)(2,1)} %get-tuple-element.77, bf16[768,192]{1,0:T(8,128)(2,1)} %copy-done.23, bf16[768,192]{1,0:T(8,128)(2,1)} %copy-done.22, ...), dimensions={1} | concatenate | bytes 7077888 | tf_op jit(solution)/shard_map/concatenate | solution.py:346
  367.5 4.8 convolution_add_fusion
  374.1 61.1 %psum.7 = f32[768,4]{0,1:T(4,128)S(1)} all-reduce(f32[768,4]{0,1:T(4,128)S(1)} %pad_maximum_fusion.16), channel_id=1, replica_groups=mesh['row'=8,'col'=4] {'row','col'}, use_global_device_ids=true, to_apply=%region_16.17 | all-reduce | flops 3072 | bytes 24576 | tf_op jit(solution)/shard_map/psum | solution.py:350
  442.1 157.4 %reduce-scatter.5.cloned.1.call-done = bf16[96,2304]{1,0:T(8,128)(2,1)} async-done(((bf16[3072,2304]{1,0:T(8,128)(2,1)}), bf16[96,2304]{1,0:T(8,128)(2,1)}) %reduce-scatter.5.cloned.1.call-update) | async-done | bytes 442384 | tf_op jit(solution)/shard_map/reduce_scatter | solution.py:304
  (311 shorter events, 94.8 us)
Async XLA Ops:
  7.2 3.7 copy-start.56
  7.2 3.7 copy-start.57
  7.2 73.4 %all-gather.3.cloned.1.call-start = ((), (), s32[]{:S(2)}) async-start(), calls=%async_computation.2 | async-start | bytes 5677056 | tf_op jit(solution)/shard_map/all_gather | solution.py:227
  8.3 3.5 copy-start.43
  10.8 176.8 %all-gather.5.cloned.1.call-start = ((), (), s32[]{:S(2)}) async-start(), calls=%async_computation.3 | async-start | bytes 14598144 | tf_op jit(solution)/shard_map/all_gather | solution.py:227
  10.9 4.9 copy-start.66
  10.9 4.9 copy-start.67
  11.8 427.6 %reduce-scatter.7.cloned.1.call-start = ((), (), s32[]{:S(2)}) async-start(), calls=%async_computation.5 | async-start | bytes 4866048
  12.8 74.8 %collective-permute-start = (bf16[256,768]{1,0:T(8,128)(2,1)}, bf16[256,768]{1,0:T(8,128)(2,1)}, u32[]{:S(2)}, u32[]{:S(2)}) collective-permute-start(bf16[256,768]{1,0:T(8,128)(2,1)} %get-tuple-element.126), channel_id=1, source_target_pairs={{0,2},{1,3},{2,0},{3,1},{4,6},{5,7},{6,4},{7,5},{8,10},{9,11},{10,... | collective-permute-start | bytes 1179656 | tf_op jit(solution)/shard_map/ppermute | solution.py:199
  15.8 9.9 %collective-permute-start.1 = (s32[256,2]{0,1:T(2,128)S(1)}, s32[256,2]{0,1:T(2,128)S(1)}, u32[]{:S(2)}, u32[]{:S(2)}) collective-permute-start(s32[256,2]{0,1:T(2,128)S(1)} %bitcast.291), channel_id=1, source_target_pairs={{0,2},{1,3},{2,0},{3,1},{4,6},{5,7},{6,4},{7,5},{8,10},{9,11},{10,... | collective-permute-start | bytes 6152 | tf_op jit(solution)/shard_map/ppermute | solution.py:199
  25.7 84.7 %copy-start.60 = (s32[512,1]{0,1:T(1,128)}, s32[512,1]{0,1:T(1,128)S(1)}, u32[]{:S(2)}) copy-start(s32[512,1]{0,1:T(1,128)S(1)} %get-tuple-element.133) | copy-start | bytes 6148
  80.5 8.1 %copy-start.54 = (bf16[256,768]{1,0:T(8,128)(2,1)S(1)}, bf16[256,768]{1,0:T(8,128)(2,1)}, u32[]{:S(2)}) copy-start(bf16[256,768]{1,0:T(8,128)(2,1)} %get-tuple-element.125) | copy-start | bytes 1179652
  87.5 14.5 %copy-start.16 = (bf16[768,192]{1,0:T(8,128)(2,1)}, bf16[768,192]{1,0:T(8,128)(2,1)S(1)}, u32[]{:S(2)}) copy-start(bf16[768,192]{1,0:T(8,128)(2,1)S(1)} %get-tuple-element.69) | copy-start | bytes 884740
  96.4 2.3 copy-start.48
  102.1 2.5 copy-start.9
  102.1 2.5 copy-start.10
  106.4 14.4 %collective-permute-start.2 = (bf16[512,1536]{1,0:T(8,128)(2,1)}, bf16[512,1536]{1,0:T(8,128)(2,1)}, u32[]{:S(2)}, u32[]{:S(2)}) collective-permute-start(bf16[512,1536]{1,0:T(8,128)(2,1)} %pad_maximum_fusion.4), channel_id=1, source_target_pairs={{0,1},{1,0},{2,3},{3,2},{4,5},{5,4},{6,7},{7,6},{8,9},{9,8},{10,11... | collective-permute-start | bytes 4718600 | tf_op jit(solution)/shard_map/ppermute | solution.py:202
  108.9 98.7 %collective-permute-start.5 = (f32[256,768]{1,0:T(8,128)}, f32[256,768]{1,0:T(8,128)}, u32[]{:S(2)}, u32[]{:S(2)}) collective-permute-start(f32[256,768]{1,0:T(8,128)} %get-tuple-element.107), channel_id=1, source_target_pairs={{0,2},{1,3},{2,0},{3,1},{4,6},{5,7},{6,4},{7,5},{8,10},{9,11},{10,... | collective-permute-start | bytes 2359304 | tf_op jit(solution)/shard_map/ppermute | solution.py:199
  110.4 1.2 collective-permute-start.3
  111.6 4.1 copy-start.65
  115.7 2.4 copy-start.7
  140.4 2.9 copy-start.49
  187.5 2.4 copy-start.44
  194.0 5.7 copy-start.53
  199.8 6.3 %copy-start.40 = (bf16[512,768]{1,0:T(8,128)(2,1)}, bf16[512,768]{1,0:T(8,128)(2,1)S(1)}, u32[]{:S(2)}) copy-start(bf16[512,768]{1,0:T(8,128)(2,1)S(1)} %get-tuple-element.150) | copy-start | bytes 2359300
  208.4 2.4 copy-start.61
  213.5 18.0 %copy-start.34 = (bf16[512,768]{1,0:T(8,128)(2,1)}, bf16[512,768]{1,0:T(8,128)(2,1)S(1)}, u32[]{:S(2)}) copy-start(bf16[512,768]{1,0:T(8,128)(2,1)S(1)} %get-tuple-element.61) | copy-start | bytes 2359300
  224.3 10.4 %copy-start.32 = (bf16[512,768]{1,0:T(8,128)(2,1)}, bf16[512,768]{1,0:T(8,128)(2,1)S(1)}, u32[]{:S(2)}) copy-start(bf16[512,768]{1,0:T(8,128)(2,1)S(1)} %get-tuple-element.93) | copy-start | bytes 2359300
  238.6 2.3 copy-start.3
  263.7 2.8 copy-start.11
  267.0 2.6 copy-start.1
  271.0 12.5 %collective-permute-start.6 = (bf16[512,1536]{1,0:T(8,128)(2,1)}, bf16[512,1536]{1,0:T(8,128)(2,1)}, u32[]{:S(2)}, u32[]{:S(2)}) collective-permute-start(bf16[512,1536]{1,0:T(8,128)(2,1)} %slice.476), channel_id=1, source_target_pairs={{0,1},{1,0},{2,3},{3,2},{4,5},{5,4},{6,7},{7,6},{8,9},{9,8},{10,11... | collective-permute-start | bytes 4718600 | tf_op jit(solution)/shard_map/ppermute | solution.py:202
  271.2 3.2 copy-start.4
  274.4 9.0 %slice-start = ((s8[6291456]{0:T(1024)(128)(4,1)}), s8[4194304]{0:T(1024)(128)(4,1)S(1)}, s32[]{:S(2)}) async-start(s8[6291456]{0:T(1024)(128)(4,1)} %bitcast.238), calls=%async_computation.6 | async-start | bytes 8388608
  276.5 3.1 copy-start.41
  278.3 5.2 slice-start.1
  301.8 4.6 copy-start.42
  301.8 4.6 copy-start.55
  316.0 3.1 copy-start.36
  316.0 283.4 %reduce-scatter.5.cloned.1.call-start = ((), (), s32[]{:S(2)}) async-start(), calls=%async_computation.4 | async-start | bytes 14598144 | tf_op jit(solution)/shard_map/reduce_scatter | solution.py:304
  317.1 2.0 copy-start.71
  358.9 7.0 %copy-start.12 = (bf16[512,768]{1,0:T(8,128)(2,1)S(1)}, bf16[512,768]{1,0:T(8,128)(2,1)}, u32[]{:S(2)}) copy-start(bf16[512,768]{1,0:T(8,128)(2,1)} %get-tuple-element.105) | copy-start | bytes 2359300
  358.9 8.5 %copy-start.64 = (f32[768]{0:T(1024)S(1)}, f32[768]{0:T(1024)}, u32[]{:S(2)}) copy-start(f32[768]{0:T(1024)} %get-tuple-element.56) | copy-start | bytes 9220
  358.9 8.5 %copy-start.63 = (f32[768]{0:T(1024)S(1)}, f32[768]{0:T(1024)}, u32[]{:S(2)}) copy-start(f32[768]{0:T(1024)} %get-tuple-element.52) | copy-start | bytes 9220
  366.0 70.0 %collective-permute-start.4 = (bf16[256,768]{1,0:T(8,128)(2,1)S(1)}, bf16[256,768]{1,0:T(8,128)(2,1)}, u32[]{:S(2)}, u32[]{:S(2)}) collective-permute-start(bf16[256,768]{1,0:T(8,128)(2,1)S(1)} %slice.363), channel_id=1, source_target_pairs={{0,2},{1,3},{2,0},{3,1},{4,6},{5,7},{6,4},{7,5},{8,10},{9,11},{10,... | collective-permute-start | bytes 1179656 | tf_op jit(solution)/shard_map/ppermute | solution.py:199
  373.5 64.6 %collective-permute-start.7 = (f32[256,768]{1,0:T(8,128)S(1)}, f32[256,768]{1,0:T(8,128)S(1)}, u32[]{:S(2)}, u32[]{:S(2)}) collective-permute-start(f32[256,768]{1,0:T(8,128)S(1)} %slice.373), channel_id=1, source_target_pairs={{0,2},{1,3},{2,0},{3,1},{4,6},{5,7},{6,4},{7,5},{8,10},{9,11},{10,... | collective-permute-start | bytes 2359304 | tf_op jit(solution)/shard_map/ppermute | solution.py:199
  435.9 2.1 copy-start.29
  599.5 2.3 copy-start.15
  (53 other events, 66.3 us)
Sparse Core Ops, SparseCore 0:
  11.6 68.9 all-gather.2
  83.5 103.9 all-gather.4
  316.2 114.4 reduce-scatter.6
  437.5 161.9 reduce-scatter.4

commit v2 on v1

--- a/solution.py
+++ b/solution.py
@@ -186,128 +186,265 @@
     )(q, k, v, do, logs, delta, seg_q[None, :], seg_k[:, None])
 
 
+def factors_of(n):
+    out = []
+    while n > 1:
+        step = 4 if n % 4 == 0 else (2 if n % 2 == 0 else n)
+        out.append(step)
+        n //= step
+    return out
+
+
+class Links:
+    def __init__(self, mesh):
+        self.rows = mesh.shape["row"]
+        self.cols = mesh.shape["col"]
+        self.digits = factors_of(self.rows // 2)
+
+    def locate(self):
+        row = lax.axis_index("row")
+        col = lax.axis_index("col")
+        x = row % 2
+        place = row // 2
+        ring = []
+        for size in reversed(self.digits):
+            ring.insert(0, place % size)
+            place = place // size
+        return ring, x, col // (self.cols // 2), col % 2
+
+    def send(self, v, move):
+        pairs = []
+        for row in range(self.rows):
+            for col in range(self.cols):
+                place, ring = row // 2, []
+                for size in reversed(self.digits):
+                    ring.insert(0, place % size)
+                    place //= size
+                ring, x, y, k = move(ring, row % 2, col // (self.cols // 2), col % 2)
+                place = 0
+                for size, digit in zip(self.digits, ring):
+                    place = place * size + digit % size
+                pairs.append(
+                    (row * self.cols + col, (place * 2 + x) * self.cols + y * (self.cols // 2) + k)
+                )
+        return lax.ppermute(v, ("row", "col"), pairs)
+
+    def across(self, v):
+        return self.send(v, lambda ring, x, y, k: (ring, x, 1 - y, k))
+
+    def beside(self, v):
+        return self.send(v, lambda ring, x, y, k: (ring, x, y, 1 - k))
+
+    def near(self, v):
+        return self.send(
+            v, lambda ring, x, y, k: (ring, x, 1 - y, k) if k else (ring, 1 - x, y, k)
+        )
+
+    def far(self, v):
+        return self.send(
+            v, lambda ring, x, y, k: (ring, 1 - x, y, k) if k else (ring, x, 1 - y, k)
+        )
+
+    def shift(self, v, axis, step):
+        def move(ring, x, y, k):
+            moved = list(ring)
+            moved[axis] = ring[axis] + step
+            return moved, x, y, k
+
+        return self.send(v, move)
+
+    def gather(self, shard, odd):
+        block = shard
+        for axis in reversed(range(len(self.digits))):
+            block = jnp.concatenate(
+                [block] + [self.shift(block, axis, -d) for d in range(1, self.digits[axis])], axis=0
+            )
+        b = self.near(block)
+        c = self.far(block)
+        d = self.far(b)
+        mine = [block, b, c, d]
+        theirs = [self.beside(v) for v in mine]
+        out = {}
+        for k, (a, b, c, d), flip in ((0, mine, odd), (1, theirs, jnp.logical_not(odd))):
+            out[0, k] = jnp.concatenate([a, jnp.where(flip, c, b)], axis=0)
+            out[1, k] = jnp.concatenate([jnp.where(flip, b, c), d], axis=0)
+        return out
+
+    def scatter(self, parts, odd):
+        came = [self.beside(parts[y, 1]) for y in range(2)]
+        cut = parts[0, 0].shape[0] // 2
+
+        def total(y, x):
+            rows = slice(x * cut, (x + 1) * cut)
+            return parts[y, 0][rows].astype(f32) + came[y][rows].astype(f32)
+
+        first = jnp.where(odd, total(0, 1), total(1, 0)).astype(bf16)
+        second = total(1, 1).astype(bf16)
+        got_first, got_second = self.far(first), self.far(second)
+        third = (jnp.where(odd, total(1, 0), total(0, 1)) + got_second.astype(f32)).astype(bf16)
+        block = total(0, 0) + got_first.astype(f32) + self.near(third).astype(f32)
+        for axis in range(len(self.digits)):
+            size = self.digits[axis]
+            pieces = jnp.split(block, size, axis=0)
+            block = pieces[0]
+            for d in range(1, size):
+                block = block + self.shift(pieces[d].astype(bf16), axis, d).astype(f32)
+        return block
+
+
+def relative_order(links, depth):
+    ring, x, _, _ = links.locate()
+    where = lax.broadcasted_iota(jnp.int32, (1, links.rows * depth), 1)
+    block, inside = where // depth, where % depth
+    steps = links.rows // 2
+    place = block % steps
+    parts = []
+    for axis in reversed(range(len(links.digits))):
+        size = links.digits[axis]
+        parts.insert(0, (place % size + ring[axis]) % size)
+        place = place // size
+    row = jnp.zeros_like(block)
+    for size, part in zip(links.digits, parts):
+        row = row * size + part
+    row = row * 2 + jnp.bitwise_xor(x, block // steps)
+    return row * depth + inside
+
+
 def on_device(
-    tokens, segments, positions, w_qkv, w_out, w_gate_up, w_down, norm_gain, norm_bias, cotangent
+    links, tokens, segments, positions, w_qkv, w_out, w_gate_up, w_down, norm_gain, norm_bias, cotangent
 ):
-    peers = lax.axis_size("col")
-    rings = lax.axis_size("row")
-    half = tokens.shape[0]
-    side = lax.axis_index("col") // (peers // half)
+    ring, x_place, side, core = links.locate()
+    odd = core == 1
     scale = 1.0 / math.sqrt(HD)
-
-    def across(v):
-        return lax.ppermute(v, "col", [(i, (i + peers // 2) % peers) for i in range(peers)])
-
-    def beside(v):
-        return lax.ppermute(v, "col", [(i, i ^ 1) for i in range(peers)])
-
-    def to_sequence(v):
-        own = lax.dynamic_index_in_dim(v, side, 0, keepdims=False)
-        other = lax.dynamic_index_in_dim(v, 1 - side, 0, keepdims=False)
-        return jnp.concatenate([own, across(other)], axis=0)
-
-    def from_sequence(v):
-        rows = v.shape[0] // 2
-        came = across(v[rows:])
-        own = v[:rows]
-        first = side == 0
-        return jnp.stack([jnp.where(first, own, came), jnp.where(first, came, own)], axis=0)
-
     depth = w_qkv.shape[0]
     width = tokens.shape[2]
     head_cols = w_qkv.shape[2]
     hid = w_gate_up.shape[2]
+    rows = 2 * tokens.shape[1]
+    quarters = [(0, 0), (0, 1), (1, 0), (1, 1)]
+
+    source = relative_order(links, depth)
+    swap = (lax.broadcasted_iota(jnp.int32, (width, width), 0) == source).astype(bf16)
+
+    def to_relative(v):
+        if v.dtype == bf16:
+            return dot(v, swap)
+        high = v.astype(bf16)
+        low = (v - high.astype(f32)).astype(bf16)
+        return dot(high, swap) + dot(low, swap)
+
+    def from_relative(v):
+        if v.dtype == bf16:
+            return dot(v, swap, NT)
+        high = v.astype(bf16)
+        low = (v - high.astype(f32)).astype(bf16)
+        return dot(high, swap, NT) + dot(low, swap, NT)
+
+    def own_and_other(v):
+        own = lax.dynamic_index_in_dim(v, side, 0, keepdims=False)
+        return own, lax.dynamic_index_in_dim(v, 1 - side, 0, keepdims=False)
+
+    def from_sequence(own, came):
+        first = side == 0
+        return jnp.stack([jnp.where(first, own, came), jnp.where(first, came, own)], axis=0)
 
     norms = jnp.concatenate([norm_gain, norm_bias], axis=1)
-    norms = jnp.pad(norms, ((0, 0), (0, 128 - norms.shape[1])))
-    pack_a = jnp.concatenate([w_qkv.reshape(depth, -1), w_out.T, norms], axis=1)
-    pack_b = jnp.concatenate([w_gate_up.reshape(depth, -1), w_down.T], axis=1)
-
-    def gathered(v):
-        return lax.all_gather(v, ("col", "row"), axis=0, tiled=True).reshape(peers, width, -1)
-
-    full_a = gathered(pack_a)
-    full_b = gathered(pack_b)
-
-    x = to_sequence(tokens)
-    seg_pos = to_sequence(jnp.stack([segments, positions], axis=2))
-    seg = seg_pos[:, 0]
-    seg_all = jnp.concatenate([seg, beside(seg)], axis=0)
-    cosine, sine = rope_tables(seg_pos[:, 1], width // HD)
-    dy = to_sequence(cotangent)
-
-    def columns(lo):
-        return jnp.concatenate(
-            [full_a[c, :, lo : lo + head_cols] for c in range(peers)], axis=1
+    norms = jnp.pad(norms, ((0, 0), (0, 64 - norms.shape[1])))
+    half = hid // 2
+    shards = [jnp.concatenate([w_qkv.reshape(depth, -1), norms], axis=1)]
+    down_t = w_down.T
+    for h in range(2):
+        cols = slice(h * half, (h + 1) * half)
+        shards.append(
+            jnp.concatenate(
+                ([w_out.T] if h == 0 else [])
+                + [down_t[:, cols], w_gate_up[:, 0, cols], w_gate_up[:, 1, cols]],
+                axis=1,
+            )
         )
-
-    wq, wk, wv = columns(0), columns(head_cols), columns(2 * head_cols)
-    wo_t = columns(3 * head_cols)
-    gains = full_a[0, :, 4 * head_cols : 4 * head_cols + 2].astype(f32)
-    biases = full_a[0, :, 4 * head_cols + 2 : 4 * head_cols + 4].astype(f32)
-
-    q = (rotate(dot(x, wq), cosine, sine)).astype(bf16)
+    tokens_own, tokens_other = own_and_other(tokens)
+    tokens_came = links.across(tokens_other)
+    small_own, small_other = own_and_other(jnp.stack([segments, positions], axis=1))
+    small_came = links.across(small_other)
+    full = [links.gather(s, odd) for s in shards]
+
+    x = to_relative(jnp.concatenate([tokens_own, tokens_came], axis=0)).astype(bf16)
+    small = jnp.concatenate([small_own, small_came], axis=1)
+    seg = small[0]
+    seg_all = jnp.concatenate([seg, links.beside(seg)], axis=0)
+    cosine, sine = rope_tables(small[1], width // HD)
+    dy_own, dy_other = own_and_other(cotangent)
+    dy_came = links.across(dy_other.astype(bf16))
+    dy = jnp.concatenate([to_relative(dy_own), to_relative(dy_came)], axis=0)
+
+    def columns(which, lo, size):
+        return jnp.concatenate([full[which][c][:, lo : lo + size] for c in quarters], axis=1)
+
+    wq, wk, wv = (columns(0, p * head_cols, head_cols) for p in range(3))
+    wo_t = columns(1, 0, head_cols)
+    norm_cols = full[0][0, 0][:, 3 * head_cols : 3 * head_cols + 4].astype(f32).T
+    gains, biases = norm_cols[:2], norm_cols[2:]
+
+    q = rotate(dot(x, wq), cosine, sine)
     k = rotate(dot(x, wk), cosine, sine).astype(bf16)
     v = dot(x, wv).astype(bf16)
-    kv = jnp.concatenate([k, v], axis=1)
-    kv_all = jnp.concatenate([kv, beside(kv)], axis=0)
-    k_all = kv_all[:, :width]
-    v_all = kv_all[:, width:]
-    q_small = q * jnp.asarray(scale, bf16)
+
+    def swapped_heads(v):
+        parts = jnp.split(v, 4, axis=1)
+        return [parts[1], parts[0], parts[3], parts[2]]
+
+    kv_came = links.beside(jnp.concatenate(swapped_heads(k) + swapped_heads(v), axis=1))
+    k_all = jnp.concatenate([k, kv_came[:, :width]], axis=0)
+    v_all = jnp.concatenate([v, kv_came[:, width:]], axis=0)
+    q_small = (q.astype(bf16) * jnp.asarray(scale, bf16)).astype(bf16)
     attended, logs = attend(q_small, k_all, v_all, seg, seg_all)
     branch = dot(attended, wo_t, NT)
     n1, s1 = normalize(x.astype(f32) + branch)
-    first = n1 * gains[:, 0] + biases[:, 0]
+    first = n1 * gains[0] + biases[0]
     first_low = first.astype(bf16)
-    gates = []
-    ups = []
+    gates, ups, hiddens, downs, gate_ups = {}, {}, {}, {}, {}
     feed = jnp.zeros(first.shape, f32)
-    for c in range(peers):
-        gates.append(dot(first_low, full_b[c, :, :hid]))
-        ups.append(dot(first_low, full_b[c, :, hid : 2 * hid]))
-        hidden = (jax.nn.silu(gates[c]) * ups[c]).astype(bf16)
-        feed = feed + dot(hidden, full_b[c, :, 2 * hid :], NT)
+    for h in range(2):
+        base = head_cols if h == 0 else 0
+        for c in quarters:
+            w = full[1 + h][c]
+            downs[h, c] = w[:, base : base + half]
+            gate_ups[h, c] = w[:, base + half : base + 3 * half]
+            both = dot(first_low, gate_ups[h, c])
+            gates[h, c], ups[h, c] = both[:, :half], both[:, half:]
+            hiddens[h, c] = (jax.nn.silu(gates[h, c]) * ups[h, c]).astype(bf16)
+            feed = feed + dot(hiddens[h, c], downs[h, c], NT)
     n2, s2 = normalize(first + feed)
-    layer_out = (n2 * gains[:, 1] + biases[:, 1]).astype(bf16)
+    layer_out = (n2 * gains[1] + biases[1]).astype(bf16)
 
     gain_two = jnp.sum(dy * n2, axis=0)
     bias_two = jnp.sum(dy, axis=0)
-    dh2 = norm_back(dy * gains[:, 1], n2, s2)
+    dh2 = norm_back(dy * gains[1], n2, s2)
     dfeed = dh2.astype(bf16)
+    grads = {}
+    for c in quarters:
+        grads[c] = jnp.concatenate(
+            [dot(dfeed, hiddens[h, c], TN).astype(bf16) for h in range(2)], axis=1
+        )
+    own_down = links.scatter(grads, odd)
     dfirst = dh2
-    grads_b = []
-    for c in range(peers):
-        dhidden = dot(dfeed, full_b[c, :, 2 * hid :])
-        sg = jax.nn.sigmoid(gates[c])
-        silu = gates[c] * sg
-        dgate = (dhidden * ups[c] * sg * (1.0 + gates[c] * (1.0 - sg))).astype(bf16)
-        dup = (dhidden * silu).astype(bf16)
-        hidden = (silu * ups[c]).astype(bf16)
-        grads_b.append(
-            jnp.concatenate(
-                [
-                    dot(first_low, dgate, TN).astype(bf16),
-                    dot(first_low, dup, TN).astype(bf16),
-                    dot(dfeed, hidden, TN).astype(bf16),
-                ],
-                axis=1,
-            )
-        )
-        dfirst = (
-            dfirst
-            + dot(dgate, full_b[c, :, :hid], NT)
-            + dot(dup, full_b[c, :, hid : 2 * hid], NT)
-        )
-
-    def scattered(grads):
-        both = jnp.stack(grads, axis=0).reshape(peers * width, -1)
-        return lax.psum_scatter(both, ("col", "row"), scatter_dimension=0, tiled=True).astype(f32)
-
-    own_b = scattered(grads_b)
+    own_gate_up = []
+    for h in range(2):
+        grads = {}
+        for c in quarters:
+            dhidden = dot(dfeed, downs[h, c])
+            gate, up = gates[h, c], ups[h, c]
+            sg = jax.nn.sigmoid(gate)
+            dgate = dhidden * up * sg * (1.0 + gate * (1.0 - sg))
+            dup = dhidden * (gate * sg)
+            dgate_up = jnp.concatenate([dgate, dup], axis=1).astype(bf16)
+            grads[c] = dot(first_low, dgate_up, TN).astype(bf16)
+            dfirst = dfirst + dot(dgate_up, gate_ups[h, c], NT)
+        own_gate_up.append(links.scatter(grads, odd))
 
     gain_one = jnp.sum(dfirst * n1, axis=0)
     bias_one = jnp.sum(dfirst, axis=0)
-    dh1 = norm_back(dfirst * gains[:, 0], n1, s1)
+    dh1 = norm_back(dfirst * gains[0], n1, s1)
     dbranch = dh1.astype(bf16)
     do = dot(dbranch, wo_t).astype(bf16)
     delta = jnp.sum(
@@ -323,43 +460,49 @@
         seg,
         seg_all,
     )
-    rows = x.shape[0]
-    dkv = jnp.concatenate([dk, dv], axis=1)
-    dkv_sum = dkv[:rows] + beside(dkv[rows:].astype(bf16)).astype(f32)
-    dproj = jnp.concatenate(
-        [rotate(dq, cosine, -sine), rotate(dkv_sum[:, :width], cosine, -sine), dkv_sum[:, width:]],
+    dkv_came = links.beside(
+        jnp.concatenate(swapped_heads(dk[rows:]) + swapped_heads(dv[rows:]), axis=1).astype(bf16)
+    ).astype(f32)
+    dk = dk[:rows] + dkv_came[:, :width]
+    dv = (dv[:rows] + dkv_came[:, width:]).astype(bf16)
+    dq = rotate(dq, cosine, -sine).astype(bf16)
+    dk = rotate(dk, cosine, -sine).astype(bf16)
+    small_grads = jnp.stack([gain_one, gain_two, bias_one, bias_two], axis=1).astype(bf16)
+    small_grads = jnp.pad(small_grads, ((0, 0), (0, 124)))
+    grads = {}
+    for i, c in enumerate(quarters):
+        cols = slice(i * head_cols, (i + 1) * head_cols)
+        grads[c] = jnp.concatenate(
+            [dot(x, d[:, cols], TN).astype(bf16) for d in (dq, dk, dv)]
+            + [dot(dbranch, attended[:, cols], TN).astype(bf16), small_grads],
+            axis=1,
+        )
+    own_attn = links.scatter(grads, odd)
+    input_grad = from_relative(dh1 + dot(dq, wq, NT) + dot(dk, wk, NT) + dot(dv, wv, NT))
+    mine = rows // 2
+    input_grad = from_sequence(
+        input_grad[:mine], links.across(input_grad[mine:].astype(bf16)).astype(f32)
+    )
+    layer_out = from_relative(layer_out).astype(bf16)
+    layer_out = from_sequence(layer_out[:mine], links.across(layer_out[mine:]))
+
+    gate_up_grad = jnp.stack(
+        [
+            jnp.concatenate([own_gate_up[h][:, p * half : (p + 1) * half] for h in range(2)], axis=1)
+            for p in range(2)
+        ],
         axis=1,
-    ).astype(bf16)
-    d_qkv = dot(x, dproj, TN).astype(bf16)
-    d_out = dot(dbranch, attended, TN).astype(bf16)
-    grads_a = []
-    for c in range(peers):
-        lo = c * head_cols
-        grads_a.append(
-            jnp.concatenate(
-                [d_qkv[:, p * width + lo : p * width + lo + head_cols] for p in range(3)]
-                + [d_out[:, lo : lo + head_cols]],
-                axis=1,
-            )
-        )
-    own_a = scattered(grads_a)
-    w_all = jnp.concatenate([wq, wk, wv], axis=1)
-    input_grad = from_sequence(dh1 + dot(dproj, w_all, NT))
-    layer_out = from_sequence(layer_out)
-
-    small = lax.psum(
-        jnp.stack([gain_one, gain_two, bias_one, bias_two], axis=1), ("row", "col")
-    )
-    small = lax.dynamic_slice_in_dim(small, lax.axis_index("row") * depth, depth, axis=0)
+    )
+    edge = 4 * head_cols
     return (
         layer_out,
         input_grad,
-        own_a[:, : 3 * head_cols].reshape(depth, 3, head_cols),
-        own_a[:, 3 * head_cols :].T,
-        own_b[:, : 2 * hid].reshape(depth, 2, hid),
-        own_b[:, 2 * hid :].T,
-        small[:, :2],
-        small[:, 2:],
+        own_attn[:, : 3 * head_cols].reshape(depth, 3, head_cols),
+        own_attn[:, 3 * head_cols : edge].T,
+        gate_up_grad,
+        own_down.T,
+        own_attn[:, edge : edge + 2],
+        own_attn[:, edge + 2 : edge + 4],
     )
 
 
@@ -387,5 +530,5 @@
         P("row", None),
     )
     return jax.shard_map(
-        on_device, mesh=mesh, in_specs=in_specs, out_specs=out_specs, check_vma=False
-    )
+        functools.partial(on_device, Links(mesh)), mesh=mesh, in_specs=in_specs, out_specs=out_specs, check_vma=False
+    )

time: 617 us -> 541 us (0.88)
  the two profiles are of different devices: /device:TPU:0 before, /device:TPU:26 now
where the time goes in v2:
time: 541 us; the launch traced here: 531 us
  waiting for transfers between devices  126 us (23%)
  other arithmetic  98.8 us (18%)
  matrix products  95 us (18%)
  local copies, waits for them, and re-layouts  92.7 us (17%)
  starting transfers between devices  80 us (15%)
  Pallas kernels  35.7 us (7%)
    ppermute x70, waiting for transfers between devices, send(): return lax.ppermute(v, ('row', 'col'), pairs)  126 us
    dot_general x79, matrix products, dot(): return lax.dot_general(a, b, dims, preferred_element_type=f32)  95 us
    ppermute x70, starting transfers between devices, send(): return lax.ppermute(v, ('row', 'col'), pairs)  80 us
    unnamed x248, local copies, waits for them, and re-layouts  21.7 us
    pallas_call x1, Pallas kernels, attend_back(): pl.pallas_call(attend_back_kernel, grid=(pairs,), in_specs=[pl.BlockSpec(...  19.8 us
    pallas_call x1, Pallas kernels, attend(): pl.pallas_call(attend_kernel, grid=(pairs,), in_specs=[pl.BlockSpec((rows...  15.9 us
    concatenate x3, other arithmetic, columns(): jnp.concatenate([full[which][c][:, lo:lo + size] for c in quarters], axis=1)  15.7 us
    mul x6, local copies, waits for them, and re-layouts, rotate(): return (heads * cosine + swapped * sine).reshape(rows, width)  12.8 us
  transfers between devices with their start and end apart: 70, of which 18 were waited for; matrix products, arithmetic and copies ran while one was open for 44% of the time, Pallas kernels for 7%

profile of v2, /device:TPU:26, one launch (start us, length us, event | category | flops | bytes accessed | tf_op | source)
XLA Modules:
  0.0 531.2 jit_solution(15076670572018889963)
XLA Ops:
  4.0 3.0 collective-permute-start.3
  24.8 2.9 collective-permute-start.26
  32.0 2.9 collective-permute-start.16
  34.9 5.7 %collective-permute-done.25 = bf16[96,1152]{0,1:T(8,128)(2,1)S(1)} collective-permute-done((bf16[96,1152]{0,1:T(8,128)(2,1)}, bf16[96,1152]{0,1:T(8,128)(2,1)S(1)}, u32[]{:S(2)}, u32[]{:S(2)}) %collective-permute-start.25) | collective-permute-done | bytes 221216 | tf_op jit(solution)/shard_map/ppermute | solution.py:230
  45.2 4.3 collective-permute-done.14
  50.1 19.0 %collective-permute-done.15 = bf16[96,1344]{0,1:T(8,128)(2,1)S(1)} collective-permute-done((bf16[96,1344]{0,1:T(8,128)(2,1)}, bf16[96,1344]{0,1:T(8,128)(2,1)S(1)}, u32[]{:S(2)}, u32[]{:S(2)}) %collective-permute-start.15) | collective-permute-done | bytes 258080 | tf_op jit(solution)/shard_map/ppermute | solution.py:230
  80.5 2.7 collective-permute-done.4
  85.3 2.9 concatenate.185
  89.8 3.8 collective-permute-done.28
  93.6 8.6 %collective-permute-done.27 = bf16[384,1152]{0,1:T(8,128)(2,1)} collective-permute-done((bf16[384,1152]{0,1:T(8,128)(2,1)}, bf16[384,1152]{0,1:T(8,128)(2,1)}, u32[]{:S(2)}, u32[]{:S(2)}) %collective-permute-start.27) | collective-permute-done | bytes 884768 | tf_op jit(solution)/shard_map/ppermute | solution.py:230
  106.5 3.9 concatenate.210
  113.1 10.1 %collective-permute-done.9 = bf16[384,640]{0,1:T(8,128)(2,1)} collective-permute-done((bf16[384,640]{0,1:T(8,128)(2,1)}, bf16[384,640]{0,1:T(8,128)(2,1)}, u32[]{:S(2)}, u32[]{:S(2)}) %collective-permute-start.9) | collective-permute-done | bytes 491552 | tf_op jit(solution)/shard_map/ppermute | solution.py:230
  127.6 5.2 concatenate.203
  133.8 6.6 %fusion.44 = (bf16[768,768]{0,1:T(8,128)(2,1)}, bf16[768,768]{0,1:T(8,128)(2,1)S(1)}) fusion(bf16[384,640]{0,1:T(8,128)(2,1)} %collective-permute-done.10, bf16[384,640]{0,1:T(8,128)(2,1)} %get-tuple-element.131, bf16[384,640]{0,1:T(8,128)(2,1)} %collective-permute-done.9, bf16[384,640]{0,1:T(8,128)(2,1)S(1)} %get-tuple-element.129, ...), kind=kLoop, calls=%fused_computation.136 | loop fusion | flops 26542080 | bytes 5898240 | tf_op jit(solution)/shard_map/concatenate | solution.py:381
  143.5 3.1 copy.101
  146.6 4.5 fusion.42
  154.1 3.0 copy.104
  161.7 3.1 copy.105
  168.1 3.0 copy.102
  175.5 4.2 concatenate.197
  180.3 3.1 fusion.72.q_ref
  183.4 2.8 broadcast_select_fusion.4
  196.9 15.9 %attend.1 = (bf16[512,768]{1,0:T(8,128)(2,1)}, f32[6,512,2]{2,1,0:T(8,128)}) custom-call(bf16[512,768]{1,0:T(8,128)(2,1)} %fusion.72.q_ref, bf16[1024,768]{1,0:T(8,128)(2,1)} %pad_maximum_fusion.k_ref, bf16[1024,768]{1,0:T(8,128)(2,1)} %pad_maximum_fusion.1.v_ref, s32[512,1]{1,0:T(8,128)} %copy.106.segq_ref, s32[1,1024]{1,0:T(1,128)} %bitcast.183), custom_call_target="tpu_custom_call" | custom-call | flops 6442450944 | bytes 6291456 | tf_op jit(solution)/shard_map/attend/pallas_call | solution.py:90
  215.4 4.6 fusion.45
  298.4 3.5 multiply_reduce_fusion.1
  305.8 3.1 copy.129
  311.1 19.8 %attend_back.1 = (f32[512,768]{1,0:T(8,128)}, f32[1024,768]{1,0:T(8,128)}, f32[1024,768]{1,0:T(8,128)}) custom-call(bf16[512,768]{1,0:T(8,128)(2,1)} %fusion.72.q_ref, bf16[1024,768]{1,0:T(8,128)(2,1)} %pad_maximum_fusion.k_ref, bf16[1024,768]{1,0:T(8,128)(2,1)} %pad_maximum_fusion.1.v_ref, bf16[512,768]{1,0:T(8,128)(2,1)} %get-tuple-element.188.do_ref, ...), custom_call_target="tpu_custom_call" | custom-call | flops 16106127360 | bytes 15728640 | tf_op jit(solution)/shard_map/attend_back/pallas_call | solution.py:159
  335.5 4.4 concatenate.224
  340.4 3.0 copy.132
  354.1 7.4 %collective-permute-done.34 = bf16[256,768]{1,0:T(8,128)(2,1)S(1)} collective-permute-done((bf16[256,768]{1,0:T(8,128)(2,1)S(1)}, bf16[256,768]{1,0:T(8,128)(2,1)S(1)}, u32[]{:S(2)}, u32[]{:S(2)}) %collective-permute-start.34) | collective-permute-done | bytes 393248 | tf_op jit(solution)/shard_map/ppermute | solution.py:230
  380.1 3.0 copy.133
  383.2 3.0 copy.136
  386.2 2.9 add_convert_fusion.1
  411.2 5.3 collective-permute-done.57
  419.4 5.5 %collective-permute-done.37 = bf16[256,768]{1,0:T(8,128)(2,1)S(1)} collective-permute-done((bf16[256,768]{1,0:T(8,128)(2,1)S(1)}, bf16[256,768]{1,0:T(8,128)(2,1)S(1)}, u32[]{:S(2)}, u32[]{:S(2)}) %collective-permute-start.37) | collective-permute-done | bytes 393248 | tf_op jit(solution)/shard_map/ppermute | solution.py:230
  427.7 9.9 %collective-permute-done.64 = bf16[384,768]{1,0:T(8,128)(2,1)S(1)} collective-permute-done((bf16[384,768]{1,0:T(8,128)(2,1)S(1)}, bf16[384,768]{1,0:T(8,128)(2,1)S(1)}, u32[]{:S(2)}, u32[]{:S(2)}) %collective-permute-start.64) | collective-permute-done | bytes 589856 | tf_op jit(solution)/shard_map/ppermute | solution.py:230
  441.3 8.9 %collective-permute-done.48 = bf16[384,768]{1,0:T(8,128)(2,1)S(1)} collective-permute-done((bf16[384,768]{1,0:T(8,128)(2,1)S(1)}, bf16[384,768]{1,0:T(8,128)(2,1)S(1)}, u32[]{:S(2)}, u32[]{:S(2)}) %collective-permute-start.48) | collective-permute-done | bytes 589856 | tf_op jit(solution)/shard_map/ppermute | solution.py:230
  451.7 10.0 %collective-permute-start.51 = (bf16[96,768]{1,0:T(8,128)(2,1)S(1)}, bf16[96,768]{1,0:T(8,128)(2,1)S(1)}, u32[]{:S(2)}, u32[]{:S(2)}) collective-permute-start(bf16[96,768]{1,0:T(8,128)(2,1)S(1)} %get-tuple-element.148), channel_id=1, source_target_pairs={{0,8},{1,9},{2,10},{3,11},{4,12},{5,13},{6,14},{7,15},{8,16},{9,17... | collective-permute-start | bytes 442376 | tf_op jit(solution)/shard_map/ppermute | solution.py:230
  461.7 4.1 collective-permute-start.52
  465.8 3.9 collective-permute-start.53
  472.5 5.5 %collective-permute-done.52 = bf16[96,768]{1,0:T(8,128)(2,1)S(1)} collective-permute-done((bf16[96,768]{1,0:T(8,128)(2,1)S(1)}, bf16[96,768]{1,0:T(8,128)(2,1)S(1)}, u32[]{:S(2)}, u32[]{:S(2)}) %collective-permute-start.52) | collective-permute-done | bytes 147488 | tf_op jit(solution)/shard_map/ppermute | solution.py:230
  478.0 7.2 %collective-permute-start.61 = (bf16[96,768]{1,0:T(8,128)(2,1)S(1)}, bf16[96,768]{1,0:T(8,128)(2,1)S(1)}, u32[]{:S(2)}, u32[]{:S(2)}) collective-permute-start(bf16[96,768]{1,0:T(8,128)(2,1)S(1)} %get-tuple-element.152), channel_id=1, source_target_pairs={{0,24},{1,25},{2,26},{3,27},{4,28},{5,29},{6,30},{7,31},{8,0},{9,1... | collective-permute-start | bytes 442376 | tf_op jit(solution)/shard_map/ppermute | solution.py:230
  485.4 6.6 %collective-permute-done.60 = bf16[96,768]{1,0:T(8,128)(2,1)S(1)} collective-permute-done((bf16[96,768]{1,0:T(8,128)(2,1)S(1)}, bf16[96,768]{1,0:T(8,128)(2,1)S(1)}, u32[]{:S(2)}, u32[]{:S(2)}) %collective-permute-start.60) | collective-permute-done | bytes 147488 | tf_op jit(solution)/shard_map/ppermute | solution.py:230
  492.0 3.1 collective-permute-start.69
  495.8 2.8 collective-permute-start.40
  500.1 8.0 %collective-permute-done.40 = bf16[384,896]{0,1:T(8,128)(2,1)S(1)} collective-permute-done((bf16[384,896]{0,1:T(8,128)(2,1)S(1)}, bf16[384,896]{0,1:T(8,128)(2,1)S(1)}, u32[]{:S(2)}, u32[]{:S(2)}) %collective-permute-start.40) | collective-permute-done | bytes 688160 | tf_op jit(solution)/shard_map/ppermute | solution.py:230
  515.4 3.7 collective-permute-done.43
  519.1 9.7 %collective-permute-done.44 = bf16[96,896]{0,1:T(8,128)(2,1)S(1)} collective-permute-done((bf16[96,896]{0,1:T(8,128)(2,1)S(1)}, bf16[96,896]{0,1:T(8,128)(2,1)S(1)}, u32[]{:S(2)}, u32[]{:S(2)}) %collective-permute-start.44) | collective-permute-done | bytes 172064 | tf_op jit(solution)/shard_map/ppermute | solution.py:230
  (560 shorter events, 255.0 us)
Async XLA Ops:
  3.2 21.6 %collective-permute-start.1 = (bf16[96,640]{0,1:T(8,128)(2,1)}, bf16[96,640]{0,1:T(8,128)(2,1)S(1)}, u32[]{:S(2)}, u32[]{:S(2)}) collective-permute-start(bf16[96,640]{0,1:T(8,128)(2,1)} %pad_maximum_fusion.47), channel_id=1, source_target_pairs={{0,24},{1,25},{2,26},{3,27},{4,28},{5,29},{6,30},{7,31},{8,0},{9,1... | collective-permute-start | bytes 368648 | tf_op jit(solution)/shard_map/ppermute | solution.py:230
  3.6 25.8 %collective-permute-start.2 = (bf16[96,640]{0,1:T(8,128)(2,1)}, bf16[96,640]{0,1:T(8,128)(2,1)}, u32[]{:S(2)}, u32[]{:S(2)}) collective-permute-start(bf16[96,640]{0,1:T(8,128)(2,1)} %pad_maximum_fusion.47), channel_id=1, source_target_pairs={{0,16},{1,17},{2,18},{3,19},{4,20},{5,21},{6,22},{7,23},{8,24},{9,... | collective-permute-start | bytes 368648 | tf_op jit(solution)/shard_map/ppermute | solution.py:230
  4.0 25.6 %collective-permute-start.3 = (bf16[96,640]{0,1:T(8,128)(2,1)}, bf16[96,640]{0,1:T(8,128)(2,1)}, u32[]{:S(2)}, u32[]{:S(2)}) collective-permute-start(bf16[96,640]{0,1:T(8,128)(2,1)} %pad_maximum_fusion.47), channel_id=1, source_target_pairs={{0,8},{1,9},{2,10},{3,11},{4,12},{5,13},{6,14},{7,15},{8,16},{9,17... | collective-permute-start | bytes 368648 | tf_op jit(solution)/shard_map/ppermute | solution.py:230
  12.4 19.6 %collective-permute-start.24 = (bf16[96,1152]{0,1:T(8,128)(2,1)}, bf16[96,1152]{0,1:T(8,128)(2,1)}, u32[]{:S(2)}, u32[]{:S(2)}) collective-permute-start(bf16[96,1152]{0,1:T(8,128)(2,1)} %pad_maximum_fusion.46), channel_id=1, source_target_pairs={{0,24},{1,25},{2,26},{3,27},{4,28},{5,29},{6,30},{7,31},{8,0},{9,1... | collective-permute-start | bytes 663560 | tf_op jit(solution)/shard_map/ppermute | solution.py:230
  29.5 20.1 %collective-permute-start.14 = (bf16[96,1344]{0,1:T(8,128)(2,1)}, bf16[96,1344]{0,1:T(8,128)(2,1)S(1)}, u32[]{:S(2)}, u32[]{:S(2)}) collective-permute-start(bf16[96,1344]{0,1:T(8,128)(2,1)} %pad_maximum_fusion.45), channel_id=1, source_target_pairs={{0,24},{1,25},{2,26},{3,27},{4,28},{5,29},{6,30},{7,31},{8,0},{9,1... | collective-permute-start | bytes 774152 | tf_op jit(solution)/shard_map/ppermute | solution.py:230
  29.6 39.5 %collective-permute-start.15 = (bf16[96,1344]{0,1:T(8,128)(2,1)}, bf16[96,1344]{0,1:T(8,128)(2,1)S(1)}, u32[]{:S(2)}, u32[]{:S(2)}) collective-permute-start(bf16[96,1344]{0,1:T(8,128)(2,1)} %pad_maximum_fusion.45), channel_id=1, source_target_pairs={{0,16},{1,17},{2,18},{3,19},{4,20},{5,21},{6,22},{7,23},{8,24},{9,... | collective-permute-start | bytes 774152 | tf_op jit(solution)/shard_map/ppermute | solution.py:230
  32.0 38.7 %collective-permute-start.16 = (bf16[96,1344]{0,1:T(8,128)(2,1)S(1)}, bf16[96,1344]{0,1:T(8,128)(2,1)S(1)}, u32[]{:S(2)}, u32[]{:S(2)}) collective-permute-start(bf16[96,1344]{0,1:T(8,128)(2,1)S(1)} %copy-done.51), channel_id=1, source_target_pairs={{0,8},{1,9},{2,10},{3,11},{4,12},{5,13},{6,14},{7,15},{8,16},{9,17... | collective-permute-start | bytes 774152 | tf_op jit(solution)/shard_map/ppermute | solution.py:230
  40.6 32.2 %collective-permute-start = (bf16[256,768]{1,0:T(8,128)(2,1)}, bf16[256,768]{1,0:T(8,128)(2,1)S(1)}, u32[]{:S(2)}, u32[]{:S(2)}) collective-permute-start(bf16[256,768]{1,0:T(8,128)(2,1)} %get-tuple-element.141), channel_id=1, source_target_pairs={{0,2},{1,3},{2,0},{3,1},{4,6},{5,7},{6,4},{7,5},{8,10},{9,11},{10,... | collective-permute-start | bytes 1179656 | tf_op jit(solution)/shard_map/ppermute | solution.py:230
  42.6 32.5 %collective-permute-start.35 = (bf16[256,768]{1,0:T(8,128)(2,1)}, bf16[256,768]{1,0:T(8,128)(2,1)S(1)}, u32[]{:S(2)}, u32[]{:S(2)}) collective-permute-start(bf16[256,768]{1,0:T(8,128)(2,1)} %fusion.106), channel_id=1, source_target_pairs={{0,2},{1,3},{2,0},{3,1},{4,6},{5,7},{6,4},{7,5},{8,10},{9,11},{10,... | collective-permute-start | bytes 1179656 | tf_op jit(solution)/shard_map/ppermute | solution.py:230
  49.5 29.4 %collective-permute-start.5 = (bf16[384,640]{0,1:T(8,128)(2,1)S(1)}, bf16[384,640]{0,1:T(8,128)(2,1)}, u32[]{:S(2)}, u32[]{:S(2)}) collective-permute-start(bf16[384,640]{0,1:T(8,128)(2,1)S(1)} %pad_maximum_fusion.44), channel_id=1, source_target_pairs={{0,4},{1,3},{2,6},{3,1},{4,0},{5,7},{6,2},{7,5},{8,12},{9,11},{10,... | collective-permute-start | bytes 1474568 | tf_op jit(solution)/shard_map/ppermute | solution.py:230
  70.7 22.9 %collective-permute-start.28 = (bf16[384,1152]{0,1:T(8,128)(2,1)}, bf16[384,1152]{0,1:T(8,128)(2,1)}, u32[]{:S(2)}, u32[]{:S(2)}) collective-permute-start(bf16[384,1152]{0,1:T(8,128)(2,1)} %pad_maximum_fusion.9), channel_id=1, source_target_pairs={{0,4},{1,3},{2,6},{3,1},{4,0},{5,7},{6,2},{7,5},{8,12},{9,11},{10,... | collective-permute-start | bytes 2654216 | tf_op jit(solution)/shard_map/ppermute | solution.py:230
  72.9 29.4 %collective-permute-start.27 = (bf16[384,1152]{0,1:T(8,128)(2,1)}, bf16[384,1152]{0,1:T(8,128)(2,1)}, u32[]{:S(2)}, u32[]{:S(2)}) collective-permute-start(bf16[384,1152]{0,1:T(8,128)(2,1)} %pad_maximum_fusion.9), channel_id=1, source_target_pairs={{0,2},{1,5},{2,0},{3,7},{4,6},{5,1},{6,4},{7,3},{8,10},{9,13},{10,... | collective-permute-start | bytes 2654216 | tf_op jit(solution)/shard_map/ppermute | solution.py:230
  75.1 48.1 %collective-permute-start.18 = (bf16[384,1344]{0,1:T(8,128)(2,1)}, bf16[384,1344]{0,1:T(8,128)(2,1)}, u32[]{:S(2)}, u32[]{:S(2)}) collective-permute-start(bf16[384,1344]{0,1:T(8,128)(2,1)} %pad_maximum_fusion.8), channel_id=1, source_target_pairs={{0,4},{1,3},{2,6},{3,1},{4,0},{5,7},{6,2},{7,5},{8,12},{9,11},{10,... | collective-permute-start | bytes 3096584 | tf_op jit(solution)/shard_map/ppermute | solution.py:230
  78.9 45.2 %collective-permute-start.17 = (bf16[384,1344]{0,1:T(8,128)(2,1)}, bf16[384,1344]{0,1:T(8,128)(2,1)}, u32[]{:S(2)}, u32[]{:S(2)}) collective-permute-start(bf16[384,1344]{0,1:T(8,128)(2,1)} %pad_maximum_fusion.8), channel_id=1, source_target_pairs={{0,2},{1,5},{2,0},{3,7},{4,6},{5,1},{6,4},{7,3},{8,10},{9,13},{10,... | collective-permute-start | bytes 3096584 | tf_op jit(solution)/shard_map/ppermute | solution.py:230
  89.2 21.2 %collective-permute-start.8 = (bf16[384,640]{0,1:T(8,128)(2,1)}, bf16[384,640]{0,1:T(8,128)(2,1)}, u32[]{:S(2)}, u32[]{:S(2)}) collective-permute-start(bf16[384,640]{0,1:T(8,128)(2,1)} %collective-permute-done.5), channel_id=1, source_target_pairs={{0,1},{1,0},{2,3},{3,2},{4,5},{5,4},{6,7},{7,6},{8,9},{9,8},{10,11... | collective-permute-start | bytes 1474568 | tf_op jit(solution)/shard_map/ppermute | solution.py:230
  102.2 21.0 %collective-permute-start.9 = (bf16[384,640]{0,1:T(8,128)(2,1)}, bf16[384,640]{0,1:T(8,128)(2,1)}, u32[]{:S(2)}, u32[]{:S(2)}) collective-permute-start(bf16[384,640]{0,1:T(8,128)(2,1)} %collective-permute-done.5), channel_id=1, source_target_pairs={{0,2},{1,5},{2,0},{3,7},{4,6},{5,1},{6,4},{7,3},{8,10},{9,13},{10,... | collective-permute-start | bytes 1474568 | tf_op jit(solution)/shard_map/ppermute | solution.py:230
  110.4 22.4 %collective-permute-start.6 = (bf16[384,640]{0,1:T(8,128)(2,1)}, bf16[384,640]{0,1:T(8,128)(2,1)}, u32[]{:S(2)}, u32[]{:S(2)}) collective-permute-start(bf16[384,640]{0,1:T(8,128)(2,1)} %copy-done.90), channel_id=1, source_target_pairs={{0,1},{1,0},{2,3},{3,2},{4,5},{5,4},{6,7},{7,6},{8,9},{9,8},{10,11... | collective-permute-start | bytes 1474568 | tf_op jit(solution)/shard_map/ppermute | solution.py:230
  110.4 69.3 %collective-permute-start.31 = (bf16[384,1152]{0,1:T(8,128)(2,1)}, bf16[384,1152]{0,1:T(8,128)(2,1)}, u32[]{:S(2)}, u32[]{:S(2)}) collective-permute-start(bf16[384,1152]{0,1:T(8,128)(2,1)} %collective-permute-done.28), channel_id=1, source_target_pairs={{0,1},{1,0},{2,3},{3,2},{4,5},{5,4},{6,7},{7,6},{8,9},{9,8},{10,11... | collective-permute-start | bytes 2654216 | tf_op jit(solution)/shard_map/ppermute | solution.py:230
  123.2 56.6 %collective-permute-start.30 = (bf16[384,1152]{0,1:T(8,128)(2,1)}, bf16[384,1152]{0,1:T(8,128)(2,1)}, u32[]{:S(2)}, u32[]{:S(2)}) collective-permute-start(bf16[384,1152]{0,1:T(8,128)(2,1)} %collective-permute-done.27), channel_id=1, source_target_pairs={{0,1},{1,0},{2,3},{3,2},{4,5},{5,4},{6,7},{7,6},{8,9},{9,8},{10,11... | collective-permute-start | bytes 2654216 | tf_op jit(solution)/shard_map/ppermute | solution.py:230
  123.2 64.9 %collective-permute-start.32 = (bf16[384,1152]{0,1:T(8,128)(2,1)}, bf16[384,1152]{0,1:T(8,128)(2,1)}, u32[]{:S(2)}, u32[]{:S(2)}) collective-permute-start(bf16[384,1152]{0,1:T(8,128)(2,1)} %collective-permute-done.28), channel_id=1, source_target_pairs={{0,2},{1,5},{2,0},{3,7},{4,6},{5,1},{6,4},{7,3},{8,10},{9,13},{10,... | collective-permute-start | bytes 2654216 | tf_op jit(solution)/shard_map/ppermute | solution.py:230
  132.8 55.7 %collective-permute-start.21 = (bf16[384,1344]{0,1:T(8,128)(2,1)}, bf16[384,1344]{0,1:T(8,128)(2,1)}, u32[]{:S(2)}, u32[]{:S(2)}) collective-permute-start(bf16[384,1344]{0,1:T(8,128)(2,1)} %collective-permute-done.18), channel_id=1, source_target_pairs={{0,1},{1,0},{2,3},{3,2},{4,5},{5,4},{6,7},{7,6},{8,9},{9,8},{10,11... | collective-permute-start | bytes 3096584 | tf_op jit(solution)/shard_map/ppermute | solution.py:230
  132.8 50.5 %collective-permute-start.22 = (bf16[384,1344]{0,1:T(8,128)(2,1)}, bf16[384,1344]{0,1:T(8,128)(2,1)}, u32[]{:S(2)}, u32[]{:S(2)}) collective-permute-start(bf16[384,1344]{0,1:T(8,128)(2,1)} %collective-permute-done.18), channel_id=1, source_target_pairs={{0,2},{1,5},{2,0},{3,7},{4,6},{5,1},{6,4},{7,3},{8,10},{9,13},{10,... | collective-permute-start | bytes 3096584 | tf_op jit(solution)/shard_map/ppermute | solution.py:230
  188.0 49.2 %collective-permute-start.29 = (bf16[384,1152]{0,1:T(8,128)(2,1)}, bf16[384,1152]{0,1:T(8,128)(2,1)}, u32[]{:S(2)}, u32[]{:S(2)}) collective-permute-start(bf16[384,1152]{0,1:T(8,128)(2,1)} %pad_maximum_fusion.9), channel_id=1, source_target_pairs={{0,1},{1,0},{2,3},{3,2},{4,5},{5,4},{6,7},{7,6},{8,9},{9,8},{10,11... | collective-permute-start | bytes 2654216 | tf_op jit(solution)/shard_map/ppermute | solution.py:230
  188.5 52.4 %collective-permute-start.33 = (bf16[384,1152]{0,1:T(8,128)(2,1)}, bf16[384,1152]{0,1:T(8,128)(2,1)}, u32[]{:S(2)}, u32[]{:S(2)}) collective-permute-start(bf16[384,1152]{0,1:T(8,128)(2,1)} %collective-permute-done.32), channel_id=1, source_target_pairs={{0,1},{1,0},{2,3},{3,2},{4,5},{5,4},{6,7},{7,6},{8,9},{9,8},{10,11... | collective-permute-start | bytes 2654216 | tf_op jit(solution)/shard_map/ppermute | solution.py:230
  188.6 26.8 %collective-permute-start.23 = (bf16[384,1344]{0,1:T(8,128)(2,1)}, bf16[384,1344]{0,1:T(8,128)(2,1)}, u32[]{:S(2)}, u32[]{:S(2)}) collective-permute-start(bf16[384,1344]{0,1:T(8,128)(2,1)} %collective-permute-done.22), channel_id=1, source_target_pairs={{0,1},{1,0},{2,3},{3,2},{4,5},{5,4},{6,7},{7,6},{8,9},{9,8},{10,11... | collective-permute-start | bytes 3096584 | tf_op jit(solution)/shard_map/ppermute | solution.py:230
  276.3 86.2 %collective-permute-start.63 = (bf16[768,768]{1,0:T(8,128)(2,1)}, bf16[768,768]{1,0:T(8,128)(2,1)}, u32[]{:S(2)}, u32[]{:S(2)}) collective-permute-start(bf16[768,768]{1,0:T(8,128)(2,1)} %pad_maximum_fusion.7), channel_id=1, source_target_pairs={{0,1},{1,0},{2,3},{3,2},{4,5},{5,4},{6,7},{7,6},{8,9},{9,8},{10,11... | collective-permute-start | bytes 3538952 | tf_op jit(solution)/shard_map/ppermute | solution.py:230
  278.3 86.8 %collective-permute-start.47 = (bf16[768,768]{1,0:T(8,128)(2,1)}, bf16[768,768]{1,0:T(8,128)(2,1)}, u32[]{:S(2)}, u32[]{:S(2)}) collective-permute-start(bf16[768,768]{1,0:T(8,128)(2,1)} %convolution_convert_fusion.4), channel_id=1, source_target_pairs={{0,1},{1,0},{2,3},{3,2},{4,5},{5,4},{6,7},{7,6},{8,9},{9,8},{10,11... | collective-permute-start | bytes 3538952 | tf_op jit(solution)/shard_map/ppermute | solution.py:230
  282.3 84.9 %collective-permute-start.55 = (bf16[768,768]{1,0:T(8,128)(2,1)}, bf16[768,768]{1,0:T(8,128)(2,1)}, u32[]{:S(2)}, u32[]{:S(2)}) collective-permute-start(bf16[768,768]{1,0:T(8,128)(2,1)} %convolution_convert_fusion), channel_id=1, source_target_pairs={{0,1},{1,0},{2,3},{3,2},{4,5},{5,4},{6,7},{7,6},{8,9},{9,8},{10,11... | collective-permute-start | bytes 3538952 | tf_op jit(solution)/shard_map/ppermute | solution.py:230
  339.9 30.5 %collective-permute-start.36 = (bf16[512,1536]{1,0:T(8,128)(2,1)}, bf16[512,1536]{1,0:T(8,128)(2,1)}, u32[]{:S(2)}, u32[]{:S(2)}) collective-permute-start(bf16[512,1536]{1,0:T(8,128)(2,1)} %concatenate.224), channel_id=1, source_target_pairs={{0,1},{1,0},{2,3},{3,2},{4,5},{5,4},{6,7},{7,6},{8,9},{9,8},{10,11... | collective-permute-start | bytes 4718600 | tf_op jit(solution)/shard_map/ppermute | solution.py:230
  361.5 41.2 %collective-permute-start.62 = (bf16[768,768]{1,0:T(8,128)(2,1)}, bf16[768,768]{1,0:T(8,128)(2,1)}, u32[]{:S(2)}, u32[]{:S(2)}) collective-permute-start(bf16[768,768]{1,0:T(8,128)(2,1)} %pad_maximum_fusion.6), channel_id=1, source_target_pairs={{0,1},{1,0},{2,3},{3,2},{4,5},{5,4},{6,7},{7,6},{8,9},{9,8},{10,11... | collective-permute-start | bytes 3538952 | tf_op jit(solution)/shard_map/ppermute | solution.py:230
  362.5 43.5 %collective-permute-start.46 = (bf16[768,768]{1,0:T(8,128)(2,1)}, bf16[768,768]{1,0:T(8,128)(2,1)}, u32[]{:S(2)}, u32[]{:S(2)}) collective-permute-start(bf16[768,768]{1,0:T(8,128)(2,1)} %convolution_convert_fusion.6), channel_id=1, source_target_pairs={{0,1},{1,0},{2,3},{3,2},{4,5},{5,4},{6,7},{7,6},{8,9},{9,8},{10,11... | collective-permute-start | bytes 3538952 | tf_op jit(solution)/shard_map/ppermute | solution.py:230
  365.1 44.9 %collective-permute-start.54 = (bf16[768,768]{1,0:T(8,128)(2,1)}, bf16[768,768]{1,0:T(8,128)(2,1)}, u32[]{:S(2)}, u32[]{:S(2)}) collective-permute-start(bf16[768,768]{1,0:T(8,128)(2,1)} %convolution_convert_fusion.2), channel_id=1, source_target_pairs={{0,1},{1,0},{2,3},{3,2},{4,5},{5,4},{6,7},{7,6},{8,9},{9,8},{10,11... | collective-permute-start | bytes 3538952 | tf_op jit(solution)/shard_map/ppermute | solution.py:230
  367.1 36.9 %collective-permute-start.65 = (bf16[384,768]{1,0:T(8,128)(2,1)}, bf16[384,768]{1,0:T(8,128)(2,1)}, u32[]{:S(2)}, u32[]{:S(2)}) collective-permute-start(bf16[384,768]{1,0:T(8,128)(2,1)} %add_convert_fusion.8), channel_id=1, source_target_pairs={{0,2},{1,5},{2,0},{3,7},{4,6},{5,1},{6,4},{7,3},{8,10},{9,13},{10,... | collective-permute-start | bytes 1769480 | tf_op jit(solution)/shard_map/ppermute | solution.py:230
  370.4 36.7 %collective-permute-start.49 = (bf16[384,768]{1,0:T(8,128)(2,1)}, bf16[384,768]{1,0:T(8,128)(2,1)}, u32[]{:S(2)}, u32[]{:S(2)}) collective-permute-start(bf16[384,768]{1,0:T(8,128)(2,1)} %add_convert_fusion.12), channel_id=1, source_target_pairs={{0,2},{1,5},{2,0},{3,7},{4,6},{5,1},{6,4},{7,3},{8,10},{9,13},{10,... | collective-permute-start | bytes 1769480 | tf_op jit(solution)/shard_map/ppermute | solution.py:230
  404.0 67.0 %collective-permute-start.39 = (bf16[768,896]{0,1:T(8,128)(2,1)S(1)}, bf16[768,896]{0,1:T(8,128)(2,1)S(1)}, u32[]{:S(2)}, u32[]{:S(2)}) collective-permute-start(bf16[768,896]{0,1:T(8,128)(2,1)S(1)} %constant_dynamic-update-slice_fusion.3), channel_id=1, source_target_pairs={{0,1},{1,0},{2,3},{3,2},{4,5},{5,4},{6,7},{7,6},{8,9},{9,8},{10,11... | collective-permute-start | bytes 4128776 | tf_op jit(solution)/shard_map/ppermute | solution.py:230
  406.0 18.9 %collective-permute-start.37 = (bf16[256,768]{1,0:T(8,128)(2,1)S(1)}, bf16[256,768]{1,0:T(8,128)(2,1)S(1)}, u32[]{:S(2)}, u32[]{:S(2)}) collective-permute-start(bf16[256,768]{1,0:T(8,128)(2,1)S(1)} %slice.951), channel_id=1, source_target_pairs={{0,2},{1,3},{2,0},{3,1},{4,6},{5,7},{6,4},{7,5},{8,10},{9,11},{10,... | collective-permute-start | bytes 1179656 | tf_op jit(solution)/shard_map/ppermute | solution.py:230
  407.0 30.5 %collective-permute-start.64 = (bf16[384,768]{1,0:T(8,128)(2,1)S(1)}, bf16[384,768]{1,0:T(8,128)(2,1)S(1)}, u32[]{:S(2)}, u32[]{:S(2)}) collective-permute-start(bf16[384,768]{1,0:T(8,128)(2,1)S(1)} %get-tuple-element.67), channel_id=1, source_target_pairs={{0,2},{1,5},{2,0},{3,7},{4,6},{5,1},{6,4},{7,3},{8,10},{9,13},{10,... | collective-permute-start | bytes 1769480 | tf_op jit(solution)/shard_map/ppermute | solution.py:230
  410.0 28.7 %collective-permute-start.66 = (bf16[384,768]{1,0:T(8,128)(2,1)S(1)}, bf16[384,768]{1,0:T(8,128)(2,1)S(1)}, u32[]{:S(2)}, u32[]{:S(2)}) collective-permute-start(bf16[384,768]{1,0:T(8,128)(2,1)S(1)} %get-tuple-element.68), channel_id=1, source_target_pairs={{0,4},{1,3},{2,6},{3,1},{4,0},{5,7},{6,2},{7,5},{8,12},{9,11},{10,... | collective-permute-start | bytes 1769480 | tf_op jit(solution)/shard_map/ppermute | solution.py:230
  416.5 33.7 %collective-permute-start.48 = (bf16[384,768]{1,0:T(8,128)(2,1)S(1)}, bf16[384,768]{1,0:T(8,128)(2,1)S(1)}, u32[]{:S(2)}, u32[]{:S(2)}) collective-permute-start(bf16[384,768]{1,0:T(8,128)(2,1)S(1)} %get-tuple-element.69), channel_id=1, source_target_pairs={{0,2},{1,5},{2,0},{3,7},{4,6},{5,1},{6,4},{7,3},{8,10},{9,13},{10,... | collective-permute-start | bytes 1769480 | tf_op jit(solution)/shard_map/ppermute | solution.py:230
  424.9 25.3 %collective-permute-start.50 = (bf16[384,768]{1,0:T(8,128)(2,1)S(1)}, bf16[384,768]{1,0:T(8,128)(2,1)S(1)}, u32[]{:S(2)}, u32[]{:S(2)}) collective-permute-start(bf16[384,768]{1,0:T(8,128)(2,1)S(1)} %get-tuple-element.70), channel_id=1, source_target_pairs={{0,4},{1,3},{2,6},{3,1},{4,0},{5,7},{6,2},{7,5},{8,12},{9,11},{10,... | collective-permute-start | bytes 1769480 | tf_op jit(solution)/shard_map/ppermute | solution.py:230
  437.6 24.1 %collective-permute-start.56 = (bf16[384,768]{1,0:T(8,128)(2,1)S(1)}, bf16[384,768]{1,0:T(8,128)(2,1)S(1)}, u32[]{:S(2)}, u32[]{:S(2)}) collective-permute-start(bf16[384,768]{1,0:T(8,128)(2,1)S(1)} %get-tuple-element.71), channel_id=1, source_target_pairs={{0,2},{1,5},{2,0},{3,7},{4,6},{5,1},{6,4},{7,3},{8,10},{9,13},{10,... | collective-permute-start | bytes 1769480 | tf_op jit(solution)/shard_map/ppermute | solution.py:230
  438.7 27.0 %collective-permute-start.58 = (bf16[384,768]{1,0:T(8,128)(2,1)S(1)}, bf16[384,768]{1,0:T(8,128)(2,1)S(1)}, u32[]{:S(2)}, u32[]{:S(2)}) collective-permute-start(bf16[384,768]{1,0:T(8,128)(2,1)S(1)} %get-tuple-element.72), channel_id=1, source_target_pairs={{0,4},{1,3},{2,6},{3,1},{4,0},{5,7},{6,2},{7,5},{8,12},{9,11},{10,... | collective-permute-start | bytes 1769480 | tf_op jit(solution)/shard_map/ppermute | solution.py:230
  450.2 45.0 %collective-permute-start.38 = (bf16[768,896]{0,1:T(8,128)(2,1)S(1)}, bf16[768,896]{0,1:T(8,128)(2,1)S(1)}, u32[]{:S(2)}, u32[]{:S(2)}) collective-permute-start(bf16[768,896]{0,1:T(8,128)(2,1)S(1)} %get-tuple-element.173), channel_id=1, source_target_pairs={{0,1},{1,0},{2,3},{3,2},{4,5},{5,4},{6,7},{7,6},{8,9},{9,8},{10,11... | collective-permute-start | bytes 4128776 | tf_op jit(solution)/shard_map/ppermute | solution.py:230
  451.7 20.7 %collective-permute-start.51 = (bf16[96,768]{1,0:T(8,128)(2,1)S(1)}, bf16[96,768]{1,0:T(8,128)(2,1)S(1)}, u32[]{:S(2)}, u32[]{:S(2)}) collective-permute-start(bf16[96,768]{1,0:T(8,128)(2,1)S(1)} %get-tuple-element.148), channel_id=1, source_target_pairs={{0,8},{1,9},{2,10},{3,11},{4,12},{5,13},{6,14},{7,15},{8,16},{9,17... | collective-permute-start | bytes 442376 | tf_op jit(solution)/shard_map/ppermute | solution.py:230
  471.3 24.0 %collective-permute-start.41 = (bf16[384,896]{0,1:T(8,128)(2,1)S(1)}, bf16[384,896]{0,1:T(8,128)(2,1)S(1)}, u32[]{:S(2)}, u32[]{:S(2)}) collective-permute-start(bf16[384,896]{0,1:T(8,128)(2,1)S(1)} %add_convert_fusion.6), channel_id=1, source_target_pairs={{0,2},{1,5},{2,0},{3,7},{4,6},{5,1},{6,4},{7,3},{8,10},{9,13},{10,... | collective-permute-start | bytes 2064392 | tf_op jit(solution)/shard_map/ppermute | solution.py:230
  485.4 28.9 %collective-permute-start.67 = (bf16[96,768]{1,0:T(8,128)(2,1)S(1)}, bf16[96,768]{1,0:T(8,128)(2,1)S(1)}, u32[]{:S(2)}, u32[]{:S(2)}) collective-permute-start(bf16[96,768]{1,0:T(8,128)(2,1)S(1)} %get-tuple-element.145), channel_id=1, source_target_pairs={{0,8},{1,9},{2,10},{3,11},{4,12},{5,13},{6,14},{7,15},{8,16},{9,17... | collective-permute-start | bytes 442376 | tf_op jit(solution)/shard_map/ppermute | solution.py:230
  492.0 22.6 %collective-permute-start.68 = (bf16[96,768]{1,0:T(8,128)(2,1)S(1)}, bf16[96,768]{1,0:T(8,128)(2,1)S(1)}, u32[]{:S(2)}, u32[]{:S(2)}) collective-permute-start(bf16[96,768]{1,0:T(8,128)(2,1)S(1)} %get-tuple-element.147), channel_id=1, source_target_pairs={{0,16},{1,17},{2,18},{3,19},{4,20},{5,21},{6,22},{7,23},{8,24},{9,... | collective-permute-start | bytes 442376 | tf_op jit(solution)/shard_map/ppermute | solution.py:230
  492.0 22.5 %collective-permute-start.69 = (bf16[96,768]{1,0:T(8,128)(2,1)S(1)}, bf16[96,768]{1,0:T(8,128)(2,1)S(1)}, u32[]{:S(2)}, u32[]{:S(2)}) collective-permute-start(bf16[96,768]{1,0:T(8,128)(2,1)S(1)} %get-tuple-element.146), channel_id=1, source_target_pairs={{0,24},{1,25},{2,26},{3,27},{4,28},{5,29},{6,30},{7,31},{8,0},{9,1... | collective-permute-start | bytes 442376 | tf_op jit(solution)/shard_map/ppermute | solution.py:230
  (142 other events, 1218.0 us)

commit v3 on v2

v3 whole, which is shorter than its diff:
```python
import functools
import math

import jax
import jax.numpy as jnp
from jax import lax
from jax.experimental import pallas as pl
from jax.experimental.pallas import tpu as pltpu
from jax.sharding import PartitionSpec as P

HD = 64
PAIR = 2 * HD
QROWS = 256
epsilon = 1e-12
rope_base = 1000.0
masked_score = -1e30
f32 = jnp.float32
bf16 = jnp.bfloat16

NN = (((1,), (0,)), ((), ()))
NT = (((1,), (1,)), ((), ()))
TN = (((0,), (0,)), ((), ()))


def dot(a, b, dims=NN):
    return lax.dot_general(a, b, dims, preferred_element_type=f32)


def rope_tables(positions, width):
    half_dim = HD // 2
    freq = rope_base ** (-jnp.arange(half_dim, dtype=f32) / half_dim)
    angles = positions.astype(f32)[:, None] * freq[None, :]
    cosine, sine = jnp.cos(angles), jnp.sin(angles)
    times = width // HD
    return (
        jnp.tile(jnp.concatenate([cosine, cosine], axis=1), (1, times)),
        jnp.tile(jnp.concatenate([-sine, sine], axis=1), (1, times)),
    )


def rotated(values, cosine, sine):
    width = values.shape[1]
    lane = lax.broadcasted_iota(jnp.int32, values.shape, 1)
    up = pltpu.roll(values, width - HD // 2, 1)
    down = pltpu.roll(values, HD // 2, 1)
    return values * cosine + jnp.where(lane % HD < HD // 2, up, down) * sine


def normalize(hidden):
    centred = hidden - jnp.mean(hidden, axis=-1, keepdims=True)
    variance = jnp.mean(centred * centred, axis=-1, keepdims=True)
    inv_std = lax.rsqrt(variance + epsilon)
    return (centred * inv_std, inv_std)


def norm_back(grad_norm, normed, inv_std):
    return inv_std * (
        grad_norm
        - jnp.mean(grad_norm, axis=-1, keepdims=True)
        - normed * jnp.mean(grad_norm * normed, axis=-1, keepdims=True)
    )


BLOCKS = 10


def block_starts(width):
    half, quarter = width // 2, width // 4
    return [(0, 0), (0, half), (1, 0), (1, half), (1, half + quarter)]


def weight_copies(blocks, w_ref, sems, core):
    copies = []
    for k in range(2):
        for block, (y, row) in zip(blocks[5 * k : 5 * k + 5], block_starts(w_ref.shape[1])):
            slot = 2 * y + jnp.bitwise_xor(core, k)
            copies.append(
                pltpu.make_async_copy(
                    block, w_ref.at[slot, pl.ds(row, block.shape[0])], sems.at[slot]
                )
            )
    return copies


def start_weights(blocks, w_ref, sems, core):
    @pl.when(pl.program_id(0) == 0)
    def _():
        for copy in weight_copies(blocks, w_ref, sems, core):
            copy.start()


def wait_weights(w_ref, sems, slot):
    pltpu.make_async_copy(w_ref.at[slot], w_ref.at[slot], sems.at[slot]).wait()


def weight_scratch(blocks):
    width = 2 * blocks[0].shape[0]
    return [
        pltpu.VMEM((4, width, blocks[0].shape[1]), bf16),
        pltpu.SemaphoreType.DMA((4,)),
    ]


ANY = pl.BlockSpec(memory_space=pl.ANY)


def cost(flops, nbytes, exps=0):
    return pl.CostEstimate(flops=int(flops), bytes_accessed=int(nbytes), transcendentals=int(exps))


def whole(shape):
    return pl.BlockSpec(shape, lambda *_: (0,) * len(shape))


def qkv_kernel(core_ref, x_ref, cos_ref, sin_ref, *rest):
    blocks, (q_ref, kv_ref, wo_ref, w_ref, sems) = rest[:BLOCKS], rest[BLOCKS:]
    slot = pl.program_id(0)
    start_weights(blocks, w_ref, sems, core_ref[0])
    wait_weights(w_ref, sems, slot)
    lane = lax.broadcasted_iota(jnp.int32, (w_ref.shape[1], 4 * HD), 1)
    cosine, sine = cos_ref[...], sin_ref[...]
    part = w_ref.shape[2] // 3
    x = x_ref[...]
    q = dot(x, w_ref[slot, :, :part])
    q_ref[...] = (rotated(q, cosine, sine) * (1.0 / math.sqrt(HD))).astype(bf16)
    k = dot(x, w_ref[slot, :, part : 2 * part])
    kv_ref[:, :part] = rotated(k, cosine, sine).astype(bf16)
    kv_ref[:, part:] = dot(x, w_ref[slot, :, 2 * part :]).astype(bf16)
    out = jnp.zeros(lane.shape, f32)
    for h in range(3):
        piece = w_ref[slot, :, h * part : (h + 1) * part].astype(f32)
        piece = pltpu.roll(piece, (h + 1) * HD, 1)
        out = jnp.where(lane // HD == h, piece, out)
    wo_ref[...] = out.astype(bf16)


def qkv(core, x, cosine, sine, blocks):
    rows, width = x.shape
    part = blocks[0].shape[1] // 3
    grid_spec = pltpu.PrefetchScalarGridSpec(
        num_scalar_prefetch=1,
        grid=(4,),
        in_specs=[whole((rows, width)), whole((rows, part)), whole((rows, part))] + [ANY] * BLOCKS,
        out_specs=[
            pl.BlockSpec((rows, part), lambda i, core: (0, i)),
            pl.BlockSpec((rows, 2 * part), lambda i, core: (0, i)),
            pl.BlockSpec((width, part), lambda i, core: (0, i)),
        ],
        scratch_shapes=weight_scratch(blocks),
    )
    return pl.pallas_call(
        qkv_kernel,
        grid_spec=grid_spec,
        out_shape=[
            jax.ShapeDtypeStruct((rows, 4 * part), bf16),
            jax.ShapeDtypeStruct((rows, 8 * part), bf16),
            jax.ShapeDtypeStruct((width, 4 * part), bf16),
        ],
        cost_estimate=cost(24 * rows * width * part, 40 * width * part),
        name="qkv",
    )(core, x, cosine, sine, *blocks)


def attend_kernel(q_ref, own_ref, other_ref, segq_ref, segk_ref, out_ref, log_ref):
    rows, part = q_ref.shape
    low_half = lax.broadcasted_iota(jnp.int32, (QROWS, PAIR), 1) < HD
    keys = jnp.concatenate([own_ref[:, :part], other_ref[:, :part]], axis=0)
    values = jnp.concatenate([own_ref[:, part:], other_ref[:, part:]], axis=0)
    values_t = values.T
    for block in range(rows // QROWS):
        span = slice(block * QROWS, (block + 1) * QROWS)
        q = q_ref[span, :]
        bias = jnp.where(segk_ref[...] == segq_ref[:, span], 0.0, masked_score)
        parts = []
        for h in range(3):
            pair = slice(h // 2 * PAIR, (h // 2 + 1) * PAIR)
            mine = low_half if h % 2 == 0 else jnp.logical_not(low_half)
            masked = jnp.where(mine, q[:, pair], jnp.zeros((QROWS, PAIR), bf16))
            scores = dot(keys[:, pair], masked, NT) + bias
            top = jnp.max(scores, axis=0, keepdims=True)
            expo = jnp.exp(scores - top)
            total = jnp.sum(expo, axis=0, keepdims=True)
            out = dot(values_t[h * HD : (h + 1) * HD, :], expo.astype(bf16))
            parts.append(out / total)
            log_ref[0, h : h + 1, span] = top + jnp.log(total)
        parts.append(jnp.zeros((HD, QROWS), f32))
        out_ref[span, :] = jnp.concatenate(parts, axis=0).T.astype(bf16)


def attend(q, kv_own, kv_other, seg_q, seg_k):
    rows, width = q.shape
    part = width // 4
    keys = seg_k.shape[0]
    by_part = lambda j: (0, j)
    return pl.pallas_call(
        attend_kernel,
        grid=(4,),
        in_specs=[
            pl.BlockSpec((rows, part), by_part),
            pl.BlockSpec((rows, 2 * part), by_part),
            pl.BlockSpec((rows, 2 * part), by_part),
            whole((1, rows)),
            whole((keys, 1)),
        ],
        out_specs=[
            pl.BlockSpec((rows, part), by_part),
            pl.BlockSpec((1, 8, rows), lambda j: (j, 0, 0)),
        ],
        out_shape=[
            jax.ShapeDtypeStruct((rows, width), bf16),
            jax.ShapeDtypeStruct((4, 8, rows), f32),
        ],
        cost_estimate=cost(16 * rows * keys * width, 12 * keys * width, rows * keys * 12),
        name="attend",
    )(q, kv_own, kv_other, seg_q, seg_k)


def attend_back_kernel(
    q_ref, own_ref, other_ref, do_ref, log_ref, delta_ref, segq_ref, segk_ref, cos_ref, sin_ref,
    dq_ref, dkv_own_ref, dkv_other_ref,
):
    rows, part = q_ref.shape
    low_half = lax.broadcasted_iota(jnp.int32, (QROWS, PAIR), 1) < HD
    keys = jnp.concatenate([own_ref[:, :part], other_ref[:, :part]], axis=0)
    values = jnp.concatenate([own_ref[:, part:], other_ref[:, part:]], axis=0)
    keys_t = keys.T
    dk = [0.0, 0.0]
    dv = [0.0, 0.0]
    for block in range(rows // QROWS):
        span = slice(block * QROWS, (block + 1) * QROWS)
        q = q_ref[span, :]
        do = do_ref[span, :]
        bias = jnp.where(segk_ref[...] == segq_ref[:, span], 0.0, masked_score)
        dq = []
        for h in range(3):
            pair = slice(h // 2 * PAIR, (h // 2 + 1) * PAIR)
            mine = low_half if h % 2 == 0 else jnp.logical_not(low_half)
            zero = jnp.zeros((QROWS, PAIR), bf16)
            q_head = jnp.where(mine, q[:, pair], zero)
            do_head = jnp.where(mine, do[:, pair], zero)
            scores = dot(keys[:, pair], q_head, NT) + bias
            probs = jnp.exp(scores - log_ref[0, h : h + 1, span])
            dprobs = dot(values[:, pair], do_head, NT)
            dscores = (probs * (dprobs - delta_ref[0, h : h + 1, span])).astype(bf16)
            dv[h // 2] = dv[h // 2] + dot(probs.astype(bf16), do_head)
            dk[h // 2] = dk[h // 2] + dot(dscores, q_head)
            dq.append(dot(keys_t[h * HD : (h + 1) * HD, :], dscores))
        dq.append(jnp.zeros((HD, QROWS), f32))
        dq = (jnp.concatenate(dq, axis=0) * (1.0 / math.sqrt(HD))).T
        dq_ref[span, :] = rotated(dq, cos_ref[span, :], -sin_ref[span, :]).astype(bf16)
    for i, pieces in enumerate((dk, dv)):
        for p in range(2):
            lanes = slice(i * part + p * PAIR, i * part + (p + 1) * PAIR)
            dkv_own_ref[:, lanes] = pieces[p][:rows]
            dkv_other_ref[:, lanes] = pieces[p][rows:].astype(bf16)


def attend_back(q, kv_own, kv_other, do, logs, delta, seg_q, seg_k, cosine, sine):
    rows, width = q.shape
    part = width // 4
    keys = seg_k.shape[0]
    by_part = lambda j: (0, j)
    stat = pl.BlockSpec((1, 8, rows), lambda j: (j, 0, 0))
    return pl.pallas_call(
        attend_back_kernel,
        grid=(4,),
        in_specs=[
            pl.BlockSpec((rows, part), by_part),
            pl.BlockSpec((rows, 2 * part), by_part),
            pl.BlockSpec((rows, 2 * part), by_part),
            pl.BlockSpec((rows, part), by_part),
            stat,
            stat,
            whole((1, rows)),
            whole((keys, 1)),
            whole((rows, part)),
            whole((rows, part)),
        ],
        out_specs=[
            pl.BlockSpec((rows, part), by_part),
            pl.BlockSpec((rows, 2 * part), by_part),
            pl.BlockSpec((rows, 2 * part), by_part),
        ],
        out_shape=[
            jax.ShapeDtypeStruct((rows, width), bf16),
            jax.ShapeDtypeStruct((rows, 2 * width), f32),
            jax.ShapeDtypeStruct((rows, 2 * width), bf16),
        ],
        cost_estimate=cost(40 * rows * keys * width, 30 * keys * width, rows * keys * 12),
        name="attend_back",
    )(q, kv_own, kv_other, do, logs, delta, seg_q, seg_k, cosine, sine)


def first_kernel(x_ref, att_ref, wo_ref, norm_a_ref, norm_b_ref, n_ref, s_ref, low_ref, low_t_ref, gains_ref):
    norms = jnp.concatenate([norm_a_ref[...], norm_b_ref[...]], axis=0).astype(f32).T
    gains_ref[...] = norms[:8]
    branch = dot(att_ref[...], wo_ref[...], NT)
    normed, inv = normalize(x_ref[...].astype(f32) + branch)
    n_ref[...] = normed
    s_ref[...] = jnp.broadcast_to(inv, s_ref.shape)
    first = normed * norms[0:1] + norms[2:3]
    low_ref[...] = first.astype(bf16)
    low_t_ref[...] = first.T.astype(bf16)


def first_norm(x, attended, wo, norm_a, norm_b):
    rows, width = x.shape
    at = norm_a.shape[1] // 128 - 1
    strip = pl.BlockSpec((width // 2, 128), lambda i: (0, at))
    return pl.pallas_call(
        first_kernel,
        grid=(1,),
        in_specs=[whole(x.shape), whole(attended.shape), whole(wo.shape), strip, strip],
        out_specs=[
            whole((rows, width)), whole((rows, 128)), whole((rows, width)), whole((width, rows)), whole((8, width)),
        ],
        out_shape=[
            jax.ShapeDtypeStruct((rows, width), f32),
            jax.ShapeDtypeStruct((rows, 128), f32),
            jax.ShapeDtypeStruct((rows, width), bf16),
            jax.ShapeDtypeStruct((width, rows), bf16),
            jax.ShapeDtypeStruct((8, width), f32),
        ],
        cost_estimate=cost(2 * rows * width * wo.shape[1], 16 * rows * width),
        name="first_norm",
    )(x, attended, wo, norm_a, norm_b)


def mlp_kernel(has_base, core_ref, low_ref, *rest):
    if has_base:
        base_ref, rest = rest[0], rest[1:]
    blocks, (act_ref, feed_ref, w_ref, sems) = rest[:BLOCKS], rest[BLOCKS:]
    slot = pl.program_id(0)
    half = act_ref.shape[3]
    start_weights(blocks, w_ref, sems, core_ref[0])

    @pl.when(slot == 0)
    def _():
        feed_ref[...] = base_ref[...] if has_base else jnp.zeros_like(feed_ref)

    wait_weights(w_ref, sems, slot)

    def body(i, _):
        span = pl.ds(pl.multiple_of(i * QROWS, QROWS), QROWS)
        low = low_ref[span, :]
        gate = dot(low, w_ref[slot, :, half : 2 * half])
        up = dot(low, w_ref[slot, :, 2 * half : 3 * half])
        hidden = (gate / (1.0 + jnp.exp(-gate)) * up).astype(bf16)
        act_ref[0, 0, span, :] = gate.astype(bf16)
        act_ref[0, 1, span, :] = up.astype(bf16)
        act_ref[0, 2, span, :] = hidden
        feed_ref[span, :] += dot(hidden, w_ref[slot, :, :half], NT)
        return 0

    lax.fori_loop(0, low_ref.shape[0] // QROWS, body, 0)


def mlp(core, low, base, blocks, half):
    rows, width = low.shape
    has_base = base is not None
    extra = [base] if has_base else []
    grid_spec = pltpu.PrefetchScalarGridSpec(
        num_scalar_prefetch=1,
        grid=(4,),
        in_specs=[whole((rows, width))] + [whole((rows, width))] * has_base + [ANY] * BLOCKS,
        out_specs=[
            pl.BlockSpec((1, 3, rows, half), lambda i, core: (i, 0, 0, 0)),
            whole((rows, width)),
        ],
        scratch_shapes=weight_scratch(blocks),
    )
    return pl.pallas_call(
        functools.partial(mlp_kernel, has_base),
        grid_spec=grid_spec,
        out_shape=[
            jax.ShapeDtypeStruct((4, 3, rows, half), bf16),
            jax.ShapeDtypeStruct((rows, width), f32),
        ],
        cost_estimate=cost(24 * rows * width * half, 60 * half * width, 4 * rows * half),
        name="mlp",
    )(core, low, *extra, *blocks)


def second_kernel(n_ref, gains_ref, feed_ref, dy_ref, out_ref, dh_ref, low_ref, low_t_ref, sums_ref):
    first = n_ref[...] * gains_ref[0:1] + gains_ref[2:3]
    normed, inv = normalize(first + feed_ref[...])
    out_ref[...] = (normed * gains_ref[1:2] + gains_ref[3:4]).astype(bf16)
    dy = dy_ref[...]
    sums_ref[...] = jnp.zeros_like(sums_ref)
    sums_ref[1:2] = jnp.sum(dy * normed, axis=0, keepdims=True)
    sums_ref[3:4] = jnp.sum(dy, axis=0, keepdims=True)
    dh = norm_back(dy * gains_ref[1:2], normed, inv)
    dh_ref[...] = dh
    low_ref[...] = dh.astype(bf16)
    low_t_ref[...] = dh.T.astype(bf16)


def second_norm(n1, gains, feed, dy):
    rows, width = n1.shape
    full = whole((rows, width))
    return pl.pallas_call(
        second_kernel,
        grid=(1,),
        in_specs=[full, whole((8, width)), full, full],
        out_specs=[full, full, full, whole((width, rows)), whole((8, width))],
        out_shape=[
            jax.ShapeDtypeStruct((rows, width), bf16),
            jax.ShapeDtypeStruct((rows, width), f32),
            jax.ShapeDtypeStruct((rows, width), bf16),
            jax.ShapeDtypeStruct((width, rows), bf16),
            jax.ShapeDtypeStruct((8, width), f32),
        ],
        cost_estimate=cost(40 * rows * width, 22 * rows * width),
        name="second_norm",
    )(n1, gains, feed, dy)


def for_slot(i, core):
    return 2 * (i % 2) + jnp.bitwise_xor(core[0], 1 - i // 2)


def to_other(i, core):
    return jnp.minimum(i, 1)


def to_own(i, core):
    return jnp.maximum(i - 2, 0)


def mlp_back_kernel(core_ref, base_ref, dfeed_ref, dfeed_t_ref, low_t_ref, act_ref, *rest):
    blocks, (dfirst_ref, send_ref, keep_ref, w_ref, sems, part_ref) = rest[:BLOCKS], rest[BLOCKS:]
    step = pl.program_id(0)
    slot = for_slot(step, core_ref)
    half = act_ref.shape[3]
    start_weights(blocks, w_ref, sems, core_ref[0])

    @pl.when(step == 0)
    def _():
        dfirst_ref[...] = base_ref[...]

    wait_weights(w_ref, sems, slot)

    def body(i, _):
        span = pl.ds(pl.multiple_of(i * QROWS, QROWS), QROWS)
        dhidden = dot(dfeed_ref[span, :], w_ref[slot, :, :half])
        gate = act_ref[0, 0, span, :].astype(f32)
        up = act_ref[0, 1, span, :].astype(f32)
        sg = 1.0 / (1.0 + jnp.exp(-gate))
        dgate = dhidden * up * sg * (1.0 + gate * (1.0 - sg))
        dup = dhidden * (gate * sg)
        part_ref[span, :half] = dgate.astype(bf16)
        part_ref[span, half:] = dup.astype(bf16)
        dfirst_ref[span, :] += dot(part_ref[span, :], w_ref[slot, :, half : 3 * half], NT)
        return 0

    lax.fori_loop(0, dfeed_ref.shape[0] // QROWS, body, 0)

    def emit(out_ref):
        out_ref[0, :, half:] = dot(low_t_ref[...], part_ref[...]).astype(bf16)
        out_ref[0, :, :half] = dot(dfeed_t_ref[...], act_ref[0, 2]).astype(bf16)

    @pl.when(step < 2)
    def _():
        emit(send_ref)

    @pl.when(step >= 2)
    def _():
        emit(keep_ref)


def mlp_back(core, base, dfeed, dfeed_t, low_t, act, blocks):
    rows, width = dfeed.shape
    half = act.shape[3]
    full = whole((rows, width))
    grid_spec = pltpu.PrefetchScalarGridSpec(
        num_scalar_prefetch=1,
        grid=(4,),
        in_specs=[
            full,
            full,
            whole((width, rows)),
            whole((width, rows)),
            pl.BlockSpec((1, 3, rows, half), lambda i, core: (for_slot(i, core), 0, 0, 0)),
        ]
        + [ANY] * BLOCKS,
        out_specs=[
            full,
            pl.BlockSpec((1, width, 3 * half), lambda i, core: (to_other(i, core), 0, 0)),
            pl.BlockSpec((1, width, 3 * half), lambda i, core: (to_own(i, core), 0, 0)),
        ],
        scratch_shapes=weight_scratch(blocks) + [pltpu.VMEM((rows, 2 * half), bf16)],
    )
    return pl.pallas_call(
        mlp_back_kernel,
        grid_spec=grid_spec,
        out_shape=[
            jax.ShapeDtypeStruct((rows, width), f32),
            jax.ShapeDtypeStruct((2, width, 3 * half), bf16),
            jax.ShapeDtypeStruct((2, width, 3 * half), bf16),
        ],
        cost_estimate=cost(48 * rows * width * half, 100 * half * width, 4 * rows * half),
        name="mlp_back",
    )(core, base, dfeed, dfeed_t, low_t, act, *blocks)


def first_back_kernel(
    dfirst_ref, n_ref, s_ref, gains_ref, sums_ref, wo_ref, att_ref, dh_ref, low_t_ref, do_ref, delta_ref, cols_ref
):
    dfirst, normed = dfirst_ref[...], n_ref[...]
    rows, width = dfirst.shape
    lanes = att_ref.shape[1]
    gain_sum = jnp.sum(dfirst * normed, axis=0, keepdims=True)
    bias_sum = jnp.sum(dfirst, axis=0, keepdims=True)
    sums = sums_ref[...]
    stacked = jnp.concatenate(
        [gain_sum, sums[1:2], bias_sum, sums[3:4], jnp.zeros((124, width), f32)], axis=0
    )
    cols_ref[...] = stacked.T.astype(bf16)
    dh = norm_back(dfirst * gains_ref[0:1], normed, s_ref[:, 0:1])
    dh_ref[...] = dh
    low = dh.astype(bf16)
    low_t_ref[...] = dh.T.astype(bf16)
    do = dot(low, wo_ref[...]).astype(bf16)
    do_ref[...] = do
    prod = do.astype(f32) * att_ref[...].astype(f32)
    high = prod.astype(bf16)
    rest = (prod - high.astype(f32)).astype(bf16)
    row = lax.broadcasted_iota(jnp.int32, (32, lanes), 0)
    lane = lax.broadcasted_iota(jnp.int32, (32, lanes), 1) // HD
    pick = jnp.where(row // 8 * 4 + row % 8 == lane, 1.0, 0.0)
    pick = jnp.where(row % 8 < 4, pick, 0.0).astype(bf16)
    delta = dot(pick, high, NT) + dot(pick, rest, NT)
    for j in range(4):
        delta_ref[j] = delta[8 * j : 8 * j + 8]


def first_back(dfirst, n1, s1, gains, sums, wo, attended):
    rows, width = n1.shape
    full = whole((rows, width))
    lanes = attended.shape[1]
    return pl.pallas_call(
        first_back_kernel,
        grid=(1,),
        in_specs=[
            full, full, whole((rows, 128)), whole((8, width)), whole((8, width)), whole(wo.shape), whole(attended.shape),
        ],
        out_specs=[full, whole((width, rows)), whole((rows, lanes)), whole((4, 8, rows)), whole((width, 128))],
        out_shape=[
            jax.ShapeDtypeStruct((rows, width), f32),
            jax.ShapeDtypeStruct((width, rows), bf16),
            jax.ShapeDtypeStruct((rows, lanes), bf16),
            jax.ShapeDtypeStruct((4, 8, rows), f32),
            jax.ShapeDtypeStruct((width, 128), bf16),
        ],
        cost_estimate=cost(2 * rows * width * lanes, 20 * rows * width),
        name="first_back",
    )(dfirst, n1, s1, gains, sums, wo, attended)


def qkv_back_kernel(core_ref, dh_ref, dq_ref, own_ref, came_ref, cos_ref, sin_ref, x_t_ref, low_t_ref, att_ref, cols_ref, *rest):
    blocks, (grad_ref, send_ref, keep_ref, w_ref, sems, part_ref) = rest[:BLOCKS], rest[BLOCKS:]
    step = pl.program_id(0)
    slot = for_slot(step, core_ref)
    part = dq_ref.shape[1]
    start_weights(blocks, w_ref, sems, core_ref[0])

    @pl.when(step == 0)
    def _():
        grad_ref[...] = dh_ref[...]

    part_ref[:, :part] = dq_ref[...]
    dk = own_ref[:, :part] + came_ref[:, :part].astype(f32)
    part_ref[:, part : 2 * part] = rotated(dk, cos_ref[...], -sin_ref[...]).astype(bf16)
    dv = own_ref[:, part:] + came_ref[:, part:].astype(f32)
    part_ref[:, 2 * part :] = dv.astype(bf16)
    wait_weights(w_ref, sems, slot)
    grad_ref[...] += dot(part_ref[...], w_ref[slot], NT)
    d_out = dot(low_t_ref[...], att_ref[...])
    lane = lax.broadcasted_iota(jnp.int32, d_out.shape, 1)

    def emit(out_ref):
        for h in range(3):
            lanes = slice(h * part, (h + 1) * part)
            piece = dot(x_t_ref[...], part_ref[:, lanes])
            moved = pltpu.roll(d_out, (3 - h) * HD, 1)
            out_ref[0, :, lanes] = jnp.where(lane < 3 * HD, piece, moved).astype(bf16)
        out_ref[0, :, 3 * part :] = cols_ref[...]

    @pl.when(step < 2)
    def _():
        emit(send_ref)

    @pl.when(step >= 2)
    def _():
        emit(keep_ref)


def qkv_back(core, dh, dq, own, came, cosine, sine, x_t, low_t, attended, cols, blocks):
    rows, width = dh.shape
    part = dq.shape[1] // 4
    full = whole((rows, width))
    grid_spec = pltpu.PrefetchScalarGridSpec(
        num_scalar_prefetch=1,
        grid=(4,),
        in_specs=[
            full,
            pl.BlockSpec((rows, part), lambda i, core: (0, for_slot(i, core))),
            pl.BlockSpec((rows, 2 * part), lambda i, core: (0, for_slot(i, core))),
            pl.BlockSpec((rows, 2 * part), lambda i, core: (0, for_slot(i, core))),
            whole((rows, part)),
            whole((rows, part)),
            whole((width, rows)),
            whole((width, rows)),
            pl.BlockSpec((rows, part), lambda i, core: (0, for_slot(i, core))),
            whole((width, 128)),
        ]
        + [ANY] * BLOCKS,
        out_specs=[
            full,
            pl.BlockSpec((1, width, 3 * part + 128), lambda i, core: (to_other(i, core), 0, 0)),
            pl.BlockSpec((1, width, 3 * part + 128), lambda i, core: (to_own(i, core), 0, 0)),
        ],
        scratch_shapes=weight_scratch(blocks) + [pltpu.VMEM((rows, 3 * part), bf16)],
    )
    return pl.pallas_call(
        qkv_back_kernel,
        grid_spec=grid_spec,
        out_shape=[
            jax.ShapeDtypeStruct((rows, width), f32),
            jax.ShapeDtypeStruct((2, width, 3 * part + 128), bf16),
            jax.ShapeDtypeStruct((2, width, 3 * part + 128), bf16),
        ],
        cost_estimate=cost(52 * rows * width * part, 80 * width * part),
        name="qkv_back",
    )(core, dh, dq, own, came, cosine, sine, x_t, low_t, attended, cols, *blocks)


def factors_of(n):
    out = []
    while n > 1:
        step = 4 if n % 4 == 0 else (2 if n % 2 == 0 else n)
        out.append(step)
        n //= step
    return out


class Links:
    def __init__(self, mesh):
        self.rows = mesh.shape["row"]
        self.cols = mesh.shape["col"]
        self.digits = factors_of(self.rows // 2)

    def locate(self):
        row = lax.axis_index("row")
        col = lax.axis_index("col")
        x = row % 2
        place = row // 2
        ring = []
        for size in reversed(self.digits):
            ring.insert(0, place % size)
            place = place // size
        return ring, x, col // (self.cols // 2), col % 2

    def send(self, v, move):
        pairs = []
        for row in range(self.rows):
            for col in range(self.cols):
                place, ring = row // 2, []
                for size in reversed(self.digits):
                    ring.insert(0, place % size)
                    place //= size
                ring, x, y, k = move(ring, row % 2, col // (self.cols // 2), col % 2)
                place = 0
                for size, digit in zip(self.digits, ring):
                    place = place * size + digit % size
                pairs.append(
                    (row * self.cols + col, (place * 2 + x) * self.cols + y * (self.cols // 2) + k)
                )
        return lax.ppermute(v, ("row", "col"), pairs)

    def across(self, v):
        return self.send(v, lambda ring, x, y, k: (ring, x, 1 - y, k))

    def beside(self, v):
        return self.send(v, lambda ring, x, y, k: (ring, x, y, 1 - k))

    def along(self, v):
        return self.send(v, lambda ring, x, y, k: (ring, 1 - x, y, k))

    def shift(self, v, axis, step):
        def move(ring, x, y, k):
            moved = list(ring)
            moved[axis] = ring[axis] + step
            return moved, x, y, k

        return self.send(v, move)

    def gather(self, shard):
        block = shard
        for axis in reversed(range(len(self.digits))):
            block = jnp.concatenate(
                [block] + [self.shift(block, axis, -d) for d in range(1, self.digits[axis])], axis=0
            )
        cut = block.shape[0] // 2
        by_x, by_y = self.along(block), self.across(block)
        mine = [block, by_x, by_y, self.across(by_x[:cut]), self.along(by_y[cut:])]
        return mine + [self.beside(v) for v in mine]

    def scatter(self, send, keep):
        came = self.beside(send)
        shape = (2, 2, 2, keep.shape[1] // 4, keep.shape[2])
        keep, came = keep.reshape(shape), came.reshape(shape)

        def total(*at):
            return keep[at].astype(f32) + came[at].astype(f32)

        every = slice(None)
        by_x = self.along(total(every, 1, 1).astype(bf16))
        by_y = self.across(total(1, every, 0).astype(bf16))
        late_x = self.along((total(0, 1, 0) + by_y[1].astype(f32)).astype(bf16))
        late_y = self.across((total(1, 0, 1) + by_x[1].astype(f32)).astype(bf16))
        low = total(0, 0, 0) + by_y[0].astype(f32) + late_x.astype(f32)
        high = total(0, 0, 1) + by_x[0].astype(f32) + late_y.astype(f32)
        block = jnp.concatenate([low, high], axis=0)
        for axis in range(len(self.digits)):
            size = self.digits[axis]
            pieces = jnp.split(block, size, axis=0)
            block = pieces[0]
            for d in range(1, size):
                block = block + self.shift(pieces[d].astype(bf16), axis, d).astype(f32)
        return block


def relative_order(links, depth):
    ring, x, _, _ = links.locate()
    where = lax.broadcasted_iota(jnp.int32, (1, links.rows * depth), 1)
    block, inside = where // depth, where % depth
    steps = links.rows // 2
    place = block % steps
    parts = []
    for axis in reversed(range(len(links.digits))):
        size = links.digits[axis]
        parts.insert(0, (place % size + ring[axis]) % size)
        place = place // size
    row = jnp.zeros_like(block)
    for size, part in zip(links.digits, parts):
        row = row * size + part
    row = row * 2 + jnp.bitwise_xor(x, block // steps)
    return row * depth + inside


def on_device(
    links, tokens, segments, positions, w_qkv, w_out, w_gate_up, w_down, norm_gain, norm_bias, cotangent
):
    ring, x_place, side, core = links.locate()
    core = core.astype(jnp.int32)[None]
    depth = w_qkv.shape[0]
    width = tokens.shape[2]
    head_cols = w_qkv.shape[2]
    hid = w_gate_up.shape[2]
    half = hid // 2
    rows = 2 * tokens.shape[1]
    mine = rows // 2
    part = head_cols + HD

    source = relative_order(links, depth)
    swap = (lax.broadcasted_iota(jnp.int32, (width, width), 0) == source).astype(bf16)

    def split(v):
        high = v.astype(bf16)
        return high, (v - high.astype(f32)).astype(bf16)

    def own_and_other(v):
        own = lax.dynamic_index_in_dim(v, side, 0, keepdims=False)
        return own, lax.dynamic_index_in_dim(v, 1 - side, 0, keepdims=False)

    def from_sequence(own, came):
        first = side == 0
        return jnp.stack([jnp.where(first, own, came), jnp.where(first, came, own)], axis=0)

    out_t = w_out.T
    attn_shard = jnp.concatenate(
        sum(
            [[w_qkv[:, p], out_t[:, p * HD : (p + 1) * HD]] for p in range(3)],
            [],
        ),
        axis=1,
    )
    norms = jnp.concatenate([norm_gain, norm_bias], axis=1)
    norms = jnp.pad(norms, ((0, 0), (0, 128 - norms.shape[1])))
    down_t = w_down.T
    mlp_shards = []
    for h in range(2):
        cols = slice(h * half, (h + 1) * half)
        pieces = [down_t[:, cols], w_gate_up[:, 0, cols], w_gate_up[:, 1, cols]]
        mlp_shards.append(jnp.concatenate(pieces + ([norms] if h == 0 else []), axis=1))

    tokens_own, tokens_other = own_and_other(tokens)
    tokens_came = links.across(tokens_other)
    small_own, small_other = own_and_other(jnp.stack([segments, positions], axis=1))
    small_came = links.across(small_other)
    attn_w = links.gather(attn_shard)
    mlp_w = [links.gather(s) for s in mlp_shards]

    x_abs = jnp.concatenate([tokens_own, tokens_came], axis=0)
    x = dot(x_abs, swap).astype(bf16)
    x_t = lax.dot_general(swap, x_abs, (((0,), (1,)), ((), ())), preferred_element_type=f32).astype(bf16)
    small = jnp.concatenate([small_own, small_came], axis=1)
    seg = small[0]
    seg_all = jnp.concatenate([seg, links.beside(seg)], axis=0)[:, None]
    seg = seg[None, :]
    cosine, sine = rope_tables(small[1], part)
    dy_own, dy_other = own_and_other(cotangent)
    dy_came = links.across(dy_other.astype(bf16))
    high, low = split(dy_own)
    dy = jnp.concatenate([dot(high, swap) + dot(low, swap), dot(dy_came, swap)], axis=0)

    q, kv, wo = qkv(core, x, cosine, sine, attn_w)
    kv_came = links.beside(kv)
    attended, logs = attend(q, kv, kv_came, seg, seg_all)
    n1, s1, low1, low1_t, gains = first_norm(x, attended, wo, mlp_w[0][0], mlp_w[0][1])
    act_a, feed = mlp(core, low1, None, mlp_w[0], half)
    act_b, feed = mlp(core, low1, feed, mlp_w[1], half)
    layer_out, dh2, dfeed, dfeed_t, sums = second_norm(n1, gains, feed, dy)
    layer_out = dot(layer_out, swap, NT).astype(bf16)
    layer_out = from_sequence(layer_out[:mine], links.across(layer_out[mine:]))

    dfirst, send, keep = mlp_back(core, dh2, dfeed, dfeed_t, low1_t, act_a, mlp_w[0])
    own_mlp = [links.scatter(send, keep)]
    dfirst, send, keep = mlp_back(core, dfirst, dfeed, dfeed_t, low1_t, act_b, mlp_w[1])
    own_mlp.append(links.scatter(send, keep))
    dh1, low_t, do, delta, cols = first_back(dfirst, n1, s1, gains, sums, wo, attended)
    dq, dkv_own, dkv_other = attend_back(q, kv, kv_came, do, logs, delta, seg, seg_all, cosine, sine)
    dkv_came = links.beside(dkv_other)
    grad, send, keep = qkv_back(
        core, dh1, dq, dkv_own, dkv_came, cosine, sine, x_t, low_t, attended, cols, attn_w
    )
    own_attn = links.scatter(send, keep)
    high, low = split(grad)
    grad = dot(high, swap, NT) + dot(low, swap, NT)
    input_grad = from_sequence(grad[:mine], links.across(grad[mine:].astype(bf16)).astype(f32))

    grad_down = jnp.concatenate([v[:, :half] for v in own_mlp], axis=1).T
    grad_gate_up = jnp.stack(
        [
            jnp.concatenate([v[:, (p + 1) * half : (p + 2) * half] for v in own_mlp], axis=1)
            for p in range(2)
        ],
        axis=1,
    )
    thirds = [own_attn[:, p * part : (p + 1) * part] for p in range(3)]
    edge = 3 * part
    return (
        layer_out,
        input_grad,
        jnp.stack([v[:, :head_cols] for v in thirds], axis=1),
        jnp.concatenate([v[:, head_cols:] for v in thirds], axis=1).T,
        grad_gate_up,
        grad_down,
        own_attn[:, edge : edge + 2],
        own_attn[:, edge + 2 : edge + 4],
    )


def solution(mesh):
    in_specs = (
        P(None, ("row", "col"), None),
        P(None, ("row", "col")),
        P(None, ("row", "col")),
        P("row", None, "col"),
        P("col", "row"),
        P("row", None, "col"),
        P("col", "row"),
        P("row", None),
        P("row", None),
        P(None, ("row", "col"), None),
    )
    out_specs = (
        P(None, ("row", "col"), None),
        P(None, ("row", "col"), None),
        P("row", None, "col"),
        P("col", "row"),
        P("row", None, "col"),
        P("col", "row"),
        P("row", None),
        P("row", None),
    )
    return jax.shard_map(
        functools.partial(on_device, Links(mesh)), mesh=mesh, in_specs=in_specs, out_specs=out_specs, check_vma=False
    )
```

time: 541 us -> 450 us (0.83)
  the two profiles are of different devices: /device:TPU:26 before, /device:TPU:0 now
where the time goes in v3:
time: 450 us; the launch traced here: 445 us
  waiting for transfers between devices  150 us (33%)
  Pallas kernels  144 us (32%)
  starting transfers between devices  94.8 us (21%)
  local copies, waits for them, and re-layouts  23 us (5%)
  other arithmetic  17.2 us (4%)
  matrix products  13.3 us (3%)
    ppermute x68, waiting for transfers between devices, send(): return lax.ppermute(v, ('row', 'col'), pairs)  150 us
    ppermute x68, starting transfers between devices, send(): return lax.ppermute(v, ('row', 'col'), pairs)  94.8 us
    pallas_call x2, Pallas kernels, mlp_back(): pl.pallas_call(mlp_back_kernel, grid_spec=grid_spec, out_shape=[jax.Shape...  38.9 us
    pallas_call x2, Pallas kernels, mlp(): pl.pallas_call(functools.partial(mlp_kernel, has_base), grid_spec=grid_sp...  22.8 us
    pallas_call x1, Pallas kernels, attend_back(): pl.pallas_call(attend_back_kernel, grid=(4,), in_specs=[pl.BlockSpec((row...  20.6 us
    pallas_call x1, Pallas kernels, attend(): pl.pallas_call(attend_kernel, grid=(4,), in_specs=[pl.BlockSpec((rows, pa...  19.8 us
    pallas_call x1, Pallas kernels, qkv_back(): pl.pallas_call(qkv_back_kernel, grid_spec=grid_spec, out_shape=[jax.Shape...  16.7 us
    dot_general x7, matrix products, dot(): return lax.dot_general(a, b, dims, preferred_element_type=f32)  10.5 us
  transfers between devices with their start and end apart: 68, of which 22 were waited for; matrix products, arithmetic and copies ran while one was open for 10% of the time, Pallas kernels for 14%

profile of v3, /device:TPU:0, one launch (start us, length us, event | category | flops | bytes accessed | tf_op | source)
XLA Modules:
  0.0 444.6 jit_solution(15288773812738050607)
XLA Ops:
  2.6 3.1 collective-permute-start.4
  5.7 2.6 collective-permute-start.3
  15.2 3.6 collective-permute-done.3
  18.9 1.8 collective-permute-start.6
  22.3 17.4 %collective-permute-start.18 = (bf16[96,1280]{1,0:T(8,128)(2,1)S(1)}, bf16[96,1280]{1,0:T(8,128)(2,1)S(1)}, u32[]{:S(2)}, u32[]{:S(2)}) collective-permute-start(bf16[96,1280]{1,0:T(8,128)(2,1)S(1)} %pad_maximum_fusion.11), channel_id=1, source_target_pairs={{0,8},{1,9},{2,10},{3,11},{4,12},{5,13},{6,14},{7,15},{8,16},{9,17... | collective-permute-start | bytes 737288 | tf_op jit(solution)/shard_map/ppermute | solution.py:679
  42.1 8.2 %collective-permute-done.28 = bf16[96,1152]{1,0:T(8,128)(2,1)S(1)} collective-permute-done((bf16[96,1152]{1,0:T(8,128)(2,1)S(1)}, bf16[96,1152]{1,0:T(8,128)(2,1)S(1)}, u32[]{:S(2)}, u32[]{:S(2)}) %collective-permute-start.28) | collective-permute-done | bytes 221216 | tf_op jit(solution)/shard_map/ppermute | solution.py:679
  50.3 4.3 collective-permute-start.16
  57.5 6.0 %collective-permute-done.17 = bf16[96,1280]{1,0:T(8,128)(2,1)S(1)} collective-permute-done((bf16[96,1280]{1,0:T(8,128)(2,1)S(1)}, bf16[96,1280]{1,0:T(8,128)(2,1)S(1)}, u32[]{:S(2)}, u32[]{:S(2)}) %collective-permute-start.17) | collective-permute-done | bytes 245792 | tf_op jit(solution)/shard_map/ppermute | solution.py:679
  68.8 3.7 collective-permute-done.7.rest_3_
  75.8 2.8 fusion.9.x_ref
  78.6 8.5 %qkv.1 = (bf16[512,1024]{1,0:T(8,128)(2,1)}, bf16[512,2048]{1,0:T(8,128)(2,1)}, bf16[768,1024]{1,0:T(8,128)(2,1)}) custom-call(s32[1]{0:T(128)} %bitcast.2.core_ref, bf16[512,768]{1,0:T(8,128)(2,1)} %fusion.9.x_ref, f32[512,256]{1,0:T(8,128)} %copy.77.cos_ref, f32[512,256]{1,0:T(8,128)} %copy.78.sin_ref, bf16[384,768]{1,0:T(8,128)(2,1)} %copy-done.10, ...), custom_call_target="tpu_custom_call" | custom-call | flops 2415919104 | bytes 7864320 | tf_op jit(solution)/shard_map/qkv/pallas_call | solution.py:151
  87.8 3.7 collective-permute-done.32.rest_3_.rest_2_
  91.5 4.7 %collective-permute-done.31.rest_2_.rest_1_ = bf16[384,1152]{1,0:T(8,128)(2,1)} collective-permute-done((bf16[384,1152]{1,0:T(8,128)(2,1)S(1)}, bf16[384,1152]{1,0:T(8,128)(2,1)}, u32[]{:S(2)}, u32[]{:S(2)}) %collective-permute-start.31) | collective-permute-done | bytes 884768 | tf_op jit(solution)/shard_map/ppermute | solution.py:679
  98.9 11.4 %collective-permute-done.20.rest_2_ = bf16[384,1280]{1,0:T(8,128)(2,1)} collective-permute-done((bf16[384,1280]{1,0:T(8,128)(2,1)S(1)}, bf16[384,1280]{1,0:T(8,128)(2,1)}, u32[]{:S(2)}, u32[]{:S(2)}) %collective-permute-start.20) | collective-permute-done | bytes 983072 | tf_op jit(solution)/shard_map/ppermute | solution.py:679
  110.9 6.3 %collective-permute-done.19.norm_b_ref.rest_1_ = bf16[384,1280]{1,0:T(8,128)(2,1)S(1)} collective-permute-done((bf16[384,1280]{1,0:T(8,128)(2,1)S(1)}, bf16[384,1280]{1,0:T(8,128)(2,1)S(1)}, u32[]{:S(2)}, u32[]{:S(2)}) %collective-permute-start.19) | collective-permute-done | bytes 983072 | tf_op jit(solution)/shard_map/ppermute | solution.py:679
  118.6 10.1 %collective-permute-done.40 = bf16[256,768]{1,0:T(8,128)(2,1)} collective-permute-done((bf16[256,768]{1,0:T(8,128)(2,1)S(1)}, bf16[256,768]{1,0:T(8,128)(2,1)}, u32[]{:S(2)}, u32[]{:S(2)}) %collective-permute-start.40) | collective-permute-done | bytes 393248 | tf_op jit(solution)/shard_map/ppermute | solution.py:679
  132.9 8.2 %collective-permute-done.22.rest_4_ = bf16[192,1280]{1,0:T(8,128)(2,1)S(1)} collective-permute-done((bf16[192,1280]{1,0:T(8,128)(2,1)S(1)}, bf16[192,1280]{1,0:T(8,128)(2,1)S(1)}, u32[]{:S(2)}, u32[]{:S(2)}) %collective-permute-start.22) | collective-permute-done | bytes 491552 | tf_op jit(solution)/shard_map/ppermute | solution.py:679
  142.6 1.7 fusion.4
  147.1 19.8 %attend.1 = (bf16[512,1024]{1,0:T(8,128)(2,1)}, f32[4,8,512]{2,1,0:T(8,128)}) custom-call(bf16[512,1024]{1,0:T(8,128)(2,1)} %get-tuple-element.44.q_ref, bf16[512,2048]{1,0:T(8,128)(2,1)} %get-tuple-element.45.own_ref, bf16[512,2048]{1,0:T(8,128)(2,1)} %collective-permute-done.14.other_ref, s32[1,512]{1,0:T(1,128)} %copy-done.17, s32[1024,1]{1,0:T(8,128)} %copy.79.segk_ref), custom_call_target="tpu_custom_call" | custom-call | flops 8589934592 | bytes 12582912 | tf_op jit(solution)/shard_map/attend/pallas_call | solution.py:195
  166.8 5.2 %first_norm.1 = (f32[512,768]{1,0:T(8,128)}, f32[512,128]{1,0:T(8,128)}, bf16[512,768]{1,0:T(8,128)(2,1)}, bf16[768,512]{1,0:T(8,128)(2,1)}, f32[8,768]{1,0:T(8,128)}) custom-call(bf16[512,768]{1,0:T(8,128)(2,1)} %fusion.9.x_ref, bf16[512,1024]{1,0:T(8,128)(2,1)} %get-tuple-element.46.att_ref, bf16[768,1024]{1,0:T(8,128)(2,1)} %get-tuple-element.47.wo_ref, ...), custom_call_target="tpu_custom_call" | custom-call | flops 805306368 | bytes 6291456 | tf_op jit(solution)/shard_map/first_norm/pallas_call | solution.py:310
  172.0 11.1 %mlp.2 = (bf16[4,3,512,384]{3,2,1,0:T(8,128)(2,1)}, f32[512,768]{1,0:T(8,128)}) custom-call(s32[1]{0:T(128)} %bitcast.2.core_ref, bf16[512,768]{1,0:T(8,128)(2,1)} %get-tuple-element.50.low_ref, bf16[384,1280]{1,0:T(8,128)(2,1)} %copy-done, bf16[384,1280]{1,0:T(8,128)(2,1)} %copy-done.4, bf16[384,1280]{1,0:T(8,128)(2,1)} %collective-permute-done.20.rest_2_, ...), custom_call_target="tpu_custom_call" | custom-call | flops 3623878656 | bytes 17694720 | tf_op jit(solution)/shard_map/mlp/pallas_call | solution.py:372
  184.6 11.7 %mlp.3 = (bf16[4,3,512,384]{3,2,1,0:T(8,128)(2,1)}, f32[512,768]{1,0:T(8,128)}) custom-call(s32[1]{0:T(128)} %bitcast.2.core_ref, bf16[512,768]{1,0:T(8,128)(2,1)} %get-tuple-element.50.low_ref, f32[512,768]{1,0:T(8,128)} %get-tuple-element.51.rest_0_, bf16[384,1152]{1,0:T(8,128)(2,1)} %copy-done.6, ...), custom_call_target="tpu_custom_call" | custom-call | flops 3623878656 | bytes 17694720 | tf_op jit(solution)/shard_map/mlp/pallas_call | solution.py:372
  196.3 5.8 %second_norm.1 = (bf16[512,768]{1,0:T(8,128)(2,1)}, f32[512,768]{1,0:T(8,128)}, bf16[512,768]{1,0:T(8,128)(2,1)}, bf16[768,512]{1,0:T(8,128)(2,1)}, f32[8,768]{1,0:T(8,128)}) custom-call(f32[512,768]{1,0:T(8,128)} %get-tuple-element.48.n_ref, f32[8,768]{1,0:T(8,128)} %get-tuple-element.49.gains_ref, f32[512,768]{1,0:T(8,128)} %get-tuple-element.52.feed_ref, ...), custom_call_target="tpu_custom_call" | custom-call | flops 15728640 | bytes 8650752 | tf_op jit(solution)/shard_map/second_norm/pallas_call | solution.py:401
  202.1 19.6 %mlp_back.2 = (f32[512,768]{1,0:T(8,128)}, bf16[2,768,1152]{2,1,0:T(8,128)(2,1)}, bf16[2,768,1152]{2,1,0:T(8,128)(2,1)}) custom-call(s32[1]{0:T(128)} %bitcast.2.core_ref, f32[512,768]{1,0:T(8,128)} %get-tuple-element.54.base_ref, bf16[512,768]{1,0:T(8,128)(2,1)} %get-tuple-element.55.dfeed_ref, bf16[768,512]{1,0:T(8,128)(2,1)} %get-tuple-element.56.dfeed_t_ref, ...), custom_call_target="tpu_custom_call" | custom-call | flops 7247757312 | bytes 29491200 | tf_op jit(solution)/shard_map/mlp_back/pallas_call | solution.py:493
  221.6 19.4 %mlp_back.3 = (f32[512,768]{1,0:T(8,128)}, bf16[2,768,1152]{2,1,0:T(8,128)(2,1)}, bf16[2,768,1152]{2,1,0:T(8,128)(2,1)}) custom-call(s32[1]{0:T(128)} %bitcast.2.core_ref, f32[512,768]{1,0:T(8,128)} %get-tuple-element.59.base_ref, bf16[512,768]{1,0:T(8,128)(2,1)} %get-tuple-element.55.dfeed_ref, bf16[768,512]{1,0:T(8,128)(2,1)} %get-tuple-element.56.dfeed_t_ref, ...), custom_call_target="tpu_custom_call" | custom-call | flops 7247757312 | bytes 29491200 | tf_op jit(solution)/shard_map/mlp_back/pallas_call | solution.py:493
  241.0 6.1 %first_back.1 = (f32[512,768]{1,0:T(8,128)}, bf16[768,512]{1,0:T(8,128)(2,1)}, bf16[512,1024]{1,0:T(8,128)(2,1)}, f32[4,8,512]{2,1,0:T(8,128)}, bf16[768,128]{1,0:T(8,128)(2,1)}) custom-call(f32[512,768]{1,0:T(8,128)} %get-tuple-element.61.dfirst_ref, f32[512,768]{1,0:T(8,128)} %get-tuple-element.48.n_ref, f32[512,128]{1,0:T(8,128)} %get-tuple-element.62.s_ref, ...), custom_call_target="tpu_custom_call" | custom-call | flops 805306368 | bytes 7864320 | tf_op jit(solution)/shard_map/first_back/pallas_call | solution.py:541
  247.1 20.6 %attend_back.1 = (bf16[512,1024]{1,0:T(8,128)(2,1)}, f32[512,2048]{1,0:T(8,128)}, bf16[512,2048]{1,0:T(8,128)(2,1)}) custom-call(bf16[512,1024]{1,0:T(8,128)(2,1)} %get-tuple-element.44.q_ref, bf16[512,2048]{1,0:T(8,128)(2,1)} %get-tuple-element.45.own_ref, bf16[512,2048]{1,0:T(8,128)(2,1)} %collective-permute-done.14.other_ref, ...), custom_call_target="tpu_custom_call" | custom-call | flops 21474836480 | bytes 31457280 | tf_op jit(solution)/shard_map/attend_back/pallas_call | solution.py:264
  267.8 2.5 collective-permute-start.42
  270.7 2.8 convolution_convert_fusion.x_t_ref
  276.6 16.7 %qkv_back.1 = (f32[512,768]{1,0:T(8,128)}, bf16[2,768,896]{2,1,0:T(8,128)(2,1)}, bf16[2,768,896]{2,1,0:T(8,128)(2,1)}) custom-call(s32[1]{0:T(128)} %bitcast.2.core_ref, f32[512,768]{1,0:T(8,128)} %get-tuple-element.64.dh_ref, bf16[512,1024]{1,0:T(8,128)(2,1)} %get-tuple-element.68.dq_ref, f32[512,2048]{1,0:T(8,128)} %get-tuple-element.69.own_ref, ...), custom_call_target="tpu_custom_call" | custom-call | flops 5234491392 | bytes 15728640 | tf_op jit(solution)/shard_map/qkv_back/pallas_call | solution.py:625
  293.3 2.9 fusion
  300.8 7.3 %collective-permute-done.43 = bf16[256,768]{1,0:T(8,128)(2,1)S(1)} collective-permute-done((bf16[256,768]{1,0:T(8,128)(2,1)S(1)}, bf16[256,768]{1,0:T(8,128)(2,1)S(1)}, u32[]{:S(2)}, u32[]{:S(2)}) %collective-permute-start.43) | collective-permute-done | bytes 393248 | tf_op jit(solution)/shard_map/ppermute | solution.py:679
  318.5 19.5 %collective-permute-done.64 = bf16[2,192,1152]{2,1,0:T(8,128)(2,1)S(1)} collective-permute-done((bf16[2,192,1152]{2,1,0:T(8,128)(2,1)S(1)}, bf16[2,192,1152]{2,1,0:T(8,128)(2,1)S(1)}, u32[]{:S(2)}, u32[]{:S(2)}) %collective-permute-start.64) | collective-permute-done | bytes 884768 | tf_op jit(solution)/shard_map/ppermute | solution.py:679
  339.7 15.0 %collective-permute-done.56 = bf16[2,192,1152]{2,1,0:T(8,128)(2,1)S(1)} collective-permute-done((bf16[2,192,1152]{2,1,0:T(8,128)(2,1)S(1)}, bf16[2,192,1152]{2,1,0:T(8,128)(2,1)S(1)}, u32[]{:S(2)}, u32[]{:S(2)}) %collective-permute-start.56) | collective-permute-done | bytes 884768 | tf_op jit(solution)/shard_map/ppermute | solution.py:679
  358.8 4.6 %collective-permute-done.65 = bf16[192,1152]{1,0:T(8,128)(2,1)S(1)} collective-permute-done((bf16[192,1152]{1,0:T(8,128)(2,1)S(1)}, bf16[192,1152]{1,0:T(8,128)(2,1)S(1)}, u32[]{:S(2)}, u32[]{:S(2)}) %collective-permute-start.65) | collective-permute-done | bytes 442400 | tf_op jit(solution)/shard_map/ppermute | solution.py:679
  364.9 1.9 collective-permute-start.66
  366.8 6.7 %collective-permute-start.67 = (bf16[96,1152]{1,0:T(8,128)(2,1)S(1)}, bf16[96,1152]{1,0:T(8,128)(2,1)S(1)}, u32[]{:S(2)}, u32[]{:S(2)}) collective-permute-start(bf16[96,1152]{1,0:T(8,128)(2,1)S(1)} %get-tuple-element.125), channel_id=1, source_target_pairs={{0,24},{1,25},{2,26},{3,27},{4,28},{5,29},{6,30},{7,31},{8,0},{9,1... | collective-permute-start | bytes 663560 | tf_op jit(solution)/shard_map/ppermute | solution.py:679
  375.4 8.8 %collective-permute-done.62 = bf16[192,1152]{1,0:T(8,128)(2,1)S(1)} collective-permute-done((bf16[192,1152]{1,0:T(8,128)(2,1)S(1)}, bf16[192,1152]{1,0:T(8,128)(2,1)S(1)}, u32[]{:S(2)}, u32[]{:S(2)}) %collective-permute-start.62) | collective-permute-done | bytes 442400 | tf_op jit(solution)/shard_map/ppermute | solution.py:679
  386.8 5.6 %collective-permute-done.54 = bf16[192,1152]{1,0:T(8,128)(2,1)S(1)} collective-permute-done((bf16[192,1152]{1,0:T(8,128)(2,1)S(1)}, bf16[192,1152]{1,0:T(8,128)(2,1)S(1)}, u32[]{:S(2)}, u32[]{:S(2)}) %collective-permute-start.54) | collective-permute-done | bytes 442400 | tf_op jit(solution)/shard_map/ppermute | solution.py:679
  392.5 4.6 %collective-permute-start.63 = (bf16[96,1152]{1,0:T(8,128)(2,1)S(1)}, bf16[96,1152]{1,0:T(8,128)(2,1)S(1)}, u32[]{:S(2)}, u32[]{:S(2)}) collective-permute-start(bf16[96,1152]{1,0:T(8,128)(2,1)S(1)} %split.87), channel_id=1, source_target_pairs={{0,8},{1,9},{2,10},{3,11},{4,12},{5,13},{6,14},{7,15},{8,16},{9,17... | collective-permute-start | bytes 663560 | tf_op jit(solution)/shard_map/ppermute | solution.py:679
  397.4 3.5 collective-permute-start.58
  400.8 5.7 %collective-permute-done.63 = bf16[96,1152]{1,0:T(8,128)(2,1)S(1)} collective-permute-done((bf16[96,1152]{1,0:T(8,128)(2,1)S(1)}, bf16[96,1152]{1,0:T(8,128)(2,1)S(1)}, u32[]{:S(2)}, u32[]{:S(2)}) %collective-permute-start.63) | collective-permute-done | bytes 221216 | tf_op jit(solution)/shard_map/ppermute | solution.py:679
  407.8 8.5 %collective-permute-done.58 = bf16[96,1152]{1,0:T(8,128)(2,1)S(1)} collective-permute-done((bf16[96,1152]{1,0:T(8,128)(2,1)S(1)}, bf16[96,1152]{1,0:T(8,128)(2,1)S(1)}, u32[]{:S(2)}, u32[]{:S(2)}) %collective-permute-start.58) | collective-permute-done | bytes 221216 | tf_op jit(solution)/shard_map/ppermute | solution.py:679
  418.3 5.6 %collective-permute-done.49 = bf16[192,896]{1,0:T(8,128)(2,1)S(1)} collective-permute-done((bf16[192,896]{1,0:T(8,128)(2,1)S(1)}, bf16[192,896]{1,0:T(8,128)(2,1)S(1)}, u32[]{:S(2)}, u32[]{:S(2)}) %collective-permute-start.49) | collective-permute-done | bytes 344096 | tf_op jit(solution)/shard_map/ppermute | solution.py:679
  425.7 3.3 collective-permute-start.50
  429.0 3.4 collective-permute-start.51
  432.6 3.4 collective-permute-start.47
  438.3 2.9 collective-permute-done.47
  (251 shorter events, 80.4 us)
Async XLA Ops:
  2.6 11.0 %collective-permute-start.4 = (bf16[96,768]{1,0:T(8,128)(2,1)S(1)}, bf16[96,768]{1,0:T(8,128)(2,1)S(1)}, u32[]{:S(2)}, u32[]{:S(2)}) collective-permute-start(bf16[96,768]{1,0:T(8,128)(2,1)S(1)} %concatenate.55), channel_id=1, source_target_pairs={{0,8},{1,9},{2,10},{3,11},{4,12},{5,13},{6,14},{7,15},{8,16},{9,17... | collective-permute-start | bytes 442376 | tf_op jit(solution)/shard_map/ppermute | solution.py:679
  5.7 13.1 %collective-permute-start.3 = (bf16[96,768]{1,0:T(8,128)(2,1)S(1)}, bf16[96,768]{1,0:T(8,128)(2,1)S(1)}, u32[]{:S(2)}, u32[]{:S(2)}) collective-permute-start(bf16[96,768]{1,0:T(8,128)(2,1)S(1)} %concatenate.55), channel_id=1, source_target_pairs={{0,16},{1,17},{2,18},{3,19},{4,20},{5,21},{6,22},{7,23},{8,24},{9,... | collective-permute-start | bytes 442376 | tf_op jit(solution)/shard_map/ppermute | solution.py:679
  12.3 28.2 %collective-permute-start.30 = (bf16[96,1152]{1,0:T(8,128)(2,1)S(1)}, bf16[96,1152]{1,0:T(8,128)(2,1)S(1)}, u32[]{:S(2)}, u32[]{:S(2)}) collective-permute-start(bf16[96,1152]{1,0:T(8,128)(2,1)S(1)} %pad_maximum_fusion.12), channel_id=1, source_target_pairs={{0,8},{1,9},{2,10},{3,11},{4,12},{5,13},{6,14},{7,15},{8,16},{9,17... | collective-permute-start | bytes 663560 | tf_op jit(solution)/shard_map/ppermute | solution.py:679
  13.0 27.5 %collective-permute-start.29 = (bf16[96,1152]{1,0:T(8,128)(2,1)S(1)}, bf16[96,1152]{1,0:T(8,128)(2,1)S(1)}, u32[]{:S(2)}, u32[]{:S(2)}) collective-permute-start(bf16[96,1152]{1,0:T(8,128)(2,1)S(1)} %pad_maximum_fusion.12), channel_id=1, source_target_pairs={{0,16},{1,17},{2,18},{3,19},{4,20},{5,21},{6,22},{7,23},{8,24},{9,... | collective-permute-start | bytes 663560 | tf_op jit(solution)/shard_map/ppermute | solution.py:679
  18.9 35.7 %collective-permute-start.6 = (bf16[384,768]{1,0:T(8,128)(2,1)S(1)}, bf16[384,768]{1,0:T(8,128)(2,1)}, u32[]{:S(2)}, u32[]{:S(2)}) collective-permute-start(bf16[384,768]{1,0:T(8,128)(2,1)S(1)} %pad_maximum_fusion.6.rest_0_), channel_id=1, source_target_pairs={{0,2},{1,3},{2,0},{3,1},{4,6},{5,7},{6,4},{7,5},{8,10},{9,11},{10,... | collective-permute-start | bytes 1769480 | tf_op jit(solution)/shard_map/ppermute | solution.py:679
  20.7 34.8 %collective-permute-start.5 = (bf16[384,768]{1,0:T(8,128)(2,1)S(1)}, bf16[384,768]{1,0:T(8,128)(2,1)}, u32[]{:S(2)}, u32[]{:S(2)}) collective-permute-start(bf16[384,768]{1,0:T(8,128)(2,1)S(1)} %pad_maximum_fusion.6.rest_0_), channel_id=1, source_target_pairs={{0,4},{1,5},{2,6},{3,7},{4,0},{5,1},{6,2},{7,3},{8,12},{9,13},{10,... | collective-permute-start | bytes 1769480 | tf_op jit(solution)/shard_map/ppermute | solution.py:679
  22.3 28.0 %collective-permute-start.18 = (bf16[96,1280]{1,0:T(8,128)(2,1)S(1)}, bf16[96,1280]{1,0:T(8,128)(2,1)S(1)}, u32[]{:S(2)}, u32[]{:S(2)}) collective-permute-start(bf16[96,1280]{1,0:T(8,128)(2,1)S(1)} %pad_maximum_fusion.11), channel_id=1, source_target_pairs={{0,8},{1,9},{2,10},{3,11},{4,12},{5,13},{6,14},{7,15},{8,16},{9,17... | collective-permute-start | bytes 737288 | tf_op jit(solution)/shard_map/ppermute | solution.py:679
  40.6 23.4 %collective-permute-start = (bf16[256,768]{1,0:T(8,128)(2,1)S(1)}, bf16[256,768]{1,0:T(8,128)(2,1)}, u32[]{:S(2)}, u32[]{:S(2)}) collective-permute-start(bf16[256,768]{1,0:T(8,128)(2,1)S(1)} %get-tuple-element.115), channel_id=1, source_target_pairs={{0,2},{1,3},{2,0},{3,1},{4,6},{5,7},{6,4},{7,5},{8,10},{9,11},{10,... | collective-permute-start | bytes 1179656 | tf_op jit(solution)/shard_map/ppermute | solution.py:679
  50.3 13.2 %collective-permute-start.17 = (bf16[96,1280]{1,0:T(8,128)(2,1)S(1)}, bf16[96,1280]{1,0:T(8,128)(2,1)S(1)}, u32[]{:S(2)}, u32[]{:S(2)}) collective-permute-start(bf16[96,1280]{1,0:T(8,128)(2,1)S(1)} %pad_maximum_fusion.11), channel_id=1, source_target_pairs={{0,16},{1,17},{2,18},{3,19},{4,20},{5,21},{6,22},{7,23},{8,24},{9,... | collective-permute-start | bytes 737288 | tf_op jit(solution)/shard_map/ppermute | solution.py:679
  50.3 13.7 %collective-permute-start.16 = (bf16[96,1280]{1,0:T(8,128)(2,1)S(1)}, bf16[96,1280]{1,0:T(8,128)(2,1)S(1)}, u32[]{:S(2)}, u32[]{:S(2)}) collective-permute-start(bf16[96,1280]{1,0:T(8,128)(2,1)S(1)} %pad_maximum_fusion.11), channel_id=1, source_target_pairs={{0,24},{1,25},{2,26},{3,27},{4,28},{5,29},{6,30},{7,31},{8,0},{9,1... | collective-permute-start | bytes 737288 | tf_op jit(solution)/shard_map/ppermute | solution.py:679
  55.6 10.8 %collective-permute-start.8 = (bf16[192,768]{1,0:T(8,128)(2,1)S(1)}, bf16[192,768]{1,0:T(8,128)(2,1)}, u32[]{:S(2)}, u32[]{:S(2)}) collective-permute-start(bf16[192,768]{1,0:T(8,128)(2,1)S(1)} %slice.360), channel_id=1, source_target_pairs={{0,4},{1,5},{2,6},{3,7},{4,0},{5,1},{6,2},{7,3},{8,12},{9,13},{10,... | collective-permute-start | bytes 884744 | tf_op jit(solution)/shard_map/ppermute | solution.py:679
  64.8 26.7 %collective-permute-start.32 = (bf16[384,1152]{1,0:T(8,128)(2,1)S(1)}, bf16[384,1152]{1,0:T(8,128)(2,1)}, u32[]{:S(2)}, u32[]{:S(2)}) collective-permute-start(bf16[384,1152]{1,0:T(8,128)(2,1)S(1)} %pad_maximum_fusion.3.rest_1_.rest_0_), channel_id=1, source_target_pairs={{0,2},{1,3},{2,0},{3,1},{4,6},{5,7},{6,4},{7,5},{8,10},{9,11},{10,... | collective-permute-start | bytes 2654216 | tf_op jit(solution)/shard_map/ppermute | solution.py:679
  73.6 22.6 %collective-permute-start.31 = (bf16[384,1152]{1,0:T(8,128)(2,1)S(1)}, bf16[384,1152]{1,0:T(8,128)(2,1)}, u32[]{:S(2)}, u32[]{:S(2)}) collective-permute-start(bf16[384,1152]{1,0:T(8,128)(2,1)S(1)} %pad_maximum_fusion.3.rest_1_.rest_0_), channel_id=1, source_target_pairs={{0,4},{1,5},{2,6},{3,7},{4,0},{5,1},{6,2},{7,3},{8,12},{9,13},{10,... | collective-permute-start | bytes 2654216 | tf_op jit(solution)/shard_map/ppermute | solution.py:679
  74.2 36.1 %collective-permute-start.20 = (bf16[384,1280]{1,0:T(8,128)(2,1)S(1)}, bf16[384,1280]{1,0:T(8,128)(2,1)}, u32[]{:S(2)}, u32[]{:S(2)}) collective-permute-start(bf16[384,1280]{1,0:T(8,128)(2,1)S(1)} %pad_maximum_fusion.2.norm_a_ref.rest_0_), channel_id=1, source_target_pairs={{0,2},{1,3},{2,0},{3,1},{4,6},{5,7},{6,4},{7,5},{8,10},{9,11},{10,... | collective-permute-start | bytes 2949128 | tf_op jit(solution)/shard_map/ppermute | solution.py:679
  74.2 43.0 %collective-permute-start.19 = (bf16[384,1280]{1,0:T(8,128)(2,1)S(1)}, bf16[384,1280]{1,0:T(8,128)(2,1)S(1)}, u32[]{:S(2)}, u32[]{:S(2)}) collective-permute-start(bf16[384,1280]{1,0:T(8,128)(2,1)S(1)} %pad_maximum_fusion.2.norm_a_ref.rest_0_), channel_id=1, source_target_pairs={{0,4},{1,5},{2,6},{3,7},{4,0},{5,1},{6,2},{7,3},{8,12},{9,13},{10,... | collective-permute-start | bytes 2949128 | tf_op jit(solution)/shard_map/ppermute | solution.py:679
  87.1 59.6 %collective-permute-start.14 = (bf16[512,2048]{1,0:T(8,128)(2,1)}, bf16[512,2048]{1,0:T(8,128)(2,1)}, u32[]{:S(2)}, u32[]{:S(2)}) collective-permute-start(bf16[512,2048]{1,0:T(8,128)(2,1)} %get-tuple-element.45.own_ref), channel_id=1, source_target_pairs={{0,1},{1,0},{2,3},{3,2},{4,5},{5,4},{6,7},{7,6},{8,9},{9,8},{10,11... | collective-permute-start | bytes 6291464 | tf_op jit(solution)/shard_map/ppermute | solution.py:679
  91.5 37.8 %collective-permute-start.23 = (bf16[384,1280]{1,0:T(8,128)(2,1)S(1)}, bf16[384,1280]{1,0:T(8,128)(2,1)S(1)}, u32[]{:S(2)}, u32[]{:S(2)}) collective-permute-start(bf16[384,1280]{1,0:T(8,128)(2,1)S(1)} %pad_maximum_fusion.2.norm_a_ref.rest_0_), channel_id=1, source_target_pairs={{0,1},{1,0},{2,3},{3,2},{4,5},{5,4},{6,7},{7,6},{8,9},{9,8},{10,11... | collective-permute-start | bytes 2949128 | tf_op jit(solution)/shard_map/ppermute | solution.py:679
  98.3 32.6 %collective-permute-start.34 = (bf16[192,1152]{1,0:T(8,128)(2,1)S(1)}, bf16[192,1152]{1,0:T(8,128)(2,1)}, u32[]{:S(2)}, u32[]{:S(2)}) collective-permute-start(bf16[192,1152]{1,0:T(8,128)(2,1)S(1)} %slice.366), channel_id=1, source_target_pairs={{0,4},{1,5},{2,6},{3,7},{4,0},{5,1},{6,2},{7,3},{8,12},{9,13},{10,... | collective-permute-start | bytes 1327112 | tf_op jit(solution)/shard_map/ppermute | solution.py:679
  110.3 20.6 %collective-permute-start.33 = (bf16[192,1152]{1,0:T(8,128)(2,1)S(1)}, bf16[192,1152]{1,0:T(8,128)(2,1)}, u32[]{:S(2)}, u32[]{:S(2)}) collective-permute-start(bf16[192,1152]{1,0:T(8,128)(2,1)S(1)} %slice.365), channel_id=1, source_target_pairs={{0,2},{1,3},{2,0},{3,1},{4,6},{5,7},{6,4},{7,5},{8,10},{9,11},{10,... | collective-permute-start | bytes 1327112 | tf_op jit(solution)/shard_map/ppermute | solution.py:679
  117.2 11.6 %collective-permute-start.40 = (bf16[256,768]{1,0:T(8,128)(2,1)S(1)}, bf16[256,768]{1,0:T(8,128)(2,1)}, u32[]{:S(2)}, u32[]{:S(2)}) collective-permute-start(bf16[256,768]{1,0:T(8,128)(2,1)S(1)} %fusion.49), channel_id=1, source_target_pairs={{0,2},{1,3},{2,0},{3,1},{4,6},{5,7},{6,4},{7,5},{8,10},{9,11},{10,... | collective-permute-start | bytes 1179656 | tf_op jit(solution)/shard_map/ppermute | solution.py:679
  128.8 12.3 %collective-permute-start.22 = (bf16[192,1280]{1,0:T(8,128)(2,1)S(1)}, bf16[192,1280]{1,0:T(8,128)(2,1)S(1)}, u32[]{:S(2)}, u32[]{:S(2)}) collective-permute-start(bf16[192,1280]{1,0:T(8,128)(2,1)S(1)} %slice.363), channel_id=1, source_target_pairs={{0,4},{1,5},{2,6},{3,7},{4,0},{5,1},{6,2},{7,3},{8,12},{9,13},{10,... | collective-permute-start | bytes 1474568 | tf_op jit(solution)/shard_map/ppermute | solution.py:679
  129.3 12.1 %collective-permute-start.21 = (bf16[192,1280]{1,0:T(8,128)(2,1)S(1)}, bf16[192,1280]{1,0:T(8,128)(2,1)}, u32[]{:S(2)}, u32[]{:S(2)}) collective-permute-start(bf16[192,1280]{1,0:T(8,128)(2,1)S(1)} %slice.362), channel_id=1, source_target_pairs={{0,2},{1,3},{2,0},{3,1},{4,6},{5,7},{6,4},{7,5},{8,10},{9,11},{10,... | collective-permute-start | bytes 1474568 | tf_op jit(solution)/shard_map/ppermute | solution.py:679
  130.9 14.7 %collective-permute-start.25 = (bf16[384,1280]{1,0:T(8,128)(2,1)}, bf16[384,1280]{1,0:T(8,128)(2,1)}, u32[]{:S(2)}, u32[]{:S(2)}) collective-permute-start(bf16[384,1280]{1,0:T(8,128)(2,1)} %collective-permute-done.20.rest_2_), channel_id=1, source_target_pairs={{0,1},{1,0},{2,3},{3,2},{4,5},{5,4},{6,7},{7,6},{8,9},{9,8},{10,11... | collective-permute-start | bytes 2949128 | tf_op jit(solution)/shard_map/ppermute | solution.py:679
  130.9 15.1 %collective-permute-start.24 = (bf16[384,1280]{1,0:T(8,128)(2,1)S(1)}, bf16[384,1280]{1,0:T(8,128)(2,1)}, u32[]{:S(2)}, u32[]{:S(2)}) collective-permute-start(bf16[384,1280]{1,0:T(8,128)(2,1)S(1)} %collective-permute-done.19.norm_b_ref.rest_1_), channel_id=1, source_target_pairs={{0,1},{1,0},{2,3},{3,2},{4,5},{5,4},{6,7},{7,6},{8,9},{9,8},{10,11... | collective-permute-start | bytes 2949128 | tf_op jit(solution)/shard_map/ppermute | solution.py:679
  145.6 37.6 %collective-permute-start.35 = (bf16[384,1152]{1,0:T(8,128)(2,1)S(1)}, bf16[384,1152]{1,0:T(8,128)(2,1)S(1)}, u32[]{:S(2)}, u32[]{:S(2)}) collective-permute-start(bf16[384,1152]{1,0:T(8,128)(2,1)S(1)} %pad_maximum_fusion.3.rest_1_.rest_0_), channel_id=1, source_target_pairs={{0,1},{1,0},{2,3},{3,2},{4,5},{5,4},{6,7},{7,6},{8,9},{9,8},{10,11... | collective-permute-start | bytes 2654216 | tf_op jit(solution)/shard_map/ppermute | solution.py:679
  146.0 37.2 %collective-permute-start.37 = (bf16[384,1152]{1,0:T(8,128)(2,1)}, bf16[384,1152]{1,0:T(8,128)(2,1)S(1)}, u32[]{:S(2)}, u32[]{:S(2)}) collective-permute-start(bf16[384,1152]{1,0:T(8,128)(2,1)} %collective-permute-done.32.rest_3_.rest_2_), channel_id=1, source_target_pairs={{0,1},{1,0},{2,3},{3,2},{4,5},{5,4},{6,7},{7,6},{8,9},{9,8},{10,11... | collective-permute-start | bytes 2654216 | tf_op jit(solution)/shard_map/ppermute | solution.py:679
  146.2 37.0 %collective-permute-start.36 = (bf16[384,1152]{1,0:T(8,128)(2,1)}, bf16[384,1152]{1,0:T(8,128)(2,1)}, u32[]{:S(2)}, u32[]{:S(2)}) collective-permute-start(bf16[384,1152]{1,0:T(8,128)(2,1)} %collective-permute-done.31.rest_2_.rest_1_), channel_id=1, source_target_pairs={{0,1},{1,0},{2,3},{3,2},{4,5},{5,4},{6,7},{7,6},{8,9},{9,8},{10,11... | collective-permute-start | bytes 2654216 | tf_op jit(solution)/shard_map/ppermute | solution.py:679
  146.5 36.6 %collective-permute-start.39 = (bf16[192,1152]{1,0:T(8,128)(2,1)}, bf16[192,1152]{1,0:T(8,128)(2,1)S(1)}, u32[]{:S(2)}, u32[]{:S(2)}) collective-permute-start(bf16[192,1152]{1,0:T(8,128)(2,1)} %collective-permute-done.34.rest_5_.rest_4_), channel_id=1, source_target_pairs={{0,1},{1,0},{2,3},{3,2},{4,5},{5,4},{6,7},{7,6},{8,9},{9,8},{10,11... | collective-permute-start | bytes 1327112 | tf_op jit(solution)/shard_map/ppermute | solution.py:679
  146.7 36.5 %collective-permute-start.38 = (bf16[192,1152]{1,0:T(8,128)(2,1)}, bf16[192,1152]{1,0:T(8,128)(2,1)}, u32[]{:S(2)}, u32[]{:S(2)}) collective-permute-start(bf16[192,1152]{1,0:T(8,128)(2,1)} %collective-permute-done.33.rest_4_.rest_3_), channel_id=1, source_target_pairs={{0,1},{1,0},{2,3},{3,2},{4,5},{5,4},{6,7},{7,6},{8,9},{9,8},{10,11... | collective-permute-start | bytes 1327112 | tf_op jit(solution)/shard_map/ppermute | solution.py:679
  270.2 39.3 %collective-permute-start.60 = (bf16[2,768,1152]{2,1,0:T(8,128)(2,1)}, bf16[2,768,1152]{2,1,0:T(8,128)(2,1)}, u32[]{:S(2)}, u32[]{:S(2)}) collective-permute-start(bf16[2,768,1152]{2,1,0:T(8,128)(2,1)} %get-tuple-element.79), channel_id=1, source_target_pairs={{0,1},{1,0},{2,3},{3,2},{4,5},{5,4},{6,7},{7,6},{8,9},{9,8},{10,11... | collective-permute-start | bytes 10616840 | tf_op jit(solution)/shard_map/ppermute | solution.py:679
  270.3 46.4 %collective-permute-start.52 = (bf16[2,768,1152]{2,1,0:T(8,128)(2,1)}, bf16[2,768,1152]{2,1,0:T(8,128)(2,1)S(1)}, u32[]{:S(2)}, u32[]{:S(2)}) collective-permute-start(bf16[2,768,1152]{2,1,0:T(8,128)(2,1)} %get-tuple-element.77), channel_id=1, source_target_pairs={{0,1},{1,0},{2,3},{3,2},{4,5},{5,4},{6,7},{7,6},{8,9},{9,8},{10,11... | collective-permute-start | bytes 10616840 | tf_op jit(solution)/shard_map/ppermute | solution.py:679
  276.1 22.6 %collective-permute-start.41 = (bf16[256,768]{1,0:T(8,128)(2,1)}, bf16[256,768]{1,0:T(8,128)(2,1)}, u32[]{:S(2)}, u32[]{:S(2)}) collective-permute-start(bf16[256,768]{1,0:T(8,128)(2,1)} %slice.368), channel_id=1, source_target_pairs={{0,2},{1,3},{2,0},{3,1},{4,6},{5,7},{6,4},{7,5},{8,10},{9,11},{10,... | collective-permute-start | bytes 1179656 | tf_op jit(solution)/shard_map/ppermute | solution.py:679
  297.2 11.0 %collective-permute-start.43 = (bf16[256,768]{1,0:T(8,128)(2,1)S(1)}, bf16[256,768]{1,0:T(8,128)(2,1)S(1)}, u32[]{:S(2)}, u32[]{:S(2)}) collective-permute-start(bf16[256,768]{1,0:T(8,128)(2,1)S(1)} %slice.538), channel_id=1, source_target_pairs={{0,2},{1,3},{2,0},{3,1},{4,6},{5,7},{6,4},{7,5},{8,10},{9,11},{10,... | collective-permute-start | bytes 1179656 | tf_op jit(solution)/shard_map/ppermute | solution.py:679
  300.8 54.5 %collective-permute-start.44 = (bf16[2,768,896]{2,1,0:T(8,128)(2,1)S(1)}, bf16[2,768,896]{2,1,0:T(8,128)(2,1)S(1)}, u32[]{:S(2)}, u32[]{:S(2)}) collective-permute-start(bf16[2,768,896]{2,1,0:T(8,128)(2,1)S(1)} %copy-done.22), channel_id=1, source_target_pairs={{0,1},{1,0},{2,3},{3,2},{4,5},{5,4},{6,7},{7,6},{8,9},{9,8},{10,11... | collective-permute-start | bytes 8257544 | tf_op jit(solution)/shard_map/ppermute | solution.py:679
  312.3 45.0 %collective-permute-start.61 = (bf16[2,192,1152]{2,1,0:T(8,128)(2,1)S(1)}, bf16[2,192,1152]{2,1,0:T(8,128)(2,1)S(1)}, u32[]{:S(2)}, u32[]{:S(2)}) collective-permute-start(bf16[2,192,1152]{2,1,0:T(8,128)(2,1)S(1)} %fusion.23), channel_id=1, source_target_pairs={{0,2},{1,3},{2,0},{3,1},{4,6},{5,7},{6,4},{7,5},{8,10},{9,11},{10,... | collective-permute-start | bytes 2654216 | tf_op jit(solution)/shard_map/ppermute | solution.py:679
  315.3 22.6 %collective-permute-start.64 = (bf16[2,192,1152]{2,1,0:T(8,128)(2,1)S(1)}, bf16[2,192,1152]{2,1,0:T(8,128)(2,1)S(1)}, u32[]{:S(2)}, u32[]{:S(2)}) collective-permute-start(bf16[2,192,1152]{2,1,0:T(8,128)(2,1)S(1)} %fusion.24), channel_id=1, source_target_pairs={{0,4},{1,5},{2,6},{3,7},{4,0},{5,1},{6,2},{7,3},{8,12},{9,13},{10,... | collective-permute-start | bytes 2654216 | tf_op jit(solution)/shard_map/ppermute | solution.py:679
  317.0 37.6 %collective-permute-start.56 = (bf16[2,192,1152]{2,1,0:T(8,128)(2,1)S(1)}, bf16[2,192,1152]{2,1,0:T(8,128)(2,1)S(1)}, u32[]{:S(2)}, u32[]{:S(2)}) collective-permute-start(bf16[2,192,1152]{2,1,0:T(8,128)(2,1)S(1)} %fusion.22), channel_id=1, source_target_pairs={{0,4},{1,5},{2,6},{3,7},{4,0},{5,1},{6,2},{7,3},{8,12},{9,13},{10,... | collective-permute-start | bytes 2654216 | tf_op jit(solution)/shard_map/ppermute | solution.py:679
  317.9 48.9 %collective-permute-start.53 = (bf16[2,192,1152]{2,1,0:T(8,128)(2,1)S(1)}, bf16[2,192,1152]{2,1,0:T(8,128)(2,1)S(1)}, u32[]{:S(2)}, u32[]{:S(2)}) collective-permute-start(bf16[2,192,1152]{2,1,0:T(8,128)(2,1)S(1)} %fusion.21), channel_id=1, source_target_pairs={{0,2},{1,3},{2,0},{3,1},{4,6},{5,7},{6,4},{7,5},{8,10},{9,11},{10,... | collective-permute-start | bytes 2654216 | tf_op jit(solution)/shard_map/ppermute | solution.py:679
  339.1 24.2 %collective-permute-start.65 = (bf16[192,1152]{1,0:T(8,128)(2,1)S(1)}, bf16[192,1152]{1,0:T(8,128)(2,1)S(1)}, u32[]{:S(2)}, u32[]{:S(2)}) collective-permute-start(bf16[192,1152]{1,0:T(8,128)(2,1)S(1)} %fusion.25), channel_id=1, source_target_pairs={{0,2},{1,3},{2,0},{3,1},{4,6},{5,7},{6,4},{7,5},{8,10},{9,11},{10,... | collective-permute-start | bytes 1327112 | tf_op jit(solution)/shard_map/ppermute | solution.py:679
  354.8 18.7 %collective-permute-start.57 = (bf16[192,1152]{1,0:T(8,128)(2,1)S(1)}, bf16[192,1152]{1,0:T(8,128)(2,1)S(1)}, u32[]{:S(2)}, u32[]{:S(2)}) collective-permute-start(bf16[192,1152]{1,0:T(8,128)(2,1)S(1)} %fusion.30), channel_id=1, source_target_pairs={{0,2},{1,3},{2,0},{3,1},{4,6},{5,7},{6,4},{7,5},{8,10},{9,11},{10,... | collective-permute-start | bytes 1327112 | tf_op jit(solution)/shard_map/ppermute | solution.py:679
  355.5 62.7 %collective-permute-start.45 = (bf16[2,192,896]{2,1,0:T(8,128)(2,1)S(1)}, bf16[2,192,896]{2,1,0:T(8,128)(2,1)S(1)}, u32[]{:S(2)}, u32[]{:S(2)}) collective-permute-start(bf16[2,192,896]{2,1,0:T(8,128)(2,1)S(1)} %fusion.38), channel_id=1, source_target_pairs={{0,2},{1,3},{2,0},{3,1},{4,6},{5,7},{6,4},{7,5},{8,10},{9,11},{10,... | collective-permute-start | bytes 2064392 | tf_op jit(solution)/shard_map/ppermute | solution.py:679
  357.3 59.1 %collective-permute-start.48 = (bf16[2,192,896]{2,1,0:T(8,128)(2,1)S(1)}, bf16[2,192,896]{2,1,0:T(8,128)(2,1)S(1)}, u32[]{:S(2)}, u32[]{:S(2)}) collective-permute-start(bf16[2,192,896]{2,1,0:T(8,128)(2,1)S(1)} %fusion.39), channel_id=1, source_target_pairs={{0,4},{1,5},{2,6},{3,7},{4,0},{5,1},{6,2},{7,3},{8,12},{9,13},{10,... | collective-permute-start | bytes 2064392 | tf_op jit(solution)/shard_map/ppermute | solution.py:679
  364.9 32.4 %collective-permute-start.66 = (bf16[96,1152]{1,0:T(8,128)(2,1)S(1)}, bf16[96,1152]{1,0:T(8,128)(2,1)S(1)}, u32[]{:S(2)}, u32[]{:S(2)}) collective-permute-start(bf16[96,1152]{1,0:T(8,128)(2,1)S(1)} %get-tuple-element.124), channel_id=1, source_target_pairs={{0,16},{1,17},{2,18},{3,19},{4,20},{5,21},{6,22},{7,23},{8,24},{9,... | collective-permute-start | bytes 663560 | tf_op jit(solution)/shard_map/ppermute | solution.py:679
  366.8 34.0 %collective-permute-start.67 = (bf16[96,1152]{1,0:T(8,128)(2,1)S(1)}, bf16[96,1152]{1,0:T(8,128)(2,1)S(1)}, u32[]{:S(2)}, u32[]{:S(2)}) collective-permute-start(bf16[96,1152]{1,0:T(8,128)(2,1)S(1)} %get-tuple-element.125), channel_id=1, source_target_pairs={{0,24},{1,25},{2,26},{3,27},{4,28},{5,29},{6,30},{7,31},{8,0},{9,1... | collective-permute-start | bytes 663560 | tf_op jit(solution)/shard_map/ppermute | solution.py:679
  392.5 14.0 %collective-permute-start.63 = (bf16[96,1152]{1,0:T(8,128)(2,1)S(1)}, bf16[96,1152]{1,0:T(8,128)(2,1)S(1)}, u32[]{:S(2)}, u32[]{:S(2)}) collective-permute-start(bf16[96,1152]{1,0:T(8,128)(2,1)S(1)} %split.87), channel_id=1, source_target_pairs={{0,8},{1,9},{2,10},{3,11},{4,12},{5,13},{6,14},{7,15},{8,16},{9,17... | collective-permute-start | bytes 663560 | tf_op jit(solution)/shard_map/ppermute | solution.py:679
  397.4 18.9 %collective-permute-start.58 = (bf16[96,1152]{1,0:T(8,128)(2,1)S(1)}, bf16[96,1152]{1,0:T(8,128)(2,1)S(1)}, u32[]{:S(2)}, u32[]{:S(2)}) collective-permute-start(bf16[96,1152]{1,0:T(8,128)(2,1)S(1)} %get-tuple-element.122), channel_id=1, source_target_pairs={{0,16},{1,17},{2,18},{3,19},{4,20},{5,21},{6,22},{7,23},{8,24},{9,... | collective-permute-start | bytes 663560 | tf_op jit(solution)/shard_map/ppermute | solution.py:679
  400.8 15.5 %collective-permute-start.59 = (bf16[96,1152]{1,0:T(8,128)(2,1)S(1)}, bf16[96,1152]{1,0:T(8,128)(2,1)S(1)}, u32[]{:S(2)}, u32[]{:S(2)}) collective-permute-start(bf16[96,1152]{1,0:T(8,128)(2,1)S(1)} %get-tuple-element.123), channel_id=1, source_target_pairs={{0,24},{1,25},{2,26},{3,27},{4,28},{5,29},{6,30},{7,31},{8,0},{9,1... | collective-permute-start | bytes 663560 | tf_op jit(solution)/shard_map/ppermute | solution.py:679
  425.7 12.6 %collective-permute-start.50 = (bf16[96,896]{1,0:T(8,128)(2,1)S(1)}, bf16[96,896]{1,0:T(8,128)(2,1)S(1)}, u32[]{:S(2)}, u32[]{:S(2)}) collective-permute-start(bf16[96,896]{1,0:T(8,128)(2,1)S(1)} %get-tuple-element.134), channel_id=1, source_target_pairs={{0,16},{1,17},{2,18},{3,19},{4,20},{5,21},{6,22},{7,23},{8,24},{9,... | collective-permute-start | bytes 516104 | tf_op jit(solution)/shard_map/ppermute | solution.py:679
  (50 other events, 601.3 us)

commit v4 on v3

--- a/solution.py
+++ b/solution.py
@@ -61,7 +61,7 @@
     )
 
 
-BLOCKS = 10
+BLOCKS = 5
 
 
 def block_starts(width):
@@ -69,24 +69,15 @@
     return [(0, 0), (0, half), (1, 0), (1, half), (1, half + quarter)]
 
 
-def weight_copies(blocks, w_ref, sems, core):
-    copies = []
-    for k in range(2):
-        for block, (y, row) in zip(blocks[5 * k : 5 * k + 5], block_starts(w_ref.shape[1])):
-            slot = 2 * y + jnp.bitwise_xor(core, k)
-            copies.append(
-                pltpu.make_async_copy(
-                    block, w_ref.at[slot, pl.ds(row, block.shape[0])], sems.at[slot]
-                )
-            )
-    return copies
-
-
-def start_weights(blocks, w_ref, sems, core):
+def start_weights(blocks, w_ref, sems):
     @pl.when(pl.program_id(0) == 0)
     def _():
-        for copy in weight_copies(blocks, w_ref, sems, core):
-            copy.start()
+        for i, block in enumerate(blocks):
+            y, row = block_starts(w_ref.shape[1])[i % BLOCKS]
+            slot = i // BLOCKS * 2 + y
+            pltpu.make_async_copy(
+                block, w_ref.at[slot, pl.ds(row, block.shape[0])], sems.at[slot]
+            ).start()
 
 
 def wait_weights(w_ref, sems, slot):
@@ -95,9 +86,10 @@
 
 def weight_scratch(blocks):
     width = 2 * blocks[0].shape[0]
+    slots = 2 * len(blocks) // BLOCKS
     return [
-        pltpu.VMEM((4, width, blocks[0].shape[1]), bf16),
-        pltpu.SemaphoreType.DMA((4,)),
+        pltpu.VMEM((slots, width, blocks[0].shape[1]), bf16),
+        pltpu.SemaphoreType.DMA((slots,)),
     ]
 
 
@@ -112,10 +104,10 @@
     return pl.BlockSpec(shape, lambda *_: (0,) * len(shape))
 
 
-def qkv_kernel(core_ref, x_ref, cos_ref, sin_ref, *rest):
-    blocks, (q_ref, kv_ref, wo_ref, w_ref, sems) = rest[:BLOCKS], rest[BLOCKS:]
+def qkv_kernel(x_ref, cos_ref, sin_ref, *rest):
+    blocks, (q_ref, kv_ref, wo_ref, w_ref, sems) = rest[: 2 * BLOCKS], rest[2 * BLOCKS :]
     slot = pl.program_id(0)
-    start_weights(blocks, w_ref, sems, core_ref[0])
+    start_weights(blocks, w_ref, sems)
     wait_weights(w_ref, sems, slot)
     lane = lax.broadcasted_iota(jnp.int32, (w_ref.shape[1], 4 * HD), 1)
     cosine, sine = cos_ref[...], sin_ref[...]
@@ -134,23 +126,19 @@
     wo_ref[...] = out.astype(bf16)
 
 
-def qkv(core, x, cosine, sine, blocks):
+def qkv(x, cosine, sine, blocks):
     rows, width = x.shape
     part = blocks[0].shape[1] // 3
-    grid_spec = pltpu.PrefetchScalarGridSpec(
-        num_scalar_prefetch=1,
-        grid=(4,),
-        in_specs=[whole((rows, width)), whole((rows, part)), whole((rows, part))] + [ANY] * BLOCKS,
-        out_specs=[
-            pl.BlockSpec((rows, part), lambda i, core: (0, i)),
-            pl.BlockSpec((rows, 2 * part), lambda i, core: (0, i)),
-            pl.BlockSpec((width, part), lambda i, core: (0, i)),
-        ],
-        scratch_shapes=weight_scratch(blocks),
-    )
     return pl.pallas_call(
         qkv_kernel,
-        grid_spec=grid_spec,
+        grid=(4,),
+        in_specs=[whole((rows, width)), whole((rows, part)), whole((rows, part))] + [ANY] * len(blocks),
+        out_specs=[
+            pl.BlockSpec((rows, part), lambda i: (0, i)),
+            pl.BlockSpec((rows, 2 * part), lambda i: (0, i)),
+            pl.BlockSpec((width, part), lambda i: (0, i)),
+        ],
+        scratch_shapes=weight_scratch(blocks),
         out_shape=[
             jax.ShapeDtypeStruct((rows, 4 * part), bf16),
             jax.ShapeDtypeStruct((rows, 8 * part), bf16),
@@ -158,7 +146,7 @@
         ],
         cost_estimate=cost(24 * rows * width * part, 40 * width * part),
         name="qkv",
-    )(core, x, cosine, sine, *blocks)
+    )(x, cosine, sine, *blocks)
 
 
 def attend_kernel(q_ref, own_ref, other_ref, segq_ref, segk_ref, out_ref, log_ref):
@@ -187,30 +175,33 @@
         out_ref[span, :] = jnp.concatenate(parts, axis=0).T.astype(bf16)
 
 
-def attend(q, kv_own, kv_other, seg_q, seg_k):
+def attend(which, q, kv_own, kv_other, seg_q, seg_k):
     rows, width = q.shape
     part = width // 4
+    width = width // 2
     keys = seg_k.shape[0]
-    by_part = lambda j: (0, j)
+    by_part = lambda j: (0, 2 * which + j)
+    flipped = lambda j: (0, 2 * (1 - which) + j)
+    out_part = lambda j: (0, j)
     return pl.pallas_call(
         attend_kernel,
-        grid=(4,),
+        grid=(2,),
         in_specs=[
             pl.BlockSpec((rows, part), by_part),
             pl.BlockSpec((rows, 2 * part), by_part),
-            pl.BlockSpec((rows, 2 * part), by_part),
+            pl.BlockSpec((rows, 2 * part), flipped),
             whole((1, rows)),
             whole((keys, 1)),
         ],
         out_specs=[
-            pl.BlockSpec((rows, part), by_part),
+            pl.BlockSpec((rows, part), out_part),
             pl.BlockSpec((1, 8, rows), lambda j: (j, 0, 0)),
         ],
         out_shape=[
             jax.ShapeDtypeStruct((rows, width), bf16),
-            jax.ShapeDtypeStruct((4, 8, rows), f32),
-        ],
-        cost_estimate=cost(16 * rows * keys * width, 12 * keys * width, rows * keys * 12),
+            jax.ShapeDtypeStruct((2, 8, rows), f32),
+        ],
+        cost_estimate=cost(16 * rows * keys * width, 12 * keys * width, rows * keys * 6),
         name="attend",
     )(q, kv_own, kv_other, seg_q, seg_k)
 
@@ -255,46 +246,49 @@
             dkv_other_ref[:, lanes] = pieces[p][rows:].astype(bf16)
 
 
-def attend_back(q, kv_own, kv_other, do, logs, delta, seg_q, seg_k, cosine, sine):
+def attend_back(which, q, kv_own, kv_other, do, logs, delta, seg_q, seg_k, cosine, sine):
     rows, width = q.shape
     part = width // 4
+    width = width // 2
     keys = seg_k.shape[0]
-    by_part = lambda j: (0, j)
-    stat = pl.BlockSpec((1, 8, rows), lambda j: (j, 0, 0))
+    by_part = lambda j: (0, 2 * which + j)
+    flipped = lambda j: (0, 2 * (1 - which) + j)
+    out_part = lambda j: (0, j)
     return pl.pallas_call(
         attend_back_kernel,
-        grid=(4,),
+        grid=(2,),
         in_specs=[
             pl.BlockSpec((rows, part), by_part),
             pl.BlockSpec((rows, 2 * part), by_part),
-            pl.BlockSpec((rows, 2 * part), by_part),
+            pl.BlockSpec((rows, 2 * part), flipped),
             pl.BlockSpec((rows, part), by_part),
-            stat,
-            stat,
+            pl.BlockSpec((1, 8, rows), lambda j: (j, 0, 0)),
+            pl.BlockSpec((1, 8, rows), lambda j: (2 * which + j, 0, 0)),
             whole((1, rows)),
             whole((keys, 1)),
             whole((rows, part)),
             whole((rows, part)),
         ],
         out_specs=[
-            pl.BlockSpec((rows, part), by_part),
-            pl.BlockSpec((rows, 2 * part), by_part),
-            pl.BlockSpec((rows, 2 * part), by_part),
+            pl.BlockSpec((rows, part), out_part),
+            pl.BlockSpec((rows, 2 * part), out_part),
+            pl.BlockSpec((rows, 2 * part), out_part),
         ],
         out_shape=[
             jax.ShapeDtypeStruct((rows, width), bf16),
             jax.ShapeDtypeStruct((rows, 2 * width), f32),
             jax.ShapeDtypeStruct((rows, 2 * width), bf16),
         ],
-        cost_estimate=cost(40 * rows * keys * width, 30 * keys * width, rows * keys * 12),
+        cost_estimate=cost(40 * rows * keys * width, 30 * keys * width, rows * keys * 6),
         name="attend_back",
     )(q, kv_own, kv_other, do, logs, delta, seg_q, seg_k, cosine, sine)
 
 
-def first_kernel(x_ref, att_ref, wo_ref, norm_a_ref, norm_b_ref, n_ref, s_ref, low_ref, low_t_ref, gains_ref):
+def first_kernel(x_ref, att_own_ref, att_other_ref, wo_ref, norm_a_ref, norm_b_ref, n_ref, s_ref, low_ref, low_t_ref, gains_ref):
     norms = jnp.concatenate([norm_a_ref[...], norm_b_ref[...]], axis=0).astype(f32).T
     gains_ref[...] = norms[:8]
-    branch = dot(att_ref[...], wo_ref[...], NT)
+    lanes = att_own_ref.shape[1]
+    branch = dot(att_own_ref[...], wo_ref[:, :lanes], NT) + dot(att_other_ref[...], wo_ref[:, lanes:], NT)
     normed, inv = normalize(x_ref[...].astype(f32) + branch)
     n_ref[...] = normed
     s_ref[...] = jnp.broadcast_to(inv, s_ref.shape)
@@ -303,14 +297,16 @@
     low_t_ref[...] = first.T.astype(bf16)
 
 
-def first_norm(x, attended, wo, norm_a, norm_b):
+def first_norm(x, att_own, att_other, wo, norm_a, norm_b):
     rows, width = x.shape
     at = norm_a.shape[1] // 128 - 1
     strip = pl.BlockSpec((width // 2, 128), lambda i: (0, at))
     return pl.pallas_call(
         first_kernel,
         grid=(1,),
-        in_specs=[whole(x.shape), whole(attended.shape), whole(wo.shape), strip, strip],
+        in_specs=[
+            whole(x.shape), whole(att_own.shape), whole(att_own.shape), whole(wo.shape), strip, strip,
+        ],
         out_specs=[
             whole((rows, width)), whole((rows, 128)), whole((rows, width)), whole((width, rows)), whole((8, width)),
         ],
@@ -323,16 +319,16 @@
         ],
         cost_estimate=cost(2 * rows * width * wo.shape[1], 16 * rows * width),
         name="first_norm",
-    )(x, attended, wo, norm_a, norm_b)
-
-
-def mlp_kernel(has_base, core_ref, low_ref, *rest):
+    )(x, att_own, att_other, wo, norm_a, norm_b)
+
+
+def mlp_kernel(has_base, low_ref, *rest):
     if has_base:
         base_ref, rest = rest[0], rest[1:]
-    blocks, (act_ref, feed_ref, w_ref, sems) = rest[:BLOCKS], rest[BLOCKS:]
+    blocks, (act_ref, feed_ref, w_ref, sems) = rest[: 2 * BLOCKS], rest[2 * BLOCKS :]
     slot = pl.program_id(0)
     half = act_ref.shape[3]
-    start_weights(blocks, w_ref, sems, core_ref[0])
+    start_weights(blocks, w_ref, sems)
 
     @pl.when(slot == 0)
     def _():
@@ -355,30 +351,26 @@
     lax.fori_loop(0, low_ref.shape[0] // QROWS, body, 0)
 
 
-def mlp(core, low, base, blocks, half):
+def mlp(low, base, blocks, half):
     rows, width = low.shape
     has_base = base is not None
     extra = [base] if has_base else []
-    grid_spec = pltpu.PrefetchScalarGridSpec(
-        num_scalar_prefetch=1,
-        grid=(4,),
-        in_specs=[whole((rows, width))] + [whole((rows, width))] * has_base + [ANY] * BLOCKS,
-        out_specs=[
-            pl.BlockSpec((1, 3, rows, half), lambda i, core: (i, 0, 0, 0)),
-            whole((rows, width)),
-        ],
-        scratch_shapes=weight_scratch(blocks),
-    )
     return pl.pallas_call(
         functools.partial(mlp_kernel, has_base),
-        grid_spec=grid_spec,
+        grid=(4,),
+        in_specs=[whole((rows, width))] * (1 + has_base) + [ANY] * len(blocks),
+        out_specs=[
+            pl.BlockSpec((1, 3, rows, half), lambda i: (i, 0, 0, 0)),
+            whole((rows, width)),
+        ],
+        scratch_shapes=weight_scratch(blocks),
         out_shape=[
             jax.ShapeDtypeStruct((4, 3, rows, half), bf16),
             jax.ShapeDtypeStruct((rows, width), f32),
         ],
         cost_estimate=cost(24 * rows * width * half, 60 * half * width, 4 * rows * half),
         name="mlp",
-    )(core, low, *extra, *blocks)
+    )(low, *extra, *blocks)
 
 
 def second_kernel(n_ref, gains_ref, feed_ref, dy_ref, out_ref, dh_ref, low_ref, low_t_ref, sums_ref):
@@ -415,26 +407,13 @@
     )(n1, gains, feed, dy)
 
 
-def for_slot(i, core):
-    return 2 * (i % 2) + jnp.bitwise_xor(core[0], 1 - i // 2)
-
-
-def to_other(i, core):
-    return jnp.minimum(i, 1)
-
-
-def to_own(i, core):
-    return jnp.maximum(i - 2, 0)
-
-
-def mlp_back_kernel(core_ref, base_ref, dfeed_ref, dfeed_t_ref, low_t_ref, act_ref, *rest):
-    blocks, (dfirst_ref, send_ref, keep_ref, w_ref, sems, part_ref) = rest[:BLOCKS], rest[BLOCKS:]
-    step = pl.program_id(0)
-    slot = for_slot(step, core_ref)
+def mlp_back_kernel(base_ref, dfeed_ref, dfeed_t_ref, low_t_ref, act_ref, *rest):
+    blocks, (dfirst_ref, grad_ref, w_ref, sems, part_ref) = rest[:BLOCKS], rest[BLOCKS:]
+    slot = pl.program_id(0)
     half = act_ref.shape[3]
-    start_weights(blocks, w_ref, sems, core_ref[0])
-
-    @pl.when(step == 0)
+    start_weights(blocks, w_ref, sems)
+
+    @pl.when(slot == 0)
     def _():
         dfirst_ref[...] = base_ref[...]
 
@@ -454,61 +433,44 @@
         return 0
 
     lax.fori_loop(0, dfeed_ref.shape[0] // QROWS, body, 0)
-
-    def emit(out_ref):
-        out_ref[0, :, half:] = dot(low_t_ref[...], part_ref[...]).astype(bf16)
-        out_ref[0, :, :half] = dot(dfeed_t_ref[...], act_ref[0, 2]).astype(bf16)
-
-    @pl.when(step < 2)
-    def _():
-        emit(send_ref)
-
-    @pl.when(step >= 2)
-    def _():
-        emit(keep_ref)
-
-
-def mlp_back(core, base, dfeed, dfeed_t, low_t, act, blocks):
+    grad_ref[0, :, half:] = dot(low_t_ref[...], part_ref[...]).astype(bf16)
+    grad_ref[0, :, :half] = dot(dfeed_t_ref[...], act_ref[0, 2]).astype(bf16)
+
+
+def mlp_back(which, base, dfeed, dfeed_t, low_t, act, blocks):
     rows, width = dfeed.shape
     half = act.shape[3]
+    blocks = blocks[which * BLOCKS : (which + 1) * BLOCKS]
     full = whole((rows, width))
-    grid_spec = pltpu.PrefetchScalarGridSpec(
-        num_scalar_prefetch=1,
-        grid=(4,),
+    return pl.pallas_call(
+        mlp_back_kernel,
+        grid=(2,),
         in_specs=[
             full,
             full,
             whole((width, rows)),
             whole((width, rows)),
-            pl.BlockSpec((1, 3, rows, half), lambda i, core: (for_slot(i, core), 0, 0, 0)),
+            pl.BlockSpec((1, 3, rows, half), lambda i: (2 * which + i, 0, 0, 0)),
         ]
         + [ANY] * BLOCKS,
-        out_specs=[
-            full,
-            pl.BlockSpec((1, width, 3 * half), lambda i, core: (to_other(i, core), 0, 0)),
-            pl.BlockSpec((1, width, 3 * half), lambda i, core: (to_own(i, core), 0, 0)),
-        ],
+        out_specs=[full, pl.BlockSpec((1, width, 3 * half), lambda i: (i, 0, 0))],
         scratch_shapes=weight_scratch(blocks) + [pltpu.VMEM((rows, 2 * half), bf16)],
-    )
-    return pl.pallas_call(
-        mlp_back_kernel,
-        grid_spec=grid_spec,
         out_shape=[
             jax.ShapeDtypeStruct((rows, width), f32),
             jax.ShapeDtypeStruct((2, width, 3 * half), bf16),
-            jax.ShapeDtypeStruct((2, width, 3 * half), bf16),
-        ],
-        cost_estimate=cost(48 * rows * width * half, 100 * half * width, 4 * rows * half),
+        ],
+        cost_estimate=cost(24 * rows * width * half, 50 * half * width, 2 * rows * half),
         name="mlp_back",
-    )(core, base, dfeed, dfeed_t, low_t, act, *blocks)
+    )(base, dfeed, dfeed_t, low_t, act, *blocks)
 
 
 def first_back_kernel(
-    dfirst_ref, n_ref, s_ref, gains_ref, sums_ref, wo_ref, att_ref, dh_ref, low_t_ref, do_ref, delta_ref, cols_ref
+    dfirst_ref, n_ref, s_ref, gains_ref, sums_ref, wo_ref, att_own_ref, att_other_ref,
+    dh_ref, low_t_ref, do_ref, delta_ref, cols_ref,
 ):
     dfirst, normed = dfirst_ref[...], n_ref[...]
     rows, width = dfirst.shape
-    lanes = att_ref.shape[1]
+    lanes = wo_ref.shape[1]
     gain_sum = jnp.sum(dfirst * normed, axis=0, keepdims=True)
     bias_sum = jnp.sum(dfirst, axis=0, keepdims=True)
     sums = sums_ref[...]
@@ -522,7 +484,8 @@
     low_t_ref[...] = dh.T.astype(bf16)
     do = dot(low, wo_ref[...]).astype(bf16)
     do_ref[...] = do
-    prod = do.astype(f32) * att_ref[...].astype(f32)
+    attended = jnp.concatenate([att_own_ref[...], att_other_ref[...]], axis=1)
+    prod = do.astype(f32) * attended.astype(f32)
     high = prod.astype(bf16)
     rest = (prod - high.astype(f32)).astype(bf16)
     row = lax.broadcasted_iota(jnp.int32, (32, lanes), 0)
@@ -534,15 +497,16 @@
         delta_ref[j] = delta[8 * j : 8 * j + 8]
 
 
-def first_back(dfirst, n1, s1, gains, sums, wo, attended):
+def first_back(dfirst, n1, s1, gains, sums, wo, att_own, att_other):
     rows, width = n1.shape
     full = whole((rows, width))
-    lanes = attended.shape[1]
+    lanes = wo.shape[1]
     return pl.pallas_call(
         first_back_kernel,
         grid=(1,),
         in_specs=[
-            full, full, whole((rows, 128)), whole((8, width)), whole((8, width)), whole(wo.shape), whole(attended.shape),
+            full, full, whole((rows, 128)), whole((8, width)), whole((8, width)),
+            whole(wo.shape), whole(att_own.shape), whole(att_own.shape),
         ],
         out_specs=[full, whole((width, rows)), whole((rows, lanes)), whole((4, 8, rows)), whole((width, 128))],
         out_shape=[
@@ -554,19 +518,20 @@
         ],
         cost_estimate=cost(2 * rows * width * lanes, 20 * rows * width),
         name="first_back",
-    )(dfirst, n1, s1, gains, sums, wo, attended)
-
-
-def qkv_back_kernel(core_ref, dh_ref, dq_ref, own_ref, came_ref, cos_ref, sin_ref, x_t_ref, low_t_ref, att_ref, cols_ref, *rest):
-    blocks, (grad_ref, send_ref, keep_ref, w_ref, sems, part_ref) = rest[:BLOCKS], rest[BLOCKS:]
-    step = pl.program_id(0)
-    slot = for_slot(step, core_ref)
+    )(dfirst, n1, s1, gains, sums, wo, att_own, att_other)
+
+
+def qkv_back_kernel(
+    base_ref, dq_ref, own_ref, came_ref, cos_ref, sin_ref, x_t_ref, low_t_ref, att_ref, cols_ref, *rest
+):
+    blocks, (sum_ref, grad_ref, w_ref, sems, part_ref) = rest[:BLOCKS], rest[BLOCKS:]
+    slot = pl.program_id(0)
     part = dq_ref.shape[1]
-    start_weights(blocks, w_ref, sems, core_ref[0])
-
-    @pl.when(step == 0)
+    start_weights(blocks, w_ref, sems)
+
+    @pl.when(slot == 0)
     def _():
-        grad_ref[...] = dh_ref[...]
+        sum_ref[...] = base_ref[...]
 
     part_ref[:, :part] = dq_ref[...]
     dk = own_ref[:, :part] + came_ref[:, :part].astype(f32)
@@ -574,65 +539,48 @@
     dv = own_ref[:, part:] + came_ref[:, part:].astype(f32)
     part_ref[:, 2 * part :] = dv.astype(bf16)
     wait_weights(w_ref, sems, slot)
-    grad_ref[...] += dot(part_ref[...], w_ref[slot], NT)
+    sum_ref[...] += dot(part_ref[...], w_ref[slot], NT)
     d_out = dot(low_t_ref[...], att_ref[...])
     lane = lax.broadcasted_iota(jnp.int32, d_out.shape, 1)
-
-    def emit(out_ref):
-        for h in range(3):
-            lanes = slice(h * part, (h + 1) * part)
-            piece = dot(x_t_ref[...], part_ref[:, lanes])
-            moved = pltpu.roll(d_out, (3 - h) * HD, 1)
-            out_ref[0, :, lanes] = jnp.where(lane < 3 * HD, piece, moved).astype(bf16)
-        out_ref[0, :, 3 * part :] = cols_ref[...]
-
-    @pl.when(step < 2)
-    def _():
-        emit(send_ref)
-
-    @pl.when(step >= 2)
-    def _():
-        emit(keep_ref)
-
-
-def qkv_back(core, dh, dq, own, came, cosine, sine, x_t, low_t, attended, cols, blocks):
-    rows, width = dh.shape
-    part = dq.shape[1] // 4
+    for h in range(3):
+        lanes = slice(h * part, (h + 1) * part)
+        piece = dot(x_t_ref[...], part_ref[:, lanes])
+        moved = pltpu.roll(d_out, (3 - h) * HD, 1)
+        grad_ref[0, :, lanes] = jnp.where(lane < 3 * HD, piece, moved).astype(bf16)
+    grad_ref[0, :, 3 * part :] = cols_ref[...]
+
+
+def qkv_back(which, base, dq, own, came, cosine, sine, x_t, low_t, attended, cols, blocks):
+    rows, width = base.shape
+    part = dq.shape[1] // 2
+    blocks = blocks[which * BLOCKS : (which + 1) * BLOCKS]
     full = whole((rows, width))
-    grid_spec = pltpu.PrefetchScalarGridSpec(
-        num_scalar_prefetch=1,
-        grid=(4,),
+    by_part = lambda i: (0, i)
+    return pl.pallas_call(
+        qkv_back_kernel,
+        grid=(2,),
         in_specs=[
             full,
-            pl.BlockSpec((rows, part), lambda i, core: (0, for_slot(i, core))),
-            pl.BlockSpec((rows, 2 * part), lambda i, core: (0, for_slot(i, core))),
-            pl.BlockSpec((rows, 2 * part), lambda i, core: (0, for_slot(i, core))),
+            pl.BlockSpec((rows, part), by_part),
+            pl.BlockSpec((rows, 2 * part), by_part),
+            pl.BlockSpec((rows, 2 * part), by_part),
             whole((rows, part)),
             whole((rows, part)),
             whole((width, rows)),
             whole((width, rows)),
-            pl.BlockSpec((rows, part), lambda i, core: (0, for_slot(i, core))),
+            pl.BlockSpec((rows, part), by_part),
             whole((width, 128)),
         ]
         + [ANY] * BLOCKS,
-        out_specs=[
-            full,
-            pl.BlockSpec((1, width, 3 * part + 128), lambda i, core: (to_other(i, core), 0, 0)),
-            pl.BlockSpec((1, width, 3 * part + 128), lambda i, core: (to_own(i, core), 0, 0)),
-        ],
+        out_specs=[full, pl.BlockSpec((1, width, 3 * part + 128), lambda i: (i, 0, 0))],
         scratch_shapes=weight_scratch(blocks) + [pltpu.VMEM((rows, 3 * part), bf16)],
-    )
-    return pl.pallas_call(
-        qkv_back_kernel,
-        grid_spec=grid_spec,
         out_shape=[
             jax.ShapeDtypeStruct((rows, width), f32),
             jax.ShapeDtypeStruct((2, width, 3 * part + 128), bf16),
-            jax.ShapeDtypeStruct((2, width, 3 * part + 128), bf16),
-        ],
-        cost_estimate=cost(52 * rows * width * part, 80 * width * part),
+        ],
+        cost_estimate=cost(26 * rows * width * part, 40 * width * part),
         name="qkv_back",
-    )(core, dh, dq, own, came, cosine, sine, x_t, low_t, attended, cols, *blocks)
+    )(base, dq, own, came, cosine, sine, x_t, low_t, attended, cols, *blocks)
 
 
 def factors_of(n):
@@ -695,40 +643,59 @@
 
         return self.send(v, move)
 
-    def gather(self, shard):
-        block = shard
+    def ring_gather(self, block):
         for axis in reversed(range(len(self.digits))):
             block = jnp.concatenate(
                 [block] + [self.shift(block, axis, -d) for d in range(1, self.digits[axis])], axis=0
             )
-        cut = block.shape[0] // 2
-        by_x, by_y = self.along(block), self.across(block)
-        mine = [block, by_x, by_y, self.across(by_x[:cut]), self.along(by_y[cut:])]
-        return mine + [self.beside(v) for v in mine]
-
-    def scatter(self, send, keep):
-        came = self.beside(send)
-        shape = (2, 2, 2, keep.shape[1] // 4, keep.shape[2])
-        keep, came = keep.reshape(shape), came.reshape(shape)
-
-        def total(*at):
-            return keep[at].astype(f32) + came[at].astype(f32)
-
-        every = slice(None)
-        by_x = self.along(total(every, 1, 1).astype(bf16))
-        by_y = self.across(total(1, every, 0).astype(bf16))
-        late_x = self.along((total(0, 1, 0) + by_y[1].astype(f32)).astype(bf16))
-        late_y = self.across((total(1, 0, 1) + by_x[1].astype(f32)).astype(bf16))
-        low = total(0, 0, 0) + by_y[0].astype(f32) + late_x.astype(f32)
-        high = total(0, 0, 1) + by_x[0].astype(f32) + late_y.astype(f32)
-        block = jnp.concatenate([low, high], axis=0)
+        return block
+
+    def ring_scatter(self, block):
         for axis in range(len(self.digits)):
             size = self.digits[axis]
             pieces = jnp.split(block, size, axis=0)
+            low = [p.astype(bf16) for p in pieces[1:]]
             block = pieces[0]
             for d in range(1, size):
-                block = block + self.shift(pieces[d].astype(bf16), axis, d).astype(f32)
+                block = block + self.shift(low[d - 1], axis, d).astype(f32)
         return block
+
+
+def tie(value, *others):
+    return lax.optimization_barrier((value, *others))[0]
+
+
+class Scatter:
+    def __init__(self, links, send):
+        self.links = links
+        self.came = links.beside(send)
+
+    def total(self, *at):
+        return self.keep[at].astype(f32) + self.came[at].astype(f32)
+
+    def first(self, keep):
+        shape = (2, 2, 2, keep.shape[1] // 4, keep.shape[2])
+        self.keep, self.came = keep.reshape(shape), self.came.reshape(shape)
+        every = slice(None)
+        to_x = self.total(every, 1, 1).astype(bf16)
+        to_y = self.total(1, every, 0).astype(bf16)
+        self.by_x, self.by_y = self.links.along(to_x), self.links.across(to_y)
+        return to_x, to_y
+
+    def second(self):
+        to_x = (self.total(0, 1, 0) + self.by_y[1].astype(f32)).astype(bf16)
+        to_y = (self.total(1, 0, 1) + self.by_x[1].astype(f32)).astype(bf16)
+        self.late_x, self.late_y = self.links.along(to_x), self.links.across(to_y)
+        return to_x, to_y
+
+    def third(self):
+        low = self.total(0, 0, 0) + self.by_y[0].astype(f32) + self.late_x.astype(f32)
+        high = self.total(0, 0, 1) + self.by_x[0].astype(f32) + self.late_y.astype(f32)
+        self.block = jnp.concatenate([low, high], axis=0)
+        return self.block
+
+    def last(self):
+        return self.links.ring_scatter(self.block)
 
 
 def relative_order(links, depth):
@@ -753,7 +720,6 @@
     links, tokens, segments, positions, w_qkv, w_out, w_gate_up, w_down, norm_gain, norm_bias, cotangent
 ):
     ring, x_place, side, core = links.locate()
-    core = core.astype(jnp.int32)[None]
     depth = w_qkv.shape[0]
     width = tokens.shape[2]
     head_cols = w_qkv.shape[2]
@@ -799,8 +765,15 @@
     tokens_came = links.across(tokens_other)
     small_own, small_other = own_and_other(jnp.stack([segments, positions], axis=1))
     small_came = links.across(small_other)
-    attn_w = links.gather(attn_shard)
-    mlp_w = [links.gather(s) for s in mlp_shards]
+    dy_own, dy_other = own_and_other(cotangent)
+
+    ring_a = links.ring_gather(attn_shard)
+    cut = ring_a.shape[0] // 2
+    x_a, y_a = links.along(ring_a), links.across(ring_a)
+    ring_b = links.ring_gather(tie(mlp_shards[0], ring_a))
+    ends_a = links.across(x_a[:cut]), links.along(y_a[cut:])
+    attn_w = [ring_a, x_a, y_a, *ends_a]
+    attn_w += [links.beside(v) for v in attn_w]
 
     x_abs = jnp.concatenate([tokens_own, tokens_came], axis=0)
     x = dot(x_abs, swap).astype(bf16)
@@ -810,35 +783,73 @@
     seg_all = jnp.concatenate([seg, links.beside(seg)], axis=0)[:, None]
     seg = seg[None, :]
     cosine, sine = rope_tables(small[1], part)
-    dy_own, dy_other = own_and_other(cotangent)
-    dy_came = links.across(dy_other.astype(bf16))
+
+    ring_b = tie(ring_b, x_a, y_a)
+    x_b, y_b = links.along(ring_b), links.across(ring_b)
+    q, kv, wo = qkv(tie(x, ring_b), cosine, sine, attn_w)
+    ring_c = links.ring_gather(tie(mlp_shards[1], ring_b))
+    kv_came = links.beside(kv)
+    att_own, logs_own = attend(0, q, kv, kv_came, seg, seg_all)
+    ring_c = tie(ring_c, x_b, y_b)
+    x_c, y_c = links.along(ring_c), links.across(ring_c)
+    ends_b = links.across(x_b[:cut]), links.along(y_b[cut:])
+    mlp_b = [ring_b, x_b, y_b, *ends_b]
+    mlp_b += [links.beside(v) for v in mlp_b]
+    att_other, logs_other = attend(1, tie(q, ring_c, x_b, y_b), kv, kv_came, seg, seg_all)
+    n1, s1, low1, low1_t, gains = first_norm(x, att_own, att_other, wo, ring_b, x_b)
+    act_b, feed = mlp(tie(low1, x_c, y_c), None, mlp_b, half)
+    ends_c = links.across(x_c[:cut]), links.along(y_c[cut:])
+    mlp_c = [ring_c, x_c, y_c, *ends_c]
+    mlp_c += [links.beside(v) for v in mlp_c]
+    act_c, feed = mlp(low1, feed, mlp_c, half)
+    dy_came = links.across(tie(dy_other.astype(bf16), y_c))
     high, low = split(dy_own)
     dy = jnp.concatenate([dot(high, swap) + dot(low, swap), dot(dy_came, swap)], axis=0)
-
-    q, kv, wo = qkv(core, x, cosine, sine, attn_w)
-    kv_came = links.beside(kv)
-    attended, logs = attend(q, kv, kv_came, seg, seg_all)
-    n1, s1, low1, low1_t, gains = first_norm(x, attended, wo, mlp_w[0][0], mlp_w[0][1])
-    act_a, feed = mlp(core, low1, None, mlp_w[0], half)
-    act_b, feed = mlp(core, low1, feed, mlp_w[1], half)
     layer_out, dh2, dfeed, dfeed_t, sums = second_norm(n1, gains, feed, dy)
+
+    back = functools.partial(mlp_back, dfeed=dfeed, dfeed_t=dfeed_t, low_t=low1_t)
+    dfirst, send = back(1, dh2, act=act_c, blocks=mlp_c)
+    sum_c = Scatter(links, send)
+    dfirst, keep = back(0, dfirst, act=act_c, blocks=mlp_c)
+    ops_c = sum_c.first(keep)
+    dfirst, send = back(1, tie(dfirst, *ops_c), act=act_b, blocks=mlp_b)
+    sum_b = Scatter(links, send)
+    dfirst, keep = back(0, dfirst, act=act_b, blocks=mlp_b)
+    ops_b = sum_b.first(keep)
+    ops_c = sum_c.second()
     layer_out = dot(layer_out, swap, NT).astype(bf16)
     layer_out = from_sequence(layer_out[:mine], links.across(layer_out[mine:]))
-
-    dfirst, send, keep = mlp_back(core, dh2, dfeed, dfeed_t, low1_t, act_a, mlp_w[0])
-    own_mlp = [links.scatter(send, keep)]
-    dfirst, send, keep = mlp_back(core, dfirst, dfeed, dfeed_t, low1_t, act_b, mlp_w[1])
-    own_mlp.append(links.scatter(send, keep))
-    dh1, low_t, do, delta, cols = first_back(dfirst, n1, s1, gains, sums, wo, attended)
-    dq, dkv_own, dkv_other = attend_back(q, kv, kv_came, do, logs, delta, seg, seg_all, cosine, sine)
-    dkv_came = links.beside(dkv_other)
-    grad, send, keep = qkv_back(
-        core, dh1, dq, dkv_own, dkv_came, cosine, sine, x_t, low_t, attended, cols, attn_w
-    )
-    own_attn = links.scatter(send, keep)
-    high, low = split(grad)
+    dh1, low_t, do, delta, cols = first_back(
+        tie(dfirst, *ops_b, *ops_c), n1, s1, gains, sums, wo, att_own, att_other
+    )
+    attend_back_ = functools.partial(
+        attend_back, q=q, kv_own=kv, kv_other=kv_came, delta=delta, seg_q=seg, seg_k=seg_all, cosine=cosine, sine=sine
+    )
+    dq_own, dkv_a, dkv_send = attend_back_(0, do=do, logs=logs_own)
+    dkv_came_other = links.beside(dkv_send)
+    block_c = sum_c.third()
+    dq_other, dkv_b, dkv_send = attend_back_(1, do=tie(do, dq_own, block_c), logs=logs_other)
+    dkv_came_own = links.beside(dkv_send)
+    own_c = sum_c.last()
+    ops_b = sum_b.second()
+    grad, send = qkv_back(
+        1, tie(dh1, *ops_b), dq_other, dkv_b, dkv_came_other, cosine, sine, x_t, low_t, att_other, cols, attn_w
+    )
+    sum_a = Scatter(links, send)
+    block_b = sum_b.third()
+    grad, keep = qkv_back(
+        0, tie(grad, block_b), dq_own, dkv_a, dkv_came_own, cosine, sine, x_t, low_t, att_own, cols, attn_w
+    )
+    own_b = sum_b.last()
+    ops_a = sum_a.first(keep)
+    high, low = split(tie(grad, *ops_a))
     grad = dot(high, swap, NT) + dot(low, swap, NT)
-    input_grad = from_sequence(grad[:mine], links.across(grad[mine:].astype(bf16)).astype(f32))
+    ops_a = sum_a.second()
+    other = tie(grad[mine:].astype(bf16), *ops_a)
+    input_grad = from_sequence(grad[:mine], links.across(other).astype(f32))
+    sum_a.third()
+    own_attn = sum_a.last()
+    own_mlp = [own_b, own_c]
 
     grad_down = jnp.concatenate([v[:, :half] for v in own_mlp], axis=1).T
     grad_gate_up = jnp.stack(

time: 450 us -> 431 us (0.958)
  waiting for transfers between devices: 150 us -> 123 us
  starting transfers between devices: 94.8 us -> 74.8 us
  other arithmetic: 17.2 us -> 34.7 us
  Pallas kernels: 144 us -> 158 us
    ppermute x68 -> x69, waiting for transfers between devices: 150 us -> 123 us  [send(): return lax.ppermute(v, ('row', 'col'), pairs)]
    ppermute x68 -> x69, starting transfers between devices: 94.8 us -> 74.8 us  [send(): return lax.ppermute(v, ('row', 'col'), pairs)]
    pallas_call x8 -> x13, Pallas kernels: 127 us -> 141 us  [the longest x4 44.9 us: mlp_back(): pl.pallas_call(mlp_back_kernel, grid=(2,), in_specs=[full, full, whole((w...]
    convert_element_type x9, other arithmetic: 5.23 us -> 17.4 us  [the longest x3 6.92 us: second(): to_y = (self.total(1, 0, 1) + self.by_x[1].astype(f32)).astype(bf16)]
  transfers between devices with their start and end apart: 68 -> 69, of which waited for: 22 -> 24; matrix products, arithmetic and copies ran while one was open for 10% -> 12% of each run, Pallas kernels for 14% -> 28%
where the time goes in v4:
time: 431 us; the launch traced here: 427 us
  Pallas kernels  158 us (37%)
  waiting for transfers between devices  123 us (29%)
  starting transfers between devices  74.8 us (17%)
  other arithmetic  34.7 us (8%)
  local copies, waits for them, and re-layouts  23.2 us (5%)
  matrix products  11.3 us (3%)
    ppermute x69, waiting for transfers between devices, send(): return lax.ppermute(v, ('row', 'col'), pairs)  123 us
    ppermute x69, starting transfers between devices, send(): return lax.ppermute(v, ('row', 'col'), pairs)  74.8 us
    pallas_call x4, Pallas kernels, mlp_back(): pl.pallas_call(mlp_back_kernel, grid=(2,), in_specs=[full, full, whole((w...  44.9 us
    pallas_call x2, Pallas kernels, attend_back(): pl.pallas_call(attend_back_kernel, grid=(2,), in_specs=[pl.BlockSpec((row...  23.7 us
    pallas_call x2, Pallas kernels, attend(): pl.pallas_call(attend_kernel, grid=(2,), in_specs=[pl.BlockSpec((rows, pa...  22.7 us
    pallas_call x2, Pallas kernels, mlp(): pl.pallas_call(functools.partial(mlp_kernel, has_base), grid=(4,), in_spe...  22.6 us
    pallas_call x2, Pallas kernels, qkv_back(): pl.pallas_call(qkv_back_kernel, grid=(2,), in_specs=[full, pl.BlockSpec((...  18.8 us
  transfers between devices with their start and end apart: 69, of which 24 were waited for; matrix products, arithmetic and copies ran while one was open for 12% of the time, Pallas kernels for 28%

profile of v4, /device:TPU:0, one launch (start us, length us, event | category | flops | bytes accessed | tf_op | source)
XLA Modules:
  0.0 426.6 jit_solution(3092575457239705184)
XLA Ops:
  2.6 3.1 collective-permute-start.3
  5.7 2.6 collective-permute-start.2
  12.5 5.5 %collective-permute-done.2 = bf16[96,768]{1,0:T(8,128)(2,1)S(1)} collective-permute-done((bf16[96,768]{1,0:T(8,128)(2,1)S(1)}, bf16[96,768]{1,0:T(8,128)(2,1)S(1)}, u32[]{:S(2)}, u32[]{:S(2)}) %collective-permute-start.2) | collective-permute-done | bytes 147488 | tf_op jit(solution)/shard_map/ppermute | solution.py:627
  21.3 3.7 collective-permute-start.6
  28.3 4.7 %collective-permute-done.6 = bf16[96,1280]{1,0:T(8,128)(2,1)S(1)} collective-permute-done((bf16[96,1280]{1,0:T(8,128)(2,1)S(1)}, bf16[96,1280]{1,0:T(8,128)(2,1)S(1)}, u32[]{:S(2)}, u32[]{:S(2)}) %collective-permute-start.6) | collective-permute-done | bytes 245792 | tf_op jit(solution)/shard_map/ppermute | solution.py:627
  34.4 6.8 %collective-permute-done.5 = bf16[96,1280]{1,0:T(8,128)(2,1)S(1)} collective-permute-done((bf16[96,1280]{1,0:T(8,128)(2,1)S(1)}, bf16[96,1280]{1,0:T(8,128)(2,1)S(1)}, u32[]{:S(2)}, u32[]{:S(2)}) %collective-permute-start.5) | collective-permute-done | bytes 245792 | tf_op jit(solution)/shard_map/ppermute | solution.py:627
  44.8 4.7 %collective-permute-start.21 = (bf16[96,1152]{1,0:T(8,128)(2,1)S(1)}, bf16[96,1152]{1,0:T(8,128)(2,1)}, u32[]{:S(2)}, u32[]{:S(2)}) collective-permute-start(bf16[96,1152]{1,0:T(8,128)(2,1)S(1)} %pad_maximum_fusion.11), channel_id=1, source_target_pairs={{0,8},{1,9},{2,10},{3,11},{4,12},{5,13},{6,14},{7,15},{8,16},{9,17... | collective-permute-start | bytes 663560 | tf_op jit(solution)/shard_map/ppermute | solution.py:627
  52.7 4.5 %collective-permute-done.21 = bf16[96,1152]{1,0:T(8,128)(2,1)} collective-permute-done((bf16[96,1152]{1,0:T(8,128)(2,1)S(1)}, bf16[96,1152]{1,0:T(8,128)(2,1)}, u32[]{:S(2)}, u32[]{:S(2)}) %collective-permute-start.21) | collective-permute-done | bytes 221216 | tf_op jit(solution)/shard_map/ppermute | solution.py:627
  63.5 2.7 fusion.9.x_ref
  66.3 3.4 collective-permute-start.20
  70.3 7.9 %qkv.1 = (bf16[512,1024]{1,0:T(8,128)(2,1)}, bf16[512,2048]{1,0:T(8,128)(2,1)}, bf16[768,1024]{1,0:T(8,128)(2,1)}) custom-call(bf16[512,768]{1,0:T(8,128)(2,1)} %fusion.9.x_ref, f32[512,256]{1,0:T(8,128)} %copy.86.cos_ref, f32[512,256]{1,0:T(8,128)} %copy.87.sin_ref, bf16[384,768]{1,0:T(8,128)(2,1)} %copy-done.8, ...), custom_call_target="tpu_custom_call" | custom-call | flops 2415919104 | bytes 7864320 | tf_op jit(solution)/shard_map/qkv/pallas_call | solution.py:132
  88.5 17.4 %collective-permute-done.25.rest_3_.rest_2_ = bf16[384,1152]{1,0:T(8,128)(2,1)} collective-permute-done((bf16[384,1152]{1,0:T(8,128)(2,1)S(1)}, bf16[384,1152]{1,0:T(8,128)(2,1)}, u32[]{:S(2)}, u32[]{:S(2)}) %collective-permute-start.25) | collective-permute-done | bytes 884768 | tf_op jit(solution)/shard_map/ppermute | solution.py:627
  106.0 9.0 %collective-permute-done.27.rest_4_ = bf16[192,1280]{1,0:T(8,128)(2,1)} collective-permute-done((bf16[192,1280]{1,0:T(8,128)(2,1)S(1)}, bf16[192,1280]{1,0:T(8,128)(2,1)}, u32[]{:S(2)}, u32[]{:S(2)}) %collective-permute-start.27) | collective-permute-done | bytes 491552 | tf_op jit(solution)/shard_map/ppermute | solution.py:627
  118.3 8.2 %collective-permute-done.40 = bf16[256,768]{1,0:T(8,128)(2,1)S(1)} collective-permute-done((bf16[256,768]{1,0:T(8,128)(2,1)S(1)}, bf16[256,768]{1,0:T(8,128)(2,1)S(1)}, u32[]{:S(2)}, u32[]{:S(2)}) %collective-permute-start.40) | collective-permute-done | bytes 393248 | tf_op jit(solution)/shard_map/ppermute | solution.py:627
  136.3 11.1 %attend.2 = (bf16[512,512]{1,0:T(8,128)(2,1)}, f32[2,8,512]{2,1,0:T(8,128)}) custom-call(bf16[512,1024]{1,0:T(8,128)(2,1)} %get-tuple-element.74.q_ref, bf16[512,2048]{1,0:T(8,128)(2,1)} %get-tuple-element.70.own_ref, bf16[512,2048]{1,0:T(8,128)(2,1)} %collective-permute-done.17.other_ref, s32[1,512]{1,0:T(1,128)} %copy-done.23, s32[1024,1]{1,0:T(8,128)} %copy.88.segk_ref), custom_call_target="tpu_custom_call" | custom-call | flops 4294967296 | bytes 6291456 | tf_op jit(solution)/shard_map/attend/pallas_call | solution.py:186
  148.0 11.6 %attend.3 = (bf16[512,512]{1,0:T(8,128)(2,1)}, f32[2,8,512]{2,1,0:T(8,128)}) custom-call(bf16[512,1024]{1,0:T(8,128)(2,1)} %get-tuple-element.74.q_ref, bf16[512,2048]{1,0:T(8,128)(2,1)} %get-tuple-element.70.own_ref, bf16[512,2048]{1,0:T(8,128)(2,1)} %collective-permute-done.17.other_ref, s32[1,512]{1,0:T(1,128)} %copy-done.23, s32[1024,1]{1,0:T(8,128)} %copy.88.segk_ref), custom_call_target="tpu_custom_call" | custom-call | flops 4294967296 | bytes 6291456 | tf_op jit(solution)/shard_map/attend/pallas_call | solution.py:186
  159.5 5.2 %first_norm.1 = (f32[512,768]{1,0:T(8,128)}, f32[512,128]{1,0:T(8,128)}, bf16[512,768]{1,0:T(8,128)(2,1)}, bf16[768,512]{1,0:T(8,128)(2,1)}, f32[8,768]{1,0:T(8,128)}) custom-call(bf16[512,768]{1,0:T(8,128)(2,1)} %fusion.9.x_ref, bf16[512,512]{1,0:T(8,128)(2,1)} %get-tuple-element.71.att_own_ref.att_ref, ...), custom_call_target="tpu_custom_call" | custom-call | flops 805306368 | bytes 6291456 | tf_op jit(solution)/shard_map/first_norm/pallas_call | solution.py:304
  164.7 11.1 %mlp.2 = (bf16[4,3,512,384]{3,2,1,0:T(8,128)(2,1)}, f32[512,768]{1,0:T(8,128)}) custom-call(bf16[512,768]{1,0:T(8,128)(2,1)} %get-tuple-element.80.low_ref, bf16[384,1280]{1,0:T(8,128)(2,1)} %copy-done, bf16[384,1280]{1,0:T(8,128)(2,1)} %copy-done.9, bf16[384,1280]{1,0:T(8,128)(2,1)} %collective-permute-done.23.rest_2_, ...), custom_call_target="tpu_custom_call" | custom-call | flops 3623878656 | bytes 17694720 | tf_op jit(solution)/shard_map/mlp/pallas_call | solution.py:358
  177.2 11.5 %mlp.3 = (bf16[4,3,512,384]{3,2,1,0:T(8,128)(2,1)}, f32[512,768]{1,0:T(8,128)}) custom-call(bf16[512,768]{1,0:T(8,128)(2,1)} %get-tuple-element.80.low_ref, f32[512,768]{1,0:T(8,128)} %get-tuple-element.81.rest_0_, bf16[384,1152]{1,0:T(8,128)(2,1)} %copy-done.13, bf16[384,1152]{1,0:T(8,128)(2,1)} %collective-permute-done.24.rest_2_.rest_1_, ...), custom_call_target="tpu_custom_call" | custom-call | flops 3623878656 | bytes 17694720 | tf_op jit(solution)/shard_map/mlp/pallas_call | solution.py:358
  188.7 5.8 %second_norm.1 = (bf16[512,768]{1,0:T(8,128)(2,1)}, f32[512,768]{1,0:T(8,128)}, bf16[512,768]{1,0:T(8,128)(2,1)}, bf16[768,512]{1,0:T(8,128)(2,1)}, f32[8,768]{1,0:T(8,128)}) custom-call(f32[512,768]{1,0:T(8,128)} %get-tuple-element.77.n_ref, f32[8,768]{1,0:T(8,128)} %get-tuple-element.78.gains_ref, f32[512,768]{1,0:T(8,128)} %get-tuple-element.82.feed_ref, ...), custom_call_target="tpu_custom_call" | custom-call | flops 15728640 | bytes 8650752 | tf_op jit(solution)/shard_map/second_norm/pallas_call | solution.py:393
  194.5 11.1 %mlp_back.4 = (f32[512,768]{1,0:T(8,128)}, bf16[2,768,1152]{2,1,0:T(8,128)(2,1)}) custom-call(f32[512,768]{1,0:T(8,128)} %get-tuple-element.85.base_ref, bf16[512,768]{1,0:T(8,128)(2,1)} %get-tuple-element.86.dfeed_ref, bf16[768,512]{1,0:T(8,128)(2,1)} %get-tuple-element.87.dfeed_t_ref, bf16[768,512]{1,0:T(8,128)(2,1)} %get-tuple-element.88.low_t_ref, ...), custom_call_target="tpu_custom_call" | custom-call | flops 3623878656 | bytes 14745600 | tf_op jit(solution)/shard_map/mlp_back/pallas_call | solution.py:445
  206.1 11.3 %mlp_back.5 = (f32[512,768]{1,0:T(8,128)}, bf16[2,768,1152]{2,1,0:T(8,128)(2,1)}) custom-call(f32[512,768]{1,0:T(8,128)} %get-tuple-element.90.base_ref, bf16[512,768]{1,0:T(8,128)(2,1)} %get-tuple-element.86.dfeed_ref, bf16[768,512]{1,0:T(8,128)(2,1)} %get-tuple-element.87.dfeed_t_ref, bf16[768,512]{1,0:T(8,128)(2,1)} %get-tuple-element.88.low_t_ref, ...), custom_call_target="tpu_custom_call" | custom-call | flops 3623878656 | bytes 14745600 | tf_op jit(solution)/shard_map/mlp_back/pallas_call | solution.py:445
  217.4 3.0 fusion.22
  220.4 2.4 fusion.21
  222.8 11.3 %mlp_back.6 = (f32[512,768]{1,0:T(8,128)}, bf16[2,768,1152]{2,1,0:T(8,128)(2,1)}) custom-call(f32[512,768]{1,0:T(8,128)} %get-tuple-element.94.base_ref, bf16[512,768]{1,0:T(8,128)(2,1)} %get-tuple-element.86.dfeed_ref, bf16[768,512]{1,0:T(8,128)(2,1)} %get-tuple-element.87.dfeed_t_ref, bf16[768,512]{1,0:T(8,128)(2,1)} %get-tuple-element.88.low_t_ref, ...), custom_call_target="tpu_custom_call" | custom-call | flops 3623878656 | bytes 14745600 | tf_op jit(solution)/shard_map/mlp_back/pallas_call | solution.py:445
  236.2 2.9 convolution_convert_fusion.x_t_ref
  241.7 14.9 %collective-permute-done.45 = bf16[2,192,1152]{2,1,0:T(8,128)(2,1)} collective-permute-done((bf16[2,192,1152]{2,1,0:T(8,128)(2,1)}, bf16[2,192,1152]{2,1,0:T(8,128)(2,1)}, u32[]{:S(2)}, u32[]{:S(2)}) %collective-permute-start.45) | collective-permute-done | bytes 884768 | tf_op jit(solution)/shard_map/ppermute | solution.py:627
  258.6 2.9 fusion.33
  263.1 3.8 collective-permute-done.41
  267.9 11.3 %mlp_back.7 = (f32[512,768]{1,0:T(8,128)}, bf16[2,768,1152]{2,1,0:T(8,128)(2,1)}) custom-call(f32[512,768]{1,0:T(8,128)} %get-tuple-element.96.base_ref, bf16[512,768]{1,0:T(8,128)(2,1)} %get-tuple-element.86.dfeed_ref, bf16[768,512]{1,0:T(8,128)(2,1)} %get-tuple-element.87.dfeed_t_ref, bf16[768,512]{1,0:T(8,128)(2,1)} %get-tuple-element.88.low_t_ref, ...), custom_call_target="tpu_custom_call" | custom-call | flops 3623878656 | bytes 14745600 | tf_op jit(solution)/shard_map/mlp_back/pallas_call | solution.py:445
  279.2 2.5 fusion.26
  282.5 3.8 collective-permute-start.65
  287.1 3.0 collective-permute-start.67
  294.2 6.1 %first_back.1 = (f32[512,768]{1,0:T(8,128)}, bf16[768,512]{1,0:T(8,128)(2,1)}, bf16[512,1024]{1,0:T(8,128)(2,1)}, f32[4,8,512]{2,1,0:T(8,128)}, bf16[768,128]{1,0:T(8,128)(2,1)}) custom-call(f32[512,768]{1,0:T(8,128)} %get-tuple-element.100.dfirst_ref, f32[512,768]{1,0:T(8,128)} %get-tuple-element.77.n_ref, f32[512,128]{1,0:T(8,128)} %get-tuple-element.101.s_ref, ...), custom_call_target="tpu_custom_call" | custom-call | flops 805306368 | bytes 7864320 | tf_op jit(solution)/shard_map/first_back/pallas_call | solution.py:504
  300.4 11.9 %attend_back.2 = (bf16[512,512]{1,0:T(8,128)(2,1)}, f32[512,1024]{1,0:T(8,128)}, bf16[512,1024]{1,0:T(8,128)(2,1)}) custom-call(bf16[512,1024]{1,0:T(8,128)(2,1)} %get-tuple-element.74.q_ref, bf16[512,2048]{1,0:T(8,128)(2,1)} %get-tuple-element.70.own_ref, bf16[512,2048]{1,0:T(8,128)(2,1)} %collective-permute-done.17.other_ref, ...), custom_call_target="tpu_custom_call" | custom-call | flops 10737418240 | bytes 15728640 | tf_op jit(solution)/shard_map/attend_back/pallas_call | solution.py:257
  312.4 11.7 %attend_back.3 = (bf16[512,512]{1,0:T(8,128)(2,1)}, f32[512,1024]{1,0:T(8,128)}, bf16[512,1024]{1,0:T(8,128)(2,1)}) custom-call(bf16[512,1024]{1,0:T(8,128)(2,1)} %get-tuple-element.74.q_ref, bf16[512,2048]{1,0:T(8,128)(2,1)} %get-tuple-element.70.own_ref, bf16[512,2048]{1,0:T(8,128)(2,1)} %collective-permute-done.17.other_ref, ...), custom_call_target="tpu_custom_call" | custom-call | flops 10737418240 | bytes 15728640 | tf_op jit(solution)/shard_map/attend_back/pallas_call | solution.py:257
  324.2 2.7 fusion.31
  326.9 9.4 %qkv_back.2 = (f32[512,768]{1,0:T(8,128)}, bf16[2,768,896]{2,1,0:T(8,128)(2,1)}) custom-call(f32[512,768]{1,0:T(8,128)} %get-tuple-element.104.base_ref, bf16[512,512]{1,0:T(8,128)(2,1)} %get-tuple-element.111.dq_ref, f32[512,1024]{1,0:T(8,128)} %get-tuple-element.112.own_ref, bf16[512,1024]{1,0:T(8,128)(2,1)} %collective-permute-done.48.came_ref, ...), custom_call_target="tpu_custom_call" | custom-call | flops 2617245696 | bytes 7864320 | tf_op jit(solution)/shard_map/qkv_back/pallas_call | solution.py:559
  343.3 8.1 %collective-permute-done.61 = bf16[192,1152]{1,0:T(8,128)(2,1)S(1)} collective-permute-done((bf16[192,1152]{1,0:T(8,128)(2,1)}, bf16[192,1152]{1,0:T(8,128)(2,1)S(1)}, u32[]{:S(2)}, u32[]{:S(2)}) %collective-permute-start.61) | collective-permute-done | bytes 442400 | tf_op jit(solution)/shard_map/ppermute | solution.py:627
  354.5 2.3 collective-permute-start.60
  356.9 2.4 collective-permute-start.63
  360.2 9.4 %qkv_back.3 = (f32[512,768]{1,0:T(8,128)}, bf16[2,768,896]{2,1,0:T(8,128)(2,1)}) custom-call(f32[512,768]{1,0:T(8,128)} %get-tuple-element.116.base_ref, bf16[512,512]{1,0:T(8,128)(2,1)} %get-tuple-element.108.dq_ref, f32[512,1024]{1,0:T(8,128)} %get-tuple-element.117.own_ref, bf16[512,1024]{1,0:T(8,128)(2,1)} %copy-done.12, f32[512,256]{1,0:T(8,128)} %copy.86.cos_ref, ...), custom_call_target="tpu_custom_call" | custom-call | flops 2617245696 | bytes 7864320 | tf_op jit(solution)/shard_map/qkv_back/pallas_call | solution.py:559
  369.7 2.8 collective-permute-done.62
  379.9 12.9 %collective-permute-done.52 = bf16[2,192,896]{2,1,0:T(8,128)(2,1)S(1)} collective-permute-done((bf16[2,192,896]{2,1,0:T(8,128)(2,1)S(1)}, bf16[2,192,896]{2,1,0:T(8,128)(2,1)S(1)}, u32[]{:S(2)}, u32[]{:S(2)}) %collective-permute-start.52) | collective-permute-done | bytes 688160 | tf_op jit(solution)/shard_map/ppermute | solution.py:627
  399.8 6.7 %collective-permute-done.56 = bf16[192,896]{1,0:T(8,128)(2,1)S(1)} collective-permute-done((bf16[192,896]{1,0:T(8,128)(2,1)S(1)}, bf16[192,896]{1,0:T(8,128)(2,1)S(1)}, u32[]{:S(2)}, u32[]{:S(2)}) %collective-permute-start.56) | collective-permute-done | bytes 344096 | tf_op jit(solution)/shard_map/ppermute | solution.py:627
  407.9 5.4 %collective-permute-start.55 = (bf16[96,896]{1,0:T(8,128)(2,1)S(1)}, bf16[96,896]{1,0:T(8,128)(2,1)S(1)}, u32[]{:S(2)}, u32[]{:S(2)}) collective-permute-start(bf16[96,896]{1,0:T(8,128)(2,1)S(1)} %split.89), channel_id=1, source_target_pairs={{0,8},{1,9},{2,10},{3,11},{4,12},{5,13},{6,14},{7,15},{8,16},{9,17... | collective-permute-start | bytes 516104 | tf_op jit(solution)/shard_map/ppermute | solution.py:627
  413.4 2.4 collective-permute-start.58
  417.6 5.5 %collective-permute-done.57 = bf16[96,896]{1,0:T(8,128)(2,1)S(1)} collective-permute-done((bf16[96,896]{1,0:T(8,128)(2,1)S(1)}, bf16[96,896]{1,0:T(8,128)(2,1)S(1)}, u32[]{:S(2)}, u32[]{:S(2)}) %collective-permute-start.57) | collective-permute-done | bytes 172064 | tf_op jit(solution)/shard_map/ppermute | solution.py:627
  (264 shorter events, 100.4 us)
Async XLA Ops:
  18.0 16.3 %collective-permute-start.8 = (bf16[384,768]{1,0:T(8,128)(2,1)S(1)}, bf16[384,768]{1,0:T(8,128)(2,1)S(1)}, u32[]{:S(2)}, u32[]{:S(2)}) collective-permute-start(bf16[384,768]{1,0:T(8,128)(2,1)S(1)} %pad_maximum_fusion.6.rest_0_), channel_id=1, source_target_pairs={{0,2},{1,3},{2,0},{3,1},{4,6},{5,7},{6,4},{7,5},{8,10},{9,11},{10,... | collective-permute-start | bytes 1769480 | tf_op jit(solution)/shard_map/ppermute | solution.py:627
  19.7 22.5 %collective-permute-start.7 = (bf16[384,768]{1,0:T(8,128)(2,1)S(1)}, bf16[384,768]{1,0:T(8,128)(2,1)}, u32[]{:S(2)}, u32[]{:S(2)}) collective-permute-start(bf16[384,768]{1,0:T(8,128)(2,1)S(1)} %pad_maximum_fusion.6.rest_0_), channel_id=1, source_target_pairs={{0,4},{1,5},{2,6},{3,7},{4,0},{5,1},{6,2},{7,3},{8,12},{9,13},{10,... | collective-permute-start | bytes 1769480 | tf_op jit(solution)/shard_map/ppermute | solution.py:627
  25.0 16.2 %collective-permute-start.5 = (bf16[96,1280]{1,0:T(8,128)(2,1)S(1)}, bf16[96,1280]{1,0:T(8,128)(2,1)S(1)}, u32[]{:S(2)}, u32[]{:S(2)}) collective-permute-start(bf16[96,1280]{1,0:T(8,128)(2,1)S(1)} %fusion.56), channel_id=1, source_target_pairs={{0,16},{1,17},{2,18},{3,19},{4,20},{5,21},{6,22},{7,23},{8,24},{9,... | collective-permute-start | bytes 737288 | tf_op jit(solution)/shard_map/ppermute | solution.py:627
  26.7 15.0 %collective-permute-start.4 = (bf16[96,1280]{1,0:T(8,128)(2,1)S(1)}, bf16[96,1280]{1,0:T(8,128)(2,1)}, u32[]{:S(2)}, u32[]{:S(2)}) collective-permute-start(bf16[96,1280]{1,0:T(8,128)(2,1)S(1)} %fusion.56), channel_id=1, source_target_pairs={{0,24},{1,25},{2,26},{3,27},{4,28},{5,29},{6,30},{7,31},{8,0},{9,1... | collective-permute-start | bytes 737288 | tf_op jit(solution)/shard_map/ppermute | solution.py:627
  33.0 17.5 %collective-permute-start = (bf16[256,768]{1,0:T(8,128)(2,1)S(1)}, bf16[256,768]{1,0:T(8,128)(2,1)S(1)}, u32[]{:S(2)}, u32[]{:S(2)}) collective-permute-start(bf16[256,768]{1,0:T(8,128)(2,1)S(1)} %get-tuple-element.165), channel_id=1, source_target_pairs={{0,2},{1,3},{2,0},{3,1},{4,6},{5,7},{6,4},{7,5},{8,10},{9,11},{10,... | collective-permute-start | bytes 1179656 | tf_op jit(solution)/shard_map/ppermute | solution.py:627
  34.3 16.8 %collective-permute-start.12 = (bf16[384,768]{1,0:T(8,128)(2,1)S(1)}, bf16[384,768]{1,0:T(8,128)(2,1)S(1)}, u32[]{:S(2)}, u32[]{:S(2)}) collective-permute-start(bf16[384,768]{1,0:T(8,128)(2,1)S(1)} %pad_maximum_fusion.6.rest_0_), channel_id=1, source_target_pairs={{0,1},{1,0},{2,3},{3,2},{4,5},{5,4},{6,7},{7,6},{8,9},{9,8},{10,11... | collective-permute-start | bytes 1769480 | tf_op jit(solution)/shard_map/ppermute | solution.py:627
  41.7 17.0 %collective-permute-start.11 = (bf16[192,768]{1,0:T(8,128)(2,1)S(1)}, bf16[192,768]{1,0:T(8,128)(2,1)}, u32[]{:S(2)}, u32[]{:S(2)}) collective-permute-start(bf16[192,768]{1,0:T(8,128)(2,1)S(1)} %slice.361), channel_id=1, source_target_pairs={{0,4},{1,5},{2,6},{3,7},{4,0},{5,1},{6,2},{7,3},{8,12},{9,13},{10,... | collective-permute-start | bytes 884744 | tf_op jit(solution)/shard_map/ppermute | solution.py:627
  42.3 18.4 %collective-permute-start.14 = (bf16[384,768]{1,0:T(8,128)(2,1)S(1)}, bf16[384,768]{1,0:T(8,128)(2,1)S(1)}, u32[]{:S(2)}, u32[]{:S(2)}) collective-permute-start(bf16[384,768]{1,0:T(8,128)(2,1)S(1)} %collective-permute-done.8.rest_2_), channel_id=1, source_target_pairs={{0,1},{1,0},{2,3},{3,2},{4,5},{5,4},{6,7},{7,6},{8,9},{9,8},{10,11... | collective-permute-start | bytes 1769480 | tf_op jit(solution)/shard_map/ppermute | solution.py:627
  51.1 32.0 %collective-permute-start.23 = (bf16[384,1280]{1,0:T(8,128)(2,1)S(1)}, bf16[384,1280]{1,0:T(8,128)(2,1)}, u32[]{:S(2)}, u32[]{:S(2)}) collective-permute-start(bf16[384,1280]{1,0:T(8,128)(2,1)S(1)} %pad_maximum_fusion.2.norm_a_ref.rest_0_), channel_id=1, source_target_pairs={{0,2},{1,3},{2,0},{3,1},{4,6},{5,7},{6,4},{7,5},{8,10},{9,11},{10,... | collective-permute-start | bytes 2949128 | tf_op jit(solution)/shard_map/ppermute | solution.py:627
  57.2 26.0 %collective-permute-start.22 = (bf16[384,1280]{1,0:T(8,128)(2,1)S(1)}, bf16[384,1280]{1,0:T(8,128)(2,1)S(1)}, u32[]{:S(2)}, u32[]{:S(2)}) collective-permute-start(bf16[384,1280]{1,0:T(8,128)(2,1)S(1)} %pad_maximum_fusion.2.norm_a_ref.rest_0_), channel_id=1, source_target_pairs={{0,4},{1,5},{2,6},{3,7},{4,0},{5,1},{6,2},{7,3},{8,12},{9,13},{10,... | collective-permute-start | bytes 2949128 | tf_op jit(solution)/shard_map/ppermute | solution.py:627
  66.3 13.8 %collective-permute-start.20 = (bf16[96,1152]{1,0:T(8,128)(2,1)S(1)}, bf16[96,1152]{1,0:T(8,128)(2,1)S(1)}, u32[]{:S(2)}, u32[]{:S(2)}) collective-permute-start(bf16[96,1152]{1,0:T(8,128)(2,1)S(1)} %pad_maximum_fusion.11), channel_id=1, source_target_pairs={{0,16},{1,17},{2,18},{3,19},{4,20},{5,21},{6,22},{7,23},{8,24},{9,... | collective-permute-start | bytes 663560 | tf_op jit(solution)/shard_map/ppermute | solution.py:627
  69.7 12.5 %collective-permute-start.19 = (bf16[96,1152]{1,0:T(8,128)(2,1)S(1)}, bf16[96,1152]{1,0:T(8,128)(2,1)S(1)}, u32[]{:S(2)}, u32[]{:S(2)}) collective-permute-start(bf16[96,1152]{1,0:T(8,128)(2,1)S(1)} %pad_maximum_fusion.11), channel_id=1, source_target_pairs={{0,24},{1,25},{2,26},{3,27},{4,28},{5,29},{6,30},{7,31},{8,0},{9,1... | collective-permute-start | bytes 663560 | tf_op jit(solution)/shard_map/ppermute | solution.py:627
  70.0 16.9 %collective-permute-start.28 = (bf16[384,1280]{1,0:T(8,128)(2,1)S(1)}, bf16[384,1280]{1,0:T(8,128)(2,1)}, u32[]{:S(2)}, u32[]{:S(2)}) collective-permute-start(bf16[384,1280]{1,0:T(8,128)(2,1)S(1)} %pad_maximum_fusion.2.norm_a_ref.rest_0_), channel_id=1, source_target_pairs={{0,1},{1,0},{2,3},{3,2},{4,5},{5,4},{6,7},{7,6},{8,9},{9,8},{10,11... | collective-permute-start | bytes 2949128 | tf_op jit(solution)/shard_map/ppermute | solution.py:627
  80.0 56.1 %collective-permute-start.17 = (bf16[512,2048]{1,0:T(8,128)(2,1)}, bf16[512,2048]{1,0:T(8,128)(2,1)}, u32[]{:S(2)}, u32[]{:S(2)}) collective-permute-start(bf16[512,2048]{1,0:T(8,128)(2,1)} %get-tuple-element.70.own_ref), channel_id=1, source_target_pairs={{0,1},{1,0},{2,3},{3,2},{4,5},{5,4},{6,7},{7,6},{8,9},{9,8},{10,11... | collective-permute-start | bytes 6291464 | tf_op jit(solution)/shard_map/ppermute | solution.py:627
  83.2 22.8 %collective-permute-start.25 = (bf16[384,1152]{1,0:T(8,128)(2,1)S(1)}, bf16[384,1152]{1,0:T(8,128)(2,1)}, u32[]{:S(2)}, u32[]{:S(2)}) collective-permute-start(bf16[384,1152]{1,0:T(8,128)(2,1)S(1)} %pad_maximum_fusion.3.rest_1_.rest_0_), channel_id=1, source_target_pairs={{0,2},{1,3},{2,0},{3,1},{4,6},{5,7},{6,4},{7,5},{8,10},{9,11},{10,... | collective-permute-start | bytes 2654216 | tf_op jit(solution)/shard_map/ppermute | solution.py:627
  83.7 33.6 %collective-permute-start.24 = (bf16[384,1152]{1,0:T(8,128)(2,1)S(1)}, bf16[384,1152]{1,0:T(8,128)(2,1)}, u32[]{:S(2)}, u32[]{:S(2)}) collective-permute-start(bf16[384,1152]{1,0:T(8,128)(2,1)S(1)} %pad_maximum_fusion.3.rest_1_.rest_0_), channel_id=1, source_target_pairs={{0,4},{1,5},{2,6},{3,7},{4,0},{5,1},{6,2},{7,3},{8,12},{9,13},{10,... | collective-permute-start | bytes 2654216 | tf_op jit(solution)/shard_map/ppermute | solution.py:627
  86.0 29.0 %collective-permute-start.27 = (bf16[192,1280]{1,0:T(8,128)(2,1)S(1)}, bf16[192,1280]{1,0:T(8,128)(2,1)}, u32[]{:S(2)}, u32[]{:S(2)}) collective-permute-start(bf16[192,1280]{1,0:T(8,128)(2,1)S(1)} %slice.364), channel_id=1, source_target_pairs={{0,4},{1,5},{2,6},{3,7},{4,0},{5,1},{6,2},{7,3},{8,12},{9,13},{10,... | collective-permute-start | bytes 1474568 | tf_op jit(solution)/shard_map/ppermute | solution.py:627
  86.9 28.1 %collective-permute-start.26 = (bf16[192,1280]{1,0:T(8,128)(2,1)S(1)}, bf16[192,1280]{1,0:T(8,128)(2,1)}, u32[]{:S(2)}, u32[]{:S(2)}) collective-permute-start(bf16[192,1280]{1,0:T(8,128)(2,1)S(1)} %slice.363), channel_id=1, source_target_pairs={{0,2},{1,3},{2,0},{3,1},{4,6},{5,7},{6,4},{7,5},{8,10},{9,11},{10,... | collective-permute-start | bytes 1474568 | tf_op jit(solution)/shard_map/ppermute | solution.py:627
  105.9 27.5 %collective-permute-start.30 = (bf16[384,1280]{1,0:T(8,128)(2,1)}, bf16[384,1280]{1,0:T(8,128)(2,1)}, u32[]{:S(2)}, u32[]{:S(2)}) collective-permute-start(bf16[384,1280]{1,0:T(8,128)(2,1)} %collective-permute-done.23.rest_2_), channel_id=1, source_target_pairs={{0,1},{1,0},{2,3},{3,2},{4,5},{5,4},{6,7},{7,6},{8,9},{9,8},{10,11... | collective-permute-start | bytes 2949128 | tf_op jit(solution)/shard_map/ppermute | solution.py:627
  115.0 20.7 %collective-permute-start.29 = (bf16[384,1280]{1,0:T(8,128)(2,1)S(1)}, bf16[384,1280]{1,0:T(8,128)(2,1)}, u32[]{:S(2)}, u32[]{:S(2)}) collective-permute-start(bf16[384,1280]{1,0:T(8,128)(2,1)S(1)} %collective-permute-done.22.norm_b_ref.rest_1_), channel_id=1, source_target_pairs={{0,1},{1,0},{2,3},{3,2},{4,5},{5,4},{6,7},{7,6},{8,9},{9,8},{10,11... | collective-permute-start | bytes 2949128 | tf_op jit(solution)/shard_map/ppermute | solution.py:627
  117.3 14.8 %collective-permute-start.32 = (bf16[192,1280]{1,0:T(8,128)(2,1)}, bf16[192,1280]{1,0:T(8,128)(2,1)}, u32[]{:S(2)}, u32[]{:S(2)}) collective-permute-start(bf16[192,1280]{1,0:T(8,128)(2,1)} %collective-permute-done.27.rest_4_), channel_id=1, source_target_pairs={{0,1},{1,0},{2,3},{3,2},{4,5},{5,4},{6,7},{7,6},{8,9},{9,8},{10,11... | collective-permute-start | bytes 1474568 | tf_op jit(solution)/shard_map/ppermute | solution.py:627
  132.2 15.2 %collective-permute-start.34 = (bf16[192,1152]{1,0:T(8,128)(2,1)}, bf16[192,1152]{1,0:T(8,128)(2,1)}, u32[]{:S(2)}, u32[]{:S(2)}) collective-permute-start(bf16[192,1152]{1,0:T(8,128)(2,1)} %slice.366), channel_id=1, source_target_pairs={{0,4},{1,5},{2,6},{3,7},{4,0},{5,1},{6,2},{7,3},{8,12},{9,13},{10,... | collective-permute-start | bytes 1327112 | tf_op jit(solution)/shard_map/ppermute | solution.py:627
  133.4 14.5 %collective-permute-start.33 = (bf16[192,1152]{1,0:T(8,128)(2,1)S(1)}, bf16[192,1152]{1,0:T(8,128)(2,1)}, u32[]{:S(2)}, u32[]{:S(2)}) collective-permute-start(bf16[192,1152]{1,0:T(8,128)(2,1)S(1)} %slice.365), channel_id=1, source_target_pairs={{0,2},{1,3},{2,0},{3,1},{4,6},{5,7},{6,4},{7,5},{8,10},{9,11},{10,... | collective-permute-start | bytes 1327112 | tf_op jit(solution)/shard_map/ppermute | solution.py:627
  135.7 40.1 %collective-permute-start.35 = (bf16[384,1152]{1,0:T(8,128)(2,1)S(1)}, bf16[384,1152]{1,0:T(8,128)(2,1)S(1)}, u32[]{:S(2)}, u32[]{:S(2)}) collective-permute-start(bf16[384,1152]{1,0:T(8,128)(2,1)S(1)} %pad_maximum_fusion.3.rest_1_.rest_0_), channel_id=1, source_target_pairs={{0,1},{1,0},{2,3},{3,2},{4,5},{5,4},{6,7},{7,6},{8,9},{9,8},{10,11... | collective-permute-start | bytes 2654216 | tf_op jit(solution)/shard_map/ppermute | solution.py:627
  135.7 40.1 %collective-permute-start.37 = (bf16[384,1152]{1,0:T(8,128)(2,1)}, bf16[384,1152]{1,0:T(8,128)(2,1)S(1)}, u32[]{:S(2)}, u32[]{:S(2)}) collective-permute-start(bf16[384,1152]{1,0:T(8,128)(2,1)} %collective-permute-done.25.rest_3_.rest_2_), channel_id=1, source_target_pairs={{0,1},{1,0},{2,3},{3,2},{4,5},{5,4},{6,7},{7,6},{8,9},{9,8},{10,11... | collective-permute-start | bytes 2654216 | tf_op jit(solution)/shard_map/ppermute | solution.py:627
  136.2 39.7 %collective-permute-start.36 = (bf16[384,1152]{1,0:T(8,128)(2,1)}, bf16[384,1152]{1,0:T(8,128)(2,1)}, u32[]{:S(2)}, u32[]{:S(2)}) collective-permute-start(bf16[384,1152]{1,0:T(8,128)(2,1)} %collective-permute-done.24.rest_2_.rest_1_), channel_id=1, source_target_pairs={{0,1},{1,0},{2,3},{3,2},{4,5},{5,4},{6,7},{7,6},{8,9},{9,8},{10,11... | collective-permute-start | bytes 2654216 | tf_op jit(solution)/shard_map/ppermute | solution.py:627
  147.4 28.4 %collective-permute-start.39 = (bf16[192,1152]{1,0:T(8,128)(2,1)}, bf16[192,1152]{1,0:T(8,128)(2,1)}, u32[]{:S(2)}, u32[]{:S(2)}) collective-permute-start(bf16[192,1152]{1,0:T(8,128)(2,1)} %collective-permute-done.34.rest_5_.rest_4_), channel_id=1, source_target_pairs={{0,1},{1,0},{2,3},{3,2},{4,5},{5,4},{6,7},{7,6},{8,9},{9,8},{10,11... | collective-permute-start | bytes 1327112 | tf_op jit(solution)/shard_map/ppermute | solution.py:627
  147.9 27.9 %collective-permute-start.38 = (bf16[192,1152]{1,0:T(8,128)(2,1)}, bf16[192,1152]{1,0:T(8,128)(2,1)S(1)}, u32[]{:S(2)}, u32[]{:S(2)}) collective-permute-start(bf16[192,1152]{1,0:T(8,128)(2,1)} %collective-permute-done.33.rest_4_.rest_3_), channel_id=1, source_target_pairs={{0,1},{1,0},{2,3},{3,2},{4,5},{5,4},{6,7},{7,6},{8,9},{9,8},{10,11... | collective-permute-start | bytes 1327112 | tf_op jit(solution)/shard_map/ppermute | solution.py:627
  234.1 56.1 %collective-permute-start.43 = (bf16[2,768,1152]{2,1,0:T(8,128)(2,1)}, bf16[2,768,1152]{2,1,0:T(8,128)(2,1)S(1)}, u32[]{:S(2)}, u32[]{:S(2)}) collective-permute-start(bf16[2,768,1152]{2,1,0:T(8,128)(2,1)} %get-tuple-element.99), channel_id=1, source_target_pairs={{0,1},{1,0},{2,3},{3,2},{4,5},{5,4},{6,7},{7,6},{8,9},{9,8},{10,11... | collective-permute-start | bytes 10616840 | tf_op jit(solution)/shard_map/ppermute | solution.py:627
  234.2 22.3 %collective-permute-start.45 = (bf16[2,192,1152]{2,1,0:T(8,128)(2,1)}, bf16[2,192,1152]{2,1,0:T(8,128)(2,1)}, u32[]{:S(2)}, u32[]{:S(2)}) collective-permute-start(bf16[2,192,1152]{2,1,0:T(8,128)(2,1)} %fusion.21), channel_id=1, source_target_pairs={{0,4},{1,5},{2,6},{3,7},{4,0},{5,1},{6,2},{7,3},{8,12},{9,13},{10,... | collective-permute-start | bytes 2654216 | tf_op jit(solution)/shard_map/ppermute | solution.py:627
  235.8 22.8 %collective-permute-start.44 = (bf16[2,192,1152]{2,1,0:T(8,128)(2,1)}, bf16[2,192,1152]{2,1,0:T(8,128)(2,1)}, u32[]{:S(2)}, u32[]{:S(2)}) collective-permute-start(bf16[2,192,1152]{2,1,0:T(8,128)(2,1)} %fusion.22), channel_id=1, source_target_pairs={{0,2},{1,3},{2,0},{3,1},{4,6},{5,7},{6,4},{7,5},{8,10},{9,11},{10,... | collective-permute-start | bytes 2654216 | tf_op jit(solution)/shard_map/ppermute | solution.py:627
  240.0 26.9 %collective-permute-start.41 = (bf16[256,768]{1,0:T(8,128)(2,1)S(1)}, bf16[256,768]{1,0:T(8,128)(2,1)S(1)}, u32[]{:S(2)}, u32[]{:S(2)}) collective-permute-start(bf16[256,768]{1,0:T(8,128)(2,1)S(1)} %slice.368), channel_id=1, source_target_pairs={{0,2},{1,3},{2,0},{3,1},{4,6},{5,7},{6,4},{7,5},{8,10},{9,11},{10,... | collective-permute-start | bytes 1179656 | tf_op jit(solution)/shard_map/ppermute | solution.py:627
  261.5 17.6 %collective-permute-start.66 = (bf16[192,1152]{1,0:T(8,128)(2,1)}, bf16[192,1152]{1,0:T(8,128)(2,1)}, u32[]{:S(2)}, u32[]{:S(2)}) collective-permute-start(bf16[192,1152]{1,0:T(8,128)(2,1)} %get-tuple-element.154), channel_id=1, source_target_pairs={{0,2},{1,3},{2,0},{3,1},{4,6},{5,7},{6,4},{7,5},{8,10},{9,11},{10,... | collective-permute-start | bytes 1327112 | tf_op jit(solution)/shard_map/ppermute | solution.py:627
  261.9 17.2 %collective-permute-start.64 = (bf16[192,1152]{1,0:T(8,128)(2,1)}, bf16[192,1152]{1,0:T(8,128)(2,1)}, u32[]{:S(2)}, u32[]{:S(2)}) collective-permute-start(bf16[192,1152]{1,0:T(8,128)(2,1)} %get-tuple-element.155), channel_id=1, source_target_pairs={{0,4},{1,5},{2,6},{3,7},{4,0},{5,1},{6,2},{7,3},{8,12},{9,13},{10,... | collective-permute-start | bytes 1327112 | tf_op jit(solution)/shard_map/ppermute | solution.py:627
  282.5 57.1 %collective-permute-start.65 = (bf16[96,1152]{1,0:T(8,128)(2,1)}, bf16[96,1152]{1,0:T(8,128)(2,1)}, u32[]{:S(2)}, u32[]{:S(2)}) collective-permute-start(bf16[96,1152]{1,0:T(8,128)(2,1)} %split.87), channel_id=1, source_target_pairs={{0,8},{1,9},{2,10},{3,11},{4,12},{5,13},{6,14},{7,15},{8,16},{9,17... | collective-permute-start | bytes 663560 | tf_op jit(solution)/shard_map/ppermute | solution.py:627
  287.1 54.1 %collective-permute-start.67 = (bf16[96,1152]{1,0:T(8,128)(2,1)}, bf16[96,1152]{1,0:T(8,128)(2,1)}, u32[]{:S(2)}, u32[]{:S(2)}) collective-permute-start(bf16[96,1152]{1,0:T(8,128)(2,1)} %get-tuple-element.174), channel_id=1, source_target_pairs={{0,16},{1,17},{2,18},{3,19},{4,20},{5,21},{6,22},{7,23},{8,24},{9,... | collective-permute-start | bytes 663560 | tf_op jit(solution)/shard_map/ppermute | solution.py:627
  292.4 31.7 %collective-permute-start.47 = (bf16[2,192,1152]{2,1,0:T(8,128)(2,1)}, bf16[2,192,1152]{2,1,0:T(8,128)(2,1)}, u32[]{:S(2)}, u32[]{:S(2)}) collective-permute-start(bf16[2,192,1152]{2,1,0:T(8,128)(2,1)} %fusion.23), channel_id=1, source_target_pairs={{0,4},{1,5},{2,6},{3,7},{4,0},{5,1},{6,2},{7,3},{8,12},{9,13},{10,... | collective-permute-start | bytes 2654216 | tf_op jit(solution)/shard_map/ppermute | solution.py:627
  292.9 31.3 %collective-permute-start.46 = (bf16[2,192,1152]{2,1,0:T(8,128)(2,1)}, bf16[2,192,1152]{2,1,0:T(8,128)(2,1)}, u32[]{:S(2)}, u32[]{:S(2)}) collective-permute-start(bf16[2,192,1152]{2,1,0:T(8,128)(2,1)} %fusion.24), channel_id=1, source_target_pairs={{0,2},{1,3},{2,0},{3,1},{4,6},{5,7},{6,4},{7,5},{8,10},{9,11},{10,... | collective-permute-start | bytes 2654216 | tf_op jit(solution)/shard_map/ppermute | solution.py:627
  312.3 14.6 %collective-permute-start.48 = (bf16[512,1024]{1,0:T(8,128)(2,1)}, bf16[512,1024]{1,0:T(8,128)(2,1)}, u32[]{:S(2)}, u32[]{:S(2)}) collective-permute-start(bf16[512,1024]{1,0:T(8,128)(2,1)} %get-tuple-element.113), channel_id=1, source_target_pairs={{0,1},{1,0},{2,3},{3,2},{4,5},{5,4},{6,7},{7,6},{8,9},{9,8},{10,11... | collective-permute-start | bytes 3145736 | tf_op jit(solution)/shard_map/ppermute | solution.py:627
  324.1 17.1 %collective-permute-start.68 = (bf16[96,1152]{1,0:T(8,128)(2,1)}, bf16[96,1152]{1,0:T(8,128)(2,1)}, u32[]{:S(2)}, u32[]{:S(2)}) collective-permute-start(bf16[96,1152]{1,0:T(8,128)(2,1)} %get-tuple-element.175), channel_id=1, source_target_pairs={{0,24},{1,25},{2,26},{3,27},{4,28},{5,29},{6,30},{7,31},{8,0},{9,1... | collective-permute-start | bytes 663560 | tf_op jit(solution)/shard_map/ppermute | solution.py:627
  336.3 36.3 %collective-permute-start.50 = (bf16[2,768,896]{2,1,0:T(8,128)(2,1)}, bf16[2,768,896]{2,1,0:T(8,128)(2,1)}, u32[]{:S(2)}, u32[]{:S(2)}) collective-permute-start(bf16[2,768,896]{2,1,0:T(8,128)(2,1)} %get-tuple-element.121), channel_id=1, source_target_pairs={{0,1},{1,0},{2,3},{3,2},{4,5},{5,4},{6,7},{7,6},{8,9},{9,8},{10,11... | collective-permute-start | bytes 8257544 | tf_op jit(solution)/shard_map/ppermute | solution.py:627
  343.3 16.0 %collective-permute-start.49 = (bf16[512,1024]{1,0:T(8,128)(2,1)S(1)}, bf16[512,1024]{1,0:T(8,128)(2,1)S(1)}, u32[]{:S(2)}, u32[]{:S(2)}) collective-permute-start(bf16[512,1024]{1,0:T(8,128)(2,1)S(1)} %copy-done.28), channel_id=1, source_target_pairs={{0,1},{1,0},{2,3},{3,2},{4,5},{5,4},{6,7},{7,6},{8,9},{9,8},{10,11... | collective-permute-start | bytes 3145736 | tf_op jit(solution)/shard_map/ppermute | solution.py:627
  354.5 15.2 %collective-permute-start.60 = (bf16[96,1152]{1,0:T(8,128)(2,1)S(1)}, bf16[96,1152]{1,0:T(8,128)(2,1)S(1)}, u32[]{:S(2)}, u32[]{:S(2)}) collective-permute-start(bf16[96,1152]{1,0:T(8,128)(2,1)S(1)} %split.88), channel_id=1, source_target_pairs={{0,8},{1,9},{2,10},{3,11},{4,12},{5,13},{6,14},{7,15},{8,16},{9,17... | collective-permute-start | bytes 663560 | tf_op jit(solution)/shard_map/ppermute | solution.py:627
  356.8 15.6 %collective-permute-start.62 = (bf16[96,1152]{1,0:T(8,128)(2,1)S(1)}, bf16[96,1152]{1,0:T(8,128)(2,1)S(1)}, u32[]{:S(2)}, u32[]{:S(2)}) collective-permute-start(bf16[96,1152]{1,0:T(8,128)(2,1)S(1)} %get-tuple-element.172), channel_id=1, source_target_pairs={{0,16},{1,17},{2,18},{3,19},{4,20},{5,21},{6,22},{7,23},{8,24},{9,... | collective-permute-start | bytes 663560 | tf_op jit(solution)/shard_map/ppermute | solution.py:627
  356.9 15.6 %collective-permute-start.63 = (bf16[96,1152]{1,0:T(8,128)(2,1)S(1)}, bf16[96,1152]{1,0:T(8,128)(2,1)S(1)}, u32[]{:S(2)}, u32[]{:S(2)}) collective-permute-start(bf16[96,1152]{1,0:T(8,128)(2,1)S(1)} %get-tuple-element.173), channel_id=1, source_target_pairs={{0,24},{1,25},{2,26},{3,27},{4,28},{5,29},{6,30},{7,31},{8,0},{9,1... | collective-permute-start | bytes 663560 | tf_op jit(solution)/shard_map/ppermute | solution.py:627
  375.4 17.3 %collective-permute-start.52 = (bf16[2,192,896]{2,1,0:T(8,128)(2,1)S(1)}, bf16[2,192,896]{2,1,0:T(8,128)(2,1)S(1)}, u32[]{:S(2)}, u32[]{:S(2)}) collective-permute-start(bf16[2,192,896]{2,1,0:T(8,128)(2,1)S(1)} %fusion.38), channel_id=1, source_target_pairs={{0,4},{1,5},{2,6},{3,7},{4,0},{5,1},{6,2},{7,3},{8,12},{9,13},{10,... | collective-permute-start | bytes 2064392 | tf_op jit(solution)/shard_map/ppermute | solution.py:627
  377.1 17.0 %collective-permute-start.51 = (bf16[2,192,896]{2,1,0:T(8,128)(2,1)S(1)}, bf16[2,192,896]{2,1,0:T(8,128)(2,1)S(1)}, u32[]{:S(2)}, u32[]{:S(2)}) collective-permute-start(bf16[2,192,896]{2,1,0:T(8,128)(2,1)S(1)} %fusion.39), channel_id=1, source_target_pairs={{0,2},{1,3},{2,0},{3,1},{4,6},{5,7},{6,4},{7,5},{8,10},{9,11},{10,... | collective-permute-start | bytes 2064392 | tf_op jit(solution)/shard_map/ppermute | solution.py:627
  399.0 16.7 %collective-permute-start.53 = (bf16[256,768]{1,0:T(8,128)(2,1)S(1)}, bf16[256,768]{1,0:T(8,128)(2,1)S(1)}, u32[]{:S(2)}, u32[]{:S(2)}) collective-permute-start(bf16[256,768]{1,0:T(8,128)(2,1)S(1)} %slice.538), channel_id=1, source_target_pairs={{0,2},{1,3},{2,0},{3,1},{4,6},{5,7},{6,4},{7,5},{8,10},{9,11},{10,... | collective-permute-start | bytes 1179656 | tf_op jit(solution)/shard_map/ppermute | solution.py:627
  (56 other events, 663.8 us)

commit v5 on v4

v5 whole, which is shorter than its diff:
```python
import functools
import math

import jax
import jax.numpy as jnp
from jax import lax
from jax.experimental import pallas as pl
from jax.experimental.pallas import tpu as pltpu
from jax.sharding import PartitionSpec as P

HD = 64
PAIR = 2 * HD
QROWS = 256
epsilon = 1e-12
rope_base = 1000.0
masked_score = -1e30
f32 = jnp.float32
bf16 = jnp.bfloat16

NN = (((1,), (0,)), ((), ()))
NT = (((1,), (1,)), ((), ()))
TN = (((0,), (0,)), ((), ()))


def dot(a, b, dims=NN):
    return lax.dot_general(a, b, dims, preferred_element_type=f32)


def rope_tables(positions, width):
    half_dim = HD // 2
    freq = rope_base ** (-jnp.arange(half_dim, dtype=f32) / half_dim)
    angles = positions.astype(f32)[:, None] * freq[None, :]
    cosine, sine = jnp.cos(angles), jnp.sin(angles)
    times = width // HD
    return (
        jnp.tile(jnp.concatenate([cosine, cosine], axis=1), (1, times)),
        jnp.tile(jnp.concatenate([-sine, sine], axis=1), (1, times)),
    )


def rotated(values, cosine, sine):
    width = values.shape[1]
    lane = lax.broadcasted_iota(jnp.int32, values.shape, 1)
    up = pltpu.roll(values, width - HD // 2, 1)
    down = pltpu.roll(values, HD // 2, 1)
    return values * cosine + jnp.where(lane % HD < HD // 2, up, down) * sine


def normalize(hidden):
    centred = hidden - jnp.mean(hidden, axis=-1, keepdims=True)
    variance = jnp.mean(centred * centred, axis=-1, keepdims=True)
    inv_std = lax.rsqrt(variance + epsilon)
    return (centred * inv_std, inv_std)


def norm_back(grad_norm, normed, inv_std):
    return inv_std * (
        grad_norm
        - jnp.mean(grad_norm, axis=-1, keepdims=True)
        - normed * jnp.mean(grad_norm * normed, axis=-1, keepdims=True)
    )


BLOCKS = 5


def block_starts(width):
    half, quarter = width // 2, width // 4
    return [(0, 0), (0, half), (1, 0), (1, half), (1, half + quarter)]


def start_weights(blocks, w_ref, sems):
    @pl.when(pl.program_id(0) == 0)
    def _():
        for block, (slot, row) in zip(blocks, block_starts(w_ref.shape[1])):
            pltpu.make_async_copy(
                block, w_ref.at[slot, pl.ds(row, block.shape[0])], sems.at[slot]
            ).start()


def wait_weights(w_ref, sems, slot):
    pltpu.make_async_copy(w_ref.at[slot], w_ref.at[slot], sems.at[slot]).wait()


def weight_scratch(blocks):
    width = 2 * blocks[0].shape[0]
    return [
        pltpu.VMEM((2, width, blocks[0].shape[1]), bf16),
        pltpu.SemaphoreType.DMA((2,)),
    ]


ANY = pl.BlockSpec(memory_space=pl.ANY)


def cost(flops, nbytes, exps=0):
    return pl.CostEstimate(flops=int(flops), bytes_accessed=int(nbytes), transcendentals=int(exps))


def whole(shape):
    return pl.BlockSpec(shape, lambda *_: (0,) * len(shape))


def qkv_kernel(own_ref, other_ref, cos_ref, sin_ref, *rest):
    blocks, (q_ref, kv_ref, wo_ref, w_ref, sems) = rest[:BLOCKS], rest[BLOCKS:]
    slot = pl.program_id(0)
    start_weights(blocks, w_ref, sems)
    wait_weights(w_ref, sems, slot)
    part = w_ref.shape[2] // 3
    rows = own_ref.shape[0]
    for i, x_ref in enumerate((own_ref, other_ref)):
        span = slice(i * rows, (i + 1) * rows)
        cosine, sine = cos_ref[span, :], sin_ref[span, :]
        x = x_ref[...]
        q = dot(x, w_ref[slot, :, :part])
        q_ref[span, :] = (rotated(q, cosine, sine) * (1.0 / math.sqrt(HD))).astype(bf16)
        k = dot(x, w_ref[slot, :, part : 2 * part])
        kv_ref[span, :part] = rotated(k, cosine, sine).astype(bf16)
        kv_ref[span, part:] = dot(x, w_ref[slot, :, 2 * part :]).astype(bf16)
    lane = lax.broadcasted_iota(jnp.int32, (w_ref.shape[1], part), 1)
    out = jnp.zeros(lane.shape, f32)
    for h in range(3):
        piece = w_ref[slot, :, h * part : (h + 1) * part].astype(f32)
        piece = pltpu.roll(piece, (h + 1) * HD, 1)
        out = jnp.where(lane // HD == h, piece, out)
    wo_ref[...] = out.astype(bf16)


def qkv(own, other, cosine, sine, blocks):
    rows, width = own.shape
    part = blocks[0].shape[1] // 3
    table = whole((2 * rows, part))
    return pl.pallas_call(
        qkv_kernel,
        grid=(2,),
        in_specs=[whole((rows, width))] * 2 + [table] * 2 + [ANY] * BLOCKS,
        out_specs=[
            pl.BlockSpec((2 * rows, part), lambda i: (0, i)),
            pl.BlockSpec((2 * rows, 2 * part), lambda i: (0, i)),
            pl.BlockSpec((width, part), lambda i: (0, i)),
        ],
        scratch_shapes=weight_scratch(blocks),
        out_shape=[
            jax.ShapeDtypeStruct((2 * rows, 2 * part), bf16),
            jax.ShapeDtypeStruct((2 * rows, 4 * part), bf16),
            jax.ShapeDtypeStruct((width, 2 * part), bf16),
        ],
        cost_estimate=cost(24 * rows * width * part, 40 * width * part),
        name="qkv",
    )(own, other, cosine, sine, *blocks)


def attend_kernel(q_ref, kv_ref, segq_ref, segk_ref, out_ref, log_ref, vt_ref):
    block, part = q_ref.shape
    low_half = lax.broadcasted_iota(jnp.int32, (block, PAIR), 1) < HD

    @pl.when(pl.program_id(0) == 0)
    def _():
        vt_ref[...] = kv_ref[:, part:].T

    q = q_ref[...]
    bias = jnp.where(segk_ref[...] == segq_ref[...], 0.0, masked_score)
    parts = []
    for h in range(3):
        pair = slice(h // 2 * PAIR, (h // 2 + 1) * PAIR)
        mine = low_half if h % 2 == 0 else jnp.logical_not(low_half)
        masked = jnp.where(mine, q[:, pair], jnp.zeros((block, PAIR), bf16))
        scores = dot(kv_ref[:, pair], masked, NT) + bias
        top = jnp.max(scores, axis=0, keepdims=True)
        expo = jnp.exp(scores - top)
        total = jnp.sum(expo, axis=0, keepdims=True)
        out = dot(vt_ref[h * HD : (h + 1) * HD, :], expo.astype(bf16))
        parts.append(out / total)
        log_ref[h : h + 1, :] = top + jnp.log(total)
    parts.append(jnp.zeros((HD, block), f32))
    out_ref[...] = jnp.concatenate(parts, axis=0).T.astype(bf16)


def attend(quarter, q, kv, seg_row, seg_col):
    rows = q.shape[0]
    part = q.shape[1] // 2
    return pl.pallas_call(
        attend_kernel,
        grid=(rows // QROWS,),
        in_specs=[
            pl.BlockSpec((QROWS, part), lambda i: (i, quarter)),
            pl.BlockSpec((rows, 2 * part), lambda i: (0, quarter)),
            pl.BlockSpec((1, QROWS), lambda i: (0, i)),
            whole((rows, 1)),
        ],
        out_specs=[
            pl.BlockSpec((QROWS, part), lambda i: (i, 0)),
            pl.BlockSpec((8, QROWS), lambda i: (0, i)),
        ],
        out_shape=[
            jax.ShapeDtypeStruct((rows, part), bf16),
            jax.ShapeDtypeStruct((8, rows), f32),
        ],
        scratch_shapes=[pltpu.VMEM((part, rows), bf16)],
        cost_estimate=cost(16 * rows * rows * part, 12 * rows * part, rows * rows * 3),
        name="attend",
    )(q, kv, seg_row, seg_col)


def attend_back_kernel(
    q_ref, kv_ref, own_ref, other_ref, wo_ref, att_ref, log_ref, segq_ref, segk_ref, cos_ref, sin_ref,
    dq_ref, dkv_ref, kt_ref, dk_ref, dv_ref,
):
    step = pl.program_id(0)
    block, part = q_ref.shape
    low_half = lax.broadcasted_iota(jnp.int32, (block, PAIR), 1) < HD

    @pl.when(step == 0)
    def _():
        kt_ref[...] = kv_ref[:, :part].T
        dk_ref[...] = jnp.zeros_like(dk_ref)
        dv_ref[...] = jnp.zeros_like(dv_ref)

    low = jnp.where(step < pl.num_programs(0) // 2, own_ref[...], other_ref[...])
    do = dot(low, wo_ref[...]).astype(bf16)
    prod = do.astype(f32) * att_ref[...].astype(f32)
    high = prod.astype(bf16)
    rest = (prod - high.astype(f32)).astype(bf16)
    row = lax.broadcasted_iota(jnp.int32, (8, part), 0)
    lane = lax.broadcasted_iota(jnp.int32, (8, part), 1) // HD
    pick = jnp.where(row == lane, 1.0, 0.0).astype(bf16)
    delta = dot(pick, high, NT) + dot(pick, rest, NT)

    q = q_ref[...]
    bias = jnp.where(segk_ref[...] == segq_ref[...], 0.0, masked_score)
    zero = jnp.zeros((block, PAIR), bf16)
    dq = []
    for h in range(3):
        pair = slice(h // 2 * PAIR, (h // 2 + 1) * PAIR)
        values = slice(part + h // 2 * PAIR, part + (h // 2 + 1) * PAIR)
        mine = low_half if h % 2 == 0 else jnp.logical_not(low_half)
        q_head = jnp.where(mine, q[:, pair], zero)
        do_head = jnp.where(mine, do[:, pair], zero)
        scores = dot(kv_ref[:, pair], q_head, NT) + bias
        probs = jnp.exp(scores - log_ref[h : h + 1, :])
        dprobs = dot(kv_ref[:, values], do_head, NT)
        dscores = (probs * (dprobs - delta[h : h + 1, :])).astype(bf16)
        dv_ref[:, pair] += dot(probs.astype(bf16), do_head)
        dk_ref[:, pair] += dot(dscores, q_head)
        dq.append(dot(kt_ref[h * HD : (h + 1) * HD, :], dscores))
    dq.append(jnp.zeros((HD, block), f32))
    dq = (jnp.concatenate(dq, axis=0) * (1.0 / math.sqrt(HD))).T
    span = pl.ds(pl.multiple_of(step * block, block), block)
    dq_ref[...] = rotated(dq, cos_ref[span, :], -sin_ref[span, :]).astype(bf16)

    @pl.when(step == pl.num_programs(0) - 1)
    def _():
        dkv_ref[:, :part] = rotated(dk_ref[...], cos_ref[...], -sin_ref[...]).astype(bf16)
        dkv_ref[:, part:] = dv_ref[...].astype(bf16)


def attend_back(quarter, q, kv, own, other, wo, att, logs, seg_row, seg_col, cosine, sine):
    rows = q.shape[0]
    width = own.shape[1]
    part = q.shape[1] // 2
    steps = rows // QROWS
    return pl.pallas_call(
        attend_back_kernel,
        grid=(steps,),
        in_specs=[
            pl.BlockSpec((QROWS, part), lambda i: (i, quarter)),
            pl.BlockSpec((rows, 2 * part), lambda i: (0, quarter)),
            pl.BlockSpec((QROWS, width), lambda i: (jnp.minimum(i, steps // 2 - 1), 0)),
            pl.BlockSpec((QROWS, width), lambda i: (jnp.maximum(i - steps // 2, 0), 0)),
            pl.BlockSpec((width, part), lambda i: (0, quarter)),
            pl.BlockSpec((QROWS, part), lambda i: (i, 0)),
            pl.BlockSpec((8, QROWS), lambda i: (0, i)),
            pl.BlockSpec((1, QROWS), lambda i: (0, i)),
            whole((rows, 1)),
            whole((rows, part)),
            whole((rows, part)),
        ],
        out_specs=[
            pl.BlockSpec((QROWS, part), lambda i: (i, 0)),
            whole((rows, 2 * part)),
        ],
        out_shape=[
            jax.ShapeDtypeStruct((rows, part), bf16),
            jax.ShapeDtypeStruct((rows, 2 * part), bf16),
        ],
        scratch_shapes=[
            pltpu.VMEM((part, rows), bf16),
            pltpu.VMEM((rows, part), f32),
            pltpu.VMEM((rows, part), f32),
        ],
        cost_estimate=cost(40 * rows * rows * part, 30 * rows * part, rows * rows * 3),
        name="attend_back",
    )(q, kv, own, other, wo, att, logs, seg_row, seg_col, cosine, sine)


def project_kernel(att_a_ref, att_b_ref, wo_ref, own_ref, send_ref):
    part = att_a_ref.shape[1]
    rows = own_ref.shape[0]
    for out_ref, span in ((send_ref, slice(rows, 2 * rows)), (own_ref, slice(0, rows))):
        out = dot(att_a_ref[span, :], wo_ref[:, :part], NT) + dot(att_b_ref[span, :], wo_ref[:, part:], NT)
        out_ref[...] = out.astype(out_ref.dtype)


def project(att_a, att_b, wo):
    rows, part = att_a.shape
    rows = rows // 2
    width = wo.shape[0]
    return pl.pallas_call(
        project_kernel,
        grid=(1,),
        in_specs=[whole(att_a.shape)] * 2 + [whole(wo.shape)],
        out_specs=[whole((rows, width))] * 2,
        out_shape=[
            jax.ShapeDtypeStruct((rows, width), f32),
            jax.ShapeDtypeStruct((rows, width), bf16),
        ],
        cost_estimate=cost(8 * rows * width * part, 16 * rows * width),
        name="project",
    )(att_a, att_b, wo)


def first_kernel(
    x_ref, own_ref, came_ref, norm_a_ref, norm_b_ref, n_ref, s_ref, low_ref, low_t_ref, gains_ref
):
    norms = jnp.concatenate([norm_a_ref[...], norm_b_ref[...]], axis=0).astype(f32).T
    gains_ref[...] = norms[:8]
    branch = own_ref[...] + came_ref[...].astype(f32)
    normed, inv = normalize(x_ref[...].astype(f32) + branch)
    n_ref[...] = normed
    s_ref[...] = jnp.broadcast_to(inv, s_ref.shape)
    first = normed * norms[0:1] + norms[2:3]
    low_ref[...] = first.astype(bf16)
    low_t_ref[...] = first.T.astype(bf16)


def first_norm(x, own, came, norm_a, norm_b):
    rows, width = x.shape
    at = norm_a.shape[1] // 128 - 1
    strip = pl.BlockSpec((width // 2, 128), lambda i: (0, at))
    return pl.pallas_call(
        first_kernel,
        grid=(1,),
        in_specs=[whole(x.shape)] * 3 + [strip] * 2,
        out_specs=[
            whole((rows, width)), whole((rows, 128)), whole((rows, width)), whole((width, rows)), whole((8, width)),
        ],
        out_shape=[
            jax.ShapeDtypeStruct((rows, width), f32),
            jax.ShapeDtypeStruct((rows, 128), f32),
            jax.ShapeDtypeStruct((rows, width), bf16),
            jax.ShapeDtypeStruct((width, rows), bf16),
            jax.ShapeDtypeStruct((8, width), f32),
        ],
        cost_estimate=cost(20 * rows * width, 16 * rows * width),
        name="first_norm",
    )(x, own, came, norm_a, norm_b)


def mlp_kernel(has_base, low_ref, *rest):
    if has_base:
        base_ref, rest = rest[0], rest[1:]
    blocks, (act_ref, feed_ref, w_ref, sems, sum_ref) = rest[:BLOCKS], rest[BLOCKS:]
    slot = pl.program_id(0)
    half = act_ref.shape[3]
    start_weights(blocks, w_ref, sems)

    @pl.when(slot == 0)
    def _():
        sum_ref[...] = base_ref[...] if has_base else jnp.zeros_like(sum_ref)

    wait_weights(w_ref, sems, slot)

    def body(i, _):
        span = pl.ds(pl.multiple_of(i * QROWS, QROWS), QROWS)
        low = low_ref[span, :]
        gate = dot(low, w_ref[slot, :, half : 2 * half])
        up = dot(low, w_ref[slot, :, 2 * half : 3 * half])
        hidden = (gate / (1.0 + jnp.exp(-gate)) * up).astype(bf16)
        act_ref[0, 0, span, :] = gate.astype(bf16)
        act_ref[0, 1, span, :] = up.astype(bf16)
        act_ref[0, 2, span, :] = hidden
        sum_ref[span, :] += dot(hidden, w_ref[slot, :, :half], NT)
        return 0

    lax.fori_loop(0, low_ref.shape[0] // QROWS, body, 0)

    @pl.when(slot == 1)
    def _():
        feed_ref[...] = sum_ref[...].astype(feed_ref.dtype)


def mlp(low, base, blocks, half, dtype):
    rows, width = low.shape
    has_base = base is not None
    extra = [base] if has_base else []
    return pl.pallas_call(
        functools.partial(mlp_kernel, has_base),
        grid=(2,),
        in_specs=[whole((rows, width))] * (1 + has_base) + [ANY] * BLOCKS,
        out_specs=[
            pl.BlockSpec((1, 3, rows, half), lambda i: (i, 0, 0, 0)),
            whole((rows, width)),
        ],
        scratch_shapes=weight_scratch(blocks) + [pltpu.VMEM((rows, width), f32)],
        out_shape=[
            jax.ShapeDtypeStruct((2, 3, rows, half), bf16),
            jax.ShapeDtypeStruct((rows, width), dtype),
        ],
        cost_estimate=cost(12 * rows * width * half, 30 * half * width, 2 * rows * half),
        name="mlp",
    )(low, *extra, *blocks)


def second_kernel(
    n_ref, gains_ref, feed_ref, came_ref, dy_ref, out_ref, dh_ref, low_ref, low_t_ref, sums_ref
):
    first = n_ref[...] * gains_ref[0:1] + gains_ref[2:3]
    normed, inv = normalize(first + feed_ref[...] + came_ref[...].astype(f32))
    out_ref[...] = (normed * gains_ref[1:2] + gains_ref[3:4]).astype(bf16)
    dy = dy_ref[...]
    sums_ref[...] = jnp.zeros_like(sums_ref)
    sums_ref[1:2] = jnp.sum(dy * normed, axis=0, keepdims=True)
    sums_ref[3:4] = jnp.sum(dy, axis=0, keepdims=True)
    dh = norm_back(dy * gains_ref[1:2], normed, inv)
    dh_ref[...] = dh
    low_ref[...] = dh.astype(bf16)
    low_t_ref[...] = dh.T.astype(bf16)


def second_norm(n1, gains, feed, came, dy):
    rows, width = n1.shape
    full = whole((rows, width))
    return pl.pallas_call(
        second_kernel,
        grid=(1,),
        in_specs=[full, whole((8, width)), full, full, full],
        out_specs=[full, full, full, whole((width, rows)), whole((8, width))],
        out_shape=[
            jax.ShapeDtypeStruct((rows, width), bf16),
            jax.ShapeDtypeStruct((rows, width), f32),
            jax.ShapeDtypeStruct((rows, width), bf16),
            jax.ShapeDtypeStruct((width, rows), bf16),
            jax.ShapeDtypeStruct((8, width), f32),
        ],
        cost_estimate=cost(40 * rows * width, 22 * rows * width),
        name="second_norm",
    )(n1, gains, feed, came, dy)


def mlp_back_kernel(has_base, *rest):
    dfeeds, dfeeds_t, lows_t, acts = rest[:2], rest[2:4], rest[4:6], rest[6:8]
    rest = rest[8:]
    if has_base:
        bases, rest = rest[:2], rest[2:]
    blocks, rest = rest[:BLOCKS], rest[BLOCKS:]
    own_ref, other_ref, to_x_ref, to_y_ref, keep_ref, w_ref, sems, part_ref, sum_ref = rest
    slot = pl.program_id(0)
    rows = own_ref.shape[0]
    half = acts[0].shape[3]
    start_weights(blocks, w_ref, sems)

    @pl.when(slot == 0)
    def _():
        for i in range(2):
            sum_ref[i * rows : (i + 1) * rows, :] = (
                bases[i][...] if has_base else jnp.zeros((rows, sum_ref.shape[1]), f32)
            )

    wait_weights(w_ref, sems, slot)

    for i in range(2):

        def body(j, _):
            span = pl.ds(pl.multiple_of(j * QROWS, QROWS), QROWS)
            both = pl.ds(pl.multiple_of(i * rows + j * QROWS, QROWS), QROWS)
            dhidden = dot(dfeeds[i][span, :], w_ref[slot, :, :half])
            gate = acts[i][0, 0, span, :].astype(f32)
            up = acts[i][0, 1, span, :].astype(f32)
            sg = 1.0 / (1.0 + jnp.exp(-gate))
            dgate = dhidden * up * sg * (1.0 + gate * (1.0 - sg))
            dup = dhidden * (gate * sg)
            part_ref[both, :half] = dgate.astype(bf16)
            part_ref[both, half:] = dup.astype(bf16)
            sum_ref[both, :] += dot(part_ref[both, :], w_ref[slot, :, half : 3 * half], NT)
            return 0

        lax.fori_loop(0, rows // QROWS, body, 0)
    gate_up = (
        dot(lows_t[0][...], part_ref[:rows, :]) + dot(lows_t[1][...], part_ref[rows:, :])
    ).astype(bf16)
    down = (
        dot(dfeeds_t[0][...], acts[0][0, 2]) + dot(dfeeds_t[1][...], acts[1][0, 2])
    ).astype(bf16)
    cut = keep_ref.shape[1]

    def emit(out_ref, at, block):
        span = slice(block * cut, (block + 1) * cut)
        out_ref[at, :, :half] = down[span]
        out_ref[at, :, half:] = gate_up[span]

    emit(to_x_ref, 0, 3)

    @pl.when(slot == 0)
    def _():
        for block in range(3):
            emit(keep_ref, block, block)

    @pl.when(slot == 1)
    def _():
        emit(to_y_ref, 0, 0)
        emit(to_y_ref, 1, 2)
        emit(keep_ref, 3, 1)
        own_ref[...] = sum_ref[:rows, :]
        other_ref[...] = sum_ref[rows:, :].astype(other_ref.dtype)


def mlp_back(bases, dfeeds, dfeeds_t, lows_t, acts, blocks):
    rows, width = dfeeds[0].shape
    half = acts[0].shape[3]
    has_base = bases is not None
    full = whole((rows, width))
    return pl.pallas_call(
        functools.partial(mlp_back_kernel, has_base),
        grid=(2,),
        in_specs=[full] * 2
        + [whole((width, rows))] * 4
        + [pl.BlockSpec((1, 3, rows, half), lambda i: (i, 0, 0, 0))] * 2
        + [full] * (2 * has_base)
        + [ANY] * BLOCKS,
        out_specs=[
            full,
            full,
            pl.BlockSpec((1, width // 4, 3 * half), lambda i: (i, 0, 0)),
            whole((2, width // 4, 3 * half)),
            whole((4, width // 4, 3 * half)),
        ],
        scratch_shapes=weight_scratch(blocks)
        + [pltpu.VMEM((2 * rows, 2 * half), bf16), pltpu.VMEM((2 * rows, width), f32)],
        out_shape=[
            jax.ShapeDtypeStruct((rows, width), f32),
            jax.ShapeDtypeStruct((rows, width), bf16 if has_base else f32),
            jax.ShapeDtypeStruct((2, width // 4, 3 * half), bf16),
            jax.ShapeDtypeStruct((2, width // 4, 3 * half), bf16),
            jax.ShapeDtypeStruct((4, width // 4, 3 * half), bf16),
        ],
        cost_estimate=cost(48 * rows * width * half, 100 * half * width, 4 * rows * half),
        name="mlp_back",
    )(*dfeeds, *dfeeds_t, *lows_t, *acts, *(bases if has_base else ()), *blocks)


def first_back_kernel(
    base_ref, own_ref, came_ref, n_ref, s_ref, gains_ref, sums_ref, dh_ref, low_ref, low_t_ref, cols_ref
):
    dfirst = base_ref[...] + own_ref[...] + came_ref[...].astype(f32)
    normed = n_ref[...]
    width = dfirst.shape[1]
    gain_sum = jnp.sum(dfirst * normed, axis=0, keepdims=True)
    bias_sum = jnp.sum(dfirst, axis=0, keepdims=True)
    sums = sums_ref[...]
    stacked = jnp.concatenate(
        [gain_sum, sums[1:2], bias_sum, sums[3:4], jnp.zeros((124, width), f32)], axis=0
    )
    cols_ref[...] = stacked.T.astype(bf16)
    dh = norm_back(dfirst * gains_ref[0:1], normed, s_ref[:, 0:1])
    dh_ref[...] = dh
    low_ref[...] = dh.astype(bf16)
    low_t_ref[...] = dh.T.astype(bf16)


def first_back(base, own, came, n1, s1, gains, sums):
    rows, width = n1.shape
    full = whole((rows, width))
    return pl.pallas_call(
        first_back_kernel,
        grid=(1,),
        in_specs=[full] * 4 + [whole((rows, 128)), whole((8, width)), whole((8, width))],
        out_specs=[full, full, whole((width, rows)), whole((width, 128))],
        out_shape=[
            jax.ShapeDtypeStruct((rows, width), f32),
            jax.ShapeDtypeStruct((rows, width), bf16),
            jax.ShapeDtypeStruct((width, rows), bf16),
            jax.ShapeDtypeStruct((width, 128), bf16),
        ],
        cost_estimate=cost(40 * rows * width, 20 * rows * width),
        name="first_back",
    )(base, own, came, n1, s1, gains, sums)


def qkv_back_kernel(
    quarter, has_base, dq_ref, dkv_ref, x_a_ref, x_b_ref, low_a_ref, low_b_ref, att_ref, cols_ref, *rest
):
    if has_base:
        bases, rest = rest[:2], rest[2:]
    blocks, (own_ref, other_ref, send_ref, keep_ref, w_ref, sem) = rest[:3], rest[3:]
    rows = own_ref.shape[0]
    part = dq_ref.shape[1]
    starts = [row for slot, row in block_starts(w_ref.shape[0]) if slot == quarter]
    for block, row in zip(blocks, starts):
        pltpu.make_async_copy(block, w_ref.at[pl.ds(row, block.shape[0])], sem).start()
    d_out = dot(low_a_ref[...], att_ref[:rows, :]) + dot(low_b_ref[...], att_ref[rows:, :])
    lane = lax.broadcasted_iota(jnp.int32, d_out.shape, 1)
    cut = keep_ref.shape[1]
    if quarter == 0:
        places = [(keep_ref, 0), (keep_ref, 1), (keep_ref, 2), (send_ref, 0)]
    else:
        places = [(send_ref, 0), (keep_ref, 0), (send_ref, 1), (send_ref, 2)]

    def emit(value, lanes):
        for block, (out_ref, at) in enumerate(places):
            out_ref[at, :, lanes] = value[block * cut : (block + 1) * cut]

    for h in range(3):
        source, at = (dq_ref, 0) if h == 0 else (dkv_ref, (h - 1) * part)
        piece = dot(x_a_ref[...], source[:rows, at : at + part]) + dot(x_b_ref[...], source[rows:, at : at + part])
        moved = pltpu.roll(d_out, (3 - h) * HD, 1)
        emit(jnp.where(lane < 3 * HD, piece, moved).astype(bf16), slice(h * part, (h + 1) * part))
    emit(cols_ref[...], slice(3 * part, 3 * part + 128))
    pltpu.make_async_copy(w_ref, w_ref, sem).wait()
    for i, out_ref in enumerate((own_ref, other_ref)):
        span = slice(i * rows, (i + 1) * rows)
        total = dot(dq_ref[span, :], w_ref[:, :part], NT) + dot(dkv_ref[span, :], w_ref[:, part:], NT)
        if has_base:
            total = total + bases[i][...]
        out_ref[...] = total.astype(out_ref.dtype)


def qkv_back(quarter, bases, dq, dkv, x_t, low_t, att, cols, blocks):
    rows = dq.shape[0] // 2
    width = cols.shape[0]
    part = dq.shape[1]
    has_base = bases is not None
    full = whole((rows, width))
    turned = whole((width, rows))
    blocks = [b for b, (slot, _) in zip(blocks, block_starts(width)) if slot == quarter]
    blocks += [blocks[0]] * (3 - len(blocks))
    counts = (1, 3) if quarter == 0 else (3, 1)
    pieces = [(n, width // 4, 3 * part + 128) for n in counts]
    return pl.pallas_call(
        functools.partial(qkv_back_kernel, quarter, has_base),
        grid=(1,),
        in_specs=[whole(dq.shape), whole(dkv.shape)]
        + [turned] * 4
        + [whole(att.shape), whole((width, 128))]
        + [full] * (2 * has_base)
        + [ANY] * 3,
        out_specs=[full, full] + [whole(p) for p in pieces],
        scratch_shapes=[pltpu.VMEM((width, 3 * part), bf16), pltpu.SemaphoreType.DMA],
        out_shape=[
            jax.ShapeDtypeStruct((rows, width), f32),
            jax.ShapeDtypeStruct((rows, width), bf16 if has_base else f32),
        ]
        + [jax.ShapeDtypeStruct(p, bf16) for p in pieces],
        cost_estimate=cost(26 * rows * width * part, 40 * width * part),
        name="qkv_back",
    )(dq, dkv, *x_t, *low_t, att, cols, *(bases if has_base else ()), *blocks)


def factors_of(n):
    out = []
    while n > 1:
        step = 4 if n % 4 == 0 else (2 if n % 2 == 0 else n)
        out.append(step)
        n //= step
    return out


class Links:
    def __init__(self, mesh):
        self.rows = mesh.shape["row"]
        self.cols = mesh.shape["col"]
        self.digits = factors_of(self.rows // 2)

    def locate(self):
        row = lax.axis_index("row")
        col = lax.axis_index("col")
        x = row % 2
        place = row // 2
        ring = []
        for size in reversed(self.digits):
            ring.insert(0, place % size)
            place = place // size
        return ring, x, col // (self.cols // 2), col % 2

    def send(self, v, move):
        pairs = []
        for row in range(self.rows):
            for col in range(self.cols):
                place, ring = row // 2, []
                for size in reversed(self.digits):
                    ring.insert(0, place % size)
                    place //= size
                ring, x, y, k = move(ring, row % 2, col // (self.cols // 2), col % 2)
                place = 0
                for size, digit in zip(self.digits, ring):
                    place = place * size + digit % size
                pairs.append(
                    (row * self.cols + col, (place * 2 + x) * self.cols + y * (self.cols // 2) + k)
                )
        return lax.ppermute(v, ("row", "col"), pairs)

    def across(self, v):
        return self.send(v, lambda ring, x, y, k: (ring, x, 1 - y, k))

    def beside(self, v):
        return self.send(v, lambda ring, x, y, k: (ring, x, y, 1 - k))

    def along(self, v):
        return self.send(v, lambda ring, x, y, k: (ring, 1 - x, y, k))

    def shift(self, v, axis, step):
        def move(ring, x, y, k):
            moved = list(ring)
            moved[axis] = ring[axis] + step
            return moved, x, y, k

        return self.send(v, move)

    def ring_gather(self, block):
        for axis in reversed(range(len(self.digits))):
            block = jnp.concatenate(
                [block] + [self.shift(block, axis, -d) for d in range(1, self.digits[axis])], axis=0
            )
        return block

    def ring_scatter(self, block):
        for axis in range(len(self.digits)):
            size = self.digits[axis]
            pieces = jnp.split(block, size, axis=0)
            low = [p.astype(bf16) for p in pieces[1:]]
            block = pieces[0]
            for d in range(1, size):
                block = block + self.shift(low[d - 1], axis, d).astype(f32)
        return block


def tie(value, *others):
    return lax.optimization_barrier((value, *others))[0]


class Scatter:
    def __init__(self, links, to_x, to_y, keep):
        self.links, self.keep = links, keep
        self.by_x = [links.along(v) for v in to_x]
        self.by_y = links.across(to_y)

    def second(self):
        by_x = self.by_x[0][1] if len(self.by_x) == 1 else self.by_x[1][0]
        to_x = (self.keep[2].astype(f32) + self.by_y[1].astype(f32)).astype(bf16)
        to_y = (self.keep[3].astype(f32) + by_x.astype(f32)).astype(bf16)
        self.late_x, self.late_y = self.links.along(to_x), self.links.across(to_y)
        return to_x, to_y

    def third(self):
        low = self.keep[0].astype(f32) + self.by_y[0].astype(f32) + self.late_x.astype(f32)
        high = self.keep[1].astype(f32) + self.by_x[0][0].astype(f32) + self.late_y.astype(f32)
        self.block = jnp.concatenate([low, high], axis=0)
        return self.block

    def last(self):
        return self.links.ring_scatter(self.block)


def relative_order(links, depth):
    ring, x, _, _ = links.locate()
    where = lax.broadcasted_iota(jnp.int32, (1, links.rows * depth), 1)
    block, inside = where // depth, where % depth
    steps = links.rows // 2
    place = block % steps
    parts = []
    for axis in reversed(range(len(links.digits))):
        size = links.digits[axis]
        parts.insert(0, (place % size + ring[axis]) % size)
        place = place // size
    row = jnp.zeros_like(block)
    for size, part in zip(links.digits, parts):
        row = row * size + part
    row = row * 2 + jnp.bitwise_xor(x, block // steps)
    return row * depth + inside


def on_device(
    links, tokens, segments, positions, w_qkv, w_out, w_gate_up, w_down, norm_gain, norm_bias, cotangent
):
    ring, x_place, side, core = links.locate()
    depth = w_qkv.shape[0]
    width = tokens.shape[2]
    head_cols = w_qkv.shape[2]
    hid = w_gate_up.shape[2]
    half = hid // 2
    rows = 2 * tokens.shape[1]
    mine = rows // 2
    part = head_cols + HD

    source = relative_order(links, depth)
    swap = (lax.broadcasted_iota(jnp.int32, (width, width), 0) == source).astype(bf16)

    def split(v):
        high = v.astype(bf16)
        return high, (v - high.astype(f32)).astype(bf16)

    def own_and_other(v):
        own = lax.dynamic_index_in_dim(v, side, 0, keepdims=False)
        return own, lax.dynamic_index_in_dim(v, 1 - side, 0, keepdims=False)

    def from_sequence(own, came):
        first = side == 0
        return jnp.stack([jnp.where(first, own, came), jnp.where(first, came, own)], axis=0)

    out_t = w_out.T
    attn_shard = jnp.concatenate(
        sum(
            [[w_qkv[:, p], out_t[:, p * HD : (p + 1) * HD]] for p in range(3)],
            [],
        ),
        axis=1,
    )
    norms = jnp.concatenate([norm_gain, norm_bias], axis=1)
    norms = jnp.pad(norms, ((0, 0), (0, 128 - norms.shape[1])))
    down_t = w_down.T
    mlp_shards = []
    for h in range(2):
        cols = slice(h * half, (h + 1) * half)
        pieces = [down_t[:, cols], w_gate_up[:, 0, cols], w_gate_up[:, 1, cols]]
        mlp_shards.append(jnp.concatenate(pieces + ([norms] if h == 0 else []), axis=1))

    tokens_own, tokens_other = own_and_other(tokens)
    tokens_came = links.across(tokens_other)
    small_own, small_other = own_and_other(jnp.stack([segments, positions], axis=1))
    small_came = links.across(small_other)
    dy_own, dy_other = own_and_other(cotangent)

    ring_a = links.ring_gather(attn_shard)
    cut = ring_a.shape[0] // 2
    x_a, y_a = links.along(ring_a), links.across(ring_a)
    ring_b = links.ring_gather(tie(mlp_shards[0], ring_a))
    attn_w = [ring_a, x_a, y_a, links.across(x_a[:cut]), links.along(y_a[cut:])]

    x_abs = jnp.concatenate([tokens_own, tokens_came], axis=0)
    x = dot(x_abs, swap).astype(bf16)
    x_other = links.beside(x)
    x_t = lax.dot_general(swap, x_abs, (((0,), (1,)), ((), ())), preferred_element_type=f32).astype(bf16)
    x_t = [x_t, links.beside(x_t)]
    small = jnp.concatenate([small_own, small_came], axis=1)
    small = jnp.concatenate([small, links.beside(small)], axis=1)
    seg_row, seg_col = small[0][None, :], small[0][:, None]
    cosine, sine = rope_tables(small[1], part)

    ring_b = tie(ring_b, x_a, y_a)
    x_b, y_b = links.along(ring_b), links.across(ring_b)
    q, kv, wo = qkv(tie(x, ring_b), x_other, cosine, sine, attn_w)
    ring_c = links.ring_gather(tie(mlp_shards[1], ring_b))
    att_0, logs_0 = attend(0, q, kv, seg_row, seg_col)
    ring_c = tie(ring_c, x_b, y_b)
    x_c, y_c = links.along(ring_c), links.across(ring_c)
    mlp_b = [ring_b, x_b, y_b, links.across(x_b[:cut]), links.along(y_b[cut:])]
    att_1, logs_1 = attend(1, tie(q, ring_c, x_b, y_b), kv, seg_row, seg_col)
    own, send = project(att_0, att_1, wo)
    n1, s1, low, low_t, gains = first_norm(x, own, links.beside(send), ring_b, x_b)
    low_other = links.beside(low)
    low1_t = [low_t, links.beside(low_t)]
    act_b_own, feed = mlp(low, None, mlp_b, half, f32)
    act_b_other, feed_other = mlp(tie(low_other, x_c, y_c), None, mlp_b, half, f32)
    mlp_c = [ring_c, x_c, y_c, links.across(x_c[:cut]), links.along(y_c[cut:])]
    act_c_other, send = mlp(low_other, feed_other, mlp_c, half, bf16)
    came = links.beside(send)
    act_c_own, feed = mlp(tie(low, send), feed, mlp_c, half, f32)
    dy_came = links.across(tie(dy_other.astype(bf16), y_c))
    high, low = split(dy_own)
    dy = jnp.concatenate([dot(high, swap) + dot(low, swap), dot(dy_came, swap)], axis=0)
    layer_out, dh2, dfeed, dfeed_t, sums = second_norm(n1, gains, feed, came, dy)
    dfeeds = [dfeed, links.beside(dfeed)]
    dfeeds_t = [dfeed_t, links.beside(dfeed_t)]

    own, other, to_x, to_y, keep = mlp_back(None, dfeeds, dfeeds_t, low1_t, (act_c_own, act_c_other), mlp_c)
    sum_c = Scatter(links, [to_x], to_y, keep)
    own, other, to_x, to_y, keep = mlp_back(
        (own, other), dfeeds, dfeeds_t, low1_t, (act_b_own, act_b_other), mlp_b
    )
    came = links.beside(other)
    sum_b = Scatter(links, [to_x], to_y, keep)
    ops_c = sum_c.second()
    dh1, low, low_t, cols = first_back(tie(dh2, *ops_c), own, came, n1, s1, gains, sums)
    lows = [low, links.beside(low)]
    low_t = [low_t, links.beside(low_t)]
    cols = (cols.astype(f32) + links.beside(cols).astype(f32)).astype(bf16)
    layer_out = dot(layer_out, swap, NT).astype(bf16)
    layer_out = from_sequence(layer_out[:mine], links.across(layer_out[mine:]))

    dq, dkv = attend_back(1, q, kv, *lows, wo, att_1, logs_1, seg_row, seg_col, cosine, sine)
    block_c = sum_c.third()
    own, other, send, keep_1 = qkv_back(1, None, tie(dq, block_c), dkv, x_t, low_t, att_1, cols, attn_w)
    own_c = sum_c.last()
    ops_b = sum_b.second()
    dq, dkv = attend_back(
        0, tie(q, own, *ops_b), kv, *lows, wo, att_0, logs_0, seg_row, seg_col, cosine, sine
    )
    block_b = sum_b.third()
    to_y, to_x = send[:2], [send[2:]]
    own, other, send, keep_0 = qkv_back(0, (own, other), tie(dq, block_b), dkv, x_t, low_t, att_0, cols, attn_w)
    own_b = sum_b.last()
    sum_a = Scatter(links, [send] + to_x, to_y, jnp.concatenate([keep_0, keep_1], axis=0))
    grad = dh1 + own + links.beside(other).astype(f32)
    high, low = split(grad)
    grad = dot(high, swap, NT) + dot(low, swap, NT)
    ops_a = sum_a.second()
    other = tie(grad[mine:].astype(bf16), *ops_a)
    input_grad = from_sequence(grad[:mine], links.across(other).astype(f32))
    sum_a.third()
    own_attn = sum_a.last()
    own_mlp = [own_b, own_c]

    grad_down = jnp.concatenate([v[:, :half] for v in own_mlp], axis=1).T
    grad_gate_up = jnp.stack(
        [
            jnp.concatenate([v[:, (p + 1) * half : (p + 2) * half] for v in own_mlp], axis=1)
            for p in range(2)
        ],
        axis=1,
    )
    thirds = [own_attn[:, p * part : (p + 1) * part] for p in range(3)]
    edge = 3 * part
    return (
        layer_out,
        input_grad,
        jnp.stack([v[:, :head_cols] for v in thirds], axis=1),
        jnp.concatenate([v[:, head_cols:] for v in thirds], axis=1).T,
        grad_gate_up,
        grad_down,
        own_attn[:, edge : edge + 2],
        own_attn[:, edge + 2 : edge + 4],
    )


def solution(mesh):
    in_specs = (
        P(None, ("row", "col"), None),
        P(None, ("row", "col")),
        P(None, ("row", "col")),
        P("row", None, "col"),
        P("col", "row"),
        P("row", None, "col"),
        P("col", "row"),
        P("row", None),
        P("row", None),
        P(None, ("row", "col"), None),
    )
    out_specs = (
        P(None, ("row", "col"), None),
        P(None, ("row", "col"), None),
        P("row", None, "col"),
        P("col", "row"),
        P("row", None, "col"),
        P("col", "row"),
        P("row", None),
        P("row", None),
    )
    return jax.shard_map(
        functools.partial(on_device, Links(mesh)), mesh=mesh, in_specs=in_specs, out_specs=out_specs, check_vma=False
    )
```

time: 431 us -> 444 us (1.030)
  other arithmetic: 34.7 us -> 16.9 us
  waiting for transfers between devices: 123 us -> 140 us
  Pallas kernels: 158 us -> 171 us
    ppermute x69 -> x62, waiting for transfers between devices: 123 us -> 140 us  [send(): return lax.ppermute(v, ('row', 'col'), pairs)]
    convert_element_type x9 -> x5, other arithmetic: 17.4 us -> 4.29 us  [the longest x3 3.48 us: second(): to_y = (self.keep[3].astype(f32) + by_x.astype(f32)).astype(bf16)]
    pallas_call x15 -> x16, Pallas kernels: 152 us -> 164 us  [the longest x2 39.6 us: mlp_back(): pl.pallas_call(functools.partial(mlp_back_kernel, has_base), grid=(2,), i...]
    ppermute x69 -> x62, starting transfers between devices: 74.8 us -> 71.7 us  [send(): return lax.ppermute(v, ('row', 'col'), pairs)]
    unnamed x77 -> x113, local copies, waits for them, and re-layouts: 7.67 us -> 10.4 us
  transfers between devices with their start and end apart: 69 -> 62, of which waited for: 24 -> 25; matrix products, arithmetic and copies ran while one was open for 12% -> 9% of each run, Pallas kernels for 28% -> 25%
where the time goes in v5:
time: 444 us; the launch traced here: 437 us
  Pallas kernels  171 us (39%)
  waiting for transfers between devices  140 us (32%)
  starting transfers between devices  71.7 us (16%)
  local copies, waits for them, and re-layouts  24.3 us (5%)
  other arithmetic  16.9 us (4%)
  matrix products  11.4 us (3%)
    ppermute x62, waiting for transfers between devices, send(): return lax.ppermute(v, ('row', 'col'), pairs)  140 us
    ppermute x62, starting transfers between devices, send(): return lax.ppermute(v, ('row', 'col'), pairs)  71.7 us
    pallas_call x2, Pallas kernels, mlp_back(): pl.pallas_call(functools.partial(mlp_back_kernel, has_base), grid=(2,), i...  39.6 us
    pallas_call x2, Pallas kernels, attend_back(): pl.pallas_call(attend_back_kernel, grid=(steps,), in_specs=[pl.BlockSpec(...  32.6 us
    pallas_call x4, Pallas kernels, mlp(): pl.pallas_call(functools.partial(mlp_kernel, has_base), grid=(2,), in_spe...  31.9 us
    pallas_call x2, Pallas kernels, attend(): pl.pallas_call(attend_kernel, grid=(rows // QROWS,), in_specs=[pl.BlockSp...  22.3 us
    pallas_call x2, Pallas kernels, qkv_back(): pl.pallas_call(functools.partial(qkv_back_kernel, quarter, has_base), gri...  15.9 us
    unnamed x113, local copies, waits for them, and re-layouts  10.4 us
  transfers between devices with their start and end apart: 62, of which 25 were waited for; matrix products, arithmetic and copies ran while one was open for 9% of the time, Pallas kernels for 25%

profile of v5, /device:TPU:0, one launch (start us, length us, event | category | flops | bytes accessed | tf_op | source)
XLA Modules:
  0.0 437.2 jit_solution(8998562446876096768)
XLA Ops:
  2.7 5.1 %collective-permute-start.1 = (bf16[96,768]{1,0:T(8,128)(2,1)S(1)}, bf16[96,768]{1,0:T(8,128)(2,1)S(1)}, u32[]{:S(2)}, u32[]{:S(2)}) collective-permute-start(bf16[96,768]{1,0:T(8,128)(2,1)S(1)} %concatenate.57), channel_id=1, source_target_pairs={{0,24},{1,25},{2,26},{3,27},{4,28},{5,29},{6,30},{7,31},{8,0},{9,1... | collective-permute-start | bytes 442376 | tf_op jit(solution)/shard_map/ppermute | solution.py:699
  13.0 7.1 %collective-permute-done.10 = s32[2,256]{1,0:T(2,128)S(1)} collective-permute-done((s32[2,256]{1,0:T(2,128)S(1)}, s32[2,256]{1,0:T(2,128)S(1)}, u32[]{:S(2)}, u32[]{:S(2)}) %collective-permute-start.10) | collective-permute-done | bytes 2080 | tf_op jit(solution)/shard_map/ppermute | solution.py:699
  21.4 3.1 collective-permute-start.4
  29.3 1.7 fusion.9.own_ref.x_ref
  31.1 16.1 %collective-permute-done.5 = bf16[96,1280]{1,0:T(8,128)(2,1)S(1)} collective-permute-done((bf16[96,1280]{1,0:T(8,128)(2,1)S(1)}, bf16[96,1280]{1,0:T(8,128)(2,1)S(1)}, u32[]{:S(2)}, u32[]{:S(2)}) %collective-permute-start.5) | collective-permute-done | bytes 245792 | tf_op jit(solution)/shard_map/ppermute | solution.py:699
  48.9 1.9 collective-permute-start.16
  56.3 11.7 %collective-permute-done.15 = bf16[96,1152]{1,0:T(8,128)(2,1)S(1)} collective-permute-done((bf16[96,1152]{1,0:T(8,128)(2,1)S(1)}, bf16[96,1152]{1,0:T(8,128)(2,1)S(1)}, u32[]{:S(2)}, u32[]{:S(2)}) %collective-permute-start.15) | collective-permute-done | bytes 221216 | tf_op jit(solution)/shard_map/ppermute | solution.py:699
  75.1 2.0 pad_maximum_fusion.3.rest_1_.rest_8_
  77.2 5.6 %collective-permute-done.12.rest_3_.rest_1_ = bf16[192,768]{1,0:T(8,128)(2,1)} collective-permute-done((bf16[192,768]{1,0:T(8,128)(2,1)}, bf16[192,768]{1,0:T(8,128)(2,1)}, u32[]{:S(2)}, u32[]{:S(2)}) %collective-permute-start.12) | collective-permute-done | bytes 294944 | tf_op jit(solution)/shard_map/ppermute | solution.py:699
  82.8 8.5 %qkv.1 = (bf16[1024,512]{1,0:T(8,128)(2,1)}, bf16[1024,1024]{1,0:T(8,128)(2,1)}, bf16[768,512]{1,0:T(8,128)(2,1)}) custom-call(bf16[512,768]{1,0:T(8,128)(2,1)} %fusion.9.own_ref.x_ref, bf16[512,768]{1,0:T(8,128)(2,1)} %collective-permute-done.9.other_ref, f32[1024,256]{1,0:T(8,128)} %copy.54.cos_ref, f32[1024,256]{1,0:T(8,128)} %copy.55.sin_ref, ...), custom_call_target="tpu_custom_call" | custom-call | flops 2415919104 | bytes 7864320 | tf_op jit(solution)/shard_map/qkv/pallas_call | solution.py:133
  91.3 11.0 %attend.2 = (bf16[1024,256]{1,0:T(8,128)(2,1)}, f32[8,1024]{1,0:T(8,128)}) custom-call(bf16[1024,512]{1,0:T(8,128)(2,1)} %get-tuple-element.126.q_ref, bf16[1024,1024]{1,0:T(8,128)(2,1)} %get-tuple-element.77.kv_ref, s32[1,1024]{1,0:T(1,128)} %get-tuple-element.211.segq_ref, s32[1024,1]{1,0:T(8,128)} %copy.56.segk_ref), custom_call_target="tpu_custom_call" | custom-call | flops 4294967296 | bytes 3145728 | tf_op jit(solution)/shard_map/attend/pallas_call | solution.py:182
  102.3 11.3 %attend.3 = (bf16[1024,256]{1,0:T(8,128)(2,1)}, f32[8,1024]{1,0:T(8,128)}) custom-call(bf16[1024,512]{1,0:T(8,128)(2,1)} %get-tuple-element.126.q_ref, bf16[1024,1024]{1,0:T(8,128)(2,1)} %get-tuple-element.77.kv_ref, s32[1,1024]{1,0:T(1,128)} %get-tuple-element.211.segq_ref, s32[1024,1]{1,0:T(8,128)} %copy.56.segk_ref), custom_call_target="tpu_custom_call" | custom-call | flops 4294967296 | bytes 3145728 | tf_op jit(solution)/shard_map/attend/pallas_call | solution.py:182
  113.7 3.6 project.1
  120.9 4.4 %first_norm.1 = (f32[512,768]{1,0:T(8,128)}, f32[512,128]{1,0:T(8,128)}, bf16[512,768]{1,0:T(8,128)(2,1)}, bf16[768,512]{1,0:T(8,128)(2,1)}, f32[8,768]{1,0:T(8,128)}) custom-call(bf16[512,768]{1,0:T(8,128)(2,1)} %fusion.9.own_ref.x_ref, f32[512,768]{1,0:T(8,128)} %get-tuple-element.84.own_ref, bf16[512,768]{1,0:T(8,128)(2,1)} %copy-done.17, ...), custom_call_target="tpu_custom_call" | custom-call | flops 7864320 | bytes 6291456 | tf_op jit(solution)/shard_map/first_norm/pallas_call | solution.py:340
  129.3 10.7 %collective-permute-done.21.rest_2_.rest_9_ = bf16[384,1152]{1,0:T(8,128)(2,1)S(1)} collective-permute-done((bf16[384,1152]{1,0:T(8,128)(2,1)}, bf16[384,1152]{1,0:T(8,128)(2,1)S(1)}, u32[]{:S(2)}, u32[]{:S(2)}) %collective-permute-start.21) | collective-permute-done | bytes 884768 | tf_op jit(solution)/shard_map/ppermute | solution.py:699
  146.5 5.3 %collective-permute-done.23.rest_3_.rest_13_ = bf16[192,1280]{1,0:T(8,128)(2,1)S(1)} collective-permute-done((bf16[192,1280]{1,0:T(8,128)(2,1)S(1)}, bf16[192,1280]{1,0:T(8,128)(2,1)S(1)}, u32[]{:S(2)}, u32[]{:S(2)}) %collective-permute-start.23) | collective-permute-done | bytes 491552 | tf_op jit(solution)/shard_map/ppermute | solution.py:699
  153.3 7.7 %mlp.4 = (bf16[2,3,512,384]{3,2,1,0:T(8,128)(2,1)}, f32[512,768]{1,0:T(8,128)}) custom-call(bf16[512,768]{1,0:T(8,128)(2,1)} %copy-done.44, bf16[384,1280]{1,0:T(8,128)(2,1)} %copy-done.1, bf16[384,1280]{1,0:T(8,128)(2,1)} %copy-done.2, bf16[384,1280]{1,0:T(8,128)(2,1)} %collective-permute-done.18.rest_2_.rest_12_, bf16[192,1280]{1,0:T(8,128)(2,1)} %copy-done.47, ...), custom_call_target="tpu_custom_call" | custom-call | flops 1811939328 | bytes 8847360 | tf_op jit(solution)/shard_map/mlp/pallas_call | solution.py:396
  161.3 8.1 %mlp.5 = (bf16[2,3,512,384]{3,2,1,0:T(8,128)(2,1)}, bf16[512,768]{1,0:T(8,128)(2,1)}) custom-call(bf16[512,768]{1,0:T(8,128)(2,1)} %copy-done.44, f32[512,768]{1,0:T(8,128)} %get-tuple-element.90.rest_0_, bf16[384,1152]{1,0:T(8,128)(2,1)} %pad_maximum_fusion.3.rest_1_.rest_8_, bf16[384,1152]{1,0:T(8,128)(2,1)} %copy-done.25, ...), custom_call_target="tpu_custom_call" | custom-call | flops 1811939328 | bytes 8847360 | tf_op jit(solution)/shard_map/mlp/pallas_call | solution.py:396
  169.5 1.9 fusion.11
  171.9 8.0 %mlp.6 = (bf16[2,3,512,384]{3,2,1,0:T(8,128)(2,1)}, f32[512,768]{1,0:T(8,128)}) custom-call(bf16[512,768]{1,0:T(8,128)(2,1)} %get-tuple-element.92.low_ref, bf16[384,1280]{1,0:T(8,128)(2,1)} %copy-done.1, bf16[384,1280]{1,0:T(8,128)(2,1)} %copy-done.2, bf16[384,1280]{1,0:T(8,128)(2,1)} %collective-permute-done.18.rest_2_.rest_12_, ...), custom_call_target="tpu_custom_call" | custom-call | flops 1811939328 | bytes 8847360 | tf_op jit(solution)/shard_map/mlp/pallas_call | solution.py:396
  182.9 8.1 %mlp.7 = (bf16[2,3,512,384]{3,2,1,0:T(8,128)(2,1)}, f32[512,768]{1,0:T(8,128)}) custom-call(bf16[512,768]{1,0:T(8,128)(2,1)} %get-tuple-element.92.low_ref, f32[512,768]{1,0:T(8,128)} %get-tuple-element.93.rest_0_, bf16[384,1152]{1,0:T(8,128)(2,1)} %pad_maximum_fusion.3.rest_1_.rest_8_, bf16[384,1152]{1,0:T(8,128)(2,1)} %copy-done.25, ...), custom_call_target="tpu_custom_call" | custom-call | flops 1811939328 | bytes 8847360 | tf_op jit(solution)/shard_map/mlp/pallas_call | solution.py:396
  191.9 6.1 %second_norm.1 = (bf16[512,768]{1,0:T(8,128)(2,1)}, f32[512,768]{1,0:T(8,128)}, bf16[512,768]{1,0:T(8,128)(2,1)}, bf16[768,512]{1,0:T(8,128)(2,1)}, f32[8,768]{1,0:T(8,128)}) custom-call(f32[512,768]{1,0:T(8,128)} %get-tuple-element.86.n_ref, f32[8,768]{1,0:T(8,128)} %get-tuple-element.87.gains_ref, f32[512,768]{1,0:T(8,128)} %get-tuple-element.94.feed_ref, ...), custom_call_target="tpu_custom_call" | custom-call | flops 15728640 | bytes 8650752 | tf_op jit(solution)/shard_map/second_norm/pallas_call | solution.py:433
  198.5 2.0 collective-permute-done.30.rest_1_
  202.6 19.2 %mlp_back.2 = (f32[512,768]{1,0:T(8,128)}, f32[512,768]{1,0:T(8,128)}, bf16[2,192,1152]{2,1,0:T(8,128)(2,1)}, bf16[2,192,1152]{2,1,0:T(8,128)(2,1)}, bf16[4,192,1152]{2,1,0:T(8,128)(2,1)}) custom-call(bf16[512,768]{1,0:T(8,128)(2,1)} %get-tuple-element.98.rest_0_, bf16[512,768]{1,0:T(8,128)(2,1)} %copy-done.45, bf16[768,512]{1,0:T(8,128)(2,1)} %get-tuple-element.99.rest_2_, ...), custom_call_target="tpu_custom_call" | custom-call | flops 7247757312 | bytes 29491200 | tf_op jit(solution)/shard_map/mlp_back/pallas_call | solution.py:522
  221.7 20.5 %mlp_back.3 = (f32[512,768]{1,0:T(8,128)}, bf16[512,768]{1,0:T(8,128)(2,1)}, bf16[2,192,1152]{2,1,0:T(8,128)(2,1)}, bf16[2,192,1152]{2,1,0:T(8,128)(2,1)}, bf16[4,192,1152]{2,1,0:T(8,128)(2,1)}) custom-call(bf16[512,768]{1,0:T(8,128)(2,1)} %get-tuple-element.98.rest_0_, bf16[512,768]{1,0:T(8,128)(2,1)} %copy-done.45, ...), custom_call_target="tpu_custom_call" | custom-call | flops 7247757312 | bytes 29491200 | tf_op jit(solution)/shard_map/mlp_back/pallas_call | solution.py:522
  246.4 1.7 convolution_convert_fusion.x_a_ref
  249.7 15.4 %collective-permute-done.40 = bf16[2,192,1152]{2,1,0:T(8,128)(2,1)} collective-permute-done((bf16[2,192,1152]{2,1,0:T(8,128)(2,1)}, bf16[2,192,1152]{2,1,0:T(8,128)(2,1)}, u32[]{:S(2)}, u32[]{:S(2)}) %collective-permute-start.40) | collective-permute-done | bytes 884768 | tf_op jit(solution)/shard_map/ppermute | solution.py:699
  266.7 2.3 fusion.31
  268.9 15.0 %collective-permute-done.33 = bf16[2,192,1152]{2,1,0:T(8,128)(2,1)S(1)} collective-permute-done((bf16[2,192,1152]{2,1,0:T(8,128)(2,1)}, bf16[2,192,1152]{2,1,0:T(8,128)(2,1)S(1)}, u32[]{:S(2)}, u32[]{:S(2)}) %collective-permute-start.33) | collective-permute-done | bytes 884768 | tf_op jit(solution)/shard_map/ppermute | solution.py:699
  287.4 5.4 %first_back.1 = (f32[512,768]{1,0:T(8,128)}, bf16[512,768]{1,0:T(8,128)(2,1)}, bf16[768,512]{1,0:T(8,128)(2,1)}, bf16[768,128]{1,0:T(8,128)(2,1)}) custom-call(f32[512,768]{1,0:T(8,128)} %get-tuple-element.106.base_ref, f32[512,768]{1,0:T(8,128)} %get-tuple-element.111.own_ref, bf16[512,768]{1,0:T(8,128)(2,1)} %collective-permute-done.35.came_ref, ...), custom_call_target="tpu_custom_call" | custom-call | flops 15728640 | bytes 7864320 | tf_op jit(solution)/shard_map/first_back/pallas_call | solution.py:573
  297.8 4.1 collective-permute-done.54
  302.0 1.8 fusion.22
  305.5 2.1 collective-permute-done.57
  307.6 2.2 collective-permute-start.56
  311.7 5.2 %collective-permute-done.55 = bf16[96,1152]{1,0:T(8,128)(2,1)S(1)} collective-permute-done((bf16[96,1152]{1,0:T(8,128)(2,1)S(1)}, bf16[96,1152]{1,0:T(8,128)(2,1)S(1)}, u32[]{:S(2)}, u32[]{:S(2)}) %collective-permute-start.55) | collective-permute-done | bytes 221216 | tf_op jit(solution)/shard_map/ppermute | solution.py:699
  316.8 6.9 %collective-permute-done.56 = bf16[96,1152]{1,0:T(8,128)(2,1)S(1)} collective-permute-done((bf16[96,1152]{1,0:T(8,128)(2,1)S(1)}, bf16[96,1152]{1,0:T(8,128)(2,1)S(1)}, u32[]{:S(2)}, u32[]{:S(2)}) %collective-permute-start.56) | collective-permute-done | bytes 221216 | tf_op jit(solution)/shard_map/ppermute | solution.py:699
  323.7 10.4 %collective-permute-start.58 = (bf16[96,1152]{1,0:T(8,128)(2,1)S(1)}, bf16[96,1152]{1,0:T(8,128)(2,1)S(1)}, u32[]{:S(2)}, u32[]{:S(2)}) collective-permute-start(bf16[96,1152]{1,0:T(8,128)(2,1)S(1)} %split.87), channel_id=1, source_target_pairs={{0,8},{1,9},{2,10},{3,11},{4,12},{5,13},{6,14},{7,15},{8,16},{9,17... | collective-permute-start | bytes 663560 | tf_op jit(solution)/shard_map/ppermute | solution.py:699
  335.3 8.5 %collective-permute-done.61 = bf16[96,1152]{1,0:T(8,128)(2,1)S(1)} collective-permute-done((bf16[96,1152]{1,0:T(8,128)(2,1)S(1)}, bf16[96,1152]{1,0:T(8,128)(2,1)S(1)}, u32[]{:S(2)}, u32[]{:S(2)}) %collective-permute-start.61) | collective-permute-done | bytes 221216 | tf_op jit(solution)/shard_map/ppermute | solution.py:699
  344.9 16.3 %attend_back.2 = (bf16[1024,256]{1,0:T(8,128)(2,1)}, bf16[1024,512]{1,0:T(8,128)(2,1)}) custom-call(bf16[1024,512]{1,0:T(8,128)(2,1)} %get-tuple-element.126.q_ref, bf16[1024,1024]{1,0:T(8,128)(2,1)} %get-tuple-element.77.kv_ref, bf16[512,768]{1,0:T(8,128)(2,1)} %get-tuple-element.116.own_ref, bf16[512,768]{1,0:T(8,128)(2,1)} %copy-done.39, ...), custom_call_target="tpu_custom_call" | custom-call | flops 10737418240 | bytes 7864320 | tf_op jit(solution)/shard_map/attend_back/pallas_call | solution.py:262
  362.1 7.5 %qkv_back.2 = (f32[512,768]{1,0:T(8,128)}, f32[512,768]{1,0:T(8,128)}, bf16[3,192,896]{2,1,0:T(8,128)(2,1)}, bf16[1,192,896]{2,1,0:T(8,128)(2,1)}) custom-call(bf16[1024,256]{1,0:T(8,128)(2,1)} %get-tuple-element.118.dq_ref, bf16[1024,512]{1,0:T(8,128)(2,1)} %get-tuple-element.119.dkv_ref, bf16[768,512]{1,0:T(8,128)(2,1)} %convolution_convert_fusion.x_a_ref, ...), custom_call_target="tpu_custom_call" | custom-call | flops 2617245696 | bytes 7864320 | tf_op jit(solution)/shard_map/qkv_back/pallas_call | solution.py:638
  372.6 16.3 %attend_back.3 = (bf16[1024,256]{1,0:T(8,128)(2,1)}, bf16[1024,512]{1,0:T(8,128)(2,1)}) custom-call(bf16[1024,512]{1,0:T(8,128)(2,1)} %get-tuple-element.126.q_ref, bf16[1024,1024]{1,0:T(8,128)(2,1)} %get-tuple-element.77.kv_ref, bf16[512,768]{1,0:T(8,128)(2,1)} %get-tuple-element.116.own_ref, bf16[512,768]{1,0:T(8,128)(2,1)} %copy-done.39, ...), custom_call_target="tpu_custom_call" | custom-call | flops 10737418240 | bytes 7864320 | tf_op jit(solution)/shard_map/attend_back/pallas_call | solution.py:262
  390.5 8.5 %qkv_back.3 = (f32[512,768]{1,0:T(8,128)}, bf16[512,768]{1,0:T(8,128)(2,1)}, bf16[1,192,896]{2,1,0:T(8,128)(2,1)}, bf16[3,192,896]{2,1,0:T(8,128)(2,1)}) custom-call(bf16[1024,256]{1,0:T(8,128)(2,1)} %get-tuple-element.128.dq_ref, bf16[1024,512]{1,0:T(8,128)(2,1)} %get-tuple-element.129.dkv_ref, bf16[768,512]{1,0:T(8,128)(2,1)} %convolution_convert_fusion.x_a_ref, ...), custom_call_target="tpu_custom_call" | custom-call | flops 2617245696 | bytes 7864320 | tf_op jit(solution)/shard_map/qkv_back/pallas_call | solution.py:638
  403.2 3.7 collective-permute-done.43
  406.9 1.7 collective-permute-start.46
  412.2 2.0 collective-permute-done.49
  414.2 4.8 %collective-permute-done.46 = bf16[192,896]{1,0:T(8,128)(2,1)S(1)} collective-permute-done((bf16[192,896]{1,0:T(8,128)(2,1)S(1)}, bf16[192,896]{1,0:T(8,128)(2,1)S(1)}, u32[]{:S(2)}, u32[]{:S(2)}) %collective-permute-start.46) | collective-permute-done | bytes 344096 | tf_op jit(solution)/shard_map/ppermute | solution.py:699
  424.2 7.1 %collective-permute-done.50 = bf16[96,896]{1,0:T(8,128)(2,1)S(1)} collective-permute-done((bf16[96,896]{1,0:T(8,128)(2,1)S(1)}, bf16[96,896]{1,0:T(8,128)(2,1)S(1)}, u32[]{:S(2)}, u32[]{:S(2)}) %collective-permute-start.50) | collective-permute-done | bytes 172064 | tf_op jit(solution)/shard_map/ppermute | solution.py:699
  431.4 2.4 collective-permute-done.47
  (286 shorter events, 93.2 us)
Async XLA Ops:
  2.7 18.6 %collective-permute-start.1 = (bf16[96,768]{1,0:T(8,128)(2,1)S(1)}, bf16[96,768]{1,0:T(8,128)(2,1)S(1)}, u32[]{:S(2)}, u32[]{:S(2)}) collective-permute-start(bf16[96,768]{1,0:T(8,128)(2,1)S(1)} %concatenate.57), channel_id=1, source_target_pairs={{0,24},{1,25},{2,26},{3,27},{4,28},{5,29},{6,30},{7,31},{8,0},{9,1... | collective-permute-start | bytes 442376 | tf_op jit(solution)/shard_map/ppermute | solution.py:699
  7.8 13.5 %collective-permute-start.2 = (bf16[96,768]{1,0:T(8,128)(2,1)S(1)}, bf16[96,768]{1,0:T(8,128)(2,1)S(1)}, u32[]{:S(2)}, u32[]{:S(2)}) collective-permute-start(bf16[96,768]{1,0:T(8,128)(2,1)S(1)} %concatenate.57), channel_id=1, source_target_pairs={{0,16},{1,17},{2,18},{3,19},{4,20},{5,21},{6,22},{7,23},{8,24},{9,... | collective-permute-start | bytes 442376 | tf_op jit(solution)/shard_map/ppermute | solution.py:699
  7.8 13.5 %collective-permute-start.3 = (bf16[96,768]{1,0:T(8,128)(2,1)S(1)}, bf16[96,768]{1,0:T(8,128)(2,1)S(1)}, u32[]{:S(2)}, u32[]{:S(2)}) collective-permute-start(bf16[96,768]{1,0:T(8,128)(2,1)S(1)} %concatenate.57), channel_id=1, source_target_pairs={{0,8},{1,9},{2,10},{3,11},{4,12},{5,13},{6,14},{7,15},{8,16},{9,17... | collective-permute-start | bytes 442376 | tf_op jit(solution)/shard_map/ppermute | solution.py:699
  10.0 17.1 %collective-permute-start = (bf16[256,768]{1,0:T(8,128)(2,1)S(1)}, bf16[256,768]{1,0:T(8,128)(2,1)S(1)}, u32[]{:S(2)}, u32[]{:S(2)}) collective-permute-start(bf16[256,768]{1,0:T(8,128)(2,1)S(1)} %get-tuple-element.177), channel_id=1, source_target_pairs={{0,2},{1,3},{2,0},{3,1},{4,6},{5,7},{6,4},{7,5},{8,10},{9,11},{10,... | collective-permute-start | bytes 1179656 | tf_op jit(solution)/shard_map/ppermute | solution.py:699
  24.5 22.6 %collective-permute-start.5 = (bf16[96,1280]{1,0:T(8,128)(2,1)S(1)}, bf16[96,1280]{1,0:T(8,128)(2,1)S(1)}, u32[]{:S(2)}, u32[]{:S(2)}) collective-permute-start(bf16[96,1280]{1,0:T(8,128)(2,1)S(1)} %fusion.44), channel_id=1, source_target_pairs={{0,16},{1,17},{2,18},{3,19},{4,20},{5,21},{6,22},{7,23},{8,24},{9,... | collective-permute-start | bytes 737288 | tf_op jit(solution)/shard_map/ppermute | solution.py:699
  25.4 21.8 %collective-permute-start.6 = (bf16[96,1280]{1,0:T(8,128)(2,1)S(1)}, bf16[96,1280]{1,0:T(8,128)(2,1)S(1)}, u32[]{:S(2)}, u32[]{:S(2)}) collective-permute-start(bf16[96,1280]{1,0:T(8,128)(2,1)S(1)} %fusion.44), channel_id=1, source_target_pairs={{0,8},{1,9},{2,10},{3,11},{4,12},{5,13},{6,14},{7,15},{8,16},{9,17... | collective-permute-start | bytes 737288 | tf_op jit(solution)/shard_map/ppermute | solution.py:699
  25.6 21.6 %collective-permute-start.7 = (bf16[384,768]{1,0:T(8,128)(2,1)S(1)}, bf16[384,768]{1,0:T(8,128)(2,1)S(1)}, u32[]{:S(2)}, u32[]{:S(2)}) collective-permute-start(bf16[384,768]{1,0:T(8,128)(2,1)S(1)} %pad_maximum_fusion.6.rest_0_.rest_2_.rest_4_), channel_id=1, source_target_pairs={{0,4},{1,5},{2,6},{3,7},{4,0},{5,1},{6,2},{7,3},{8,12},{9,13},{10,... | collective-permute-start | bytes 1769480 | tf_op jit(solution)/shard_map/ppermute | solution.py:699
  27.1 20.1 %collective-permute-start.8 = (bf16[384,768]{1,0:T(8,128)(2,1)S(1)}, bf16[384,768]{1,0:T(8,128)(2,1)S(1)}, u32[]{:S(2)}, u32[]{:S(2)}) collective-permute-start(bf16[384,768]{1,0:T(8,128)(2,1)S(1)} %pad_maximum_fusion.6.rest_0_.rest_2_.rest_4_), channel_id=1, source_target_pairs={{0,2},{1,3},{2,0},{3,1},{4,6},{5,7},{6,4},{7,5},{8,10},{9,11},{10,... | collective-permute-start | bytes 1769480 | tf_op jit(solution)/shard_map/ppermute | solution.py:699
  31.0 51.8 %collective-permute-start.9 = (bf16[512,768]{1,0:T(8,128)(2,1)}, bf16[512,768]{1,0:T(8,128)(2,1)}, u32[]{:S(2)}, u32[]{:S(2)}) collective-permute-start(bf16[512,768]{1,0:T(8,128)(2,1)} %fusion.9.own_ref.x_ref), channel_id=1, source_target_pairs={{0,1},{1,0},{2,3},{3,2},{4,5},{5,4},{6,7},{7,6},{8,9},{9,8},{10,11... | collective-permute-start | bytes 2359304 | tf_op jit(solution)/shard_map/ppermute | solution.py:699
  47.4 20.7 %collective-permute-start.15 = (bf16[96,1152]{1,0:T(8,128)(2,1)S(1)}, bf16[96,1152]{1,0:T(8,128)(2,1)S(1)}, u32[]{:S(2)}, u32[]{:S(2)}) collective-permute-start(bf16[96,1152]{1,0:T(8,128)(2,1)S(1)} %pad_maximum_fusion.13), channel_id=1, source_target_pairs={{0,16},{1,17},{2,18},{3,19},{4,20},{5,21},{6,22},{7,23},{8,24},{9,... | collective-permute-start | bytes 663560 | tf_op jit(solution)/shard_map/ppermute | solution.py:699
  48.9 20.6 %collective-permute-start.16 = (bf16[96,1152]{1,0:T(8,128)(2,1)S(1)}, bf16[96,1152]{1,0:T(8,128)(2,1)S(1)}, u32[]{:S(2)}, u32[]{:S(2)}) collective-permute-start(bf16[96,1152]{1,0:T(8,128)(2,1)S(1)} %pad_maximum_fusion.13), channel_id=1, source_target_pairs={{0,8},{1,9},{2,10},{3,11},{4,12},{5,13},{6,14},{7,15},{8,16},{9,17... | collective-permute-start | bytes 663560 | tf_op jit(solution)/shard_map/ppermute | solution.py:699
  51.4 50.9 %collective-permute-start.17 = (bf16[384,1280]{1,0:T(8,128)(2,1)S(1)}, bf16[384,1280]{1,0:T(8,128)(2,1)S(1)}, u32[]{:S(2)}, u32[]{:S(2)}) collective-permute-start(bf16[384,1280]{1,0:T(8,128)(2,1)S(1)} %pad_maximum_fusion.2.norm_a_ref.rest_0_.rest_10_), channel_id=1, source_target_pairs={{0,4},{1,5},{2,6},{3,7},{4,0},{5,1},{6,2},{7,3},{8,12},{9,13},{10,... | collective-permute-start | bytes 2949128 | tf_op jit(solution)/shard_map/ppermute | solution.py:699
  54.8 47.5 %collective-permute-start.18 = (bf16[384,1280]{1,0:T(8,128)(2,1)S(1)}, bf16[384,1280]{1,0:T(8,128)(2,1)}, u32[]{:S(2)}, u32[]{:S(2)}) collective-permute-start(bf16[384,1280]{1,0:T(8,128)(2,1)S(1)} %pad_maximum_fusion.2.norm_a_ref.rest_0_.rest_10_), channel_id=1, source_target_pairs={{0,2},{1,3},{2,0},{3,1},{4,6},{5,7},{6,4},{7,5},{8,10},{9,11},{10,... | collective-permute-start | bytes 2949128 | tf_op jit(solution)/shard_map/ppermute | solution.py:699
  68.0 14.7 %collective-permute-start.12 = (bf16[192,768]{1,0:T(8,128)(2,1)}, bf16[192,768]{1,0:T(8,128)(2,1)}, u32[]{:S(2)}, u32[]{:S(2)}) collective-permute-start(bf16[192,768]{1,0:T(8,128)(2,1)} %slice.260), channel_id=1, source_target_pairs={{0,2},{1,3},{2,0},{3,1},{4,6},{5,7},{6,4},{7,5},{8,10},{9,11},{10,... | collective-permute-start | bytes 884744 | tf_op jit(solution)/shard_map/ppermute | solution.py:699
  69.6 13.2 %collective-permute-start.13 = (bf16[192,768]{1,0:T(8,128)(2,1)}, bf16[192,768]{1,0:T(8,128)(2,1)}, u32[]{:S(2)}, u32[]{:S(2)}) collective-permute-start(bf16[192,768]{1,0:T(8,128)(2,1)} %slice.261), channel_id=1, source_target_pairs={{0,4},{1,5},{2,6},{3,7},{4,0},{5,1},{6,2},{7,3},{8,12},{9,13},{10,... | collective-permute-start | bytes 884744 | tf_op jit(solution)/shard_map/ppermute | solution.py:699
  117.3 22.7 %collective-permute-start.21 = (bf16[384,1152]{1,0:T(8,128)(2,1)}, bf16[384,1152]{1,0:T(8,128)(2,1)S(1)}, u32[]{:S(2)}, u32[]{:S(2)}) collective-permute-start(bf16[384,1152]{1,0:T(8,128)(2,1)} %pad_maximum_fusion.3.rest_1_.rest_8_), channel_id=1, source_target_pairs={{0,4},{1,5},{2,6},{3,7},{4,0},{5,1},{6,2},{7,3},{8,12},{9,13},{10,... | collective-permute-start | bytes 2654216 | tf_op jit(solution)/shard_map/ppermute | solution.py:699
  118.5 23.1 %collective-permute-start.22 = (bf16[384,1152]{1,0:T(8,128)(2,1)}, bf16[384,1152]{1,0:T(8,128)(2,1)}, u32[]{:S(2)}, u32[]{:S(2)}) collective-permute-start(bf16[384,1152]{1,0:T(8,128)(2,1)} %pad_maximum_fusion.3.rest_1_.rest_8_), channel_id=1, source_target_pairs={{0,2},{1,3},{2,0},{3,1},{4,6},{5,7},{6,4},{7,5},{8,10},{9,11},{10,... | collective-permute-start | bytes 2654216 | tf_op jit(solution)/shard_map/ppermute | solution.py:699
  125.4 20.2 %collective-permute-start.20 = (bf16[512,768]{1,0:T(8,128)(2,1)}, bf16[512,768]{1,0:T(8,128)(2,1)S(1)}, u32[]{:S(2)}, u32[]{:S(2)}) collective-permute-start(bf16[512,768]{1,0:T(8,128)(2,1)} %get-tuple-element.92.low_ref), channel_id=1, source_target_pairs={{0,1},{1,0},{2,3},{3,2},{4,5},{5,4},{6,7},{7,6},{8,9},{9,8},{10,11... | collective-permute-start | bytes 2359304 | tf_op jit(solution)/shard_map/ppermute | solution.py:699
  125.4 26.3 %collective-permute-start.23 = (bf16[192,1280]{1,0:T(8,128)(2,1)S(1)}, bf16[192,1280]{1,0:T(8,128)(2,1)S(1)}, u32[]{:S(2)}, u32[]{:S(2)}) collective-permute-start(bf16[192,1280]{1,0:T(8,128)(2,1)S(1)} %slice.264), channel_id=1, source_target_pairs={{0,2},{1,3},{2,0},{3,1},{4,6},{5,7},{6,4},{7,5},{8,10},{9,11},{10,... | collective-permute-start | bytes 1474568 | tf_op jit(solution)/shard_map/ppermute | solution.py:699
  128.0 23.8 %collective-permute-start.24 = (bf16[192,1280]{1,0:T(8,128)(2,1)S(1)}, bf16[192,1280]{1,0:T(8,128)(2,1)S(1)}, u32[]{:S(2)}, u32[]{:S(2)}) collective-permute-start(bf16[192,1280]{1,0:T(8,128)(2,1)S(1)} %slice.265), channel_id=1, source_target_pairs={{0,4},{1,5},{2,6},{3,7},{4,0},{5,1},{6,2},{7,3},{8,12},{9,13},{10,... | collective-permute-start | bytes 1474568 | tf_op jit(solution)/shard_map/ppermute | solution.py:699
  140.0 21.3 %collective-permute-start.25 = (bf16[192,1152]{1,0:T(8,128)(2,1)S(1)}, bf16[192,1152]{1,0:T(8,128)(2,1)}, u32[]{:S(2)}, u32[]{:S(2)}) collective-permute-start(bf16[192,1152]{1,0:T(8,128)(2,1)S(1)} %slice.266), channel_id=1, source_target_pairs={{0,2},{1,3},{2,0},{3,1},{4,6},{5,7},{6,4},{7,5},{8,10},{9,11},{10,... | collective-permute-start | bytes 1327112 | tf_op jit(solution)/shard_map/ppermute | solution.py:699
  142.6 18.7 %collective-permute-start.26 = (bf16[192,1152]{1,0:T(8,128)(2,1)S(1)}, bf16[192,1152]{1,0:T(8,128)(2,1)}, u32[]{:S(2)}, u32[]{:S(2)}) collective-permute-start(bf16[192,1152]{1,0:T(8,128)(2,1)S(1)} %slice.267), channel_id=1, source_target_pairs={{0,4},{1,5},{2,6},{3,7},{4,0},{5,1},{6,2},{7,3},{8,12},{9,13},{10,... | collective-permute-start | bytes 1327112 | tf_op jit(solution)/shard_map/ppermute | solution.py:699
  145.6 34.3 %collective-permute-start.28 = (bf16[256,768]{1,0:T(8,128)(2,1)S(1)}, bf16[256,768]{1,0:T(8,128)(2,1)}, u32[]{:S(2)}, u32[]{:S(2)}) collective-permute-start(bf16[256,768]{1,0:T(8,128)(2,1)S(1)} %fusion.36), channel_id=1, source_target_pairs={{0,2},{1,3},{2,0},{3,1},{4,6},{5,7},{6,4},{7,5},{8,10},{9,11},{10,... | collective-permute-start | bytes 1179656 | tf_op jit(solution)/shard_map/ppermute | solution.py:699
  169.4 21.6 %collective-permute-start.27 = (bf16[512,768]{1,0:T(8,128)(2,1)}, bf16[512,768]{1,0:T(8,128)(2,1)S(1)}, u32[]{:S(2)}, u32[]{:S(2)}) collective-permute-start(bf16[512,768]{1,0:T(8,128)(2,1)} %get-tuple-element.91), channel_id=1, source_target_pairs={{0,1},{1,0},{2,3},{3,2},{4,5},{5,4},{6,7},{7,6},{8,9},{9,8},{10,11... | collective-permute-start | bytes 2359304 | tf_op jit(solution)/shard_map/ppermute | solution.py:699
  171.4 27.1 %collective-permute-start.32 = (bf16[768,512]{1,0:T(8,128)(2,1)S(1)}, bf16[768,512]{1,0:T(8,128)(2,1)S(1)}, u32[]{:S(2)}, u32[]{:S(2)}) collective-permute-start(bf16[768,512]{1,0:T(8,128)(2,1)S(1)} %copy-done.40), channel_id=1, source_target_pairs={{0,1},{1,0},{2,3},{3,2},{4,5},{5,4},{6,7},{7,6},{8,9},{9,8},{10,11... | collective-permute-start | bytes 2359304 | tf_op jit(solution)/shard_map/ppermute | solution.py:699
  242.2 22.9 %collective-permute-start.40 = (bf16[2,192,1152]{2,1,0:T(8,128)(2,1)}, bf16[2,192,1152]{2,1,0:T(8,128)(2,1)}, u32[]{:S(2)}, u32[]{:S(2)}) collective-permute-start(bf16[2,192,1152]{2,1,0:T(8,128)(2,1)} %get-tuple-element.124), channel_id=1, source_target_pairs={{0,2},{1,3},{2,0},{3,1},{4,6},{5,7},{6,4},{7,5},{8,10},{9,11},{10,... | collective-permute-start | bytes 2654216 | tf_op jit(solution)/shard_map/ppermute | solution.py:699
  243.8 22.9 %collective-permute-start.41 = (bf16[2,192,1152]{2,1,0:T(8,128)(2,1)}, bf16[2,192,1152]{2,1,0:T(8,128)(2,1)}, u32[]{:S(2)}, u32[]{:S(2)}) collective-permute-start(bf16[2,192,1152]{2,1,0:T(8,128)(2,1)} %get-tuple-element.125), channel_id=1, source_target_pairs={{0,4},{1,5},{2,6},{3,7},{4,0},{5,1},{6,2},{7,3},{8,12},{9,13},{10,... | collective-permute-start | bytes 2654216 | tf_op jit(solution)/shard_map/ppermute | solution.py:699
  244.6 39.3 %collective-permute-start.33 = (bf16[2,192,1152]{2,1,0:T(8,128)(2,1)}, bf16[2,192,1152]{2,1,0:T(8,128)(2,1)S(1)}, u32[]{:S(2)}, u32[]{:S(2)}) collective-permute-start(bf16[2,192,1152]{2,1,0:T(8,128)(2,1)} %get-tuple-element.104), channel_id=1, source_target_pairs={{0,2},{1,3},{2,0},{3,1},{4,6},{5,7},{6,4},{7,5},{8,10},{9,11},{10,... | collective-permute-start | bytes 2654216 | tf_op jit(solution)/shard_map/ppermute | solution.py:699
  245.1 39.6 %collective-permute-start.34 = (bf16[2,192,1152]{2,1,0:T(8,128)(2,1)}, bf16[2,192,1152]{2,1,0:T(8,128)(2,1)S(1)}, u32[]{:S(2)}, u32[]{:S(2)}) collective-permute-start(bf16[2,192,1152]{2,1,0:T(8,128)(2,1)} %get-tuple-element.105), channel_id=1, source_target_pairs={{0,4},{1,5},{2,6},{3,7},{4,0},{5,1},{6,2},{7,3},{8,12},{9,13},{10,... | collective-permute-start | bytes 2654216 | tf_op jit(solution)/shard_map/ppermute | solution.py:699
  248.1 113.2 %collective-permute-start.37 = (bf16[768,512]{1,0:T(8,128)(2,1)}, bf16[768,512]{1,0:T(8,128)(2,1)}, u32[]{:S(2)}, u32[]{:S(2)}) collective-permute-start(bf16[768,512]{1,0:T(8,128)(2,1)} %convolution_convert_fusion.x_a_ref), channel_id=1, source_target_pairs={{0,1},{1,0},{2,3},{3,2},{4,5},{5,4},{6,7},{7,6},{8,9},{9,8},{10,11... | collective-permute-start | bytes 2359304 | tf_op jit(solution)/shard_map/ppermute | solution.py:699
  265.1 27.8 %collective-permute-start.29 = (bf16[256,768]{1,0:T(8,128)(2,1)}, bf16[256,768]{1,0:T(8,128)(2,1)}, u32[]{:S(2)}, u32[]{:S(2)}) collective-permute-start(bf16[256,768]{1,0:T(8,128)(2,1)} %slice.269), channel_id=1, source_target_pairs={{0,2},{1,3},{2,0},{3,1},{4,6},{5,7},{6,4},{7,5},{8,10},{9,11},{10,... | collective-permute-start | bytes 1179656 | tf_op jit(solution)/shard_map/ppermute | solution.py:699
  266.7 20.8 %collective-permute-start.35 = (bf16[512,768]{1,0:T(8,128)(2,1)S(1)}, bf16[512,768]{1,0:T(8,128)(2,1)}, u32[]{:S(2)}, u32[]{:S(2)}) collective-permute-start(bf16[512,768]{1,0:T(8,128)(2,1)S(1)} %copy-done.42), channel_id=1, source_target_pairs={{0,1},{1,0},{2,3},{3,2},{4,5},{5,4},{6,7},{7,6},{8,9},{9,8},{10,11... | collective-permute-start | bytes 2359304 | tf_op jit(solution)/shard_map/ppermute | solution.py:699
  284.0 13.9 %collective-permute-start.52 = (bf16[192,1152]{1,0:T(8,128)(2,1)}, bf16[192,1152]{1,0:T(8,128)(2,1)}, u32[]{:S(2)}, u32[]{:S(2)}) collective-permute-start(bf16[192,1152]{1,0:T(8,128)(2,1)} %get-tuple-element.169), channel_id=1, source_target_pairs={{0,4},{1,5},{2,6},{3,7},{4,0},{5,1},{6,2},{7,3},{8,12},{9,13},{10,... | collective-permute-start | bytes 1327112 | tf_op jit(solution)/shard_map/ppermute | solution.py:699
  284.8 17.2 %collective-permute-start.54 = (bf16[192,1152]{1,0:T(8,128)(2,1)}, bf16[192,1152]{1,0:T(8,128)(2,1)}, u32[]{:S(2)}, u32[]{:S(2)}) collective-permute-start(bf16[192,1152]{1,0:T(8,128)(2,1)} %get-tuple-element.168), channel_id=1, source_target_pairs={{0,2},{1,3},{2,0},{3,1},{4,6},{5,7},{6,4},{7,5},{8,10},{9,11},{10,... | collective-permute-start | bytes 1327112 | tf_op jit(solution)/shard_map/ppermute | solution.py:699
  295.2 12.4 %collective-permute-start.57 = (bf16[192,1152]{1,0:T(8,128)(2,1)S(1)}, bf16[192,1152]{1,0:T(8,128)(2,1)S(1)}, u32[]{:S(2)}, u32[]{:S(2)}) collective-permute-start(bf16[192,1152]{1,0:T(8,128)(2,1)S(1)} %copy-done.21), channel_id=1, source_target_pairs={{0,4},{1,5},{2,6},{3,7},{4,0},{5,1},{6,2},{7,3},{8,12},{9,13},{10,... | collective-permute-start | bytes 1327112 | tf_op jit(solution)/shard_map/ppermute | solution.py:699
  296.4 14.1 %collective-permute-start.59 = (bf16[192,1152]{1,0:T(8,128)(2,1)S(1)}, bf16[192,1152]{1,0:T(8,128)(2,1)S(1)}, u32[]{:S(2)}, u32[]{:S(2)}) collective-permute-start(bf16[192,1152]{1,0:T(8,128)(2,1)S(1)} %copy-done.20), channel_id=1, source_target_pairs={{0,2},{1,3},{2,0},{3,1},{4,6},{5,7},{6,4},{7,5},{8,10},{9,11},{10,... | collective-permute-start | bytes 1327112 | tf_op jit(solution)/shard_map/ppermute | solution.py:699
  297.8 46.2 %collective-permute-start.36 = (bf16[512,768]{1,0:T(8,128)(2,1)S(1)}, bf16[512,768]{1,0:T(8,128)(2,1)S(1)}, u32[]{:S(2)}, u32[]{:S(2)}) collective-permute-start(bf16[512,768]{1,0:T(8,128)(2,1)S(1)} %copy-done.38), channel_id=1, source_target_pairs={{0,1},{1,0},{2,3},{3,2},{4,5},{5,4},{6,7},{7,6},{8,9},{9,8},{10,11... | collective-permute-start | bytes 2359304 | tf_op jit(solution)/shard_map/ppermute | solution.py:699
  303.8 13.0 %collective-permute-start.55 = (bf16[96,1152]{1,0:T(8,128)(2,1)S(1)}, bf16[96,1152]{1,0:T(8,128)(2,1)S(1)}, u32[]{:S(2)}, u32[]{:S(2)}) collective-permute-start(bf16[96,1152]{1,0:T(8,128)(2,1)S(1)} %get-tuple-element.184), channel_id=1, source_target_pairs={{0,16},{1,17},{2,18},{3,19},{4,20},{5,21},{6,22},{7,23},{8,24},{9,... | collective-permute-start | bytes 663560 | tf_op jit(solution)/shard_map/ppermute | solution.py:699
  307.6 16.1 %collective-permute-start.56 = (bf16[96,1152]{1,0:T(8,128)(2,1)S(1)}, bf16[96,1152]{1,0:T(8,128)(2,1)S(1)}, u32[]{:S(2)}, u32[]{:S(2)}) collective-permute-start(bf16[96,1152]{1,0:T(8,128)(2,1)S(1)} %get-tuple-element.185), channel_id=1, source_target_pairs={{0,24},{1,25},{2,26},{3,27},{4,28},{5,29},{6,30},{7,31},{8,0},{9,1... | collective-permute-start | bytes 663560 | tf_op jit(solution)/shard_map/ppermute | solution.py:699
  310.5 13.2 %collective-permute-start.53 = (bf16[96,1152]{1,0:T(8,128)(2,1)S(1)}, bf16[96,1152]{1,0:T(8,128)(2,1)S(1)}, u32[]{:S(2)}, u32[]{:S(2)}) collective-permute-start(bf16[96,1152]{1,0:T(8,128)(2,1)S(1)} %split.88), channel_id=1, source_target_pairs={{0,8},{1,9},{2,10},{3,11},{4,12},{5,13},{6,14},{7,15},{8,16},{9,17... | collective-permute-start | bytes 663560 | tf_op jit(solution)/shard_map/ppermute | solution.py:699
  316.8 18.5 %collective-permute-start.60 = (bf16[96,1152]{1,0:T(8,128)(2,1)S(1)}, bf16[96,1152]{1,0:T(8,128)(2,1)S(1)}, u32[]{:S(2)}, u32[]{:S(2)}) collective-permute-start(bf16[96,1152]{1,0:T(8,128)(2,1)S(1)} %get-tuple-element.186), channel_id=1, source_target_pairs={{0,16},{1,17},{2,18},{3,19},{4,20},{5,21},{6,22},{7,23},{8,24},{9,... | collective-permute-start | bytes 663560 | tf_op jit(solution)/shard_map/ppermute | solution.py:699
  323.7 20.1 %collective-permute-start.61 = (bf16[96,1152]{1,0:T(8,128)(2,1)S(1)}, bf16[96,1152]{1,0:T(8,128)(2,1)S(1)}, u32[]{:S(2)}, u32[]{:S(2)}) collective-permute-start(bf16[96,1152]{1,0:T(8,128)(2,1)S(1)} %get-tuple-element.187), channel_id=1, source_target_pairs={{0,24},{1,25},{2,26},{3,27},{4,28},{5,29},{6,30},{7,31},{8,0},{9,1... | collective-permute-start | bytes 663560 | tf_op jit(solution)/shard_map/ppermute | solution.py:699
  323.7 20.1 %collective-permute-start.58 = (bf16[96,1152]{1,0:T(8,128)(2,1)S(1)}, bf16[96,1152]{1,0:T(8,128)(2,1)S(1)}, u32[]{:S(2)}, u32[]{:S(2)}) collective-permute-start(bf16[96,1152]{1,0:T(8,128)(2,1)S(1)} %split.87), channel_id=1, source_target_pairs={{0,8},{1,9},{2,10},{3,11},{4,12},{5,13},{6,14},{7,15},{8,16},{9,17... | collective-permute-start | bytes 663560 | tf_op jit(solution)/shard_map/ppermute | solution.py:699
  335.3 25.9 %collective-permute-start.38 = (bf16[768,512]{1,0:T(8,128)(2,1)S(1)}, bf16[768,512]{1,0:T(8,128)(2,1)S(1)}, u32[]{:S(2)}, u32[]{:S(2)}) collective-permute-start(bf16[768,512]{1,0:T(8,128)(2,1)S(1)} %copy-done.15), channel_id=1, source_target_pairs={{0,1},{1,0},{2,3},{3,2},{4,5},{5,4},{6,7},{7,6},{8,9},{9,8},{10,11... | collective-permute-start | bytes 2359304 | tf_op jit(solution)/shard_map/ppermute | solution.py:699
  371.8 30.5 %collective-permute-start.44 = (bf16[1,192,896]{2,1,0:T(8,128)(2,1)S(1)}, bf16[1,192,896]{2,1,0:T(8,128)(2,1)S(1)}, u32[]{:S(2)}, u32[]{:S(2)}) collective-permute-start(bf16[1,192,896]{2,1,0:T(8,128)(2,1)S(1)} %slice.229), channel_id=1, source_target_pairs={{0,4},{1,5},{2,6},{3,7},{4,0},{5,1},{6,2},{7,3},{8,12},{9,13},{10,... | collective-permute-start | bytes 1032200 | tf_op jit(solution)/shard_map/ppermute | solution.py:699
  388.9 17.9 %collective-permute-start.43 = (bf16[2,192,896]{2,1,0:T(8,128)(2,1)S(1)}, bf16[2,192,896]{2,1,0:T(8,128)(2,1)S(1)}, u32[]{:S(2)}, u32[]{:S(2)}) collective-permute-start(bf16[2,192,896]{2,1,0:T(8,128)(2,1)S(1)} %slice.227), channel_id=1, source_target_pairs={{0,2},{1,3},{2,0},{3,1},{4,6},{5,7},{6,4},{7,5},{8,10},{9,11},{10,... | collective-permute-start | bytes 2064392 | tf_op jit(solution)/shard_map/ppermute | solution.py:699
  410.7 12.2 %collective-permute-start.45 = (bf16[256,768]{1,0:T(8,128)(2,1)S(1)}, bf16[256,768]{1,0:T(8,128)(2,1)S(1)}, u32[]{:S(2)}, u32[]{:S(2)}) collective-permute-start(bf16[256,768]{1,0:T(8,128)(2,1)S(1)} %slice.330), channel_id=1, source_target_pairs={{0,2},{1,3},{2,0},{3,1},{4,6},{5,7},{6,4},{7,5},{8,10},{9,11},{10,... | collective-permute-start | bytes 1179656 | tf_op jit(solution)/shard_map/ppermute | solution.py:699
  419.3 12.1 %collective-permute-start.50 = (bf16[96,896]{1,0:T(8,128)(2,1)S(1)}, bf16[96,896]{1,0:T(8,128)(2,1)S(1)}, u32[]{:S(2)}, u32[]{:S(2)}) collective-permute-start(bf16[96,896]{1,0:T(8,128)(2,1)S(1)} %get-tuple-element.196), channel_id=1, source_target_pairs={{0,16},{1,17},{2,18},{3,19},{4,20},{5,21},{6,22},{7,23},{8,24},{9,... | collective-permute-start | bytes 516104 | tf_op jit(solution)/shard_map/ppermute | solution.py:699
  (67 other events, 590.4 us)

commit v6 on v5

--- a/solution.py
+++ b/solution.py
@@ -549,7 +549,7 @@
 
 
 def first_back_kernel(
-    base_ref, own_ref, came_ref, n_ref, s_ref, gains_ref, sums_ref, dh_ref, low_ref, low_t_ref, cols_ref
+    base_ref, own_ref, came_ref, n_ref, s_ref, gains_ref, sums_ref, dh_ref, low_ref, low_t_ref
 ):
     dfirst = base_ref[...] + own_ref[...] + came_ref[...].astype(f32)
     normed = n_ref[...]
@@ -560,11 +560,12 @@
     stacked = jnp.concatenate(
         [gain_sum, sums[1:2], bias_sum, sums[3:4], jnp.zeros((124, width), f32)], axis=0
     )
-    cols_ref[...] = stacked.T.astype(bf16)
+    rows = dfirst.shape[0]
+    low_t_ref[:, rows:] = stacked.T.astype(bf16)
     dh = norm_back(dfirst * gains_ref[0:1], normed, s_ref[:, 0:1])
     dh_ref[...] = dh
     low_ref[...] = dh.astype(bf16)
-    low_t_ref[...] = dh.T.astype(bf16)
+    low_t_ref[:, :rows] = dh.T.astype(bf16)
 
 
 def first_back(base, own, came, n1, s1, gains, sums):
@@ -574,12 +575,11 @@
         first_back_kernel,
         grid=(1,),
         in_specs=[full] * 4 + [whole((rows, 128)), whole((8, width)), whole((8, width))],
-        out_specs=[full, full, whole((width, rows)), whole((width, 128))],
+        out_specs=[full, full, whole((width, rows + 128))],
         out_shape=[
             jax.ShapeDtypeStruct((rows, width), f32),
             jax.ShapeDtypeStruct((rows, width), bf16),
-            jax.ShapeDtypeStruct((width, rows), bf16),
-            jax.ShapeDtypeStruct((width, 128), bf16),
+            jax.ShapeDtypeStruct((width, rows + 128), bf16),
         ],
         cost_estimate=cost(40 * rows * width, 20 * rows * width),
         name="first_back",
@@ -587,7 +587,7 @@
 
 
 def qkv_back_kernel(
-    quarter, has_base, dq_ref, dkv_ref, x_a_ref, x_b_ref, low_a_ref, low_b_ref, att_ref, cols_ref, *rest
+    quarter, has_base, dq_ref, dkv_ref, x_a_ref, x_b_ref, low_a_ref, low_b_ref, cols_a_ref, cols_b_ref, att_ref, *rest
 ):
     if has_base:
         bases, rest = rest[:2], rest[2:]
@@ -614,7 +614,8 @@
         piece = dot(x_a_ref[...], source[:rows, at : at + part]) + dot(x_b_ref[...], source[rows:, at : at + part])
         moved = pltpu.roll(d_out, (3 - h) * HD, 1)
         emit(jnp.where(lane < 3 * HD, piece, moved).astype(bf16), slice(h * part, (h + 1) * part))
-    emit(cols_ref[...], slice(3 * part, 3 * part + 128))
+    cols = cols_a_ref[...].astype(f32) + cols_b_ref[...].astype(f32)
+    emit(cols.astype(bf16), slice(3 * part, 3 * part + 128))
     pltpu.make_async_copy(w_ref, w_ref, sem).wait()
     for i, out_ref in enumerate((own_ref, other_ref)):
         span = slice(i * rows, (i + 1) * rows)
@@ -624,9 +625,9 @@
         out_ref[...] = total.astype(out_ref.dtype)
 
 
-def qkv_back(quarter, bases, dq, dkv, x_t, low_t, att, cols, blocks):
+def qkv_back(quarter, bases, dq, dkv, x_t, low_t, att, blocks):
     rows = dq.shape[0] // 2
-    width = cols.shape[0]
+    width = low_t[0].shape[0]
     part = dq.shape[1]
     has_base = bases is not None
     full = whole((rows, width))
@@ -640,7 +641,8 @@
         grid=(1,),
         in_specs=[whole(dq.shape), whole(dkv.shape)]
         + [turned] * 4
-        + [whole(att.shape), whole((width, 128))]
+        + [pl.BlockSpec((width, 128), lambda i: (0, rows // 128))] * 2
+        + [whole(att.shape)]
         + [full] * (2 * has_base)
         + [ANY] * 3,
         out_specs=[full, full] + [whole(p) for p in pieces],
@@ -652,7 +654,7 @@
         + [jax.ShapeDtypeStruct(p, bf16) for p in pieces],
         cost_estimate=cost(26 * rows * width * part, 40 * width * part),
         name="qkv_back",
-    )(dq, dkv, *x_t, *low_t, att, cols, *(bases if has_base else ()), *blocks)
+    )(dq, dkv, *x_t, *low_t, *low_t, att, *(bases if has_base else ()), *blocks)
 
 
 def factors_of(n):
@@ -722,15 +724,17 @@
             )
         return block
 
-    def ring_scatter(self, block):
+    def ring_pieces(self, block, axis):
+        pieces = jnp.split(block, self.digits[axis], axis=0)
+        return pieces[0], [p.astype(bf16) for p in pieces[1:]]
+
+    def ring_scatter(self, own, low):
         for axis in range(len(self.digits)):
-            size = self.digits[axis]
-            pieces = jnp.split(block, size, axis=0)
-            low = [p.astype(bf16) for p in pieces[1:]]
-            block = pieces[0]
-            for d in range(1, size):
-                block = block + self.shift(low[d - 1], axis, d).astype(f32)
-        return block
+            if axis > 0:
+                own, low = self.ring_pieces(own, axis)
+            for d, piece in enumerate(low, 1):
+                own = own + self.shift(piece, axis, d).astype(f32)
+        return own
 
 
 def tie(value, *others):
@@ -753,11 +757,11 @@
     def third(self):
         low = self.keep[0].astype(f32) + self.by_y[0].astype(f32) + self.late_x.astype(f32)
         high = self.keep[1].astype(f32) + self.by_x[0][0].astype(f32) + self.late_y.astype(f32)
-        self.block = jnp.concatenate([low, high], axis=0)
-        return self.block
+        self.own, self.low = self.links.ring_pieces(jnp.concatenate([low, high], axis=0), 0)
+        return self.low
 
     def last(self):
-        return self.links.ring_scatter(self.block)
+        return self.links.ring_scatter(self.own, self.low)
 
 
 def relative_order(links, depth):
@@ -833,7 +837,8 @@
     cut = ring_a.shape[0] // 2
     x_a, y_a = links.along(ring_a), links.across(ring_a)
     ring_b = links.ring_gather(tie(mlp_shards[0], ring_a))
-    attn_w = [ring_a, x_a, y_a, links.across(x_a[:cut]), links.along(y_a[cut:])]
+    ends_a = links.across(x_a[:cut]), links.along(y_a[cut:])
+    attn_w = [ring_a, x_a, y_a, *ends_a]
 
     x_abs = jnp.concatenate([tokens_own, tokens_came], axis=0)
     x = dot(x_abs, swap).astype(bf16)
@@ -847,24 +852,28 @@
 
     ring_b = tie(ring_b, x_a, y_a)
     x_b, y_b = links.along(ring_b), links.across(ring_b)
-    q, kv, wo = qkv(tie(x, ring_b), x_other, cosine, sine, attn_w)
-    ring_c = links.ring_gather(tie(mlp_shards[1], ring_b))
+    q, kv, wo = qkv(tie(x, ring_b, *x_t), x_other, cosine, sine, attn_w)
+    ring_c = links.ring_gather(tie(mlp_shards[1], *ends_a))
     att_0, logs_0 = attend(0, q, kv, seg_row, seg_col)
-    ring_c = tie(ring_c, x_b, y_b)
+    ends_b = links.across(x_b[:cut]), links.along(y_b[cut:])
+    mlp_b = [ring_b, x_b, y_b, *ends_b]
+    att_1, logs_1 = attend(1, tie(q, ring_c, x_b, y_b), kv, seg_row, seg_col)
+    ring_c = tie(ring_c, att_1)
     x_c, y_c = links.along(ring_c), links.across(ring_c)
-    mlp_b = [ring_b, x_b, y_b, links.across(x_b[:cut]), links.along(y_b[cut:])]
-    att_1, logs_1 = attend(1, tie(q, ring_c, x_b, y_b), kv, seg_row, seg_col)
-    own, send = project(att_0, att_1, wo)
+    own, send = project(att_0, tie(att_1, *ends_b), wo)
     n1, s1, low, low_t, gains = first_norm(x, own, links.beside(send), ring_b, x_b)
     low_other = links.beside(low)
     low1_t = [low_t, links.beside(low_t)]
     act_b_own, feed = mlp(low, None, mlp_b, half, f32)
-    act_b_other, feed_other = mlp(tie(low_other, x_c, y_c), None, mlp_b, half, f32)
-    mlp_c = [ring_c, x_c, y_c, links.across(x_c[:cut]), links.along(y_c[cut:])]
+    held_x, held_y = lax.optimization_barrier((x_c, y_c, feed))[:2]
+    held_x, held_y = held_x[:cut], held_y[cut:]
+    ends_c = links.across(held_x), links.along(held_y)
+    act_b_other, feed_other = mlp(tie(low_other, held_x, held_y), None, mlp_b, half, f32)
+    mlp_c = [ring_c, x_c, y_c, *ends_c]
     act_c_other, send = mlp(low_other, feed_other, mlp_c, half, bf16)
     came = links.beside(send)
     act_c_own, feed = mlp(tie(low, send), feed, mlp_c, half, f32)
-    dy_came = links.across(tie(dy_other.astype(bf16), y_c))
+    dy_came = links.across(tie(dy_other.astype(bf16), feed_other))
     high, low = split(dy_own)
     dy = jnp.concatenate([dot(high, swap) + dot(low, swap), dot(dy_came, swap)], axis=0)
     layer_out, dh2, dfeed, dfeed_t, sums = second_norm(n1, gains, feed, came, dy)
@@ -878,27 +887,31 @@
     )
     came = links.beside(other)
     sum_b = Scatter(links, [to_x], to_y, keep)
+    sum_c.keep = tie(sum_c.keep, own)
     ops_c = sum_c.second()
-    dh1, low, low_t, cols = first_back(tie(dh2, *ops_c), own, came, n1, s1, gains, sums)
+    dh1, low, low_t = first_back(tie(dh2, *ops_c), own, came, n1, s1, gains, sums)
     lows = [low, links.beside(low)]
     low_t = [low_t, links.beside(low_t)]
-    cols = (cols.astype(f32) + links.beside(cols).astype(f32)).astype(bf16)
-    layer_out = dot(layer_out, swap, NT).astype(bf16)
-    layer_out = from_sequence(layer_out[:mine], links.across(layer_out[mine:]))
-
     dq, dkv = attend_back(1, q, kv, *lows, wo, att_1, logs_1, seg_row, seg_col, cosine, sine)
+    sum_c.keep = tie(sum_c.keep, dq)
     block_c = sum_c.third()
-    own, other, send, keep_1 = qkv_back(1, None, tie(dq, block_c), dkv, x_t, low_t, att_1, cols, attn_w)
+    sum_b.keep = tie(sum_b.keep, dq)
+    ops_b = sum_b.second()
+    own, other, send, keep_1 = qkv_back(
+        1, None, tie(dq, *block_c, *ops_b), dkv, x_t, low_t, att_1, attn_w
+    )
     own_c = sum_c.last()
-    ops_b = sum_b.second()
-    dq, dkv = attend_back(
-        0, tie(q, own, *ops_b), kv, *lows, wo, att_0, logs_0, seg_row, seg_col, cosine, sine
-    )
+    dq, dkv = attend_back(0, tie(q, own), kv, *lows, wo, att_0, logs_0, seg_row, seg_col, cosine, sine)
+    sum_b.keep = tie(sum_b.keep, dq)
     block_b = sum_b.third()
     to_y, to_x = send[:2], [send[2:]]
-    own, other, send, keep_0 = qkv_back(0, (own, other), tie(dq, block_b), dkv, x_t, low_t, att_0, cols, attn_w)
+    own, other, send, keep_0 = qkv_back(
+        0, (own, other), tie(dq, *block_b, own_c), dkv, x_t, low_t, att_0, attn_w
+    )
     own_b = sum_b.last()
     sum_a = Scatter(links, [send] + to_x, to_y, jnp.concatenate([keep_0, keep_1], axis=0))
+    layer_out = dot(layer_out, swap, NT).astype(bf16)
+    layer_out = from_sequence(layer_out[:mine], links.across(tie(layer_out[mine:], dq)))
     grad = dh1 + own + links.beside(other).astype(f32)
     high, low = split(grad)
     grad = dot(high, swap, NT) + dot(low, swap, NT)

time: 444 us -> 360 us (0.81)
  waiting for transfers between devices: 140 us -> 65.2 us
  starting transfers between devices: 71.7 us -> 58.7 us
    ppermute x62 -> x61, waiting for transfers between devices: 140 us -> 65.2 us  [send(): return lax.ppermute(v, ('row', 'col'), pairs)]
    ppermute x62 -> x61, starting transfers between devices: 71.7 us -> 58.7 us  [send(): return lax.ppermute(v, ('row', 'col'), pairs)]
    unnamed x113 -> x102, local copies, waits for them, and re-layouts: 10.4 us -> 11.3 us
  transfers between devices with their start and end apart: 62 -> 61, of which waited for: 25 -> 18; matrix products, arithmetic and copies ran while one was open for 9% -> 14% of each run, Pallas kernels for 25% -> 40%
where the time goes in v6:
time: 360 us; the launch traced here: 354 us
  Pallas kernels  169 us (47%)
  waiting for transfers between devices  65.2 us (18%)
  starting transfers between devices  58.7 us (16%)
  local copies, waits for them, and re-layouts  26.6 us (7%)
  other arithmetic  19.4 us (5%)
  matrix products  13.1 us (4%)
    ppermute x61, waiting for transfers between devices, send(): return lax.ppermute(v, ('row', 'col'), pairs)  65.2 us
    ppermute x61, starting transfers between devices, send(): return lax.ppermute(v, ('row', 'col'), pairs)  58.7 us
    pallas_call x2, Pallas kernels, mlp_back(): pl.pallas_call(functools.partial(mlp_back_kernel, has_base), grid=(2,), i...  39.5 us
    pallas_call x2, Pallas kernels, attend_back(): pl.pallas_call(attend_back_kernel, grid=(steps,), in_specs=[pl.BlockSpec(...  32.3 us
    pallas_call x4, Pallas kernels, mlp(): pl.pallas_call(functools.partial(mlp_kernel, has_base), grid=(2,), in_spe...  31.6 us
    pallas_call x2, Pallas kernels, attend(): pl.pallas_call(attend_kernel, grid=(rows // QROWS,), in_specs=[pl.BlockSp...  22 us
    pallas_call x2, Pallas kernels, qkv_back(): pl.pallas_call(functools.partial(qkv_back_kernel, quarter, has_base), gri...  16 us
    unnamed x102, local copies, waits for them, and re-layouts  11.3 us
  transfers between devices with their start and end apart: 61, of which 18 were waited for; matrix products, arithmetic and copies ran while one was open for 14% of the time, Pallas kernels for 40%

profile of v6, /device:TPU:0, one launch (start us, length us, event | category | flops | bytes accessed | tf_op | source)
XLA Modules:
  0.0 354.5 jit_solution(14292263833435853540)
XLA Ops:
  2.7 5.1 %collective-permute-start.1 = (bf16[96,768]{1,0:T(8,128)(2,1)S(1)}, bf16[96,768]{1,0:T(8,128)(2,1)S(1)}, u32[]{:S(2)}, u32[]{:S(2)}) collective-permute-start(bf16[96,768]{1,0:T(8,128)(2,1)S(1)} %concatenate.55), channel_id=1, source_target_pairs={{0,24},{1,25},{2,26},{3,27},{4,28},{5,29},{6,30},{7,31},{8,0},{9,1... | collective-permute-start | bytes 442376 | tf_op jit(solution)/shard_map/ppermute | solution.py:701
  10.0 1.6 collective-permute-start
  13.0 7.1 %collective-permute-done.11 = s32[2,256]{1,0:T(2,128)S(1)} collective-permute-done((s32[2,256]{1,0:T(2,128)S(1)}, s32[2,256]{1,0:T(2,128)S(1)}, u32[]{:S(2)}, u32[]{:S(2)}) %collective-permute-start.11) | collective-permute-done | bytes 2080 | tf_op jit(solution)/shard_map/ppermute | solution.py:701
  21.4 1.6 collective-permute-start.7
  22.9 1.5 collective-permute-start.8
  25.0 3.1 collective-permute-start.4
  29.7 1.9 convolution_convert_fusion.x_a_ref
  31.7 1.7 fusion.9.own_ref.x_ref
  33.4 3.4 collective-permute-done.7.rest_1_.rest_3_
  39.4 1.6 collective-permute-start.13
  40.9 9.3 %collective-permute-done.5 = bf16[96,1280]{1,0:T(8,128)(2,1)S(1)} collective-permute-done((bf16[96,1280]{1,0:T(8,128)(2,1)S(1)}, bf16[96,1280]{1,0:T(8,128)(2,1)S(1)}, u32[]{:S(2)}, u32[]{:S(2)}) %collective-permute-start.5) | collective-permute-done | bytes 245792 | tf_op jit(solution)/shard_map/ppermute | solution.py:701
  59.1 2.6 collective-permute-start.17
  61.7 8.2 %qkv.1 = (bf16[1024,512]{1,0:T(8,128)(2,1)}, bf16[1024,1024]{1,0:T(8,128)(2,1)}, bf16[768,512]{1,0:T(8,128)(2,1)}) custom-call(bf16[512,768]{1,0:T(8,128)(2,1)} %fusion.9.own_ref.x_ref, bf16[512,768]{1,0:T(8,128)(2,1)} %collective-permute-done.10.other_ref, f32[1024,256]{1,0:T(8,128)} %copy.54.cos_ref, f32[1024,256]{1,0:T(8,128)} %copy.55.sin_ref, ...), custom_call_target="tpu_custom_call" | custom-call | flops 2415919104 | bytes 7864320 | tf_op jit(solution)/shard_map/qkv/pallas_call | solution.py:133
  69.9 11.0 %attend.2 = (bf16[1024,256]{1,0:T(8,128)(2,1)}, f32[8,1024]{1,0:T(8,128)}) custom-call(bf16[1024,512]{1,0:T(8,128)(2,1)} %get-tuple-element.140.q_ref, bf16[1024,1024]{1,0:T(8,128)(2,1)} %get-tuple-element.86.kv_ref, s32[1,1024]{1,0:T(1,128)} %get-tuple-element.229.segq_ref, s32[1024,1]{1,0:T(8,128)} %copy.56.segk_ref), custom_call_target="tpu_custom_call" | custom-call | flops 4294967296 | bytes 3145728 | tf_op jit(solution)/shard_map/attend/pallas_call | solution.py:182
  86.0 11.0 %attend.3 = (bf16[1024,256]{1,0:T(8,128)(2,1)}, f32[8,1024]{1,0:T(8,128)}) custom-call(bf16[1024,512]{1,0:T(8,128)(2,1)} %get-tuple-element.140.q_ref, bf16[1024,1024]{1,0:T(8,128)(2,1)} %get-tuple-element.86.kv_ref, s32[1,1024]{1,0:T(1,128)} %get-tuple-element.229.segq_ref, s32[1024,1]{1,0:T(8,128)} %copy.56.segk_ref), custom_call_target="tpu_custom_call" | custom-call | flops 4294967296 | bytes 3145728 | tf_op jit(solution)/shard_map/attend/pallas_call | solution.py:182
  97.0 3.9 %project.1 = (f32[512,768]{1,0:T(8,128)}, bf16[512,768]{1,0:T(8,128)(2,1)}) custom-call(bf16[1024,256]{1,0:T(8,128)(2,1)} %get-tuple-element.87.att_a_ref.att_ref, bf16[1024,256]{1,0:T(8,128)(2,1)} %get-tuple-element.91.att_b_ref.att_ref, bf16[768,512]{1,0:T(8,128)(2,1)} %get-tuple-element.92.wo_ref), custom_call_target="tpu_custom_call" | custom-call | flops 805306368 | bytes 6291456 | tf_op jit(solution)/shard_map/project/pallas_call | solution.py:308
  104.4 4.4 %first_norm.1 = (f32[512,768]{1,0:T(8,128)}, f32[512,128]{1,0:T(8,128)}, bf16[512,768]{1,0:T(8,128)(2,1)}, bf16[768,512]{1,0:T(8,128)(2,1)}, f32[8,768]{1,0:T(8,128)}) custom-call(bf16[512,768]{1,0:T(8,128)(2,1)} %fusion.9.own_ref.x_ref, f32[512,768]{1,0:T(8,128)} %get-tuple-element.93.own_ref, bf16[512,768]{1,0:T(8,128)(2,1)} %copy-done.17, ...), custom_call_target="tpu_custom_call" | custom-call | flops 7864320 | bytes 6291456 | tf_op jit(solution)/shard_map/first_norm/pallas_call | solution.py:340
  108.9 7.7 %mlp.4 = (bf16[2,3,512,384]{3,2,1,0:T(8,128)(2,1)}, f32[512,768]{1,0:T(8,128)}) custom-call(bf16[512,768]{1,0:T(8,128)(2,1)} %get-tuple-element.105.low_ref, bf16[384,1280]{1,0:T(8,128)(2,1)} %copy-done.1, bf16[384,1280]{1,0:T(8,128)(2,1)} %copy-done.4, bf16[384,1280]{1,0:T(8,128)(2,1)} %collective-permute-done.19.rest_2_.rest_12_, ...), custom_call_target="tpu_custom_call" | custom-call | flops 1811939328 | bytes 8847360 | tf_op jit(solution)/shard_map/mlp/pallas_call | solution.py:396
  116.6 6.6 %collective-permute-done.24.rest_2_.rest_9_ = bf16[384,1152]{1,0:T(8,128)(2,1)S(1)} collective-permute-done((bf16[384,1152]{1,0:T(8,128)(2,1)}, bf16[384,1152]{1,0:T(8,128)(2,1)S(1)}, u32[]{:S(2)}, u32[]{:S(2)}) %collective-permute-start.24) | collective-permute-done | bytes 884768 | tf_op jit(solution)/shard_map/ppermute | solution.py:701
  126.0 1.6 fusion.4
  127.5 7.7 %mlp.5 = (bf16[2,3,512,384]{3,2,1,0:T(8,128)(2,1)}, f32[512,768]{1,0:T(8,128)}) custom-call(bf16[512,768]{1,0:T(8,128)(2,1)} %collective-permute-done.23.low_ref, bf16[384,1280]{1,0:T(8,128)(2,1)} %copy-done.1, bf16[384,1280]{1,0:T(8,128)(2,1)} %copy-done.4, bf16[384,1280]{1,0:T(8,128)(2,1)} %collective-permute-done.19.rest_2_.rest_12_, ...), custom_call_target="tpu_custom_call" | custom-call | flops 1811939328 | bytes 8847360 | tf_op jit(solution)/shard_map/mlp/pallas_call | solution.py:396
  137.4 8.1 %mlp.6 = (bf16[2,3,512,384]{3,2,1,0:T(8,128)(2,1)}, bf16[512,768]{1,0:T(8,128)(2,1)}) custom-call(bf16[512,768]{1,0:T(8,128)(2,1)} %collective-permute-done.23.low_ref, f32[512,768]{1,0:T(8,128)} %get-tuple-element.103.rest_0_, bf16[384,1152]{1,0:T(8,128)(2,1)} %constant_dynamic-update-slice_fusion.rest_1_.rest_8_, bf16[384,1152]{1,0:T(8,128)(2,1)} %copy-done.26, ...), custom_call_target="tpu_custom_call" | custom-call | flops 1811939328 | bytes 8847360 | tf_op jit(solution)/shard_map/mlp/pallas_call | solution.py:396
  145.5 2.1 fusion.11
  148.2 8.1 %mlp.7 = (bf16[2,3,512,384]{3,2,1,0:T(8,128)(2,1)}, f32[512,768]{1,0:T(8,128)}) custom-call(bf16[512,768]{1,0:T(8,128)(2,1)} %get-tuple-element.105.low_ref, f32[512,768]{1,0:T(8,128)} %get-tuple-element.99.rest_0_, bf16[384,1152]{1,0:T(8,128)(2,1)} %constant_dynamic-update-slice_fusion.rest_1_.rest_8_, bf16[384,1152]{1,0:T(8,128)(2,1)} %copy-done.26, ...), custom_call_target="tpu_custom_call" | custom-call | flops 1811939328 | bytes 8847360 | tf_op jit(solution)/shard_map/mlp/pallas_call | solution.py:396
  156.3 1.7 fusion.3
  160.1 6.1 %second_norm.1 = (bf16[512,768]{1,0:T(8,128)(2,1)}, f32[512,768]{1,0:T(8,128)}, bf16[512,768]{1,0:T(8,128)(2,1)}, bf16[768,512]{1,0:T(8,128)(2,1)}, f32[8,768]{1,0:T(8,128)}) custom-call(f32[512,768]{1,0:T(8,128)} %get-tuple-element.95.n_ref, f32[8,768]{1,0:T(8,128)} %get-tuple-element.96.gains_ref, f32[512,768]{1,0:T(8,128)} %get-tuple-element.106.feed_ref, ...), custom_call_target="tpu_custom_call" | custom-call | flops 15728640 | bytes 8650752 | tf_op jit(solution)/shard_map/second_norm/pallas_call | solution.py:433
  166.7 2.0 collective-permute-done.30.rest_1_
  170.7 19.3 %mlp_back.2 = (f32[512,768]{1,0:T(8,128)}, f32[512,768]{1,0:T(8,128)}, bf16[2,192,1152]{2,1,0:T(8,128)(2,1)}, bf16[2,192,1152]{2,1,0:T(8,128)(2,1)}, bf16[4,192,1152]{2,1,0:T(8,128)(2,1)}) custom-call(bf16[512,768]{1,0:T(8,128)(2,1)} %get-tuple-element.110.rest_0_, bf16[512,768]{1,0:T(8,128)(2,1)} %copy-done.39, ...), custom_call_target="tpu_custom_call" | custom-call | flops 7247757312 | bytes 29491200 | tf_op jit(solution)/shard_map/mlp_back/pallas_call | solution.py:522
  190.8 1.6 collective-permute-start.34
  192.4 20.3 %mlp_back.3 = (f32[512,768]{1,0:T(8,128)}, bf16[512,768]{1,0:T(8,128)(2,1)}, bf16[2,192,1152]{2,1,0:T(8,128)(2,1)}, bf16[2,192,1152]{2,1,0:T(8,128)(2,1)}, bf16[4,192,1152]{2,1,0:T(8,128)(2,1)}) custom-call(bf16[512,768]{1,0:T(8,128)(2,1)} %get-tuple-element.110.rest_0_, bf16[512,768]{1,0:T(8,128)(2,1)} %copy-done.39, ...), custom_call_target="tpu_custom_call" | custom-call | flops 7247757312 | bytes 29491200 | tf_op jit(solution)/shard_map/mlp_back/pallas_call | solution.py:522
  215.3 5.4 %first_back.1 = (f32[512,768]{1,0:T(8,128)}, bf16[512,768]{1,0:T(8,128)(2,1)}, bf16[768,640]{1,0:T(8,128)(2,1)}) custom-call(f32[512,768]{1,0:T(8,128)} %get-tuple-element.124.base_ref, f32[512,768]{1,0:T(8,128)} %get-tuple-element.120.own_ref, bf16[512,768]{1,0:T(8,128)(2,1)} %collective-permute-done.35.came_ref, f32[512,768]{1,0:T(8,128)} %get-tuple-element.95.n_ref, ...), custom_call_target="tpu_custom_call" | custom-call | flops 15728640 | bytes 7864320 | tf_op jit(solution)/shard_map/first_back/pallas_call | solution.py:574
  220.9 2.1 fusion.10
  228.9 16.1 %attend_back.2 = (bf16[1024,256]{1,0:T(8,128)(2,1)}, bf16[1024,512]{1,0:T(8,128)(2,1)}) custom-call(bf16[1024,512]{1,0:T(8,128)(2,1)} %get-tuple-element.140.q_ref, bf16[1024,1024]{1,0:T(8,128)(2,1)} %get-tuple-element.86.kv_ref, bf16[512,768]{1,0:T(8,128)(2,1)} %get-tuple-element.128.own_ref, bf16[512,768]{1,0:T(8,128)(2,1)} %copy-done.37, ...), custom_call_target="tpu_custom_call" | custom-call | flops 10737418240 | bytes 7864320 | tf_op jit(solution)/shard_map/attend_back/pallas_call | solution.py:262
  245.1 11.2 %collective-permute-done.37 = bf16[192,1152]{1,0:T(8,128)(2,1)S(1)} collective-permute-done((bf16[192,1152]{1,0:T(8,128)(2,1)S(1)}, bf16[192,1152]{1,0:T(8,128)(2,1)S(1)}, u32[]{:S(2)}, u32[]{:S(2)}) %collective-permute-start.37) | collective-permute-done | bytes 442400 | tf_op jit(solution)/shard_map/ppermute | solution.py:701
  256.3 1.9 fusion.22
  258.9 2.3 fusion.31
  263.4 2.8 collective-permute-start.46
  268.5 7.6 %qkv_back.2 = (f32[512,768]{1,0:T(8,128)}, f32[512,768]{1,0:T(8,128)}, bf16[3,192,896]{2,1,0:T(8,128)(2,1)}, bf16[1,192,896]{2,1,0:T(8,128)(2,1)}) custom-call(bf16[1024,256]{1,0:T(8,128)(2,1)} %get-tuple-element.136.dq_ref, bf16[1024,512]{1,0:T(8,128)(2,1)} %get-tuple-element.137.dkv_ref, bf16[768,512]{1,0:T(8,128)(2,1)} %copy-done.16, ...), custom_call_target="tpu_custom_call" | custom-call | flops 2617245696 | bytes 7864320 | tf_op jit(solution)/shard_map/qkv_back/pallas_call | solution.py:639
  276.1 16.2 %attend_back.3 = (bf16[1024,256]{1,0:T(8,128)(2,1)}, bf16[1024,512]{1,0:T(8,128)(2,1)}) custom-call(bf16[1024,512]{1,0:T(8,128)(2,1)} %get-tuple-element.140.q_ref, bf16[1024,1024]{1,0:T(8,128)(2,1)} %get-tuple-element.86.kv_ref, bf16[512,768]{1,0:T(8,128)(2,1)} %get-tuple-element.128.own_ref, bf16[512,768]{1,0:T(8,128)(2,1)} %copy-done.37, ...), custom_call_target="tpu_custom_call" | custom-call | flops 10737418240 | bytes 7864320 | tf_op jit(solution)/shard_map/attend_back/pallas_call | solution.py:262
  294.0 1.6 collective-permute-start.50
  298.9 1.6 fusion.21
  301.4 2.9 collective-permute-start.60
  305.0 8.4 %qkv_back.3 = (f32[512,768]{1,0:T(8,128)}, bf16[512,768]{1,0:T(8,128)(2,1)}, bf16[1,192,896]{2,1,0:T(8,128)(2,1)}, bf16[3,192,896]{2,1,0:T(8,128)(2,1)}) custom-call(bf16[1024,256]{1,0:T(8,128)(2,1)} %get-tuple-element.146.dq_ref, bf16[1024,512]{1,0:T(8,128)(2,1)} %get-tuple-element.147.dkv_ref, bf16[768,512]{1,0:T(8,128)(2,1)} %copy-done.16, ...), custom_call_target="tpu_custom_call" | custom-call | flops 2617245696 | bytes 7864320 | tf_op jit(solution)/shard_map/qkv_back/pallas_call | solution.py:639
  314.7 4.6 %collective-permute-done.42 = bf16[256,768]{1,0:T(8,128)(2,1)} collective-permute-done((bf16[256,768]{1,0:T(8,128)(2,1)}, bf16[256,768]{1,0:T(8,128)(2,1)}, u32[]{:S(2)}, u32[]{:S(2)}) %collective-permute-start.42) | collective-permute-done | bytes 393248 | tf_op jit(solution)/shard_map/ppermute | solution.py:701
  328.0 4.3 %collective-permute-done.55 = bf16[192,896]{1,0:T(8,128)(2,1)S(1)} collective-permute-done((bf16[192,896]{1,0:T(8,128)(2,1)S(1)}, bf16[192,896]{1,0:T(8,128)(2,1)S(1)}, u32[]{:S(2)}, u32[]{:S(2)}) %collective-permute-start.55) | collective-permute-done | bytes 344096 | tf_op jit(solution)/shard_map/ppermute | solution.py:701
  332.4 2.3 collective-permute-done.52
  335.5 2.9 collective-permute-start.57
  341.7 7.7 %collective-permute-done.56 = bf16[96,896]{1,0:T(8,128)(2,1)S(1)} collective-permute-done((bf16[96,896]{1,0:T(8,128)(2,1)S(1)}, bf16[96,896]{1,0:T(8,128)(2,1)S(1)}, u32[]{:S(2)}, u32[]{:S(2)}) %collective-permute-start.56) | collective-permute-done | bytes 172064 | tf_op jit(solution)/shard_map/ppermute | solution.py:701
  (272 shorter events, 78.7 us)
Async XLA Ops:
  2.7 18.6 %collective-permute-start.1 = (bf16[96,768]{1,0:T(8,128)(2,1)S(1)}, bf16[96,768]{1,0:T(8,128)(2,1)S(1)}, u32[]{:S(2)}, u32[]{:S(2)}) collective-permute-start(bf16[96,768]{1,0:T(8,128)(2,1)S(1)} %concatenate.55), channel_id=1, source_target_pairs={{0,24},{1,25},{2,26},{3,27},{4,28},{5,29},{6,30},{7,31},{8,0},{9,1... | collective-permute-start | bytes 442376 | tf_op jit(solution)/shard_map/ppermute | solution.py:701
  7.8 13.5 %collective-permute-start.2 = (bf16[96,768]{1,0:T(8,128)(2,1)S(1)}, bf16[96,768]{1,0:T(8,128)(2,1)S(1)}, u32[]{:S(2)}, u32[]{:S(2)}) collective-permute-start(bf16[96,768]{1,0:T(8,128)(2,1)S(1)} %concatenate.55), channel_id=1, source_target_pairs={{0,16},{1,17},{2,18},{3,19},{4,20},{5,21},{6,22},{7,23},{8,24},{9,... | collective-permute-start | bytes 442376 | tf_op jit(solution)/shard_map/ppermute | solution.py:701
  7.8 13.5 %collective-permute-start.3 = (bf16[96,768]{1,0:T(8,128)(2,1)S(1)}, bf16[96,768]{1,0:T(8,128)(2,1)S(1)}, u32[]{:S(2)}, u32[]{:S(2)}) collective-permute-start(bf16[96,768]{1,0:T(8,128)(2,1)S(1)} %concatenate.55), channel_id=1, source_target_pairs={{0,8},{1,9},{2,10},{3,11},{4,12},{5,13},{6,14},{7,15},{8,16},{9,17... | collective-permute-start | bytes 442376 | tf_op jit(solution)/shard_map/ppermute | solution.py:701
  10.0 19.0 %collective-permute-start = (bf16[256,768]{1,0:T(8,128)(2,1)S(1)}, bf16[256,768]{1,0:T(8,128)(2,1)S(1)}, u32[]{:S(2)}, u32[]{:S(2)}) collective-permute-start(bf16[256,768]{1,0:T(8,128)(2,1)S(1)} %get-tuple-element.195), channel_id=1, source_target_pairs={{0,2},{1,3},{2,0},{3,1},{4,6},{5,7},{6,4},{7,5},{8,10},{9,11},{10,... | collective-permute-start | bytes 1179656 | tf_op jit(solution)/shard_map/ppermute | solution.py:701
  21.4 15.5 %collective-permute-start.7 = (bf16[384,768]{1,0:T(8,128)(2,1)S(1)}, bf16[384,768]{1,0:T(8,128)(2,1)S(1)}, u32[]{:S(2)}, u32[]{:S(2)}) collective-permute-start(bf16[384,768]{1,0:T(8,128)(2,1)S(1)} %pad_maximum_fusion.5.rest_0_.rest_2_.rest_4_), channel_id=1, source_target_pairs={{0,4},{1,5},{2,6},{3,7},{4,0},{5,1},{6,2},{7,3},{8,12},{9,13},{10,... | collective-permute-start | bytes 1769480 | tf_op jit(solution)/shard_map/ppermute | solution.py:701
  22.9 15.1 %collective-permute-start.8 = (bf16[384,768]{1,0:T(8,128)(2,1)S(1)}, bf16[384,768]{1,0:T(8,128)(2,1)S(1)}, u32[]{:S(2)}, u32[]{:S(2)}) collective-permute-start(bf16[384,768]{1,0:T(8,128)(2,1)S(1)} %pad_maximum_fusion.5.rest_0_.rest_2_.rest_4_), channel_id=1, source_target_pairs={{0,2},{1,3},{2,0},{3,1},{4,6},{5,7},{6,4},{7,5},{8,10},{9,11},{10,... | collective-permute-start | bytes 1769480 | tf_op jit(solution)/shard_map/ppermute | solution.py:701
  25.0 14.3 %collective-permute-start.4 = (bf16[96,1280]{1,0:T(8,128)(2,1)S(1)}, bf16[96,1280]{1,0:T(8,128)(2,1)S(1)}, u32[]{:S(2)}, u32[]{:S(2)}) collective-permute-start(bf16[96,1280]{1,0:T(8,128)(2,1)S(1)} %fusion.44), channel_id=1, source_target_pairs={{0,24},{1,25},{2,26},{3,27},{4,28},{5,29},{6,30},{7,31},{8,0},{9,1... | collective-permute-start | bytes 737288 | tf_op jit(solution)/shard_map/ppermute | solution.py:701
  28.1 22.1 %collective-permute-start.5 = (bf16[96,1280]{1,0:T(8,128)(2,1)S(1)}, bf16[96,1280]{1,0:T(8,128)(2,1)S(1)}, u32[]{:S(2)}, u32[]{:S(2)}) collective-permute-start(bf16[96,1280]{1,0:T(8,128)(2,1)S(1)} %fusion.44), channel_id=1, source_target_pairs={{0,16},{1,17},{2,18},{3,19},{4,20},{5,21},{6,22},{7,23},{8,24},{9,... | collective-permute-start | bytes 737288 | tf_op jit(solution)/shard_map/ppermute | solution.py:701
  29.0 26.0 %collective-permute-start.6 = (bf16[96,1280]{1,0:T(8,128)(2,1)S(1)}, bf16[96,1280]{1,0:T(8,128)(2,1)}, u32[]{:S(2)}, u32[]{:S(2)}) collective-permute-start(bf16[96,1280]{1,0:T(8,128)(2,1)S(1)} %fusion.44), channel_id=1, source_target_pairs={{0,8},{1,9},{2,10},{3,11},{4,12},{5,13},{6,14},{7,15},{8,16},{9,17... | collective-permute-start | bytes 737288 | tf_op jit(solution)/shard_map/ppermute | solution.py:701
  36.8 22.3 %collective-permute-start.9 = (bf16[768,512]{1,0:T(8,128)(2,1)S(1)}, bf16[768,512]{1,0:T(8,128)(2,1)}, u32[]{:S(2)}, u32[]{:S(2)}) collective-permute-start(bf16[768,512]{1,0:T(8,128)(2,1)S(1)} %convolution_convert_fusion.x_a_ref), channel_id=1, source_target_pairs={{0,1},{1,0},{2,3},{3,2},{4,5},{5,4},{6,7},{7,6},{8,9},{9,8},{10,11... | collective-permute-start | bytes 2359304 | tf_op jit(solution)/shard_map/ppermute | solution.py:701
  38.0 21.1 %collective-permute-start.10 = (bf16[512,768]{1,0:T(8,128)(2,1)}, bf16[512,768]{1,0:T(8,128)(2,1)}, u32[]{:S(2)}, u32[]{:S(2)}) collective-permute-start(bf16[512,768]{1,0:T(8,128)(2,1)} %fusion.9.own_ref.x_ref), channel_id=1, source_target_pairs={{0,1},{1,0},{2,3},{3,2},{4,5},{5,4},{6,7},{7,6},{8,9},{9,8},{10,11... | collective-permute-start | bytes 2359304 | tf_op jit(solution)/shard_map/ppermute | solution.py:701
  39.4 18.0 %collective-permute-start.13 = (bf16[192,768]{1,0:T(8,128)(2,1)}, bf16[192,768]{1,0:T(8,128)(2,1)}, u32[]{:S(2)}, u32[]{:S(2)}) collective-permute-start(bf16[192,768]{1,0:T(8,128)(2,1)} %slice.260), channel_id=1, source_target_pairs={{0,2},{1,3},{2,0},{3,1},{4,6},{5,7},{6,4},{7,5},{8,10},{9,11},{10,... | collective-permute-start | bytes 884744 | tf_op jit(solution)/shard_map/ppermute | solution.py:701
  56.0 26.4 %collective-permute-start.18 = (bf16[384,1280]{1,0:T(8,128)(2,1)S(1)}, bf16[384,1280]{1,0:T(8,128)(2,1)S(1)}, u32[]{:S(2)}, u32[]{:S(2)}) collective-permute-start(bf16[384,1280]{1,0:T(8,128)(2,1)S(1)} %pad_maximum_fusion.2.norm_a_ref.rest_0_.rest_10_), channel_id=1, source_target_pairs={{0,4},{1,5},{2,6},{3,7},{4,0},{5,1},{6,2},{7,3},{8,12},{9,13},{10,... | collective-permute-start | bytes 2949128 | tf_op jit(solution)/shard_map/ppermute | solution.py:701
  57.4 26.1 %collective-permute-start.19 = (bf16[384,1280]{1,0:T(8,128)(2,1)S(1)}, bf16[384,1280]{1,0:T(8,128)(2,1)}, u32[]{:S(2)}, u32[]{:S(2)}) collective-permute-start(bf16[384,1280]{1,0:T(8,128)(2,1)S(1)} %pad_maximum_fusion.2.norm_a_ref.rest_0_.rest_10_), channel_id=1, source_target_pairs={{0,2},{1,3},{2,0},{3,1},{4,6},{5,7},{6,4},{7,5},{8,10},{9,11},{10,... | collective-permute-start | bytes 2949128 | tf_op jit(solution)/shard_map/ppermute | solution.py:701
  58.4 22.5 %collective-permute-start.15 = (bf16[96,1152]{1,0:T(8,128)(2,1)S(1)}, bf16[96,1152]{1,0:T(8,128)(2,1)S(1)}, u32[]{:S(2)}, u32[]{:S(2)}) collective-permute-start(bf16[96,1152]{1,0:T(8,128)(2,1)S(1)} %pad_maximum_fusion.12), channel_id=1, source_target_pairs={{0,24},{1,25},{2,26},{3,27},{4,28},{5,29},{6,30},{7,31},{8,0},{9,1... | collective-permute-start | bytes 663560 | tf_op jit(solution)/shard_map/ppermute | solution.py:701
  59.1 22.5 %collective-permute-start.16 = (bf16[96,1152]{1,0:T(8,128)(2,1)S(1)}, bf16[96,1152]{1,0:T(8,128)(2,1)S(1)}, u32[]{:S(2)}, u32[]{:S(2)}) collective-permute-start(bf16[96,1152]{1,0:T(8,128)(2,1)S(1)} %pad_maximum_fusion.12), channel_id=1, source_target_pairs={{0,16},{1,17},{2,18},{3,19},{4,20},{5,21},{6,22},{7,23},{8,24},{9,... | collective-permute-start | bytes 663560 | tf_op jit(solution)/shard_map/ppermute | solution.py:701
  59.1 26.2 %collective-permute-start.17 = (bf16[96,1152]{1,0:T(8,128)(2,1)S(1)}, bf16[96,1152]{1,0:T(8,128)(2,1)S(1)}, u32[]{:S(2)}, u32[]{:S(2)}) collective-permute-start(bf16[96,1152]{1,0:T(8,128)(2,1)S(1)} %pad_maximum_fusion.12), channel_id=1, source_target_pairs={{0,8},{1,9},{2,10},{3,11},{4,12},{5,13},{6,14},{7,15},{8,16},{9,17... | collective-permute-start | bytes 663560 | tf_op jit(solution)/shard_map/ppermute | solution.py:701
  82.4 14.6 %collective-permute-start.20 = (bf16[192,1280]{1,0:T(8,128)(2,1)S(1)}, bf16[192,1280]{1,0:T(8,128)(2,1)S(1)}, u32[]{:S(2)}, u32[]{:S(2)}) collective-permute-start(bf16[192,1280]{1,0:T(8,128)(2,1)S(1)} %slice.264), channel_id=1, source_target_pairs={{0,2},{1,3},{2,0},{3,1},{4,6},{5,7},{6,4},{7,5},{8,10},{9,11},{10,... | collective-permute-start | bytes 1474568 | tf_op jit(solution)/shard_map/ppermute | solution.py:701
  84.5 12.5 %collective-permute-start.21 = (bf16[192,1280]{1,0:T(8,128)(2,1)S(1)}, bf16[192,1280]{1,0:T(8,128)(2,1)S(1)}, u32[]{:S(2)}, u32[]{:S(2)}) collective-permute-start(bf16[192,1280]{1,0:T(8,128)(2,1)S(1)} %slice.265), channel_id=1, source_target_pairs={{0,4},{1,5},{2,6},{3,7},{4,0},{5,1},{6,2},{7,3},{8,12},{9,13},{10,... | collective-permute-start | bytes 1474568 | tf_op jit(solution)/shard_map/ppermute | solution.py:701
  101.0 22.3 %collective-permute-start.24 = (bf16[384,1152]{1,0:T(8,128)(2,1)}, bf16[384,1152]{1,0:T(8,128)(2,1)S(1)}, u32[]{:S(2)}, u32[]{:S(2)}) collective-permute-start(bf16[384,1152]{1,0:T(8,128)(2,1)} %constant_dynamic-update-slice_fusion.rest_1_.rest_8_), channel_id=1, source_target_pairs={{0,4},{1,5},{2,6},{3,7},{4,0},{5,1},{6,2},{7,3},{8,12},{9,13},{10,... | collective-permute-start | bytes 2654216 | tf_op jit(solution)/shard_map/ppermute | solution.py:701
  102.4 21.9 %collective-permute-start.25 = (bf16[384,1152]{1,0:T(8,128)(2,1)}, bf16[384,1152]{1,0:T(8,128)(2,1)S(1)}, u32[]{:S(2)}, u32[]{:S(2)}) collective-permute-start(bf16[384,1152]{1,0:T(8,128)(2,1)} %constant_dynamic-update-slice_fusion.rest_1_.rest_8_), channel_id=1, source_target_pairs={{0,2},{1,3},{2,0},{3,1},{4,6},{5,7},{6,4},{7,5},{8,10},{9,11},{10,... | collective-permute-start | bytes 2654216 | tf_op jit(solution)/shard_map/ppermute | solution.py:701
  108.8 18.8 %collective-permute-start.23 = (bf16[512,768]{1,0:T(8,128)(2,1)}, bf16[512,768]{1,0:T(8,128)(2,1)}, u32[]{:S(2)}, u32[]{:S(2)}) collective-permute-start(bf16[512,768]{1,0:T(8,128)(2,1)} %get-tuple-element.105.low_ref), channel_id=1, source_target_pairs={{0,1},{1,0},{2,3},{3,2},{4,5},{5,4},{6,7},{7,6},{8,9},{9,8},{10,11... | collective-permute-start | bytes 2359304 | tf_op jit(solution)/shard_map/ppermute | solution.py:701
  124.4 12.2 %collective-permute-start.26 = (bf16[192,1152]{1,0:T(8,128)(2,1)S(1)}, bf16[192,1152]{1,0:T(8,128)(2,1)S(1)}, u32[]{:S(2)}, u32[]{:S(2)}) collective-permute-start(bf16[192,1152]{1,0:T(8,128)(2,1)S(1)} %slice.212), channel_id=1, source_target_pairs={{0,2},{1,3},{2,0},{3,1},{4,6},{5,7},{6,4},{7,5},{8,10},{9,11},{10,... | collective-permute-start | bytes 1327112 | tf_op jit(solution)/shard_map/ppermute | solution.py:701
  125.5 11.3 %collective-permute-start.27 = (bf16[192,1152]{1,0:T(8,128)(2,1)S(1)}, bf16[192,1152]{1,0:T(8,128)(2,1)}, u32[]{:S(2)}, u32[]{:S(2)}) collective-permute-start(bf16[192,1152]{1,0:T(8,128)(2,1)S(1)} %slice.213), channel_id=1, source_target_pairs={{0,4},{1,5},{2,6},{3,7},{4,0},{5,1},{6,2},{7,3},{8,12},{9,13},{10,... | collective-permute-start | bytes 1327112 | tf_op jit(solution)/shard_map/ppermute | solution.py:701
  135.3 21.1 %collective-permute-start.29 = (bf16[256,768]{1,0:T(8,128)(2,1)S(1)}, bf16[256,768]{1,0:T(8,128)(2,1)}, u32[]{:S(2)}, u32[]{:S(2)}) collective-permute-start(bf16[256,768]{1,0:T(8,128)(2,1)S(1)} %fusion.36), channel_id=1, source_target_pairs={{0,2},{1,3},{2,0},{3,1},{4,6},{5,7},{6,4},{7,5},{8,10},{9,11},{10,... | collective-permute-start | bytes 1179656 | tf_op jit(solution)/shard_map/ppermute | solution.py:701
  145.4 13.8 %collective-permute-start.28 = (bf16[512,768]{1,0:T(8,128)(2,1)}, bf16[512,768]{1,0:T(8,128)(2,1)S(1)}, u32[]{:S(2)}, u32[]{:S(2)}) collective-permute-start(bf16[512,768]{1,0:T(8,128)(2,1)} %get-tuple-element.104), channel_id=1, source_target_pairs={{0,1},{1,0},{2,3},{3,2},{4,5},{5,4},{6,7},{7,6},{8,9},{9,8},{10,11... | collective-permute-start | bytes 2359304 | tf_op jit(solution)/shard_map/ppermute | solution.py:701
  147.7 19.0 %collective-permute-start.32 = (bf16[768,512]{1,0:T(8,128)(2,1)S(1)}, bf16[768,512]{1,0:T(8,128)(2,1)S(1)}, u32[]{:S(2)}, u32[]{:S(2)}) collective-permute-start(bf16[768,512]{1,0:T(8,128)(2,1)S(1)} %copy-done.35), channel_id=1, source_target_pairs={{0,1},{1,0},{2,3},{3,2},{4,5},{5,4},{6,7},{7,6},{8,9},{9,8},{10,11... | collective-permute-start | bytes 2359304 | tf_op jit(solution)/shard_map/ppermute | solution.py:701
  189.9 22.8 %collective-permute-start.33 = (bf16[2,192,1152]{2,1,0:T(8,128)(2,1)}, bf16[2,192,1152]{2,1,0:T(8,128)(2,1)S(1)}, u32[]{:S(2)}, u32[]{:S(2)}) collective-permute-start(bf16[2,192,1152]{2,1,0:T(8,128)(2,1)} %get-tuple-element.122), channel_id=1, source_target_pairs={{0,2},{1,3},{2,0},{3,1},{4,6},{5,7},{6,4},{7,5},{8,10},{9,11},{10,... | collective-permute-start | bytes 2654216 | tf_op jit(solution)/shard_map/ppermute | solution.py:701
  190.8 21.9 %collective-permute-start.34 = (bf16[2,192,1152]{2,1,0:T(8,128)(2,1)}, bf16[2,192,1152]{2,1,0:T(8,128)(2,1)S(1)}, u32[]{:S(2)}, u32[]{:S(2)}) collective-permute-start(bf16[2,192,1152]{2,1,0:T(8,128)(2,1)} %get-tuple-element.123), channel_id=1, source_target_pairs={{0,4},{1,5},{2,6},{3,7},{4,0},{5,1},{6,2},{7,3},{8,12},{9,13},{10,... | collective-permute-start | bytes 2654216 | tf_op jit(solution)/shard_map/ppermute | solution.py:701
  223.9 34.9 %collective-permute-start.39 = (bf16[2,192,1152]{2,1,0:T(8,128)(2,1)}, bf16[2,192,1152]{2,1,0:T(8,128)(2,1)}, u32[]{:S(2)}, u32[]{:S(2)}) collective-permute-start(bf16[2,192,1152]{2,1,0:T(8,128)(2,1)} %get-tuple-element.134), channel_id=1, source_target_pairs={{0,2},{1,3},{2,0},{3,1},{4,6},{5,7},{6,4},{7,5},{8,10},{9,11},{10,... | collective-permute-start | bytes 2654216 | tf_op jit(solution)/shard_map/ppermute | solution.py:701
  225.0 33.9 %collective-permute-start.40 = (bf16[2,192,1152]{2,1,0:T(8,128)(2,1)}, bf16[2,192,1152]{2,1,0:T(8,128)(2,1)}, u32[]{:S(2)}, u32[]{:S(2)}) collective-permute-start(bf16[2,192,1152]{2,1,0:T(8,128)(2,1)} %get-tuple-element.135), channel_id=1, source_target_pairs={{0,4},{1,5},{2,6},{3,7},{4,0},{5,1},{6,2},{7,3},{8,12},{9,13},{10,... | collective-permute-start | bytes 2654216 | tf_op jit(solution)/shard_map/ppermute | solution.py:701
  225.6 30.6 %collective-permute-start.37 = (bf16[192,1152]{1,0:T(8,128)(2,1)S(1)}, bf16[192,1152]{1,0:T(8,128)(2,1)S(1)}, u32[]{:S(2)}, u32[]{:S(2)}) collective-permute-start(bf16[192,1152]{1,0:T(8,128)(2,1)S(1)} %copy-done.22), channel_id=1, source_target_pairs={{0,4},{1,5},{2,6},{3,7},{4,0},{5,1},{6,2},{7,3},{8,12},{9,13},{10,... | collective-permute-start | bytes 1327112 | tf_op jit(solution)/shard_map/ppermute | solution.py:701
  227.0 29.3 %collective-permute-start.38 = (bf16[192,1152]{1,0:T(8,128)(2,1)S(1)}, bf16[192,1152]{1,0:T(8,128)(2,1)}, u32[]{:S(2)}, u32[]{:S(2)}) collective-permute-start(bf16[192,1152]{1,0:T(8,128)(2,1)S(1)} %copy-done.21), channel_id=1, source_target_pairs={{0,2},{1,3},{2,0},{3,1},{4,6},{5,7},{6,4},{7,5},{8,10},{9,11},{10,... | collective-permute-start | bytes 1327112 | tf_op jit(solution)/shard_map/ppermute | solution.py:701
  228.9 38.3 %collective-permute-start.41 = (bf16[768,640]{1,0:T(8,128)(2,1)S(1)}, bf16[768,640]{1,0:T(8,128)(2,1)S(1)}, u32[]{:S(2)}, u32[]{:S(2)}) collective-permute-start(bf16[768,640]{1,0:T(8,128)(2,1)S(1)} %copy-done.2), channel_id=1, source_target_pairs={{0,1},{1,0},{2,3},{3,2},{4,5},{5,4},{6,7},{7,6},{8,9},{9,8},{10,11... | collective-permute-start | bytes 2949128 | tf_op jit(solution)/shard_map/ppermute | solution.py:701
  261.2 37.7 %collective-permute-start.43 = (bf16[192,1152]{1,0:T(8,128)(2,1)}, bf16[192,1152]{1,0:T(8,128)(2,1)S(1)}, u32[]{:S(2)}, u32[]{:S(2)}) collective-permute-start(bf16[192,1152]{1,0:T(8,128)(2,1)} %get-tuple-element.185), channel_id=1, source_target_pairs={{0,4},{1,5},{2,6},{3,7},{4,0},{5,1},{6,2},{7,3},{8,12},{9,13},{10,... | collective-permute-start | bytes 1327112 | tf_op jit(solution)/shard_map/ppermute | solution.py:701
  261.8 37.0 %collective-permute-start.44 = (bf16[192,1152]{1,0:T(8,128)(2,1)}, bf16[192,1152]{1,0:T(8,128)(2,1)}, u32[]{:S(2)}, u32[]{:S(2)}) collective-permute-start(bf16[192,1152]{1,0:T(8,128)(2,1)} %get-tuple-element.184), channel_id=1, source_target_pairs={{0,2},{1,3},{2,0},{3,1},{4,6},{5,7},{6,4},{7,5},{8,10},{9,11},{10,... | collective-permute-start | bytes 1327112 | tf_op jit(solution)/shard_map/ppermute | solution.py:701
  263.4 30.6 %collective-permute-start.46 = (bf16[96,1152]{1,0:T(8,128)(2,1)}, bf16[96,1152]{1,0:T(8,128)(2,1)}, u32[]{:S(2)}, u32[]{:S(2)}) collective-permute-start(bf16[96,1152]{1,0:T(8,128)(2,1)} %get-tuple-element.205), channel_id=1, source_target_pairs={{0,16},{1,17},{2,18},{3,19},{4,20},{5,21},{6,22},{7,23},{8,24},{9,... | collective-permute-start | bytes 663560 | tf_op jit(solution)/shard_map/ppermute | solution.py:701
  266.3 29.4 %collective-permute-start.47 = (bf16[96,1152]{1,0:T(8,128)(2,1)}, bf16[96,1152]{1,0:T(8,128)(2,1)}, u32[]{:S(2)}, u32[]{:S(2)}) collective-permute-start(bf16[96,1152]{1,0:T(8,128)(2,1)} %get-tuple-element.204), channel_id=1, source_target_pairs={{0,24},{1,25},{2,26},{3,27},{4,28},{5,29},{6,30},{7,31},{8,0},{9,1... | collective-permute-start | bytes 663560 | tf_op jit(solution)/shard_map/ppermute | solution.py:701
  267.2 29.5 %collective-permute-start.45 = (bf16[96,1152]{1,0:T(8,128)(2,1)}, bf16[96,1152]{1,0:T(8,128)(2,1)S(1)}, u32[]{:S(2)}, u32[]{:S(2)}) collective-permute-start(bf16[96,1152]{1,0:T(8,128)(2,1)} %split.88), channel_id=1, source_target_pairs={{0,8},{1,9},{2,10},{3,11},{4,12},{5,13},{6,14},{7,15},{8,16},{9,17... | collective-permute-start | bytes 663560 | tf_op jit(solution)/shard_map/ppermute | solution.py:701
  294.0 19.4 %collective-permute-start.50 = (bf16[1,192,896]{2,1,0:T(8,128)(2,1)}, bf16[1,192,896]{2,1,0:T(8,128)(2,1)}, u32[]{:S(2)}, u32[]{:S(2)}) collective-permute-start(bf16[1,192,896]{2,1,0:T(8,128)(2,1)} %slice.237), channel_id=1, source_target_pairs={{0,4},{1,5},{2,6},{3,7},{4,0},{5,1},{6,2},{7,3},{8,12},{9,13},{10,... | collective-permute-start | bytes 1032200 | tf_op jit(solution)/shard_map/ppermute | solution.py:701
  295.6 28.7 %collective-permute-start.49 = (bf16[2,192,896]{2,1,0:T(8,128)(2,1)}, bf16[2,192,896]{2,1,0:T(8,128)(2,1)S(1)}, u32[]{:S(2)}, u32[]{:S(2)}) collective-permute-start(bf16[2,192,896]{2,1,0:T(8,128)(2,1)} %slice.235), channel_id=1, source_target_pairs={{0,2},{1,3},{2,0},{3,1},{4,6},{5,7},{6,4},{7,5},{8,10},{9,11},{10,... | collective-permute-start | bytes 2064392 | tf_op jit(solution)/shard_map/ppermute | solution.py:701
  296.6 22.7 %collective-permute-start.42 = (bf16[256,768]{1,0:T(8,128)(2,1)}, bf16[256,768]{1,0:T(8,128)(2,1)}, u32[]{:S(2)}, u32[]{:S(2)}) collective-permute-start(bf16[256,768]{1,0:T(8,128)(2,1)} %slice.267), channel_id=1, source_target_pairs={{0,2},{1,3},{2,0},{3,1},{4,6},{5,7},{6,4},{7,5},{8,10},{9,11},{10,... | collective-permute-start | bytes 1179656 | tf_op jit(solution)/shard_map/ppermute | solution.py:701
  301.2 20.6 %collective-permute-start.59 = (bf16[96,1152]{1,0:T(8,128)(2,1)}, bf16[96,1152]{1,0:T(8,128)(2,1)}, u32[]{:S(2)}, u32[]{:S(2)}) collective-permute-start(bf16[96,1152]{1,0:T(8,128)(2,1)} %get-tuple-element.203), channel_id=1, source_target_pairs={{0,16},{1,17},{2,18},{3,19},{4,20},{5,21},{6,22},{7,23},{8,24},{9,... | collective-permute-start | bytes 663560 | tf_op jit(solution)/shard_map/ppermute | solution.py:701
  301.4 20.5 %collective-permute-start.60 = (bf16[96,1152]{1,0:T(8,128)(2,1)S(1)}, bf16[96,1152]{1,0:T(8,128)(2,1)}, u32[]{:S(2)}, u32[]{:S(2)}) collective-permute-start(bf16[96,1152]{1,0:T(8,128)(2,1)S(1)} %get-tuple-element.202), channel_id=1, source_target_pairs={{0,24},{1,25},{2,26},{3,27},{4,28},{5,29},{6,30},{7,31},{8,0},{9,1... | collective-permute-start | bytes 663560 | tf_op jit(solution)/shard_map/ppermute | solution.py:701
  321.8 16.9 %collective-permute-start.48 = (bf16[512,768]{1,0:T(8,128)(2,1)S(1)}, bf16[512,768]{1,0:T(8,128)(2,1)S(1)}, u32[]{:S(2)}, u32[]{:S(2)}) collective-permute-start(bf16[512,768]{1,0:T(8,128)(2,1)S(1)} %copy-done.36), channel_id=1, source_target_pairs={{0,1},{1,0},{2,3},{3,2},{4,5},{5,4},{6,7},{7,6},{8,9},{9,8},{10,11... | collective-permute-start | bytes 2359304 | tf_op jit(solution)/shard_map/ppermute | solution.py:701
  334.9 14.5 %collective-permute-start.56 = (bf16[96,896]{1,0:T(8,128)(2,1)S(1)}, bf16[96,896]{1,0:T(8,128)(2,1)S(1)}, u32[]{:S(2)}, u32[]{:S(2)}) collective-permute-start(bf16[96,896]{1,0:T(8,128)(2,1)S(1)} %get-tuple-element.214), channel_id=1, source_target_pairs={{0,16},{1,17},{2,18},{3,19},{4,20},{5,21},{6,22},{7,23},{8,24},{9,... | collective-permute-start | bytes 516104 | tf_op jit(solution)/shard_map/ppermute | solution.py:701
  335.5 14.0 %collective-permute-start.57 = (bf16[96,896]{1,0:T(8,128)(2,1)S(1)}, bf16[96,896]{1,0:T(8,128)(2,1)S(1)}, u32[]{:S(2)}, u32[]{:S(2)}) collective-permute-start(bf16[96,896]{1,0:T(8,128)(2,1)S(1)} %get-tuple-element.215), channel_id=1, source_target_pairs={{0,24},{1,25},{2,26},{3,27},{4,28},{5,29},{6,30},{7,31},{8,0},{9,1... | collective-permute-start | bytes 516104 | tf_op jit(solution)/shard_map/ppermute | solution.py:701
  340.8 11.8 %collective-permute-start.51 = (bf16[256,768]{1,0:T(8,128)(2,1)S(1)}, bf16[256,768]{1,0:T(8,128)(2,1)S(1)}, u32[]{:S(2)}, u32[]{:S(2)}) collective-permute-start(bf16[256,768]{1,0:T(8,128)(2,1)S(1)} %slice.328), channel_id=1, source_target_pairs={{0,2},{1,3},{2,0},{3,1},{4,6},{5,7},{6,4},{7,5},{8,10},{9,11},{10,... | collective-permute-start | bytes 1179656 | tf_op jit(solution)/shard_map/ppermute | solution.py:701
  (59 other events, 404.0 us)

commit v7 on v6

--- a/solution.py
+++ b/solution.py
@@ -61,12 +61,11 @@
     )
 
 
-BLOCKS = 5
+BLOCKS = 4
 
 
 def block_starts(width):
-    half, quarter = width // 2, width // 4
-    return [(0, 0), (0, half), (1, 0), (1, half), (1, half + quarter)]
+    return [(0, 0), (0, width // 2), (1, 0), (1, width // 2)]
 
 
 def start_weights(blocks, w_ref, sems):
@@ -98,7 +97,7 @@
 
 
 def whole(shape):
-    return pl.BlockSpec(shape, lambda *_: (0,) * len(shape))
+    return pl.BlockSpec(shape, lambda *_: (0,) * len(shape), pipeline_mode=pl.Buffered(1))
 
 
 def qkv_kernel(own_ref, other_ref, cos_ref, sin_ref, *rest):
@@ -146,6 +145,7 @@
             jax.ShapeDtypeStruct((width, 2 * part), bf16),
         ],
         cost_estimate=cost(24 * rows * width * part, 40 * width * part),
+        compiler_params=pltpu.CompilerParams(vmem_limit_bytes=14 << 20),
         name="qkv",
     )(own, other, cosine, sine, *blocks)
 
@@ -198,6 +198,7 @@
         ],
         scratch_shapes=[pltpu.VMEM((part, rows), bf16)],
         cost_estimate=cost(16 * rows * rows * part, 12 * rows * part, rows * rows * 3),
+        compiler_params=pltpu.CompilerParams(vmem_limit_bytes=8 << 20),
         name="attend",
     )(q, kv, seg_row, seg_col)
 
@@ -289,6 +290,7 @@
             pltpu.VMEM((rows, part), f32),
         ],
         cost_estimate=cost(40 * rows * rows * part, 30 * rows * part, rows * rows * 3),
+        compiler_params=pltpu.CompilerParams(vmem_limit_bytes=18 << 20),
         name="attend_back",
     )(q, kv, own, other, wo, att, logs, seg_row, seg_col, cosine, sine)
 
@@ -315,6 +317,7 @@
             jax.ShapeDtypeStruct((rows, width), bf16),
         ],
         cost_estimate=cost(8 * rows * width * part, 16 * rows * width),
+        compiler_params=pltpu.CompilerParams(vmem_limit_bytes=10 << 20),
         name="project",
     )(att_a, att_b, wo)
 
@@ -352,6 +355,7 @@
             jax.ShapeDtypeStruct((8, width), f32),
         ],
         cost_estimate=cost(20 * rows * width, 16 * rows * width),
+        compiler_params=pltpu.CompilerParams(vmem_limit_bytes=10 << 20),
         name="first_norm",
     )(x, own, came, norm_a, norm_b)
 
@@ -370,19 +374,12 @@
 
     wait_weights(w_ref, sems, slot)
 
-    def body(i, _):
-        span = pl.ds(pl.multiple_of(i * QROWS, QROWS), QROWS)
-        low = low_ref[span, :]
-        gate = dot(low, w_ref[slot, :, half : 2 * half])
-        up = dot(low, w_ref[slot, :, 2 * half : 3 * half])
-        hidden = (gate / (1.0 + jnp.exp(-gate)) * up).astype(bf16)
-        act_ref[0, 0, span, :] = gate.astype(bf16)
-        act_ref[0, 1, span, :] = up.astype(bf16)
-        act_ref[0, 2, span, :] = hidden
-        sum_ref[span, :] += dot(hidden, w_ref[slot, :, :half], NT)
-        return 0
-
-    lax.fori_loop(0, low_ref.shape[0] // QROWS, body, 0)
+    gate = dot(low_ref[...], w_ref[slot, :, half : 2 * half])
+    up = dot(low_ref[...], w_ref[slot, :, 2 * half : 3 * half])
+    act_ref[0, 0] = gate.astype(bf16)
+    act_ref[0, 1] = up.astype(bf16)
+    act_ref[0, 2] = (gate / (1.0 + jnp.exp(-gate)) * up).astype(bf16)
+    sum_ref[...] += dot(act_ref[0, 2], w_ref[slot, :, :half], NT)
 
     @pl.when(slot == 1)
     def _():
@@ -407,6 +404,7 @@
             jax.ShapeDtypeStruct((rows, width), dtype),
         ],
         cost_estimate=cost(12 * rows * width * half, 30 * half * width, 2 * rows * half),
+        compiler_params=pltpu.CompilerParams(vmem_limit_bytes=14 << 20),
         name="mlp",
     )(low, *extra, *blocks)
 
@@ -443,6 +441,7 @@
             jax.ShapeDtypeStruct((8, width), f32),
         ],
         cost_estimate=cost(40 * rows * width, 22 * rows * width),
+        compiler_params=pltpu.CompilerParams(vmem_limit_bytes=14 << 20),
         name="second_norm",
     )(n1, gains, feed, came, dy)
 
@@ -469,22 +468,16 @@
     wait_weights(w_ref, sems, slot)
 
     for i in range(2):
-
-        def body(j, _):
-            span = pl.ds(pl.multiple_of(j * QROWS, QROWS), QROWS)
-            both = pl.ds(pl.multiple_of(i * rows + j * QROWS, QROWS), QROWS)
-            dhidden = dot(dfeeds[i][span, :], w_ref[slot, :, :half])
-            gate = acts[i][0, 0, span, :].astype(f32)
-            up = acts[i][0, 1, span, :].astype(f32)
-            sg = 1.0 / (1.0 + jnp.exp(-gate))
-            dgate = dhidden * up * sg * (1.0 + gate * (1.0 - sg))
-            dup = dhidden * (gate * sg)
-            part_ref[both, :half] = dgate.astype(bf16)
-            part_ref[both, half:] = dup.astype(bf16)
-            sum_ref[both, :] += dot(part_ref[both, :], w_ref[slot, :, half : 3 * half], NT)
-            return 0
-
-        lax.fori_loop(0, rows // QROWS, body, 0)
+        span = slice(i * rows, (i + 1) * rows)
+        dhidden = dot(dfeeds[i][...], w_ref[slot, :, :half])
+        gate = acts[i][0, 0].astype(f32)
+        up = acts[i][0, 1].astype(f32)
+        sg = 1.0 / (1.0 + jnp.exp(-gate))
+        dgate = dhidden * up * sg * (1.0 + gate * (1.0 - sg))
+        dup = dhidden * (gate * sg)
+        part_ref[span, :half] = dgate.astype(bf16)
+        part_ref[span, half:] = dup.astype(bf16)
+        sum_ref[span, :] += dot(part_ref[span, :], w_ref[slot, :, half : 3 * half], NT)
     gate_up = (
         dot(lows_t[0][...], part_ref[:rows, :]) + dot(lows_t[1][...], part_ref[rows:, :])
     ).astype(bf16)
@@ -544,6 +537,7 @@
             jax.ShapeDtypeStruct((4, width // 4, 3 * half), bf16),
         ],
         cost_estimate=cost(48 * rows * width * half, 100 * half * width, 4 * rows * half),
+        compiler_params=pltpu.CompilerParams(vmem_limit_bytes=28 << 20),
         name="mlp_back",
     )(*dfeeds, *dfeeds_t, *lows_t, *acts, *(bases if has_base else ()), *blocks)
 
@@ -582,6 +576,7 @@
             jax.ShapeDtypeStruct((width, rows + 128), bf16),
         ],
         cost_estimate=cost(40 * rows * width, 20 * rows * width),
+        compiler_params=pltpu.CompilerParams(vmem_limit_bytes=14 << 20),
         name="first_back",
     )(base, own, came, n1, s1, gains, sums)
 
@@ -591,7 +586,7 @@
 ):
     if has_base:
         bases, rest = rest[:2], rest[2:]
-    blocks, (own_ref, other_ref, send_ref, keep_ref, w_ref, sem) = rest[:3], rest[3:]
+    blocks, (own_ref, other_ref, send_ref, keep_ref, w_ref, sem) = rest[:2], rest[2:]
     rows = own_ref.shape[0]
     part = dq_ref.shape[1]
     starts = [row for slot, row in block_starts(w_ref.shape[0]) if slot == quarter]
@@ -633,7 +628,6 @@
     full = whole((rows, width))
     turned = whole((width, rows))
     blocks = [b for b, (slot, _) in zip(blocks, block_starts(width)) if slot == quarter]
-    blocks += [blocks[0]] * (3 - len(blocks))
     counts = (1, 3) if quarter == 0 else (3, 1)
     pieces = [(n, width // 4, 3 * part + 128) for n in counts]
     return pl.pallas_call(
@@ -644,7 +638,7 @@
         + [pl.BlockSpec((width, 128), lambda i: (0, rows // 128))] * 2
         + [whole(att.shape)]
         + [full] * (2 * has_base)
-        + [ANY] * 3,
+        + [ANY] * 2,
         out_specs=[full, full] + [whole(p) for p in pieces],
         scratch_shapes=[pltpu.VMEM((width, 3 * part), bf16), pltpu.SemaphoreType.DMA],
         out_shape=[
@@ -653,50 +647,36 @@
         ]
         + [jax.ShapeDtypeStruct(p, bf16) for p in pieces],
         cost_estimate=cost(26 * rows * width * part, 40 * width * part),
+        compiler_params=pltpu.CompilerParams(vmem_limit_bytes=16 << 20),
         name="qkv_back",
     )(dq, dkv, *x_t, *low_t, *low_t, att, *(bases if has_base else ()), *blocks)
 
 
-def factors_of(n):
-    out = []
-    while n > 1:
-        step = 4 if n % 4 == 0 else (2 if n % 2 == 0 else n)
-        out.append(step)
-        n //= step
-    return out
+def bits_of(n):
+    bits = n.bit_length() - 1
+    if 1 << bits != n:
+        raise ValueError("row count")
+    return bits
 
 
 class Links:
     def __init__(self, mesh):
         self.rows = mesh.shape["row"]
         self.cols = mesh.shape["col"]
-        self.digits = factors_of(self.rows // 2)
+        self.bits = bits_of(self.rows // 2)
 
     def locate(self):
         row = lax.axis_index("row")
         col = lax.axis_index("col")
-        x = row % 2
-        place = row // 2
-        ring = []
-        for size in reversed(self.digits):
-            ring.insert(0, place % size)
-            place = place // size
-        return ring, x, col // (self.cols // 2), col % 2
+        return row // 2, row % 2, col // (self.cols // 2), col % 2
 
     def send(self, v, move):
         pairs = []
         for row in range(self.rows):
             for col in range(self.cols):
-                place, ring = row // 2, []
-                for size in reversed(self.digits):
-                    ring.insert(0, place % size)
-                    place //= size
-                ring, x, y, k = move(ring, row % 2, col // (self.cols // 2), col % 2)
-                place = 0
-                for size, digit in zip(self.digits, ring):
-                    place = place * size + digit % size
+                ring, x, y, k = move(row // 2, row % 2, col // (self.cols // 2), col % 2)
                 pairs.append(
-                    (row * self.cols + col, (place * 2 + x) * self.cols + y * (self.cols // 2) + k)
+                    (row * self.cols + col, (ring * 2 + x) * self.cols + y * (self.cols // 2) + k)
                 )
         return lax.ppermute(v, ("row", "col"), pairs)
 
@@ -706,34 +686,31 @@
     def beside(self, v):
         return self.send(v, lambda ring, x, y, k: (ring, x, y, 1 - k))
 
+    def far(self, v):
+        return self.send(
+            v, lambda ring, x, y, k: (ring, 1 - x, y, k) if k else (ring, x, 1 - y, k)
+        )
+
     def along(self, v):
         return self.send(v, lambda ring, x, y, k: (ring, 1 - x, y, k))
 
-    def shift(self, v, axis, step):
-        def move(ring, x, y, k):
-            moved = list(ring)
-            moved[axis] = ring[axis] + step
-            return moved, x, y, k
-
-        return self.send(v, move)
+    def turned(self, v, bit):
+        return self.send(v, lambda ring, x, y, k: (ring ^ (1 << bit), x, y, k))
 
     def ring_gather(self, block):
-        for axis in reversed(range(len(self.digits))):
-            block = jnp.concatenate(
-                [block] + [self.shift(block, axis, -d) for d in range(1, self.digits[axis])], axis=0
-            )
+        for bit in reversed(range(self.bits)):
+            block = jnp.concatenate([block, self.turned(block, bit)], axis=0)
         return block
 
-    def ring_pieces(self, block, axis):
-        pieces = jnp.split(block, self.digits[axis], axis=0)
-        return pieces[0], [p.astype(bf16) for p in pieces[1:]]
+    def ring_split(self, block):
+        own, low = jnp.split(block, 2, axis=0)
+        return own, low.astype(bf16)
 
     def ring_scatter(self, own, low):
-        for axis in range(len(self.digits)):
-            if axis > 0:
-                own, low = self.ring_pieces(own, axis)
-            for d, piece in enumerate(low, 1):
-                own = own + self.shift(piece, axis, d).astype(f32)
+        for bit in range(self.bits):
+            if bit > 0:
+                own, low = self.ring_split(own)
+            own = own + self.turned(low, bit).astype(f32)
         return own
 
 
@@ -757,8 +734,8 @@
     def third(self):
         low = self.keep[0].astype(f32) + self.by_y[0].astype(f32) + self.late_x.astype(f32)
         high = self.keep[1].astype(f32) + self.by_x[0][0].astype(f32) + self.late_y.astype(f32)
-        self.own, self.low = self.links.ring_pieces(jnp.concatenate([low, high], axis=0), 0)
-        return self.low
+        self.own, self.low = self.links.ring_split(jnp.concatenate([low, high], axis=0))
+        return [self.low]
 
     def last(self):
         return self.links.ring_scatter(self.own, self.low)
@@ -770,15 +747,11 @@
     block, inside = where // depth, where % depth
     steps = links.rows // 2
     place = block % steps
-    parts = []
-    for axis in reversed(range(len(links.digits))):
-        size = links.digits[axis]
-        parts.insert(0, (place % size + ring[axis]) % size)
-        place = place // size
-    row = jnp.zeros_like(block)
-    for size, part in zip(links.digits, parts):
-        row = row * size + part
-    row = row * 2 + jnp.bitwise_xor(x, block // steps)
+    turn = jnp.zeros_like(place)
+    for bit in reversed(range(links.bits)):
+        turn = turn + (place % 2 << bit)
+        place = place // 2
+    row = jnp.bitwise_xor(ring, turn) * 2 + jnp.bitwise_xor(x, block // steps)
     return row * depth + inside
 
 
@@ -790,7 +763,7 @@
     width = tokens.shape[2]
     head_cols = w_qkv.shape[2]
     hid = w_gate_up.shape[2]
-    half = hid // 2
+    sizes = [hid - hid // 3, hid // 3]
     rows = 2 * tokens.shape[1]
     mine = rows // 2
     part = head_cols + HD
@@ -822,111 +795,113 @@
     norms = jnp.pad(norms, ((0, 0), (0, 128 - norms.shape[1])))
     down_t = w_down.T
     mlp_shards = []
-    for h in range(2):
-        cols = slice(h * half, (h + 1) * half)
+    for h, at in enumerate([0, sizes[0]]):
+        cols = slice(at, at + sizes[h])
         pieces = [down_t[:, cols], w_gate_up[:, 0, cols], w_gate_up[:, 1, cols]]
         mlp_shards.append(jnp.concatenate(pieces + ([norms] if h == 0 else []), axis=1))
 
-    tokens_own, tokens_other = own_and_other(tokens)
-    tokens_came = links.across(tokens_other)
     small_own, small_other = own_and_other(jnp.stack([segments, positions], axis=1))
     small_came = links.across(small_other)
+    tokens_own, tokens_other = own_and_other(tokens)
+    tokens_came = links.across(tie(tokens_other, attn_shard, small_other))
     dy_own, dy_other = own_and_other(cotangent)
-
+    dy_came = links.across(tie(dy_other.astype(bf16), attn_shard, small_other))
+
+    odd = core == 1
     ring_a = links.ring_gather(attn_shard)
-    cut = ring_a.shape[0] // 2
     x_a, y_a = links.along(ring_a), links.across(ring_a)
     ring_b = links.ring_gather(tie(mlp_shards[0], ring_a))
-    ends_a = links.across(x_a[:cut]), links.along(y_a[cut:])
-    attn_w = [ring_a, x_a, y_a, *ends_a]
+    turn_a = jnp.where(odd, y_a, x_a)
+    attn_w = [ring_a, x_a, y_a, links.far(turn_a)]
 
     x_abs = jnp.concatenate([tokens_own, tokens_came], axis=0)
     x = dot(x_abs, swap).astype(bf16)
     x_other = links.beside(x)
-    x_t = lax.dot_general(swap, x_abs, (((0,), (1,)), ((), ())), preferred_element_type=f32).astype(bf16)
-    x_t = [x_t, links.beside(x_t)]
     small = jnp.concatenate([small_own, small_came], axis=1)
     small = jnp.concatenate([small, links.beside(small)], axis=1)
     seg_row, seg_col = small[0][None, :], small[0][:, None]
     cosine, sine = rope_tables(small[1], part)
 
-    ring_b = tie(ring_b, x_a, y_a)
+    ring_b = tie(ring_b, turn_a)
     x_b, y_b = links.along(ring_b), links.across(ring_b)
-    q, kv, wo = qkv(tie(x, ring_b, *x_t), x_other, cosine, sine, attn_w)
-    ring_c = links.ring_gather(tie(mlp_shards[1], *ends_a))
+    ring_c = links.ring_gather(tie(mlp_shards[1], ring_b))
+    q, kv, wo = qkv(tie(x, ring_b, dy_came), x_other, cosine, sine, attn_w)
     att_0, logs_0 = attend(0, q, kv, seg_row, seg_col)
-    ends_b = links.across(x_b[:cut]), links.along(y_b[cut:])
-    mlp_b = [ring_b, x_b, y_b, *ends_b]
-    att_1, logs_1 = attend(1, tie(q, ring_c, x_b, y_b), kv, seg_row, seg_col)
-    ring_c = tie(ring_c, att_1)
+    att_1, logs_1 = attend(1, tie(q, att_0), kv, seg_row, seg_col)
+    held_x, held_y = lax.optimization_barrier((x_b, y_b, att_1))[:2]
+    turn_b = jnp.where(odd, held_y, held_x)
+    mlp_b = [ring_b, x_b, y_b, links.far(turn_b)]
+    ring_c = tie(ring_c, turn_b)
     x_c, y_c = links.along(ring_c), links.across(ring_c)
-    own, send = project(att_0, tie(att_1, *ends_b), wo)
+    own, send = project(att_0, tie(att_1, turn_b, ring_c), wo)
     n1, s1, low, low_t, gains = first_norm(x, own, links.beside(send), ring_b, x_b)
     low_other = links.beside(low)
-    low1_t = [low_t, links.beside(low_t)]
-    act_b_own, feed = mlp(low, None, mlp_b, half, f32)
+    x_t = lax.dot_general(
+        swap, tie(x_abs, low_other), (((0,), (1,)), ((), ())), preferred_element_type=f32
+    ).astype(bf16)
+    x_t = [x_t, links.beside(x_t)]
+    low1_t = [low_t, links.beside(tie(low_t, low_other))]
+    high, low_part = split(dy_own)
+    dy = jnp.concatenate([dot(high, swap) + dot(low_part, swap), dot(dy_came, swap)], axis=0)
+    act_b_own, feed = mlp(tie(low, x_t[1], low1_t[1], dy), None, mlp_b, sizes[0], f32)
+    act_b_other, feed_other = mlp(low_other, None, mlp_b, sizes[0], f32)
     held_x, held_y = lax.optimization_barrier((x_c, y_c, feed))[:2]
-    held_x, held_y = held_x[:cut], held_y[cut:]
-    ends_c = links.across(held_x), links.along(held_y)
-    act_b_other, feed_other = mlp(tie(low_other, held_x, held_y), None, mlp_b, half, f32)
-    mlp_c = [ring_c, x_c, y_c, *ends_c]
-    act_c_other, send = mlp(low_other, feed_other, mlp_c, half, bf16)
+    turn_c = jnp.where(odd, held_y, held_x)
+    mlp_c = [ring_c, x_c, y_c, links.far(turn_c)]
+    act_c_other, send = mlp(low_other, feed_other, mlp_c, sizes[1], bf16)
     came = links.beside(send)
-    act_c_own, feed = mlp(tie(low, send), feed, mlp_c, half, f32)
-    dy_came = links.across(tie(dy_other.astype(bf16), feed_other))
-    high, low = split(dy_own)
-    dy = jnp.concatenate([dot(high, swap) + dot(low, swap), dot(dy_came, swap)], axis=0)
+    act_c_own, feed = mlp(tie(low, send), feed, mlp_c, sizes[1], f32)
     layer_out, dh2, dfeed, dfeed_t, sums = second_norm(n1, gains, feed, came, dy)
     dfeeds = [dfeed, links.beside(dfeed)]
     dfeeds_t = [dfeed_t, links.beside(dfeed_t)]
 
     own, other, to_x, to_y, keep = mlp_back(None, dfeeds, dfeeds_t, low1_t, (act_c_own, act_c_other), mlp_c)
-    sum_c = Scatter(links, [to_x], to_y, keep)
+    sum_b = Scatter(links, [to_x], to_y, keep)
     own, other, to_x, to_y, keep = mlp_back(
         (own, other), dfeeds, dfeeds_t, low1_t, (act_b_own, act_b_other), mlp_b
     )
     came = links.beside(other)
-    sum_b = Scatter(links, [to_x], to_y, keep)
-    sum_c.keep = tie(sum_c.keep, own)
-    ops_c = sum_c.second()
-    dh1, low, low_t = first_back(tie(dh2, *ops_c), own, came, n1, s1, gains, sums)
+    sum_b.keep = tie(sum_b.keep, own)
+    ops_b = sum_b.second()
+    sum_c = Scatter(links, [tie(to_x, *ops_b)], tie(to_y, *ops_b), keep)
+    dh1, low, low_t = first_back(tie(dh2, *ops_b), own, came, n1, s1, gains, sums)
     lows = [low, links.beside(low)]
     low_t = [low_t, links.beside(low_t)]
     dq, dkv = attend_back(1, q, kv, *lows, wo, att_1, logs_1, seg_row, seg_col, cosine, sine)
+    sum_b.keep = tie(sum_b.keep, dq)
+    block_b = sum_b.third()
+    own, other, send, keep_1 = qkv_back(1, None, tie(dq, *block_b), dkv, x_t, low_t, att_1, attn_w)
+    own_b = sum_b.last()
+    sum_c.keep = tie(sum_c.keep, own)
+    ops_c = sum_c.second()
+    to_y, to_x = tie(send[:2], *ops_c), [tie(send[2:], *ops_c)]
+    dq, dkv = attend_back(
+        0, tie(q, own, *ops_c), kv, *lows, wo, att_0, logs_0, seg_row, seg_col, cosine, sine
+    )
     sum_c.keep = tie(sum_c.keep, dq)
     block_c = sum_c.third()
-    sum_b.keep = tie(sum_b.keep, dq)
-    ops_b = sum_b.second()
-    own, other, send, keep_1 = qkv_back(
-        1, None, tie(dq, *block_c, *ops_b), dkv, x_t, low_t, att_1, attn_w
+    own, other, send, keep_0 = qkv_back(
+        0, (own, other), tie(dq, *block_c, own_b), dkv, x_t, low_t, att_0, attn_w
     )
     own_c = sum_c.last()
-    dq, dkv = attend_back(0, tie(q, own), kv, *lows, wo, att_0, logs_0, seg_row, seg_col, cosine, sine)
-    sum_b.keep = tie(sum_b.keep, dq)
-    block_b = sum_b.third()
-    to_y, to_x = send[:2], [send[2:]]
-    own, other, send, keep_0 = qkv_back(
-        0, (own, other), tie(dq, *block_b, own_c), dkv, x_t, low_t, att_0, attn_w
-    )
-    own_b = sum_b.last()
     sum_a = Scatter(links, [send] + to_x, to_y, jnp.concatenate([keep_0, keep_1], axis=0))
-    layer_out = dot(layer_out, swap, NT).astype(bf16)
-    layer_out = from_sequence(layer_out[:mine], links.across(tie(layer_out[mine:], dq)))
     grad = dh1 + own + links.beside(other).astype(f32)
     high, low = split(grad)
     grad = dot(high, swap, NT) + dot(low, swap, NT)
     ops_a = sum_a.second()
     other = tie(grad[mine:].astype(bf16), *ops_a)
     input_grad = from_sequence(grad[:mine], links.across(other).astype(f32))
+    layer_out = dot(layer_out, swap, NT).astype(bf16)
+    layer_out = from_sequence(layer_out[:mine], links.across(tie(layer_out[mine:], *ops_a)))
     sum_a.third()
     own_attn = sum_a.last()
-    own_mlp = [own_b, own_c]
-
-    grad_down = jnp.concatenate([v[:, :half] for v in own_mlp], axis=1).T
+    own_mlp = [own_c, own_b]
+
+    grad_down = jnp.concatenate([v[:, :n] for v, n in zip(own_mlp, sizes)], axis=1).T
     grad_gate_up = jnp.stack(
         [
-            jnp.concatenate([v[:, (p + 1) * half : (p + 2) * half] for v in own_mlp], axis=1)
-            for p in range(2)
+            jnp.concatenate([v[:, p * n : (p + 1) * n] for v, n in zip(own_mlp, sizes)], axis=1)
+            for p in (1, 2)
         ],
         axis=1,
     )

time: 360 us -> 318 us (0.88)
  Pallas kernels: 169 us -> 103 us
  waiting for transfers between devices: 65.2 us -> 99.9 us
  starting transfers between devices: 58.7 us -> 48.4 us
  local copies, waits for them, and re-layouts: 26.6 us -> 35.2 us
  other arithmetic: 19.4 us -> 15 us
    ppermute x61 -> x52, waiting for transfers between devices: 65.2 us -> 99.9 us  [send(): return lax.ppermute(v, ('row', 'col'), pairs)]
    pallas_call x2, Pallas kernels: 39.5 us -> 21.7 us  [mlp_back(): pl.pallas_call(functools.partial(mlp_back_kernel, has_base), grid=(2,), i...]
    pallas_call x4, Pallas kernels: 31.6 us -> 14.8 us  [mlp(): pl.pallas_call(functools.partial(mlp_kernel, has_base), grid=(2,), in_spe...]
    ppermute x61 -> x52, starting transfers between devices: 58.7 us -> 48.4 us  [send(): return lax.ppermute(v, ('row', 'col'), pairs)]
    unnamed x102 -> x129, local copies, waits for them, and re-layouts: 11.3 us -> 20.5 us
    pallas_call x2, Pallas kernels: 16 us -> 7.43 us  [qkv_back(): pl.pallas_call(functools.partial(qkv_back_kernel, quarter, has_base), gri...]
    pallas_call x2, Pallas kernels: 32.3 us -> 27.9 us  [attend_back(): pl.pallas_call(attend_back_kernel, grid=(steps,), in_specs=[pl.BlockSpec(...]
    pallas_call x1, Pallas kernels: 6.05 us -> 1.67 us  [second_norm(): pl.pallas_call(second_kernel, grid=(1,), in_specs=[full, whole((8, width)...]
  transfers between devices with their start and end apart: 61 -> 52, of which waited for: 18 -> 21; matrix products, arithmetic and copies ran while one was open for 14% -> 13% of each run, Pallas kernels for 40% -> 27%
where the time goes in v7:
time: 318 us; the launch traced here: 314 us
  Pallas kernels  103 us (32%)
  waiting for transfers between devices  99.9 us (31%)
  starting transfers between devices  48.4 us (15%)
  local copies, waits for them, and re-layouts  35.2 us (11%)
  other arithmetic  15 us (5%)
  matrix products  9.75 us (3%)
    ppermute x52, waiting for transfers between devices, send(): return lax.ppermute(v, ('row', 'col'), pairs)  99.9 us
    ppermute x52, starting transfers between devices, send(): return lax.ppermute(v, ('row', 'col'), pairs)  48.4 us
    pallas_call x2, Pallas kernels, attend_back(): pl.pallas_call(attend_back_kernel, grid=(steps,), in_specs=[pl.BlockSpec(...  27.9 us
    pallas_call x2, Pallas kernels, mlp_back(): pl.pallas_call(functools.partial(mlp_back_kernel, has_base), grid=(2,), i...  21.7 us
    unnamed x129, local copies, waits for them, and re-layouts  20.5 us
    pallas_call x2, Pallas kernels, attend(): pl.pallas_call(attend_kernel, grid=(rows // QROWS,), in_specs=[pl.BlockSp...  18 us
    pallas_call x4, Pallas kernels, mlp(): pl.pallas_call(functools.partial(mlp_kernel, has_base), grid=(2,), in_spe...  14.8 us
    dot_general x7, matrix products, dot(): return lax.dot_general(a, b, dims, preferred_element_type=f32)  8.92 us
  transfers between devices with their start and end apart: 52, of which 21 were waited for; matrix products, arithmetic and copies ran while one was open for 13% of the time, Pallas kernels for 27%

profile of v7, /device:TPU:0, one launch (start us, length us, event | category | flops | bytes accessed | tf_op | source)
XLA Modules:
  0.0 313.5 jit_solution(14505389697751083888)
XLA Ops:
  2.6 4.1 %collective-permute-start.1 = (bf16[96,768]{1,0:T(8,128)(2,1)S(1)}, bf16[96,768]{1,0:T(8,128)(2,1)S(1)}, u32[]{:S(2)}, u32[]{:S(2)}) collective-permute-start(bf16[96,768]{1,0:T(8,128)(2,1)S(1)} %concatenate.64), channel_id=1, source_target_pairs={{0,16},{1,17},{2,18},{3,19},{4,20},{5,21},{6,22},{7,23},{8,24},{9,... | collective-permute-start | bytes 442376 | tf_op jit(solution)/shard_map/ppermute | solution.py:681
  7.5 1.6 collective-permute-start.9
  9.1 2.2 dynamic-slice_bitcast_fusion.1
  14.9 1.6 collective-permute-start.2
  16.6 6.0 %collective-permute-done.2 = bf16[192,768]{1,0:T(8,128)(2,1)S(1)} collective-permute-done((bf16[192,768]{1,0:T(8,128)(2,1)S(1)}, bf16[192,768]{1,0:T(8,128)(2,1)S(1)}, u32[]{:S(2)}, u32[]{:S(2)}) %collective-permute-start.2) | collective-permute-done | bytes 294944 | tf_op jit(solution)/shard_map/ppermute | solution.py:681
  22.6 2.6 collective-permute-start.3
  29.4 10.0 %collective-permute-done.3 = bf16[96,1664]{1,0:T(8,128)(2,1)S(1)} collective-permute-done((bf16[96,1664]{1,0:T(8,128)(2,1)S(1)}, bf16[96,1664]{1,0:T(8,128)(2,1)S(1)}, u32[]{:S(2)}, u32[]{:S(2)}) %collective-permute-start.3) | collective-permute-done | bytes 319520 | tf_op jit(solution)/shard_map/ppermute | solution.py:681
  40.2 1.7 fusion.9.own_ref.x_ref
  44.5 10.4 %collective-permute-done.4 = bf16[192,1664]{1,0:T(8,128)(2,1)S(1)} collective-permute-done((bf16[192,1664]{1,0:T(8,128)(2,1)S(1)}, bf16[192,1664]{1,0:T(8,128)(2,1)S(1)}, u32[]{:S(2)}, u32[]{:S(2)}) %collective-permute-start.4) | collective-permute-done | bytes 639008 | tf_op jit(solution)/shard_map/ppermute | solution.py:681
  55.0 3.3 %collective-permute-start.14 = (bf16[96,768]{1,0:T(8,128)(2,1)}, bf16[96,768]{1,0:T(8,128)(2,1)}, u32[]{:S(2)}, u32[]{:S(2)}) collective-permute-start(bf16[96,768]{1,0:T(8,128)(2,1)} %pad_maximum_fusion.14), channel_id=1, source_target_pairs={{0,16},{1,17},{2,18},{3,19},{4,20},{5,21},{6,22},{7,23},{8,24},{9,... | collective-permute-start | bytes 442376 | tf_op jit(solution)/shard_map/ppermute | solution.py:681
  62.2 2.0 tile.20
  64.2 2.6 copy.55.sin_ref
  71.9 1.8 collective-permute-start.15
  76.0 6.4 %qkv.1 = (bf16[1024,512]{1,0:T(8,128)(2,1)S(1)}, bf16[1024,1024]{1,0:T(8,128)(2,1)S(1)}, bf16[768,512]{1,0:T(8,128)(2,1)S(1)}) custom-call(bf16[512,768]{1,0:T(8,128)(2,1)} %fusion.9.own_ref.x_ref, bf16[512,768]{1,0:T(8,128)(2,1)} %collective-permute-done.8.other_ref, f32[1024,256]{1,0:T(8,128)S(1)} %copy.54.cos_ref, f32[1024,256]{1,0:T(8,128)S(1)} %copy-done.6, ...), custom_call_target="tpu_custom_call" | custom-call | flops 2415919104 | bytes 7864320 | tf_op jit(solution)/shard_map/qkv/pallas_call | solution.py:132
  82.5 9.0 %attend.2 = (bf16[1024,256]{1,0:T(8,128)(2,1)S(1)}, f32[8,1024]{1,0:T(8,128)S(1)}) custom-call(bf16[1024,512]{1,0:T(8,128)(2,1)S(1)} %get-tuple-element.156.q_ref, bf16[1024,1024]{1,0:T(8,128)(2,1)S(1)} %get-tuple-element.97.kv_ref, s32[1,1024]{1,0:T(1,128)S(1)} %get-tuple-element.233.segq_ref, s32[1024,1]{1,0:T(8,128)S(1)} %copy-done.17), custom_call_target="tpu_custom_call" | custom-call | flops 4294967296 | bytes 3145728 | tf_op jit(solution)/shard_map/attend/pallas_call | solution.py:182
  91.5 9.0 %attend.3 = (bf16[1024,256]{1,0:T(8,128)(2,1)S(1)}, f32[8,1024]{1,0:T(8,128)S(1)}) custom-call(bf16[1024,512]{1,0:T(8,128)(2,1)S(1)} %get-tuple-element.156.q_ref, bf16[1024,1024]{1,0:T(8,128)(2,1)S(1)} %get-tuple-element.97.kv_ref, s32[1,1024]{1,0:T(1,128)S(1)} %get-tuple-element.233.segq_ref, s32[1024,1]{1,0:T(8,128)S(1)} %copy-done.17), custom_call_target="tpu_custom_call" | custom-call | flops 4294967296 | bytes 3145728 | tf_op jit(solution)/shard_map/attend/pallas_call | solution.py:182
  103.1 2.3 collective-permute-done.16.came_ref
  105.4 2.2 first_norm.1
  114.5 1.7 fusion.3
  116.3 15.7 %collective-permute-done.18.rest_3_.rest_13_ = bf16[384,1664]{1,0:T(8,128)(2,1)S(1)} collective-permute-done((bf16[384,1664]{1,0:T(8,128)(2,1)S(1)}, bf16[384,1664]{1,0:T(8,128)(2,1)S(1)}, u32[]{:S(2)}, u32[]{:S(2)}) %collective-permute-start.18) | collective-permute-done | bytes 1277984 | tf_op jit(solution)/shard_map/ppermute | solution.py:681
  131.9 5.0 %mlp.5 = (bf16[2,3,512,512]{3,2,1,0:T(8,128)(2,1)S(1)}, f32[512,768]{1,0:T(8,128)S(1)}) custom-call(bf16[512,768]{1,0:T(8,128)(2,1)S(1)} %get-tuple-element.121.low_ref, bf16[384,1664]{1,0:T(8,128)(2,1)S(1)} %pad_maximum_fusion.2.norm_a_ref.rest_0_.rest_10_, bf16[384,1664]{1,0:T(8,128)(2,1)S(1)} %collective-permute-done.12.norm_b_ref.rest_1_.rest_11_, ...), custom_call_target="tpu_custom_call" | custom-call | flops 2415919104 | bytes 11796480 | tf_op jit(solution)/shard_map/mlp/pallas_call | solution.py:393
  136.9 1.7 copy-done.37
  139.3 4.8 %mlp.4 = (bf16[2,3,512,512]{3,2,1,0:T(8,128)(2,1)S(1)}, f32[512,768]{1,0:T(8,128)S(1)}) custom-call(bf16[512,768]{1,0:T(8,128)(2,1)S(1)} %collective-permute-done.17.low_ref, bf16[384,1664]{1,0:T(8,128)(2,1)S(1)} %pad_maximum_fusion.2.norm_a_ref.rest_0_.rest_10_, bf16[384,1664]{1,0:T(8,128)(2,1)S(1)} %collective-permute-done.12.norm_b_ref.rest_1_.rest_11_, ...), custom_call_target="tpu_custom_call" | custom-call | flops 2415919104 | bytes 11796480 | tf_op jit(solution)/shard_map/mlp/pallas_call | solution.py:393
  144.1 4.6 %collective-permute-done.23.rest_4_.rest_11_ = bf16[384,768]{1,0:T(8,128)(2,1)S(1)} collective-permute-done((bf16[384,768]{1,0:T(8,128)(2,1)S(1)}, bf16[384,768]{1,0:T(8,128)(2,1)S(1)}, u32[]{:S(2)}, u32[]{:S(2)}) %collective-permute-start.23) | collective-permute-done | bytes 589856 | tf_op jit(solution)/shard_map/ppermute | solution.py:681
  148.6 2.5 mlp.6
  151.2 2.5 mlp.7
  153.8 1.7 second_norm.1
  156.8 1.9 collective-permute-done.25.rest_1_
  159.8 8.0 %mlp_back.2 = (f32[512,768]{1,0:T(8,128)S(1)}, f32[512,768]{1,0:T(8,128)S(1)}, bf16[2,192,768]{2,1,0:T(8,128)(2,1)S(1)}, bf16[2,192,768]{2,1,0:T(8,128)(2,1)S(1)}, bf16[4,192,768]{2,1,0:T(8,128)(2,1)S(1)}) custom-call(bf16[512,768]{1,0:T(8,128)(2,1)S(1)} %get-tuple-element.125.rest_0_, bf16[512,768]{1,0:T(8,128)(2,1)S(1)} %collective-permute-done.25.rest_1_, ...), custom_call_target="tpu_custom_call" | custom-call | flops 4831838208 | bytes 19660800 | tf_op jit(solution)/shard_map/mlp_back/pallas_call | solution.py:515
  172.5 1.9 copy-done.38
  174.4 13.7 %mlp_back.3 = (f32[512,768]{1,0:T(8,128)S(1)}, bf16[512,768]{1,0:T(8,128)(2,1)S(1)}, bf16[2,192,1536]{2,1,0:T(8,128)(2,1)S(1)}, bf16[2,192,1536]{2,1,0:T(8,128)(2,1)S(1)}, bf16[4,192,1536]{2,1,0:T(8,128)(2,1)S(1)}) custom-call(bf16[512,768]{1,0:T(8,128)(2,1)S(1)} %get-tuple-element.125.rest_0_, bf16[512,768]{1,0:T(8,128)(2,1)S(1)} %collective-permute-done.25.rest_1_, ...), custom_call_target="tpu_custom_call" | custom-call | flops 9663676416 | bytes 39321600 | tf_op jit(solution)/shard_map/mlp_back/pallas_call | solution.py:515
  190.6 2.1 first_back.1
  194.0 2.1 fusion.10
  196.1 1.6 collective-permute-start.31
  201.4 1.6 copy-done.40
  204.3 14.2 %attend_back.2 = (bf16[1024,256]{1,0:T(8,128)(2,1)S(1)}, bf16[1024,512]{1,0:T(8,128)(2,1)S(1)}) custom-call(bf16[1024,512]{1,0:T(8,128)(2,1)S(1)} %copy-done.43, bf16[1024,1024]{1,0:T(8,128)(2,1)S(1)} %copy-done.40, bf16[512,768]{1,0:T(8,128)(2,1)} %get-tuple-element.142.own_ref, bf16[512,768]{1,0:T(8,128)(2,1)} %collective-permute-done.30.other_ref, ...), custom_call_target="tpu_custom_call" | custom-call | flops 10737418240 | bytes 7864320 | tf_op jit(solution)/shard_map/attend_back/pallas_call | solution.py:263
  219.1 3.6 %qkv_back.2 = (f32[512,768]{1,0:T(8,128)S(1)}, f32[512,768]{1,0:T(8,128)S(1)}, bf16[3,192,896]{2,1,0:T(8,128)(2,1)S(1)}, bf16[1,192,896]{2,1,0:T(8,128)(2,1)S(1)}) custom-call(bf16[1024,256]{1,0:T(8,128)(2,1)S(1)} %get-tuple-element.146.dq_ref, bf16[1024,512]{1,0:T(8,128)(2,1)S(1)} %get-tuple-element.147.dkv_ref, bf16[768,512]{1,0:T(8,128)(2,1)S(1)} %copy-done.9, ...), custom_call_target="tpu_custom_call" | custom-call | flops 2617245696 | bytes 7864320 | tf_op jit(solution)/shard_map/qkv_back/pallas_call | solution.py:633
  222.7 8.3 %collective-permute-done.33 = bf16[2,192,1536]{2,1,0:T(8,128)(2,1)S(1)} collective-permute-done((bf16[2,192,1536]{2,1,0:T(8,128)(2,1)S(1)}, bf16[2,192,1536]{2,1,0:T(8,128)(2,1)S(1)}, u32[]{:S(2)}, u32[]{:S(2)}) %collective-permute-start.33) | collective-permute-done | bytes 1179680 | tf_op jit(solution)/shard_map/ppermute | solution.py:681
  235.3 13.7 %attend_back.3 = (bf16[1024,256]{1,0:T(8,128)(2,1)S(1)}, bf16[1024,512]{1,0:T(8,128)(2,1)S(1)}) custom-call(bf16[1024,512]{1,0:T(8,128)(2,1)S(1)} %copy-done.44, bf16[1024,1024]{1,0:T(8,128)(2,1)S(1)} %copy-done.41, bf16[512,768]{1,0:T(8,128)(2,1)} %get-tuple-element.142.own_ref, bf16[512,768]{1,0:T(8,128)(2,1)} %collective-permute-done.30.other_ref, ...), custom_call_target="tpu_custom_call" | custom-call | flops 10737418240 | bytes 7864320 | tf_op jit(solution)/shard_map/attend_back/pallas_call | solution.py:263
  250.7 4.1 %collective-permute-done.40 = bf16[1,192,896]{2,1,0:T(8,128)(2,1)S(1)} collective-permute-done((bf16[1,192,896]{2,1,0:T(8,128)(2,1)S(1)}, bf16[1,192,896]{2,1,0:T(8,128)(2,1)S(1)}, u32[]{:S(2)}, u32[]{:S(2)}) %collective-permute-start.40) | collective-permute-done | bytes 344096 | tf_op jit(solution)/shard_map/ppermute | solution.py:681
  256.4 3.9 %qkv_back.3 = (f32[512,768]{1,0:T(8,128)S(1)}, bf16[512,768]{1,0:T(8,128)(2,1)S(1)}, bf16[1,192,896]{2,1,0:T(8,128)(2,1)S(1)}, bf16[3,192,896]{2,1,0:T(8,128)(2,1)S(1)}) custom-call(bf16[1024,256]{1,0:T(8,128)(2,1)S(1)} %get-tuple-element.160.dq_ref, bf16[1024,512]{1,0:T(8,128)(2,1)S(1)} %get-tuple-element.161.dkv_ref, bf16[768,512]{1,0:T(8,128)(2,1)S(1)} %copy-done.9, ...), custom_call_target="tpu_custom_call" | custom-call | flops 2617245696 | bytes 7864320 | tf_op jit(solution)/shard_map/qkv_back/pallas_call | solution.py:633
  261.8 5.7 %collective-permute-done.39 = bf16[2,192,896]{2,1,0:T(8,128)(2,1)S(1)} collective-permute-done((bf16[2,192,896]{2,1,0:T(8,128)(2,1)S(1)}, bf16[2,192,896]{2,1,0:T(8,128)(2,1)S(1)}, u32[]{:S(2)}, u32[]{:S(2)}) %collective-permute-start.39) | collective-permute-done | bytes 688160 | tf_op jit(solution)/shard_map/ppermute | solution.py:681
  267.6 1.6 collective-permute-start.41
  270.2 4.7 %collective-permute-done.46 = bf16[192,896]{1,0:T(8,128)(2,1)S(1)} collective-permute-done((bf16[192,896]{1,0:T(8,128)(2,1)S(1)}, bf16[192,896]{1,0:T(8,128)(2,1)S(1)}, u32[]{:S(2)}, u32[]{:S(2)}) %collective-permute-start.46) | collective-permute-done | bytes 344096 | tf_op jit(solution)/shard_map/ppermute | solution.py:681
  276.5 4.5 %collective-permute-done.41 = bf16[256,768]{1,0:T(8,128)(2,1)S(1)} collective-permute-done((bf16[256,768]{1,0:T(8,128)(2,1)S(1)}, bf16[256,768]{1,0:T(8,128)(2,1)S(1)}, u32[]{:S(2)}, u32[]{:S(2)}) %collective-permute-start.41) | collective-permute-done | bytes 393248 | tf_op jit(solution)/shard_map/ppermute | solution.py:681
  283.4 2.6 collective-permute-start.51
  286.0 8.7 %collective-permute-done.47 = bf16[192,896]{1,0:T(8,128)(2,1)S(1)} collective-permute-done((bf16[192,896]{1,0:T(8,128)(2,1)S(1)}, bf16[192,896]{1,0:T(8,128)(2,1)S(1)}, u32[]{:S(2)}, u32[]{:S(2)}) %collective-permute-start.47) | collective-permute-done | bytes 344096 | tf_op jit(solution)/shard_map/ppermute | solution.py:681
  298.9 5.8 %collective-permute-done.48 = bf16[96,896]{1,0:T(8,128)(2,1)S(1)} collective-permute-done((bf16[96,896]{1,0:T(8,128)(2,1)S(1)}, bf16[96,896]{1,0:T(8,128)(2,1)S(1)}, u32[]{:S(2)}, u32[]{:S(2)}) %collective-permute-start.48) | collective-permute-done | bytes 172064 | tf_op jit(solution)/shard_map/ppermute | solution.py:681
  (283 shorter events, 78.5 us)
Async XLA Ops:
  2.6 12.2 %collective-permute-start.1 = (bf16[96,768]{1,0:T(8,128)(2,1)S(1)}, bf16[96,768]{1,0:T(8,128)(2,1)S(1)}, u32[]{:S(2)}, u32[]{:S(2)}) collective-permute-start(bf16[96,768]{1,0:T(8,128)(2,1)S(1)} %concatenate.64), channel_id=1, source_target_pairs={{0,16},{1,17},{2,18},{3,19},{4,20},{5,21},{6,22},{7,23},{8,24},{9,... | collective-permute-start | bytes 442376 | tf_op jit(solution)/shard_map/ppermute | solution.py:681
  7.5 17.7 %collective-permute-start.9 = (s32[2,256]{1,0:T(2,128)S(1)}, s32[2,256]{1,0:T(2,128)S(1)}, u32[]{:S(2)}, u32[]{:S(2)}) collective-permute-start(s32[2,256]{1,0:T(2,128)S(1)} %bitcast.114), channel_id=1, source_target_pairs={{0,2},{1,3},{2,0},{3,1},{4,6},{5,7},{6,4},{7,5},{8,10},{9,11},{10,... | collective-permute-start | bytes 6152 | tf_op jit(solution)/shard_map/ppermute | solution.py:681
  11.3 28.8 %collective-permute-start = (bf16[256,768]{1,0:T(8,128)(2,1)S(1)}, bf16[256,768]{1,0:T(8,128)(2,1)S(1)}, u32[]{:S(2)}, u32[]{:S(2)}) collective-permute-start(bf16[256,768]{1,0:T(8,128)(2,1)S(1)} %get-tuple-element.91), channel_id=1, source_target_pairs={{0,2},{1,3},{2,0},{3,1},{4,6},{5,7},{6,4},{7,5},{8,10},{9,11},{10,... | collective-permute-start | bytes 1179656 | tf_op jit(solution)/shard_map/ppermute | solution.py:681
  11.9 57.4 %collective-permute-start.7 = (bf16[256,768]{1,0:T(8,128)(2,1)}, bf16[256,768]{1,0:T(8,128)(2,1)}, u32[]{:S(2)}, u32[]{:S(2)}) collective-permute-start(bf16[256,768]{1,0:T(8,128)(2,1)} %get-tuple-element.94), channel_id=1, source_target_pairs={{0,2},{1,3},{2,0},{3,1},{4,6},{5,7},{6,4},{7,5},{8,10},{9,11},{10,... | collective-permute-start | bytes 1179656 | tf_op jit(solution)/shard_map/ppermute | solution.py:681
  14.9 7.7 %collective-permute-start.2 = (bf16[192,768]{1,0:T(8,128)(2,1)S(1)}, bf16[192,768]{1,0:T(8,128)(2,1)S(1)}, u32[]{:S(2)}, u32[]{:S(2)}) collective-permute-start(bf16[192,768]{1,0:T(8,128)(2,1)S(1)} %pad_maximum_fusion.9), channel_id=1, source_target_pairs={{0,8},{1,9},{2,10},{3,11},{4,12},{5,13},{6,14},{7,15},{8,0},{9,1},... | collective-permute-start | bytes 884744 | tf_op jit(solution)/shard_map/ppermute | solution.py:681
  22.6 16.8 %collective-permute-start.3 = (bf16[96,1664]{1,0:T(8,128)(2,1)S(1)}, bf16[96,1664]{1,0:T(8,128)(2,1)S(1)}, u32[]{:S(2)}, u32[]{:S(2)}) collective-permute-start(bf16[96,1664]{1,0:T(8,128)(2,1)S(1)} %fusion.39), channel_id=1, source_target_pairs={{0,16},{1,17},{2,18},{3,19},{4,20},{5,21},{6,22},{7,23},{8,24},{9,... | collective-permute-start | bytes 958472 | tf_op jit(solution)/shard_map/ppermute | solution.py:681
  26.4 16.4 %collective-permute-start.5 = (bf16[384,768]{1,0:T(8,128)(2,1)S(1)}, bf16[384,768]{1,0:T(8,128)(2,1)S(1)}, u32[]{:S(2)}, u32[]{:S(2)}) collective-permute-start(bf16[384,768]{1,0:T(8,128)(2,1)S(1)} %pad_maximum_fusion.6.rest_0_.rest_2_), channel_id=1, source_target_pairs={{0,2},{1,3},{2,0},{3,1},{4,6},{5,7},{6,4},{7,5},{8,10},{9,11},{10,... | collective-permute-start | bytes 1769480 | tf_op jit(solution)/shard_map/ppermute | solution.py:681
  27.9 15.1 %collective-permute-start.6 = (bf16[384,768]{1,0:T(8,128)(2,1)S(1)}, bf16[384,768]{1,0:T(8,128)(2,1)S(1)}, u32[]{:S(2)}, u32[]{:S(2)}) collective-permute-start(bf16[384,768]{1,0:T(8,128)(2,1)S(1)} %pad_maximum_fusion.6.rest_0_.rest_2_), channel_id=1, source_target_pairs={{0,4},{1,5},{2,6},{3,7},{4,0},{5,1},{6,2},{7,3},{8,12},{9,13},{10,... | collective-permute-start | bytes 1769480 | tf_op jit(solution)/shard_map/ppermute | solution.py:681
  39.4 15.4 %collective-permute-start.4 = (bf16[192,1664]{1,0:T(8,128)(2,1)S(1)}, bf16[192,1664]{1,0:T(8,128)(2,1)S(1)}, u32[]{:S(2)}, u32[]{:S(2)}) collective-permute-start(bf16[192,1664]{1,0:T(8,128)(2,1)S(1)} %pad_maximum_fusion.5), channel_id=1, source_target_pairs={{0,8},{1,9},{2,10},{3,11},{4,12},{5,13},{6,14},{7,15},{8,0},{9,1},... | collective-permute-start | bytes 1916936 | tf_op jit(solution)/shard_map/ppermute | solution.py:681
  42.0 31.8 %collective-permute-start.8 = (bf16[512,768]{1,0:T(8,128)(2,1)}, bf16[512,768]{1,0:T(8,128)(2,1)}, u32[]{:S(2)}, u32[]{:S(2)}) collective-permute-start(bf16[512,768]{1,0:T(8,128)(2,1)} %fusion.9.own_ref.x_ref), channel_id=1, source_target_pairs={{0,1},{1,0},{2,3},{3,2},{4,5},{5,4},{6,7},{7,6},{8,9},{9,8},{10,11... | collective-permute-start | bytes 2359304 | tf_op jit(solution)/shard_map/ppermute | solution.py:681
  44.0 29.7 %collective-permute-start.11 = (bf16[384,768]{1,0:T(8,128)(2,1)}, bf16[384,768]{1,0:T(8,128)(2,1)}, u32[]{:S(2)}, u32[]{:S(2)}) collective-permute-start(bf16[384,768]{1,0:T(8,128)(2,1)} %broadcast_select_fusion.2), channel_id=1, source_target_pairs={{0,2},{1,5},{2,0},{3,7},{4,6},{5,1},{6,4},{7,3},{8,10},{9,13},{10,... | collective-permute-start | bytes 1769480 | tf_op jit(solution)/shard_map/ppermute | solution.py:681
  55.0 15.9 %collective-permute-start.14 = (bf16[96,768]{1,0:T(8,128)(2,1)}, bf16[96,768]{1,0:T(8,128)(2,1)}, u32[]{:S(2)}, u32[]{:S(2)}) collective-permute-start(bf16[96,768]{1,0:T(8,128)(2,1)} %pad_maximum_fusion.14), channel_id=1, source_target_pairs={{0,16},{1,17},{2,18},{3,19},{4,20},{5,21},{6,22},{7,23},{8,24},{9,... | collective-permute-start | bytes 442376 | tf_op jit(solution)/shard_map/ppermute | solution.py:681
  67.8 34.0 %collective-permute-start.12 = (bf16[384,1664]{1,0:T(8,128)(2,1)S(1)}, bf16[384,1664]{1,0:T(8,128)(2,1)S(1)}, u32[]{:S(2)}, u32[]{:S(2)}) collective-permute-start(bf16[384,1664]{1,0:T(8,128)(2,1)S(1)} %pad_maximum_fusion.2.norm_a_ref.rest_0_.rest_10_), channel_id=1, source_target_pairs={{0,4},{1,5},{2,6},{3,7},{4,0},{5,1},{6,2},{7,3},{8,12},{9,13},{10,... | collective-permute-start | bytes 3833864 | tf_op jit(solution)/shard_map/ppermute | solution.py:681
  69.3 32.5 %collective-permute-start.13 = (bf16[384,1664]{1,0:T(8,128)(2,1)S(1)}, bf16[384,1664]{1,0:T(8,128)(2,1)S(1)}, u32[]{:S(2)}, u32[]{:S(2)}) collective-permute-start(bf16[384,1664]{1,0:T(8,128)(2,1)S(1)} %pad_maximum_fusion.2.norm_a_ref.rest_0_.rest_10_), channel_id=1, source_target_pairs={{0,2},{1,3},{2,0},{3,1},{4,6},{5,7},{6,4},{7,5},{8,10},{9,11},{10,... | collective-permute-start | bytes 3833864 | tf_op jit(solution)/shard_map/ppermute | solution.py:681
  71.9 28.6 %collective-permute-start.15 = (bf16[192,768]{1,0:T(8,128)(2,1)S(1)}, bf16[192,768]{1,0:T(8,128)(2,1)S(1)}, u32[]{:S(2)}, u32[]{:S(2)}) collective-permute-start(bf16[192,768]{1,0:T(8,128)(2,1)S(1)} %pad_maximum_fusion.10), channel_id=1, source_target_pairs={{0,8},{1,9},{2,10},{3,11},{4,12},{5,13},{6,14},{7,15},{8,0},{9,1},... | collective-permute-start | bytes 884744 | tf_op jit(solution)/shard_map/ppermute | solution.py:681
  108.4 23.6 %collective-permute-start.18 = (bf16[384,1664]{1,0:T(8,128)(2,1)S(1)}, bf16[384,1664]{1,0:T(8,128)(2,1)S(1)}, u32[]{:S(2)}, u32[]{:S(2)}) collective-permute-start(bf16[384,1664]{1,0:T(8,128)(2,1)S(1)} %broadcast_select_fusion), channel_id=1, source_target_pairs={{0,2},{1,5},{2,0},{3,7},{4,6},{5,1},{6,4},{7,3},{8,10},{9,13},{10,... | collective-permute-start | bytes 3833864 | tf_op jit(solution)/shard_map/ppermute | solution.py:681
  110.5 5.7 %collective-permute-start.22 = (bf16[768,512]{1,0:T(8,128)(2,1)S(1)}, bf16[768,512]{1,0:T(8,128)(2,1)S(1)}, u32[]{:S(2)}, u32[]{:S(2)}) collective-permute-start(bf16[768,512]{1,0:T(8,128)(2,1)S(1)} %get-tuple-element.115.rest_4_), channel_id=1, source_target_pairs={{0,1},{1,0},{2,3},{3,2},{4,5},{5,4},{6,7},{7,6},{8,9},{9,8},{10,11... | collective-permute-start | bytes 2359304 | tf_op jit(solution)/shard_map/ppermute | solution.py:681
  111.5 4.8 %collective-permute-start.21 = (bf16[768,512]{1,0:T(8,128)(2,1)S(1)}, bf16[768,512]{1,0:T(8,128)(2,1)S(1)}, u32[]{:S(2)}, u32[]{:S(2)}) collective-permute-start(bf16[768,512]{1,0:T(8,128)(2,1)S(1)} %convolution_convert_fusion.x_a_ref), channel_id=1, source_target_pairs={{0,1},{1,0},{2,3},{3,2},{4,5},{5,4},{6,7},{7,6},{8,9},{9,8},{10,11... | collective-permute-start | bytes 2359304 | tf_op jit(solution)/shard_map/ppermute | solution.py:681
  113.3 25.3 %collective-permute-start.19 = (bf16[384,768]{1,0:T(8,128)(2,1)S(1)}, bf16[384,768]{1,0:T(8,128)(2,1)S(1)}, u32[]{:S(2)}, u32[]{:S(2)}) collective-permute-start(bf16[384,768]{1,0:T(8,128)(2,1)S(1)} %pad_maximum_fusion.7.rest_1_.rest_8_), channel_id=1, source_target_pairs={{0,4},{1,5},{2,6},{3,7},{4,0},{5,1},{6,2},{7,3},{8,12},{9,13},{10,... | collective-permute-start | bytes 1769480 | tf_op jit(solution)/shard_map/ppermute | solution.py:681
  113.9 24.7 %collective-permute-start.20 = (bf16[384,768]{1,0:T(8,128)(2,1)S(1)}, bf16[384,768]{1,0:T(8,128)(2,1)S(1)}, u32[]{:S(2)}, u32[]{:S(2)}) collective-permute-start(bf16[384,768]{1,0:T(8,128)(2,1)S(1)} %pad_maximum_fusion.7.rest_1_.rest_8_), channel_id=1, source_target_pairs={{0,2},{1,3},{2,0},{3,1},{4,6},{5,7},{6,4},{7,5},{8,10},{9,11},{10,... | collective-permute-start | bytes 1769480 | tf_op jit(solution)/shard_map/ppermute | solution.py:681
  138.7 9.9 %collective-permute-start.23 = (bf16[384,768]{1,0:T(8,128)(2,1)S(1)}, bf16[384,768]{1,0:T(8,128)(2,1)S(1)}, u32[]{:S(2)}, u32[]{:S(2)}) collective-permute-start(bf16[384,768]{1,0:T(8,128)(2,1)S(1)} %broadcast_select_fusion.1), channel_id=1, source_target_pairs={{0,2},{1,5},{2,0},{3,7},{4,6},{5,1},{6,4},{7,3},{8,10},{9,13},{10,... | collective-permute-start | bytes 1769480 | tf_op jit(solution)/shard_map/ppermute | solution.py:681
  151.1 2.6 collective-permute-start.24
  156.3 2.4 collective-permute-start.25
  156.8 3.0 collective-permute-start.26
  167.8 20.4 %collective-permute-start.27 = (bf16[2,192,768]{2,1,0:T(8,128)(2,1)S(1)}, bf16[2,192,768]{2,1,0:T(8,128)(2,1)S(1)}, u32[]{:S(2)}, u32[]{:S(2)}) collective-permute-start(bf16[2,192,768]{2,1,0:T(8,128)(2,1)S(1)} %get-tuple-element.136), channel_id=1, source_target_pairs={{0,2},{1,3},{2,0},{3,1},{4,6},{5,7},{6,4},{7,5},{8,10},{9,11},{10,... | collective-permute-start | bytes 1769480 | tf_op jit(solution)/shard_map/ppermute | solution.py:681
  168.4 19.9 %collective-permute-start.28 = (bf16[2,192,768]{2,1,0:T(8,128)(2,1)S(1)}, bf16[2,192,768]{2,1,0:T(8,128)(2,1)S(1)}, u32[]{:S(2)}, u32[]{:S(2)}) collective-permute-start(bf16[2,192,768]{2,1,0:T(8,128)(2,1)S(1)} %get-tuple-element.137), channel_id=1, source_target_pairs={{0,4},{1,5},{2,6},{3,7},{4,0},{5,1},{6,2},{7,3},{8,12},{9,13},{10,... | collective-permute-start | bytes 1769480 | tf_op jit(solution)/shard_map/ppermute | solution.py:681
  193.8 6.5 %collective-permute-start.30 = (bf16[512,768]{1,0:T(8,128)(2,1)}, bf16[512,768]{1,0:T(8,128)(2,1)}, u32[]{:S(2)}, u32[]{:S(2)}) collective-permute-start(bf16[512,768]{1,0:T(8,128)(2,1)} %get-tuple-element.142.own_ref), channel_id=1, source_target_pairs={{0,1},{1,0},{2,3},{3,2},{4,5},{5,4},{6,7},{7,6},{8,9},{9,8},{10,11... | collective-permute-start | bytes 2359304 | tf_op jit(solution)/shard_map/ppermute | solution.py:681
  196.1 22.4 %collective-permute-start.31 = (bf16[192,768]{1,0:T(8,128)(2,1)}, bf16[192,768]{1,0:T(8,128)(2,1)S(1)}, u32[]{:S(2)}, u32[]{:S(2)}) collective-permute-start(bf16[192,768]{1,0:T(8,128)(2,1)} %get-tuple-element.204), channel_id=1, source_target_pairs={{0,2},{1,3},{2,0},{3,1},{4,6},{5,7},{6,4},{7,5},{8,10},{9,11},{10,... | collective-permute-start | bytes 884744 | tf_op jit(solution)/shard_map/ppermute | solution.py:681
  197.7 37.3 %collective-permute-start.36 = (bf16[192,768]{1,0:T(8,128)(2,1)S(1)}, bf16[192,768]{1,0:T(8,128)(2,1)S(1)}, u32[]{:S(2)}, u32[]{:S(2)}) collective-permute-start(bf16[192,768]{1,0:T(8,128)(2,1)S(1)} %get-tuple-element.205), channel_id=1, source_target_pairs={{0,4},{1,5},{2,6},{3,7},{4,0},{5,1},{6,2},{7,3},{8,12},{9,13},{10,... | collective-permute-start | bytes 884744 | tf_op jit(solution)/shard_map/ppermute | solution.py:681
  199.2 31.8 %collective-permute-start.33 = (bf16[2,192,1536]{2,1,0:T(8,128)(2,1)S(1)}, bf16[2,192,1536]{2,1,0:T(8,128)(2,1)S(1)}, u32[]{:S(2)}, u32[]{:S(2)}) collective-permute-start(bf16[2,192,1536]{2,1,0:T(8,128)(2,1)S(1)} %copy-done.26), channel_id=1, source_target_pairs={{0,2},{1,3},{2,0},{3,1},{4,6},{5,7},{6,4},{7,5},{8,10},{9,11},{10,... | collective-permute-start | bytes 3538952 | tf_op jit(solution)/shard_map/ppermute | solution.py:681
  199.7 32.3 %collective-permute-start.34 = (bf16[2,192,1536]{2,1,0:T(8,128)(2,1)S(1)}, bf16[2,192,1536]{2,1,0:T(8,128)(2,1)S(1)}, u32[]{:S(2)}, u32[]{:S(2)}) collective-permute-start(bf16[2,192,1536]{2,1,0:T(8,128)(2,1)S(1)} %copy-done.24), channel_id=1, source_target_pairs={{0,4},{1,5},{2,6},{3,7},{4,0},{5,1},{6,2},{7,3},{8,12},{9,13},{10,... | collective-permute-start | bytes 3538952 | tf_op jit(solution)/shard_map/ppermute | solution.py:681
  200.3 18.8 %collective-permute-start.32 = (bf16[768,640]{1,0:T(8,128)(2,1)S(1)}, bf16[768,640]{1,0:T(8,128)(2,1)S(1)}, u32[]{:S(2)}, u32[]{:S(2)}) collective-permute-start(bf16[768,640]{1,0:T(8,128)(2,1)S(1)} %get-tuple-element.148.low_a_ref.cols_a_ref), channel_id=1, source_target_pairs={{0,1},{1,0},{2,3},{3,2},{4,5},{5,4},{6,7},{7,6},{8,9},{9,8},{10,11... | collective-permute-start | bytes 2949128 | tf_op jit(solution)/shard_map/ppermute | solution.py:681
  218.7 16.4 %collective-permute-start.37 = (bf16[192,768]{1,0:T(8,128)(2,1)S(1)}, bf16[192,768]{1,0:T(8,128)(2,1)S(1)}, u32[]{:S(2)}, u32[]{:S(2)}) collective-permute-start(bf16[192,768]{1,0:T(8,128)(2,1)S(1)} %fusion.32), channel_id=1, source_target_pairs={{0,8},{1,9},{2,10},{3,11},{4,12},{5,13},{6,14},{7,15},{8,0},{9,1},... | collective-permute-start | bytes 884744 | tf_op jit(solution)/shard_map/ppermute | solution.py:681
  232.3 23.8 %collective-permute-start.35 = (bf16[192,1536]{1,0:T(8,128)(2,1)S(1)}, bf16[192,1536]{1,0:T(8,128)(2,1)S(1)}, u32[]{:S(2)}, u32[]{:S(2)}) collective-permute-start(bf16[192,1536]{1,0:T(8,128)(2,1)S(1)} %get-tuple-element.198), channel_id=1, source_target_pairs={{0,2},{1,3},{2,0},{3,1},{4,6},{5,7},{6,4},{7,5},{8,10},{9,11},{10,... | collective-permute-start | bytes 1769480 | tf_op jit(solution)/shard_map/ppermute | solution.py:681
  232.9 49.4 %collective-permute-start.49 = (bf16[192,1536]{1,0:T(8,128)(2,1)S(1)}, bf16[192,1536]{1,0:T(8,128)(2,1)S(1)}, u32[]{:S(2)}, u32[]{:S(2)}) collective-permute-start(bf16[192,1536]{1,0:T(8,128)(2,1)S(1)} %get-tuple-element.199), channel_id=1, source_target_pairs={{0,4},{1,5},{2,6},{3,7},{4,0},{5,1},{6,2},{7,3},{8,12},{9,13},{10,... | collective-permute-start | bytes 1769480 | tf_op jit(solution)/shard_map/ppermute | solution.py:681
  234.4 20.4 %collective-permute-start.40 = (bf16[1,192,896]{2,1,0:T(8,128)(2,1)S(1)}, bf16[1,192,896]{2,1,0:T(8,128)(2,1)S(1)}, u32[]{:S(2)}, u32[]{:S(2)}) collective-permute-start(bf16[1,192,896]{2,1,0:T(8,128)(2,1)S(1)} %slice.209), channel_id=1, source_target_pairs={{0,4},{1,5},{2,6},{3,7},{4,0},{5,1},{6,2},{7,3},{8,12},{9,13},{10,... | collective-permute-start | bytes 1032200 | tf_op jit(solution)/shard_map/ppermute | solution.py:681
  235.2 15.5 %collective-permute-start.38 = (bf16[96,768]{1,0:T(8,128)(2,1)S(1)}, bf16[96,768]{1,0:T(8,128)(2,1)S(1)}, u32[]{:S(2)}, u32[]{:S(2)}) collective-permute-start(bf16[96,768]{1,0:T(8,128)(2,1)S(1)} %split.41), channel_id=1, source_target_pairs={{0,16},{1,17},{2,18},{3,19},{4,20},{5,21},{6,22},{7,23},{8,24},{9,... | collective-permute-start | bytes 442376 | tf_op jit(solution)/shard_map/ppermute | solution.py:681
  249.1 18.4 %collective-permute-start.39 = (bf16[2,192,896]{2,1,0:T(8,128)(2,1)S(1)}, bf16[2,192,896]{2,1,0:T(8,128)(2,1)S(1)}, u32[]{:S(2)}, u32[]{:S(2)}) collective-permute-start(bf16[2,192,896]{2,1,0:T(8,128)(2,1)S(1)} %slice.207), channel_id=1, source_target_pairs={{0,2},{1,3},{2,0},{3,1},{4,6},{5,7},{6,4},{7,5},{8,10},{9,11},{10,... | collective-permute-start | bytes 2064392 | tf_op jit(solution)/shard_map/ppermute | solution.py:681
  254.9 20.0 %collective-permute-start.46 = (bf16[192,896]{1,0:T(8,128)(2,1)S(1)}, bf16[192,896]{1,0:T(8,128)(2,1)S(1)}, u32[]{:S(2)}, u32[]{:S(2)}) collective-permute-start(bf16[192,896]{1,0:T(8,128)(2,1)S(1)} %fusion.38), channel_id=1, source_target_pairs={{0,2},{1,3},{2,0},{3,1},{4,6},{5,7},{6,4},{7,5},{8,10},{9,11},{10,... | collective-permute-start | bytes 1032200 | tf_op jit(solution)/shard_map/ppermute | solution.py:681
  260.3 14.7 %collective-permute-start.45 = (bf16[1,192,896]{2,1,0:T(8,128)(2,1)S(1)}, bf16[1,192,896]{2,1,0:T(8,128)(2,1)S(1)}, u32[]{:S(2)}, u32[]{:S(2)}) collective-permute-start(bf16[1,192,896]{2,1,0:T(8,128)(2,1)S(1)} %get-tuple-element.173), channel_id=1, source_target_pairs={{0,4},{1,5},{2,6},{3,7},{4,0},{5,1},{6,2},{7,3},{8,12},{9,13},{10,... | collective-permute-start | bytes 1032200 | tf_op jit(solution)/shard_map/ppermute | solution.py:681
  267.6 13.4 %collective-permute-start.41 = (bf16[256,768]{1,0:T(8,128)(2,1)S(1)}, bf16[256,768]{1,0:T(8,128)(2,1)S(1)}, u32[]{:S(2)}, u32[]{:S(2)}) collective-permute-start(bf16[256,768]{1,0:T(8,128)(2,1)S(1)} %slice.239), channel_id=1, source_target_pairs={{0,2},{1,3},{2,0},{3,1},{4,6},{5,7},{6,4},{7,5},{8,10},{9,11},{10,... | collective-permute-start | bytes 1179656 | tf_op jit(solution)/shard_map/ppermute | solution.py:681
  269.9 12.5 %collective-permute-start.50 = (bf16[192,1536]{1,0:T(8,128)(2,1)S(1)}, bf16[192,1536]{1,0:T(8,128)(2,1)S(1)}, u32[]{:S(2)}, u32[]{:S(2)}) collective-permute-start(bf16[192,1536]{1,0:T(8,128)(2,1)S(1)} %fusion.14), channel_id=1, source_target_pairs={{0,8},{1,9},{2,10},{3,11},{4,12},{5,13},{6,14},{7,15},{8,0},{9,1},... | collective-permute-start | bytes 1769480 | tf_op jit(solution)/shard_map/ppermute | solution.py:681
  274.9 20.1 %collective-permute-start.42 = (bf16[512,768]{1,0:T(8,128)(2,1)S(1)}, bf16[512,768]{1,0:T(8,128)(2,1)S(1)}, u32[]{:S(2)}, u32[]{:S(2)}) collective-permute-start(bf16[512,768]{1,0:T(8,128)(2,1)S(1)} %get-tuple-element.171), channel_id=1, source_target_pairs={{0,1},{1,0},{2,3},{3,2},{4,5},{5,4},{6,7},{7,6},{8,9},{9,8},{10,11... | collective-permute-start | bytes 2359304 | tf_op jit(solution)/shard_map/ppermute | solution.py:681
  274.9 11.1 %collective-permute-start.44 = (bf16[192,896]{1,0:T(8,128)(2,1)S(1)}, bf16[192,896]{1,0:T(8,128)(2,1)S(1)}, u32[]{:S(2)}, u32[]{:S(2)}) collective-permute-start(bf16[192,896]{1,0:T(8,128)(2,1)S(1)} %fusion.37), channel_id=1, source_target_pairs={{0,4},{1,5},{2,6},{3,7},{4,0},{5,1},{6,2},{7,3},{8,12},{9,13},{10,... | collective-permute-start | bytes 1032200 | tf_op jit(solution)/shard_map/ppermute | solution.py:681
  281.0 13.7 %collective-permute-start.47 = (bf16[192,896]{1,0:T(8,128)(2,1)S(1)}, bf16[192,896]{1,0:T(8,128)(2,1)S(1)}, u32[]{:S(2)}, u32[]{:S(2)}) collective-permute-start(bf16[192,896]{1,0:T(8,128)(2,1)S(1)} %fusion.26), channel_id=1, source_target_pairs={{0,8},{1,9},{2,10},{3,11},{4,12},{5,13},{6,14},{7,15},{8,0},{9,1},... | collective-permute-start | bytes 1032200 | tf_op jit(solution)/shard_map/ppermute | solution.py:681
  283.4 24.4 %collective-permute-start.51 = (bf16[96,1536]{1,0:T(8,128)(2,1)}, bf16[96,1536]{1,0:T(8,128)(2,1)}, u32[]{:S(2)}, u32[]{:S(2)}) collective-permute-start(bf16[96,1536]{1,0:T(8,128)(2,1)} %split.39), channel_id=1, source_target_pairs={{0,16},{1,17},{2,18},{3,19},{4,20},{5,21},{6,22},{7,23},{8,24},{9,... | collective-permute-start | bytes 884744 | tf_op jit(solution)/shard_map/ppermute | solution.py:681
  294.9 9.7 %collective-permute-start.48 = (bf16[96,896]{1,0:T(8,128)(2,1)S(1)}, bf16[96,896]{1,0:T(8,128)(2,1)S(1)}, u32[]{:S(2)}, u32[]{:S(2)}) collective-permute-start(bf16[96,896]{1,0:T(8,128)(2,1)S(1)} %split.40), channel_id=1, source_target_pairs={{0,16},{1,17},{2,18},{3,19},{4,20},{5,21},{6,22},{7,23},{8,24},{9,... | collective-permute-start | bytes 516104 | tf_op jit(solution)/shard_map/ppermute | solution.py:681
  297.9 13.1 %collective-permute-start.43 = (bf16[256,768]{1,0:T(8,128)(2,1)}, bf16[256,768]{1,0:T(8,128)(2,1)}, u32[]{:S(2)}, u32[]{:S(2)}) collective-permute-start(bf16[256,768]{1,0:T(8,128)(2,1)} %slice.300), channel_id=1, source_target_pairs={{0,2},{1,3},{2,0},{3,1},{4,6},{5,7},{6,4},{7,5},{8,10},{9,11},{10,... | collective-permute-start | bytes 1179656 | tf_op jit(solution)/shard_map/ppermute | solution.py:681
  (65 other events, 478.4 us)
